TPU v7x, 32 devices: a whole 2x2x4 slice. The times are simulated.
32 devices in a mesh: req: 16 (over z, y, core), tp: 2 (over x).
Axes of the slice: x: 2, y: 2, z: 4, core: 2. Of those that a mesh axis runs over, the one named last changes fastest.
Arguments:
- tokens: bfloat16 [4096, 2048], P(('req', 'tp')), may hold values from -6 to 6
- norm_gain: float32 [2048], replicated, may hold values from 0.1 to 1.9
- w_query: bfloat16 [2048, 2048], P('req', 'tp'), may hold values from -0.375 to 0.375
- w_kv: bfloat16 [2048, 8, 128], P('req', 'tp'), may hold values from -5 to 5
- w_out: bfloat16 [2048, 2048], P('tp', 'req'), may hold values from -0.125 to 0.125
- kv_cache: bfloat16 [1024, 128, 8, 128], P('req', None, 'tp'), may hold values from -280 to 280
- page_table: int32 [16, 64], P('req'), may hold values from 0 to 63, as said below
- cached_len: int32 [16], replicated, may hold values from 0 to 8192, as said below
- span_len: int32 [16], P('req'), may hold values from 1 to 256, as said below
Outputs:
- update: bfloat16 [4096, 2048], P(('req', 'tp'))
Inputs may be any that keep to these rules, and one draw needn't show every extreme that they name: `page_table`: each row lists pages of the pool block of the request's req index; the 1 row of one index together hold every page of that block exactly once. `cached_len`: some request has 8192 cached tokens and some has none. Tokens from span_len on are padding; some span is full and some holds one token.
All inputs are finite; a program needn't handle non-finite values.
Results may differ from a plain program's by a relative error of at most 0.02.
The roundings to bfloat16 on the way count: a program that leaves them out, or rounds other values in their place, can miss the bound.
Values may be sent and summed in bfloat16 or wider, within the bound.
No kernel may reach another device: no remote copies, remote signals or barrier semaphores. Data moves between devices by JAX's collectives and lax.ppermute only.
A program may use at most 128 MiB of HBM per device.

v0:
```python
import jax
import jax.numpy as jnp
from jax import lax
from jax.sharding import PartitionSpec as P

epsilon = 1e-05
score_scale = 0.015625
residual_scale = 0.22
rope_base = 10000000.0
masked_score = -1e30


def rotate(values, positions):
    half_dim = values.shape[-1] // 2
    frequency = rope_base ** (-(jnp.arange(half_dim, dtype=jnp.float32) * 2.0 / values.shape[-1]))
    angles = positions.astype(jnp.float32)[:, None, None] * frequency[None, None, :]
    cosine = jnp.cos(angles)
    sines = jnp.sin(angles)
    first_half = values[..., :half_dim]
    second = values[..., half_dim:]
    return jnp.concatenate(
        [first_half * cosine - second * sines, second * cosine + first_half * sines], axis=-1
    )


def block_width():
    return 4


def attend_block(softmax_state, query_rows, block_keys, block_values, allowed):
    maximum, running, weighted = softmax_state
    scores = score_scale * jnp.einsum(
        "krd,skd->krs", query_rows, block_keys, preferred_element_type=jnp.float32
    )
    scores = jnp.where(allowed, scores, masked_score)
    new_maximum = jnp.maximum(maximum, jnp.max(scores, axis=-1))
    exponent = jnp.where(allowed, jnp.exp(scores - new_maximum[..., None]), 0.0)
    rescale = jnp.exp(maximum - new_maximum)
    running = running * rescale + jnp.sum(exponent, axis=-1)
    weighted = weighted * rescale[..., None] + jnp.einsum(
        "krs,skd->krd",
        exponent.astype(jnp.bfloat16),
        block_values,
        preferred_element_type=jnp.float32,
    )
    return (new_maximum, running, weighted)


def page_pass(softmax_state, query_rows, length, live_pages, block_pages, fetcher):
    blocks = (live_pages + block_pages - 1) // block_pages

    def advance(block_index, carry):
        page_block, logical = fetcher(block_index)
        page_len = page_block.shape[1]
        head_dim = page_block.shape[3] // 2
        flat_rows = page_block.reshape(
            block_pages * page_len, page_block.shape[2], page_block.shape[3]
        )
        positions = (
            logical[:, None] * page_len + jnp.arange(page_len, dtype=jnp.int32)[None, :]
        ).reshape(-1)
        allowed = (positions < length)[None, None, :]
        return attend_block(
            carry, query_rows, flat_rows[..., :head_dim], flat_rows[..., head_dim:], allowed
        )

    return lax.fori_loop(0, blocks, advance, softmax_state)


def own_fetch(table_row, pool_cache, block_pages, stride, offset):

    def fetcher(block_index):
        logical = (
            block_index * block_pages + jnp.arange(block_pages, dtype=jnp.int32)
        ) * stride + offset
        return (jnp.take(pool_cache, table_row[logical], axis=0), logical)

    return fetcher


def empty_state(kv_heads, query_count, head_dim):
    return (
        jnp.full((kv_heads, query_count), masked_score, jnp.float32),
        jnp.zeros((kv_heads, query_count), jnp.float32),
        jnp.zeros((kv_heads, query_count, head_dim), jnp.float32),
    )


def finish(softmax_state, valid_len, span_rows, kv_heads, group_size, head_dim):
    maximum, running, weighted = softmax_state
    result = weighted / running[..., None]
    result = jnp.transpose(
        result.reshape(kv_heads, span_rows, group_size, head_dim), (1, 0, 2, 3)
    ).reshape(span_rows, -1)
    keep_rows = jnp.arange(span_rows) < valid_len
    return jnp.where(keep_rows[:, None], result, 0.0).astype(jnp.bfloat16)


def body(tokens, norm_gain, w_query, w_kv, w_out, kv_cache, page_table, cached_len, span_len):
    whole = lax.all_gather(tokens, "tp", axis=0, tiled=True)
    hidden = whole.astype(jnp.float32)
    normed = (
        hidden * lax.rsqrt(jnp.mean(hidden * hidden, axis=-1, keepdims=True) + epsilon) * norm_gain
    ).astype(jnp.bfloat16)
    tok_rows = normed.shape[0]
    requests = page_table.shape[0]
    span_rows = tok_rows // requests
    page_len = kv_cache.shape[1]
    kv_heads = w_kv.shape[1]
    head_dim = w_kv.shape[2] // 2
    query_heads = w_query.shape[1] // head_dim
    group_size = query_heads // kv_heads
    query_count = span_rows * group_size
    pieces = (
        lax.all_gather(w_query, "req", axis=0, tiled=True),
        lax.all_gather(w_kv, "req", axis=0, tiled=True),
    )
    row_count = pieces[0].shape[0]
    projected = jnp.dot(normed, pieces[0], preferred_element_type=jnp.float32)
    key_value = jnp.dot(
        normed, pieces[1].reshape(row_count, -1), preferred_element_type=jnp.float32
    )
    device = lax.axis_index("req")
    own_lengths = lax.dynamic_slice_in_dim(cached_len, device * requests, requests)
    offsets = jnp.arange(span_rows, dtype=jnp.int32)
    token_pos = jnp.arange(query_count, dtype=jnp.int32) // group_size
    member = 0
    length = own_lengths[member]
    valid_len = span_len[member]
    positions = length + offsets
    query_block = projected.reshape(span_rows, query_heads, head_dim)
    query_rot = rotate(query_block, positions).astype(jnp.bfloat16)
    query_rows = jnp.transpose(
        query_rot.reshape(span_rows, kv_heads, group_size, head_dim), (1, 0, 2, 3)
    ).reshape(kv_heads, query_count, head_dim)
    pair_block = key_value.reshape(span_rows, kv_heads, 2 * head_dim)
    new_keys = rotate(pair_block[..., :head_dim], positions).astype(jnp.bfloat16)
    new_values = pair_block[..., head_dim:].astype(jnp.bfloat16)
    allowed = (offsets[None, :] <= token_pos[:, None]) & (offsets[None, :] < valid_len)
    softmax_state = attend_block(
        empty_state(kv_heads, query_count, head_dim),
        query_rows,
        new_keys,
        new_values,
        allowed[None],
    )
    query_sets = [query_rows]
    states = [softmax_state]
    block_pages = block_width()
    member = 0
    length = own_lengths[member]
    live_pages = (length + page_len - 1) // page_len
    softmax_state = page_pass(
        states[member],
        query_sets[member],
        length,
        live_pages,
        block_pages,
        own_fetch(page_table[member], kv_cache, block_pages, 1, 0),
    )
    outputs = finish(softmax_state, span_len[member], span_rows, kv_heads, group_size, head_dim)
    partial_value = jnp.dot(
        outputs,
        lax.all_gather(w_out, "req", axis=1, tiled=True),
        preferred_element_type=jnp.float32,
    )
    summed = lax.psum_scatter(
        partial_value.astype(jnp.bfloat16), "tp", scatter_dimension=0, tiled=True
    ).astype(jnp.float32)
    return (residual_scale * summed).astype(jnp.bfloat16)


def solution(mesh):
    in_specs = (
        P(("req", "tp"), None),
        P(),
        P("req", "tp"),
        P("req", "tp", None),
        P("tp", "req"),
        P("req", None, "tp", None),
        P("req", None),
        P(),
        P("req"),
    )
    out_specs = P(("req", "tp"), None)
    return jax.shard_map(body, mesh=mesh, in_specs=in_specs, out_specs=out_specs, check_vma=False)
```

profile of v0, /device:TPU:24, one launch (start us, length us, event | category | flops | bytes accessed | tf_op | source)
XLA Modules:
  0.0 373.5 jit_solution(18265152549506895060)
XLA Ops:
  6.5 0.7 all-gather.5.cloned.1.call-update
  7.3 0.7 all-gather.9.cloned.1.call-update
  8.1 0.7 all-gather.7.cloned.1.call-update
  8.8 0.5 all-gather.11.cloned.1.call-update
  9.4 1.3 dynamic_slice.3
  10.7 0.7 add_convert_fusion.2
  12.8 0.2 multiply_cosine_fusion
  13.0 0.2 fusion.36
  13.3 17.9 %all-gather.5.cloned.1.call-done = bf16[256,2048]{1,0:T(8,128)(2,1)} async-done(((bf16[128,2048]{1,0:T(8,128)(2,1)}), bf16[256,2048]{1,0:T(8,128)(2,1)}) %all-gather.5.cloned.1.call-update) | async-done | bytes 1048592 | tf_op jit(solution)/shard_map/all_gather | solution.py:100
  31.2 1.6 fusion.23
  32.8 40.8 %all-gather.9.cloned.1.call-done = bf16[2048,4,128]{2,1,0:T(4,128)(2,1)} async-done(((bf16[128,4,128]{2,1,0:T(4,128)(2,1)}), bf16[2048,4,128]{2,1,0:T(4,128)(2,1)}) %all-gather.9.cloned.1.call-update) | async-done | bytes 2097168 | tf_op jit(solution)/shard_map/all_gather | solution.py:116
  73.5 3.0 copy.45
  76.5 0.8 fusion.26
  77.4 0.8 copy-done.3
  78.1 0.7 subtract_convert_fusion.1
  78.8 45.9 %all-gather.7.cloned.1.call-done = bf16[2048,1024]{1,0:T(8,128)(2,1)} async-done(((bf16[128,1024]{1,0:T(8,128)(2,1)}), bf16[2048,1024]{1,0:T(8,128)(2,1)}) %all-gather.7.cloned.1.call-update) | async-done | bytes 4194320 | tf_op jit(solution)/shard_map/all_gather | solution.py:115
  124.6 4.0 %fusion.38 = f32[256,1024]{0,1:T(8,128)S(1)} fusion(bf16[2048,1024]{1,0:T(8,128)(2,1)} %all-gather.7.cloned.1.call-done, bf16[256,2048]{1,0:T(8,128)(2,1)S(1)} %copy-done.1, f32[2048]{0:T(1024)S(1)} %copy-done.5, f32[256]{0:T(256)S(1)} %add_rsqrt_fusion), kind=kOutput, calls=%fused_computation.60 | convolution fusion | flops 1075838976 | bytes 6300672 | tf_op jit(solution)/shard_map/dot_general | solution.py:119
  128.7 0.2 subtract_convert_fusion
  128.8 0.6 copy.32
  129.5 0.6 copy.33
  130.1 1.4 pad_maximum_fusion
  131.6 0.3 copy.37
  131.9 0.9 fusion.20
  132.8 1.1 fusion.22
  134.0 1.3 fusion.31
  135.3 25.6 %while.14 = (s32[]{:T(128)}, f32[4,1024]{1,0:T(4,128)S(1)}, f32[4,1024]{1,0:T(4,128)S(1)}, f32[4,1024,64]{1,2,0:T(8,128)S(1)}, s32[]{:T(128)}, /*index=5*/s32[]{...) while((s32[]{:T(128)}, f32[4,1024]{1,0:T(4,128)S(1)}, ...), condition=%wide.region_6.7_spmd, body=%wide.region_3.6_spmd.sunk | while | flops 564931648 | bytes 31731532 | solution.py:67
  135.5 0.6 gather_fusion
  136.1 4.4 %gather_fusion.1 = bf16[4,128,4,128]{3,2,1,0:T(4,128)(2,1)S(1)} fusion(bf16[64,128,4,128]{3,2,1,0:T(4,128)(2,1)} %get-tuple-element.199, s32[1024]{0:T(1024)S(1)} %pad_clamp_fusion.5), kind=kCustom, calls=%fused_computation.1.clone.1 | custom fusion | bytes 1048592 | tf_op jit(solution)/shard_map/while/body/jit(_take)/gather | solution.py:76
  140.5 0.3 copy.47
  141.0 0.8 fusion.68
  141.8 1.6 bitcast_reduce_fusion.2
  143.4 2.6 fusion.71
  146.0 2.1 fusion.72
  148.2 0.6 gather_fusion
  148.8 4.4 %gather_fusion.1 = bf16[4,128,4,128]{3,2,1,0:T(4,128)(2,1)S(1)} fusion(bf16[64,128,4,128]{3,2,1,0:T(4,128)(2,1)} %get-tuple-element.199, s32[1024]{0:T(1024)S(1)} %pad_clamp_fusion.5), kind=kCustom, calls=%fused_computation.1.clone.1 | custom fusion | bytes 1048592 | tf_op jit(solution)/shard_map/while/body/jit(_take)/gather | solution.py:76
  153.2 0.3 copy.47
  153.7 0.8 fusion.68
  154.5 1.6 bitcast_reduce_fusion.2
  156.1 2.6 fusion.71
  158.7 2.1 fusion.72
  160.8 0.1 broadcast_divide_fusion
  160.9 0.5 copy.38
  161.4 0.5 copy.39
  162.0 0.1 fusion.34
  162.1 15.2 %all-gather.11.cloned.1.call-done = bf16[1024,2048]{1,0:T(8,128)(2,1)} async-done(((bf16[1024,128]{1,0:T(8,128)(2,1)}), bf16[1024,2048]{1,0:T(8,128)(2,1)}) %all-gather.11.cloned.1.call-update) | async-done | bytes 4194320 | tf_op jit(solution)/shard_map/all_gather | solution.py:164
  177.3 4.4 %convolution_convert_fusion = bf16[256,2048]{1,0:T(8,128)(2,1)} fusion(bf16[256,1024]{0,1:T(8,128)(2,1)S(1)} %fusion.34, bf16[1024,2048]{1,0:T(8,128)(2,1)} %all-gather.11.cloned.1.call-done), kind=kOutput, calls=%fused_computation.41 | convolution fusion | flops 1074266112 | bytes 5767168 | tf_op jit(solution)/shard_map/dot_general | solution.py:162
  181.7 183.3 %reduce-scatter.2.cloned.1.call-done = bf16[128,2048]{1,0:T(8,128)(2,1)} async-done(((bf16[256,2048]{1,0:T(8,128)(2,1)}), bf16[128,2048]{1,0:T(8,128)(2,1)}) %reduce-scatter.2.cloned.1.call-update) | async-done | bytes 524304 | tf_op jit(solution)/shard_map/reduce_scatter | solution.py:167
  365.0 1.9 multiply_convert_fusion
  (45 shorter events, 0.7 us)
Async XLA Ops:
  6.5 70.0 %copy-start.5 = (f32[2048]{0:T(1024)S(1)}, f32[2048]{0:T(1024)}, u32[]{:S(2)}) copy-start(f32[2048]{0:T(1024)} %param.12) | copy-start | bytes 24580
  6.5 24.6 %all-gather.5.cloned.1.call-start = ((), (), s32[]{:S(2)}) async-start(), calls=%async_computation.1 | async-start | bytes 1572864 | tf_op jit(solution)/shard_map/all_gather | solution.py:100
  7.3 66.3 %all-gather.9.cloned.1.call-start = ((), (), s32[]{:S(2)}) async-start(), calls=%async_computation.3 | async-start | bytes 2228224 | tf_op jit(solution)/shard_map/all_gather | solution.py:116
  8.0 116.6 %all-gather.7.cloned.1.call-start = ((), (), s32[]{:S(2)}) async-start(), calls=%async_computation.2 | async-start | bytes 4456448 | tf_op jit(solution)/shard_map/all_gather | solution.py:115
  8.7 168.5 %all-gather.11.cloned.1.call-start = ((), (), s32[]{:S(2)}) async-start(), calls=%async_computation.4 | async-start | bytes 4456448 | tf_op jit(solution)/shard_map/all_gather | solution.py:164
  9.3 355.7 %reduce-scatter.2.cloned.1.call-start = ((), (), s32[]{:S(2)}) async-start(), calls=%async_computation.5 | async-start | bytes 1572864 | tf_op jit(solution)/shard_map/reduce_scatter | solution.py:167
  31.2 45.4 %copy-start.1 = (bf16[256,2048]{1,0:T(8,128)(2,1)S(1)}, bf16[256,2048]{1,0:T(8,128)(2,1)}, u32[]{:S(2)}) copy-start(bf16[256,2048]{1,0:T(8,128)(2,1)} %all-gather.5.cloned.1.call-done) | copy-start | bytes 3145732
  77.3 0.8 copy-start.3
  128.8 3.1 copy-start.2
  131.9 2.1 copy-start.4
  133.9 1.3 copy-start
Sparse Core Ops, SparseCore 0:
  8.9 22.2 all-gather.4
  33.3 40.1 all-gather.8
  75.7 48.8 all-gather.6
  126.7 50.5 all-gather.10
  181.9 183.1 reduce-scatter.1
where the time goes:
time: 376 us; the launch traced here: 373 us
  waiting for transfers between devices  306 us (81%)
  matrix products  18.9 us (5%)
  local copies, waits for them, and re-layouts  18.5 us (5%)
  other arithmetic  15.1 us (4%)
  between operations  14.8 us (4%)
    reduce_scatter x1, waiting for transfers between devices, body(): lax.psum_scatter(partial_value.astype(jnp.bfloat16), 'tp', scatter_dimens...  183 us
    all_gather x1, waiting for transfers between devices, body(): lax.all_gather(w_query, 'req', axis=0, tiled=True)  45.9 us
    all_gather x1, waiting for transfers between devices, body(): lax.all_gather(w_kv, 'req', axis=0, tiled=True)  40.8 us
    all_gather x1, waiting for transfers between devices, body(): whole = lax.all_gather(tokens, 'tp', axis=0, tiled=True)  17.9 us
    all_gather x1, waiting for transfers between devices, body(): lax.all_gather(w_out, 'req', axis=1, tiled=True)  15.2 us
    gather x6, local copies, waits for them, and re-layouts, fetcher(): return (jnp.take(pool_cache, table_row[logical], axis=0), logical)  10.7 us
  transfers between devices with their start and end apart: 5, of which 5 were waited for; matrix products, arithmetic and copies ran while one was open for 12% of the time, Pallas kernels for 0%

commit v1 on v0

v1 whole, which is shorter than its diff:
```python
import functools

import jax
import jax.numpy as jnp
from jax import lax
from jax.experimental import pallas as pl
from jax.experimental.pallas import tpu as pltpu
from jax.sharding import PartitionSpec as P

epsilon = 1e-05
score_scale = 0.015625
residual_scale = 0.22
rope_base = 10000000.0
masked_score = -1e30
key_block = 1024
score_chunk = 256
value_chunk = 256
token_tile = 128
vmem_limit = 60 * 1024 * 1024


def matmul(a, b):
    return jnp.dot(a, b, preferred_element_type=jnp.float32)


def vmem():
    return pl.BlockSpec(memory_space=pltpu.VMEM)


def smem():
    return pl.BlockSpec(memory_space=pltpu.SMEM)


def params():
    return pltpu.CompilerParams(vmem_limit_bytes=vmem_limit)


def cycle_tables(count):
    depth = count // 4
    walk = [(z, 0) for z in range(depth)] + [(z, 1) for z in reversed(range(depth))]
    device = lambda chip, core: (chip[0] * 2 + chip[1]) * 2 + core
    length = len(walk)
    ahead = [
        (device(walk[k], c), device(walk[(k + 1) % length], c))
        for k in range(length)
        for c in range(2)
    ]
    back = [(b, a) for a, b in ahead]
    swap = [(i, i ^ 1) for i in range(count)]
    order = [None] * count
    for k in range(length):
        for c in range(2):
            row = []
            for step in range(length // 2):
                sources = [walk[(k - step) % length], walk[(k + step) % length]]
                for chip in sources[: 1 if step == 0 else 2]:
                    row += [device(chip, c), device(chip, 1 - c)]
            far = walk[(k + length // 2) % length]
            row += [device(far, c), device(far, 1 - c)]
            order[device(walk[k], c)] = row
    return ahead, back, swap, order


def ring_gather(shard, tables, after=None):
    ahead, back, swap, order = tables
    move = lambda value, pairs: lax.ppermute(value, "req", pairs)
    length = len(order) // 2
    half = shard.shape[0] // 2
    blocks = [shard, move(shard, swap)]
    up = down = shard
    for _ in range(length // 2 - 1):
        up, down = move(up, ahead), move(down, back)
        blocks += [up, move(up, swap), down, move(down, swap)]
    first, second = move(up[:half], ahead), move(down[half:], back)
    return blocks, [first, second, move(first, swap), move(second, swap)]


def prepare_kernel(heads, page, width, pages_step, table_ref, length_ref, *refs):
    pages = refs[:pages_step]
    key_ref, value_ref, wide = refs[pages_step:]
    step = pl.program_id(0)
    half = width // 2
    for i in range(pages_step):
        wide[...] = pages[i][0].astype(jnp.float32)
        first = (step * pages_step + i) * page
        position = first + lax.broadcasted_iota(jnp.int32, (page, width), 0)
        lane = lax.broadcasted_iota(jnp.int32, (page, width), 1)
        bias = jnp.where((lane == half) & (position >= length_ref[0]), masked_score, 0.0)
        for h in range(heads):
            rows = wide[pl.ds(h, page, stride=heads), :]
            key_ref[h, pl.ds(i * page, page), :] = jnp.where(lane < half, rows, bias).astype(
                jnp.bfloat16
            )
            turned = jnp.transpose(rows)[half:]
            value_ref[h, :, pl.ds(i * page, page)] = with_ones(turned).astype(jnp.bfloat16)


def with_ones(turned):
    row = lax.broadcasted_iota(jnp.int32, (16, turned.shape[1]), 0)
    return jnp.concatenate([turned, jnp.where(row == 0, 1.0, 0.0)], axis=0)


def prepare(cache, table, length):
    pages, page, heads, width = cache.shape
    pages_step = 4
    rows = width // 2 + 16
    flat = cache.reshape(pages, page * heads, width)
    page_spec = lambda i: pl.BlockSpec(
        (1, page * heads, width), lambda j, t, n: (t[j * pages_step + i], 0, 0)
    )
    return pl.pallas_call(
        functools.partial(prepare_kernel, heads, page, width, pages_step),
        grid_spec=pltpu.PrefetchScalarGridSpec(
            num_scalar_prefetch=2,
            grid=(table.shape[0] // pages_step,),
            in_specs=[page_spec(i) for i in range(pages_step)],
            out_specs=[
                pl.BlockSpec((heads, pages_step * page, width), lambda j, t, n: (0, j, 0)),
                pl.BlockSpec((heads, rows, pages_step * page), lambda j, t, n: (0, 0, j)),
            ],
            scratch_shapes=[pltpu.VMEM((page * heads, width), jnp.float32)],
        ),
        out_shape=[
            jax.ShapeDtypeStruct((heads, table.shape[0] * page, width), jnp.bfloat16),
            jax.ShapeDtypeStruct((heads, rows, table.shape[0] * page), jnp.bfloat16),
        ],
        cost_estimate=pl.CostEstimate(
            flops=0, bytes_accessed=4 * cache.size * cache.dtype.itemsize, transcendentals=0
        ),
        compiler_params=params(),
        name="prepare",
    )(table, length, *([flat] * pages_step))


def turn(pair, cosine, sines):
    half = pair.shape[0] // 2
    first, second = pair[:half], pair[half:]
    return jnp.concatenate(
        [first * cosine - second * sines, second * cosine + first * sines], axis=0
    )


def project_kernel(heads, group, dim, blocks, order_ref, *refs):
    chunks = refs[:blocks]
    normed_ref, cos_ref, sin_ref, query_ref, key_ref, value_ref, weight = refs[blocks:]
    rows = weight.shape[0] // order_ref.shape[0]
    if blocks == 1:
        source = chunks[0]
    else:
        source = weight
        for k in range(order_ref.shape[0]):
            start = pl.multiple_of(order_ref[k] * rows, rows)
            if k < order_ref.shape[0] - 2:
                weight[pl.ds(start, rows), :] = chunks[k][...]
            else:
                at = order_ref.shape[0] - 2 + 2 * (k - (order_ref.shape[0] - 2))
                weight[pl.ds(start, rows), :] = jnp.concatenate(
                    [chunks[at][...], chunks[at + 1][...]], axis=0
                )
    cosine, sines = cos_ref[...], sin_ref[...]
    tokens = cosine.shape[1]
    normed = normed_ref[...]
    width = group * dim
    for h in range(heads):
        turned = jnp.transpose(matmul(normed, source[:, pl.ds(h * width, width)]))
        for g in range(group):
            rotated = turn(turned[g * dim : (g + 1) * dim], cosine, sines).astype(jnp.bfloat16)
            scaled = (rotated.astype(jnp.float32) * score_scale).astype(jnp.bfloat16)
            for q in range(tokens // token_tile):
                query_ref[h, q, pl.ds(0, dim), pl.ds(g * token_tile, token_tile)] = scaled[
                    :, q * token_tile : (q + 1) * token_tile
                ]
        row = lax.broadcasted_iota(jnp.int32, (dim, group * token_tile), 0)
        for q in range(tokens // token_tile):
            query_ref[h, q, pl.ds(dim, dim), :] = jnp.where(row == 0, 1.0, 0.0).astype(jnp.bfloat16)
    for h in range(heads):
        at = heads * width + h * 2 * dim
        turned = jnp.transpose(matmul(normed, source[:, pl.ds(at, 2 * dim)]))
        keys = turn(turned[:dim], cosine, sines)
        padded = jnp.concatenate([keys, jnp.zeros_like(keys)], axis=0)
        key_ref[h] = jnp.transpose(padded).astype(jnp.bfloat16)
        value_ref[h] = with_ones(turned[dim:]).astype(jnp.bfloat16)


def project(normed, chunks, order, cosine, sines, heads, group, dim):
    tokens, width = normed.shape
    columns = chunks[0].shape[1]
    return pl.pallas_call(
        functools.partial(project_kernel, heads, group, dim, len(chunks)),
        in_specs=[smem()] + [vmem()] * (len(chunks) + 3),
        out_specs=[vmem()] * 3,
        out_shape=[
            jax.ShapeDtypeStruct(
                (heads, tokens // token_tile, 2 * dim, group * token_tile), jnp.bfloat16
            ),
            jax.ShapeDtypeStruct((heads, tokens, 2 * dim), jnp.bfloat16),
            jax.ShapeDtypeStruct((heads, dim + 16, tokens), jnp.bfloat16),
        ],
        scratch_shapes=[pltpu.VMEM((width, columns), jnp.bfloat16)],
        cost_estimate=pl.CostEstimate(
            flops=2 * tokens * width * columns,
            bytes_accessed=2 * width * columns,
            transcendentals=0,
        ),
        compiler_params=params(),
        name="project",
    )(order, *chunks, normed, cosine, sines)


def attend_kernel(
    group,
    dim,
    length_ref,
    span_ref,
    key_ref,
    value_ref,
    query_ref,
    new_key_ref,
    new_value_ref,
    out_ref,
    even,
    odd,
):
    lanes = query_ref.shape[3]
    span = new_key_ref.shape[1]
    length = length_ref[0]
    valid = span_ref[0]
    pair = 2 * key_block
    pairs = (length + pair - 1) // pair
    last_block = jnp.maximum(2 * pairs - 1, 0)

    def column_max(scores):
        return jnp.max(scores.reshape(scores.shape[0] // 8, 8, lanes), axis=0)

    def tile(q, _):
        def scores_of(block, c, target):
            start = pl.multiple_of(block * key_block + c * score_chunk, score_chunk)
            scores = matmul(key_ref[0, pl.ds(start, score_chunk), :], query_ref[0, q])
            target[pl.ds(c * score_chunk, score_chunk), :] = scores
            return column_max(scores)

        scores = matmul(new_key_ref[0], query_ref[0, q])
        source = lax.broadcasted_iota(jnp.int32, (span, lanes), 0)
        lane = lax.broadcasted_iota(jnp.int32, (span, lanes), 1)
        token = q * token_tile + lax.rem(lane, token_tile)
        scores = jnp.where((source <= token) & (source < valid), scores, masked_score)
        maximum = jnp.max(column_max(scores), axis=0, keepdims=True)
        weights = jnp.exp(scores - maximum).astype(jnp.bfloat16)
        total = matmul(new_value_ref[0], weights)

        top = scores_of(0, 0, even)
        for c in range(1, key_block // score_chunk):
            top = jnp.maximum(top, scores_of(0, c, even))

        def half(block, following, current, target, state):
            maximum, top, total = state
            new_maximum = jnp.maximum(maximum, jnp.max(top, axis=0, keepdims=True))
            total = total * jnp.exp(maximum - new_maximum)
            next_top = None
            ratio = value_chunk // score_chunk
            parts = []
            for c in range(key_block // score_chunk):
                seen = scores_of(following, c, target)
                next_top = seen if next_top is None else jnp.maximum(next_top, seen)
                part = jnp.exp(current[pl.ds(c * score_chunk, score_chunk), :] - new_maximum)
                parts.append(part.astype(jnp.bfloat16))
                if len(parts) == ratio:
                    weights = parts[0] if ratio == 1 else jnp.concatenate(parts, axis=0)
                    start = block * key_block + (c + 1 - ratio) * score_chunk
                    start = pl.multiple_of(start, value_chunk)
                    total = total + matmul(value_ref[0, :, pl.ds(start, value_chunk)], weights)
                    parts = []
            return new_maximum, next_top, total

        def advance(i, state):
            block = 2 * i
            state = half(block, block + 1, even, odd, state)
            following = jnp.minimum(block + 2, last_block)
            return half(block + 1, following, odd, even, state)

        _, _, total = lax.fori_loop(0, pairs, advance, (maximum, top, total))
        result = total[:dim] / total[dim : dim + 1]
        row = q * token_tile + lax.broadcasted_iota(jnp.int32, (token_tile, 2 * dim), 0)
        for g in range(0, group, 2):
            both = jnp.concatenate(
                [
                    result[:, g * token_tile : (g + 1) * token_tile],
                    result[:, (g + 1) * token_tile : (g + 2) * token_tile],
                ],
                axis=0,
            )
            kept = jnp.where(row < valid, jnp.transpose(both), 0.0)
            out_ref[pl.ds(pl.multiple_of(q * token_tile, token_tile), token_tile), pl.ds(g * dim, 2 * dim)] = (
                kept.astype(jnp.bfloat16)
            )
        return 0

    tiles = (valid + token_tile - 1) // token_tile
    out_ref[...] = jnp.zeros_like(out_ref)
    lax.fori_loop(0, tiles, tile, 0)


def attend(head, keys, values, queries, new_keys, new_values, length, valid):
    _, cached, width = keys.shape
    dim = width // 2
    _, tiles, _, lanes = queries.shape
    group = lanes // token_tile
    tokens = tiles * token_tile
    block = lambda array: pl.BlockSpec(
        (1,) + array.shape[1:], lambda i: (head,) + (0,) * (array.ndim - 1)
    )
    arrays = (keys, values, queries, new_keys, new_values)
    return pl.pallas_call(
        functools.partial(attend_kernel, group, dim),
        grid=(1,),
        in_specs=[smem(), smem()] + [block(a) for a in arrays],
        out_specs=pl.BlockSpec((tokens, group * dim), lambda i: (0, 0)),
        out_shape=jax.ShapeDtypeStruct((tokens, group * dim), jnp.bfloat16),
        scratch_shapes=[pltpu.VMEM((key_block, lanes), jnp.float32)] * 2,
        cost_estimate=pl.CostEstimate(
            flops=2 * cached * tokens * group * 2 * width,
            bytes_accessed=2 * cached * 2 * width,
            transcendentals=cached * tokens * group,
        ),
        compiler_params=params(),
        name="attend",
    )(length, valid, *arrays)


def emit_kernel(heads, blocks, start_ref, *refs):
    parts = refs[:heads]
    chunks = refs[heads : heads + blocks]
    out_ref = refs[heads + blocks]
    rows = out_ref.shape[1]
    start = pl.multiple_of(start_ref[0], rows)
    attended = jnp.concatenate([p[pl.ds(start, rows), :] for p in parts], axis=1)
    count = out_ref.shape[0]
    for k in range(0, count, 2):
        if k < count - 2:
            weight = jnp.concatenate([chunks[k][...], chunks[k + 1][...]], axis=1)
        else:
            at = count - 2
            own = jnp.concatenate([chunks[at][...], chunks[at + 1][...]], axis=0)
            other = jnp.concatenate([chunks[at + 2][...], chunks[at + 3][...]], axis=0)
            weight = jnp.concatenate([own, other], axis=1)
        both = matmul(attended, weight).astype(jnp.bfloat16)
        width = both.shape[1] // 2
        out_ref[k] = both[:, :width]
        out_ref[k + 1] = both[:, width:]


def emit(parts, chunks, start, rows, count):
    columns = chunks[0].shape[1]
    depth = chunks[0].shape[0]
    return pl.pallas_call(
        functools.partial(emit_kernel, len(parts), len(chunks)),
        in_specs=[smem()] + [vmem()] * (len(parts) + len(chunks)),
        out_specs=vmem(),
        out_shape=jax.ShapeDtypeStruct((count, rows, columns), jnp.bfloat16),
        cost_estimate=pl.CostEstimate(
            flops=2 * rows * depth * columns * count,
            bytes_accessed=2 * depth * columns * count,
            transcendentals=0,
        ),
        compiler_params=params(),
        name="emit",
    )(start, *parts, *chunks)


def combine_kernel(order_ref, own_ref, other_ref, out_ref):
    width = own_ref.shape[2]
    for k in range(own_ref.shape[0]):
        summed = own_ref[k].astype(jnp.float32) + other_ref[k].astype(jnp.float32)
        start = pl.multiple_of(order_ref[k] * width, width)
        out_ref[:, pl.ds(start, width)] = (residual_scale * summed).astype(jnp.bfloat16)


def combine(own, other, order):
    count, rows, columns = own.shape
    return pl.pallas_call(
        combine_kernel,
        in_specs=[smem(), vmem(), vmem()],
        out_specs=vmem(),
        out_shape=jax.ShapeDtypeStruct((rows, count * columns), jnp.bfloat16),
        compiler_params=params(),
        name="combine",
    )(order, own, other)


def rope_tables(positions, dim):
    half_dim = dim // 2
    frequency = rope_base ** (-(jnp.arange(half_dim, dtype=jnp.float32) * 2.0 / dim))
    angles = positions.astype(jnp.float32)[None, :] * frequency[:, None]
    return jnp.cos(angles), jnp.sin(angles)


def body(req_count, tp_count, tokens, norm_gain, w_query, w_kv, w_out, kv_cache, page_table, cached_len, span_len):
    fast = tp_count == 2 and req_count == 16 and w_out.shape[1] % 128 == 0
    device = lax.axis_index("req")
    rank = lax.axis_index("tp")
    heads = w_kv.shape[1]
    dim = w_kv.shape[2] // 2
    group = w_query.shape[1] // dim // heads
    own_rows = tokens.shape[0]
    weights = jnp.concatenate([w_query, w_kv.reshape(w_kv.shape[0], -1)], axis=1)
    if fast:
        tables = cycle_tables(req_count)
        order = jnp.array(tables[3], jnp.int32)[device]
        blocks, ends = ring_gather(weights, tables)
        other = lax.ppermute(tokens, "tp", [(0, 1), (1, 0)])
        whole = jnp.concatenate(
            [jnp.where(rank == 0, tokens, other), jnp.where(rank == 0, other, tokens)], axis=0
        )
        chunks = blocks + ends
    else:
        order = jnp.zeros((1,), jnp.int32)
        chunks = [lax.all_gather(weights, "req", axis=0, tiled=True)]
        whole = lax.all_gather(tokens, "tp", axis=0, tiled=True)
    hidden = whole.astype(jnp.float32)
    normed = (
        hidden * lax.rsqrt(jnp.mean(hidden * hidden, axis=-1, keepdims=True) + epsilon) * norm_gain
    ).astype(jnp.bfloat16)
    length = lax.dynamic_slice_in_dim(cached_len, device, 1)
    positions = length[0] + jnp.arange(normed.shape[0], dtype=jnp.int32)
    cosine, sines = rope_tables(positions, dim)
    keys, values = prepare(kv_cache, page_table[0], length)
    queries, new_keys, new_values = project(
        normed, chunks, order, cosine, sines, heads, group, dim
    )
    parts = [
        attend(h, keys, values, queries, new_keys, new_values, length, span_len)
        for h in range(heads)
    ]
    if not fast:
        attended = jnp.concatenate(parts, axis=1)
        gathered = lax.all_gather(w_out, "req", axis=1, tiled=True)
        partial = matmul(attended, gathered).astype(jnp.bfloat16)
        summed = lax.psum_scatter(partial, "tp", scatter_dimension=0, tiled=True)
        return (residual_scale * summed.astype(jnp.float32)).astype(jnp.bfloat16)
    blocks, ends = ring_gather(w_out, tables)
    chunks = blocks + ends
    theirs = emit(parts, chunks, ((1 - rank) * own_rows).reshape(1), own_rows, req_count)
    received = lax.ppermute(theirs, "tp", [(0, 1), (1, 0)])
    ours = emit(parts, chunks, (rank * own_rows).reshape(1), own_rows, req_count)
    return combine(ours, received, order)


def solution(mesh):
    in_specs = (
        P(("req", "tp"), None),
        P(),
        P("req", "tp"),
        P("req", "tp", None),
        P("tp", "req"),
        P("req", None, "tp", None),
        P("req", None),
        P(),
        P("req"),
    )
    out_specs = P(("req", "tp"), None)
    program = functools.partial(body, mesh.shape["req"], mesh.shape["tp"])
    return jax.shard_map(
        program, mesh=mesh, in_specs=in_specs, out_specs=out_specs, check_vma=False
    )
```

time: 376 us -> 164 us (0.44)
  the two profiles are of different devices: /device:TPU:24 before, /device:TPU:17 now
where the time goes in v1:
time: 164 us; the launch traced here: 162 us
  Pallas kernels  95.5 us (58%)
  starting transfers between devices  28.8 us (18%)
  waiting for transfers between devices  25.1 us (15%)
  local copies, waits for them, and re-layouts  8.42 us (5%)
  other arithmetic  3.04 us (2%)
    pallas_call x4, Pallas kernels, attend(): pl.pallas_call(functools.partial(attend_kernel, group, dim), grid=(1,), i...  60 us
    ppermute x34, starting transfers between devices, ring_gather(): move = lambda value, pairs: lax.ppermute(value, 'req', pairs)  27.3 us
    ppermute x34, waiting for transfers between devices, ring_gather(): move = lambda value, pairs: lax.ppermute(value, 'req', pairs)  20.9 us
    pallas_call x1, Pallas kernels, prepare(): pl.pallas_call(functools.partial(prepare_kernel, heads, page, width, page...  18.5 us
    pallas_call x2, Pallas kernels, emit(): pl.pallas_call(functools.partial(emit_kernel, len(parts), len(chunks)), i...  7.71 us
    pallas_call x1, Pallas kernels, project(): pl.pallas_call(functools.partial(project_kernel, heads, group, dim, len(c...  7.12 us
    ppermute x1, waiting for transfers between devices, body(): received = lax.ppermute(theirs, 'tp', [(0, 1), (1, 0)])  4.13 us
    unnamed x65, local copies, waits for them, and re-layouts  3.5 us
  transfers between devices with their start and end apart: 36, of which 5 were waited for; matrix products, arithmetic and copies ran while one was open for 4% of the time, Pallas kernels for 55%

profile of v1, /device:TPU:17, one launch (start us, length us, event | category | flops | bytes accessed | tf_op | source)
XLA Modules:
  0.0 161.8 jit_solution(367247348588537965)
XLA Ops:
  0.0 1.0 constant_dynamic-update-slice_fusion
  1.0 0.9 bitcast_dynamic-update-slice_fusion.refs_0_
  1.9 1.3 collective-permute-start.1
  3.4 8.5 %collective-permute-done.1.refs_2_ = bf16[128,1536]{1,0:T(8,128)(2,1)S(1)} collective-permute-done((bf16[128,1536]{1,0:T(8,128)(2,1)S(1)}, bf16[128,1536]{1,0:T(8,128)(2,1)S(1)}, u32[]{:S(2)}, u32[]{:S(2)}) %collective-permute-start.1) | collective-permute-done | bytes 393248 | tf_op jit(solution)/shard_map/ppermute | solution.py:66
  12.0 1.3 collective-permute-start.5
  13.4 1.3 collective-permute-start.19
  14.7 2.4 %collective-permute-start = (bf16[128,1536]{1,0:T(8,128)(2,1)S(1)}, bf16[128,1536]{1,0:T(8,128)(2,1)S(1)}, u32[]{:S(2)}, u32[]{:S(2)}) collective-permute-start(bf16[128,1536]{1,0:T(8,128)(2,1)S(1)} %bitcast_dynamic-update-slice_fusion.refs_0_), channel_id=1, source_target_pairs={{0,2},{2,0},{4,6},{6,4},{8,10},{10,8},{12,14},{14,12},{16,18},{18,... | collective-permute-start | bytes 1179656 | tf_op jit(solution)/shard_map/ppermute | solution.py:66
  17.3 1.2 dynamic_slice.7.length_ref
  18.5 8.3 %collective-permute-done.19.refs_6_ = bf16[1024,128]{1,0:T(8,128)(2,1)S(1)} collective-permute-done((bf16[1024,128]{1,0:T(8,128)(2,1)}, bf16[1024,128]{1,0:T(8,128)(2,1)S(1)}, u32[]{:S(2)}, u32[]{:S(2)}) %collective-permute-start.19) | collective-permute-done | bytes 262176 | tf_op jit(solution)/shard_map/ppermute | solution.py:66
  26.8 1.2 collective-permute-start.17
  28.0 0.5 add_convert_fusion
  28.6 1.3 collective-permute-start.9
  30.1 1.3 collective-permute-start.23
  31.6 1.2 dynamic-slice_bitcast_fusion.order_ref
  33.5 18.5 %prepare.1 = (bf16[4,8192,128]{2,1,0:T(8,128)(2,1)}, bf16[4,80,8192]{2,1,0:T(8,128)(2,1)}) custom-call(s32[64]{0:T(128)} %bitcast.15, s32[1]{0:T(128)} %dynamic_slice.7.length_ref, bf16[64,512,128]{2,1,0:T(8,128)(2,1)} %bitcast.10, bf16[64,512,128]{2,1,0:T(8,128)(2,1)} %bitcast.11, bf16[64,512,128]{2,1,0:T(8,128)(2,1)} %bitcast.12, ...), custom_call_target="tpu_custom_call" | custom-call | bytes 33554432 | tf_op jit(solution)/shard_map/prepare/pallas_call | solution.py:111
  52.0 0.8 multiply_sine_fusion
  52.9 3.7 %collective-permute-start.2 = (bf16[128,1536]{1,0:T(8,128)(2,1)S(1)}, bf16[128,1536]{1,0:T(8,128)(2,1)S(1)}, u32[]{:S(2)}, u32[]{:S(2)}) collective-permute-start(bf16[128,1536]{1,0:T(8,128)(2,1)S(1)} %collective-permute-done.1.refs_2_), channel_id=1, source_target_pairs={{0,2},{2,0},{4,6},{6,4},{8,10},{10,8},{12,14},{14,12},{16,18},{18,... | collective-permute-start | bytes 1179656 | tf_op jit(solution)/shard_map/ppermute | solution.py:66
  56.7 1.3 collective-permute-start.27
  58.2 1.0 collective-permute-start.6
  59.3 0.3 fusion
  59.6 0.9 slice.17
  60.5 3.6 %collective-permute-done.27.refs_14_ = bf16[1024,128]{1,0:T(8,128)(2,1)S(1)} collective-permute-done((bf16[1024,128]{1,0:T(8,128)(2,1)S(1)}, bf16[1024,128]{1,0:T(8,128)(2,1)S(1)}, u32[]{:S(2)}, u32[]{:S(2)}) %collective-permute-start.27) | collective-permute-done | bytes 262176 | tf_op jit(solution)/shard_map/ppermute | solution.py:66
  64.1 1.3 collective-permute-start.13
  65.6 1.9 %collective-permute-start.8 = (bf16[128,1536]{1,0:T(8,128)(2,1)}, bf16[128,1536]{1,0:T(8,128)(2,1)S(1)}, u32[]{:S(2)}, u32[]{:S(2)}) collective-permute-start(bf16[128,1536]{1,0:T(8,128)(2,1)} %collective-permute-done.7.refs_8_), channel_id=1, source_target_pairs={{0,2},{2,0},{4,6},{6,4},{8,10},{10,8},{12,14},{14,12},{16,18},{18,... | collective-permute-start | bytes 1179656 | tf_op jit(solution)/shard_map/ppermute | solution.py:66
  67.5 0.7 copy-done.26
  68.3 0.7 collective-permute-start.10
  69.0 0.4 collective-permute-done.13.refs_14_
  69.3 2.1 %collective-permute-start.15 = (bf16[64,1536]{1,0:T(8,128)(2,1)S(1)}, bf16[64,1536]{1,0:T(8,128)(2,1)}, u32[]{:S(2)}, u32[]{:S(2)}) collective-permute-start(bf16[64,1536]{1,0:T(8,128)(2,1)S(1)} %collective-permute-done.13.refs_14_), channel_id=1, source_target_pairs={{0,2},{2,0},{4,6},{6,4},{8,10},{10,8},{12,14},{14,12},{16,18},{18,... | collective-permute-start | bytes 589832 | tf_op jit(solution)/shard_map/ppermute | solution.py:66
  71.5 1.3 collective-permute-start.16
  72.8 1.3 fusion.2.refs_18_
  74.1 0.7 slice.18
  74.9 0.5 collective-permute-start.20
  75.5 0.5 collective-permute-start.24
  76.0 1.3 collective-permute-start.31
  77.2 7.1 %project.1 = (bf16[4,2,128,512]{3,2,1,0:T(8,128)(2,1)}, bf16[4,256,128]{2,1,0:T(8,128)(2,1)}, bf16[4,80,256]{2,1,0:T(8,128)(2,1)}) custom-call(s32[16]{0:T(128)} %dynamic-slice_bitcast_fusion.order_ref, bf16[128,1536]{1,0:T(8,128)(2,1)} %copy-done.2, bf16[128,1536]{1,0:T(8,128)(2,1)} %copy-done.24, bf16[128,1536]{1,0:T(8,128)(2,1)} %copy-done.22, ...), custom_call_target="tpu_custom_call" | custom-call | flops 1610612736 | bytes 6291456 | tf_op jit(solution)/shard_map/project/pallas_call | solution.py:188
  84.4 14.9 %attend.7.refs_3_ = bf16[256,256]{1,0:T(8,128)(2,1)} custom-call(s32[1]{0:T(128)} %dynamic_slice.7.length_ref, s32[1]{0:T(128)S(6)} %copy.14.span_ref, bf16[4,8192,128]{2,1,0:T(8,128)(2,1)} %get-tuple-element.10.key_ref, bf16[4,80,8192]{2,1,0:T(8,128)(2,1)} %get-tuple-element.11.value_ref, bf16[4,2,128,512]{3,2,1,0:T(8,128)(2,1)} %get-tuple-element.12.query_ref, ...), custom_call_target="tpu_custom_call" | custom-call | flops 4294967296 | bytes 4194304 | tf_op jit(solution)/shard_map/attend/pallas_call | solution.py:313
  99.3 14.9 %attend.6.refs_2_ = bf16[256,256]{1,0:T(8,128)(2,1)} custom-call(s32[1]{0:T(128)} %dynamic_slice.7.length_ref, s32[1]{0:T(128)S(6)} %copy.14.span_ref, bf16[4,8192,128]{2,1,0:T(8,128)(2,1)} %get-tuple-element.10.key_ref, bf16[4,80,8192]{2,1,0:T(8,128)(2,1)} %get-tuple-element.11.value_ref, bf16[4,2,128,512]{3,2,1,0:T(8,128)(2,1)} %get-tuple-element.12.query_ref, ...), custom_call_target="tpu_custom_call" | custom-call | flops 4294967296 | bytes 4194304 | tf_op jit(solution)/shard_map/attend/pallas_call | solution.py:313
  114.3 15.1 %attend.5.refs_1_ = bf16[256,256]{1,0:T(8,128)(2,1)} custom-call(s32[1]{0:T(128)} %dynamic_slice.7.length_ref, s32[1]{0:T(128)S(6)} %copy.14.span_ref, bf16[4,8192,128]{2,1,0:T(8,128)(2,1)} %get-tuple-element.10.key_ref, bf16[4,80,8192]{2,1,0:T(8,128)(2,1)} %get-tuple-element.11.value_ref, bf16[4,2,128,512]{3,2,1,0:T(8,128)(2,1)} %get-tuple-element.12.query_ref, ...), custom_call_target="tpu_custom_call" | custom-call | flops 4294967296 | bytes 4194304 | tf_op jit(solution)/shard_map/attend/pallas_call | solution.py:313
  129.5 0.5 collective-permute-start.28
  130.2 0.5 collective-permute-start.33
  130.8 14.9 %attend.4.refs_0_ = bf16[256,256]{1,0:T(8,128)(2,1)} custom-call(s32[1]{0:T(128)} %dynamic_slice.7.length_ref, s32[1]{0:T(128)S(6)} %copy.14.span_ref, bf16[4,8192,128]{2,1,0:T(8,128)(2,1)} %get-tuple-element.10.key_ref, bf16[4,80,8192]{2,1,0:T(8,128)(2,1)} %get-tuple-element.11.value_ref, bf16[4,2,128,512]{3,2,1,0:T(8,128)(2,1)} %get-tuple-element.12.query_ref, ...), custom_call_target="tpu_custom_call" | custom-call | flops 4294967296 | bytes 4194304 | tf_op jit(solution)/shard_map/attend/pallas_call | solution.py:313
  145.8 0.6 copy-done.12
  146.7 3.8 %emit.3 = bf16[16,128,128]{2,1,0:T(8,128)(2,1)} custom-call(s32[1]{0:T(128)} %bitcast.5.start_ref, bf16[256,256]{1,0:T(8,128)(2,1)} %attend.4.refs_0_, bf16[256,256]{1,0:T(8,128)(2,1)} %attend.5.refs_1_, bf16[256,256]{1,0:T(8,128)(2,1)} %attend.6.refs_2_, bf16[256,256]{1,0:T(8,128)(2,1)} %attend.7.refs_3_, bf16[1024,128]{1,0:T(8,128)(2,1)} %refs_4_.3, ...), custom_call_target="tpu_custom_call" | custom-call | flops 536870912 | bytes 4194304 | tf_op jit(solution)/shard_map/emit/pallas_call | solution.py:355
  150.6 0.2 collective-permute-start.35
  150.8 3.9 %emit.2.own_ref = bf16[16,128,128]{2,1,0:T(8,128)(2,1)} custom-call(s32[1]{0:T(128)} %bitcast.1.start_ref, bf16[256,256]{1,0:T(8,128)(2,1)} %attend.4.refs_0_, bf16[256,256]{1,0:T(8,128)(2,1)} %attend.5.refs_1_, bf16[256,256]{1,0:T(8,128)(2,1)} %attend.6.refs_2_, bf16[256,256]{1,0:T(8,128)(2,1)} %attend.7.refs_3_, bf16[1024,128]{1,0:T(8,128)(2,1)} %refs_4_.3, ...), custom_call_target="tpu_custom_call" | custom-call | flops 536870912 | bytes 4194304 | tf_op jit(solution)/shard_map/emit/pallas_call | solution.py:355
  154.7 4.1 %collective-permute-done.35.other_ref = bf16[16,128,128]{2,1,0:T(8,128)(2,1)S(1)} collective-permute-done((bf16[16,128,128]{2,1,0:T(8,128)(2,1)}, bf16[16,128,128]{2,1,0:T(8,128)(2,1)S(1)}, u32[]{:S(2)}, u32[]{:S(2)}) %collective-permute-start.35) | collective-permute-done | bytes 524320 | tf_op jit(solution)/shard_map/ppermute | solution.py:443
  158.8 0.8 copy-done.21
  159.6 2.2 %combine.1 = bf16[128,2048]{1,0:T(8,128)(2,1)} custom-call(s32[16]{0:T(128)} %dynamic-slice_bitcast_fusion.order_ref, bf16[16,128,128]{2,1,0:T(8,128)(2,1)} %emit.2.own_ref, bf16[16,128,128]{2,1,0:T(8,128)(2,1)} %copy-done.21), custom_call_target="tpu_custom_call" | custom-call | tf_op jit(solution)/shard_map/combine/pallas_call | solution.py:380
  (112 shorter events, 2.4 us)
Async XLA Ops:
  1.9 50.1 %copy-start.2 = (bf16[128,1536]{1,0:T(8,128)(2,1)}, bf16[128,1536]{1,0:T(8,128)(2,1)S(1)}, u32[]{:S(2)}) copy-start(bf16[128,1536]{1,0:T(8,128)(2,1)S(1)} %bitcast_dynamic-update-slice_fusion.refs_0_) | copy-start | bytes 1179652
  1.9 10.1 %collective-permute-start.1 = (bf16[128,1536]{1,0:T(8,128)(2,1)S(1)}, bf16[128,1536]{1,0:T(8,128)(2,1)S(1)}, u32[]{:S(2)}, u32[]{:S(2)}) collective-permute-start(bf16[128,1536]{1,0:T(8,128)(2,1)S(1)} %bitcast_dynamic-update-slice_fusion.refs_0_), channel_id=1, source_target_pairs={{0,8},{2,10},{8,16},{10,18},{16,24},{18,26},{24,28},{26,30},{28,20... | collective-permute-start | bytes 1179656 | tf_op jit(solution)/shard_map/ppermute | solution.py:66
  3.3 10.0 %collective-permute-start.3 = (bf16[128,1536]{1,0:T(8,128)(2,1)S(1)}, bf16[128,1536]{1,0:T(8,128)(2,1)S(1)}, u32[]{:S(2)}, u32[]{:S(2)}) collective-permute-start(bf16[128,1536]{1,0:T(8,128)(2,1)S(1)} %bitcast_dynamic-update-slice_fusion.refs_0_), channel_id=1, source_target_pairs={{8,0},{10,2},{16,8},{18,10},{24,16},{26,18},{28,24},{30,26},{20,28... | collective-permute-start | bytes 1179656 | tf_op jit(solution)/shard_map/ppermute | solution.py:66
  12.0 40.9 %copy-start.22 = (bf16[128,1536]{1,0:T(8,128)(2,1)}, bf16[128,1536]{1,0:T(8,128)(2,1)S(1)}, u32[]{:S(2)}) copy-start(bf16[128,1536]{1,0:T(8,128)(2,1)S(1)} %collective-permute-done.1.refs_2_) | copy-start | bytes 1179652
  12.0 16.6 %collective-permute-start.5 = (bf16[128,1536]{1,0:T(8,128)(2,1)S(1)}, bf16[128,1536]{1,0:T(8,128)(2,1)}, u32[]{:S(2)}, u32[]{:S(2)}) collective-permute-start(bf16[128,1536]{1,0:T(8,128)(2,1)S(1)} %collective-permute-done.1.refs_2_), channel_id=1, source_target_pairs={{0,8},{2,10},{8,16},{10,18},{16,24},{18,26},{24,28},{26,30},{28,20... | collective-permute-start | bytes 1179656 | tf_op jit(solution)/shard_map/ppermute | solution.py:66
  13.3 16.8 %copy-start.23 = (bf16[128,1536]{1,0:T(8,128)(2,1)}, bf16[128,1536]{1,0:T(8,128)(2,1)S(1)}, u32[]{:S(2)}) copy-start(bf16[128,1536]{1,0:T(8,128)(2,1)S(1)} %collective-permute-done.3.refs_4_) | copy-start | bytes 1179652
  13.3 16.6 %collective-permute-start.7 = (bf16[128,1536]{1,0:T(8,128)(2,1)S(1)}, bf16[128,1536]{1,0:T(8,128)(2,1)}, u32[]{:S(2)}, u32[]{:S(2)}) collective-permute-start(bf16[128,1536]{1,0:T(8,128)(2,1)S(1)} %collective-permute-done.3.refs_4_), channel_id=1, source_target_pairs={{8,0},{10,2},{16,8},{18,10},{24,16},{26,18},{28,24},{30,26},{20,28... | collective-permute-start | bytes 1179656 | tf_op jit(solution)/shard_map/ppermute | solution.py:66
  13.4 13.3 %collective-permute-start.19 = (bf16[1024,128]{1,0:T(8,128)(2,1)}, bf16[1024,128]{1,0:T(8,128)(2,1)S(1)}, u32[]{:S(2)}, u32[]{:S(2)}) collective-permute-start(bf16[1024,128]{1,0:T(8,128)(2,1)} %refs_4_.3), channel_id=1, source_target_pairs={{0,8},{2,10},{8,16},{10,18},{16,24},{18,26},{24,28},{26,30},{28,20... | collective-permute-start | bytes 786440 | tf_op jit(solution)/shard_map/ppermute | solution.py:66
  14.7 16.7 %collective-permute-start = (bf16[128,1536]{1,0:T(8,128)(2,1)S(1)}, bf16[128,1536]{1,0:T(8,128)(2,1)S(1)}, u32[]{:S(2)}, u32[]{:S(2)}) collective-permute-start(bf16[128,1536]{1,0:T(8,128)(2,1)S(1)} %bitcast_dynamic-update-slice_fusion.refs_0_), channel_id=1, source_target_pairs={{0,2},{2,0},{4,6},{6,4},{8,10},{10,8},{12,14},{14,12},{16,18},{18,... | collective-permute-start | bytes 1179656 | tf_op jit(solution)/shard_map/ppermute | solution.py:66
  17.1 13.0 %collective-permute-start.21 = (bf16[1024,128]{1,0:T(8,128)(2,1)}, bf16[1024,128]{1,0:T(8,128)(2,1)S(1)}, u32[]{:S(2)}, u32[]{:S(2)}) collective-permute-start(bf16[1024,128]{1,0:T(8,128)(2,1)} %refs_4_.3), channel_id=1, source_target_pairs={{8,0},{10,2},{16,8},{18,10},{24,16},{26,18},{28,24},{30,26},{20,28... | collective-permute-start | bytes 786440 | tf_op jit(solution)/shard_map/ppermute | solution.py:66
  26.8 48.1 %copy-start.4 = (bf16[1024,128]{1,0:T(8,128)(2,1)}, bf16[1024,128]{1,0:T(8,128)(2,1)S(1)}, u32[]{:S(2)}) copy-start(bf16[1024,128]{1,0:T(8,128)(2,1)S(1)} %collective-permute-done.19.refs_6_) | copy-start | bytes 786436
  26.8 26.1 %collective-permute-start.17 = (bf16[128,2048]{1,0:T(8,128)(2,1)}, bf16[128,2048]{1,0:T(8,128)(2,1)S(1)}, u32[]{:S(2)}, u32[]{:S(2)}) collective-permute-start(bf16[128,2048]{1,0:T(8,128)(2,1)} %param.10), channel_id=1, source_target_pairs={{0,1},{1,0},{2,3},{3,2},{4,5},{5,4},{6,7},{7,6},{8,9},{9,8},{10,11... | collective-permute-start | bytes 1572872 | tf_op jit(solution)/shard_map/ppermute | solution.py:410
  28.6 29.4 %collective-permute-start.9 = (bf16[128,1536]{1,0:T(8,128)(2,1)}, bf16[128,1536]{1,0:T(8,128)(2,1)S(1)}, u32[]{:S(2)}, u32[]{:S(2)}) collective-permute-start(bf16[128,1536]{1,0:T(8,128)(2,1)} %collective-permute-done.5.refs_6_), channel_id=1, source_target_pairs={{0,8},{2,10},{8,16},{10,18},{16,24},{18,26},{24,28},{26,30},{28,20... | collective-permute-start | bytes 1179656 | tf_op jit(solution)/shard_map/ppermute | solution.py:66
  29.9 28.3 %collective-permute-start.11 = (bf16[128,1536]{1,0:T(8,128)(2,1)}, bf16[128,1536]{1,0:T(8,128)(2,1)}, u32[]{:S(2)}, u32[]{:S(2)}) collective-permute-start(bf16[128,1536]{1,0:T(8,128)(2,1)} %collective-permute-done.7.refs_8_), channel_id=1, source_target_pairs={{8,0},{10,2},{16,8},{18,10},{24,16},{26,18},{28,24},{30,26},{20,28... | collective-permute-start | bytes 1179656 | tf_op jit(solution)/shard_map/ppermute | solution.py:66
  30.1 45.3 %copy-start.5 = (bf16[1024,128]{1,0:T(8,128)(2,1)}, bf16[1024,128]{1,0:T(8,128)(2,1)S(1)}, u32[]{:S(2)}) copy-start(bf16[1024,128]{1,0:T(8,128)(2,1)S(1)} %collective-permute-done.21.refs_8_) | copy-start | bytes 786436
  30.1 26.5 %collective-permute-start.23 = (bf16[1024,128]{1,0:T(8,128)(2,1)S(1)}, bf16[1024,128]{1,0:T(8,128)(2,1)S(1)}, u32[]{:S(2)}, u32[]{:S(2)}) collective-permute-start(bf16[1024,128]{1,0:T(8,128)(2,1)S(1)} %collective-permute-done.19.refs_6_), channel_id=1, source_target_pairs={{0,8},{2,10},{8,16},{10,18},{16,24},{18,26},{24,28},{26,30},{28,20... | collective-permute-start | bytes 786440 | tf_op jit(solution)/shard_map/ppermute | solution.py:66
  31.4 25.3 %collective-permute-start.25 = (bf16[1024,128]{1,0:T(8,128)(2,1)S(1)}, bf16[1024,128]{1,0:T(8,128)(2,1)S(1)}, u32[]{:S(2)}, u32[]{:S(2)}) collective-permute-start(bf16[1024,128]{1,0:T(8,128)(2,1)S(1)} %collective-permute-done.21.refs_8_), channel_id=1, source_target_pairs={{8,0},{10,2},{16,8},{18,10},{24,16},{26,18},{28,24},{30,26},{20,28... | collective-permute-start | bytes 786440 | tf_op jit(solution)/shard_map/ppermute | solution.py:66
  33.5 25.7 %copy-start.16 = (bf16[128,2048]{1,0:T(8,128)(2,1)S(1)}, bf16[128,2048]{1,0:T(8,128)(2,1)}, u32[]{:S(2)}) copy-start(bf16[128,2048]{1,0:T(8,128)(2,1)} %param.10) | copy-start | bytes 1572868
  52.0 20.8 %copy-start.31 = (f32[2048]{0:T(1024)S(1)}, f32[2048]{0:T(1024)}, u32[]{:S(2)}) copy-start(f32[2048]{0:T(1024)} %param.11) | copy-start | bytes 24580
  52.9 12.8 %collective-permute-start.2 = (bf16[128,1536]{1,0:T(8,128)(2,1)S(1)}, bf16[128,1536]{1,0:T(8,128)(2,1)S(1)}, u32[]{:S(2)}, u32[]{:S(2)}) collective-permute-start(bf16[128,1536]{1,0:T(8,128)(2,1)S(1)} %collective-permute-done.1.refs_2_), channel_id=1, source_target_pairs={{0,2},{2,0},{4,6},{6,4},{8,10},{10,8},{12,14},{14,12},{16,18},{18,... | collective-permute-start | bytes 1179656 | tf_op jit(solution)/shard_map/ppermute | solution.py:66
  56.6 18.9 %copy-start.6 = (bf16[1024,128]{1,0:T(8,128)(2,1)}, bf16[1024,128]{1,0:T(8,128)(2,1)S(1)}, u32[]{:S(2)}) copy-start(bf16[1024,128]{1,0:T(8,128)(2,1)S(1)} %collective-permute-done.23.refs_10_) | copy-start | bytes 786436
  56.6 10.9 %collective-permute-start.4 = (bf16[128,1536]{1,0:T(8,128)(2,1)}, bf16[128,1536]{1,0:T(8,128)(2,1)S(1)}, u32[]{:S(2)}, u32[]{:S(2)}) collective-permute-start(bf16[128,1536]{1,0:T(8,128)(2,1)} %copy-done.23), channel_id=1, source_target_pairs={{0,2},{2,0},{4,6},{6,4},{8,10},{10,8},{12,14},{14,12},{16,18},{18,... | collective-permute-start | bytes 1179656 | tf_op jit(solution)/shard_map/ppermute | solution.py:66
  56.7 72.7 %copy-start.7 = (bf16[1024,128]{1,0:T(8,128)(2,1)}, bf16[1024,128]{1,0:T(8,128)(2,1)S(1)}, u32[]{:S(2)}) copy-start(bf16[1024,128]{1,0:T(8,128)(2,1)S(1)} %collective-permute-done.25.refs_12_) | copy-start | bytes 786436
  56.7 7.4 %collective-permute-start.27 = (bf16[1024,128]{1,0:T(8,128)(2,1)S(1)}, bf16[1024,128]{1,0:T(8,128)(2,1)S(1)}, u32[]{:S(2)}, u32[]{:S(2)}) collective-permute-start(bf16[1024,128]{1,0:T(8,128)(2,1)S(1)} %collective-permute-done.23.refs_10_), channel_id=1, source_target_pairs={{0,8},{2,10},{8,16},{10,18},{16,24},{18,26},{24,28},{26,30},{28,20... | collective-permute-start | bytes 786440 | tf_op jit(solution)/shard_map/ppermute | solution.py:66
  58.0 7.4 %collective-permute-start.29 = (bf16[1024,128]{1,0:T(8,128)(2,1)S(1)}, bf16[1024,128]{1,0:T(8,128)(2,1)S(1)}, u32[]{:S(2)}, u32[]{:S(2)}) collective-permute-start(bf16[1024,128]{1,0:T(8,128)(2,1)S(1)} %collective-permute-done.25.refs_12_), channel_id=1, source_target_pairs={{8,0},{10,2},{16,8},{18,10},{24,16},{26,18},{28,24},{30,26},{20,28... | collective-permute-start | bytes 786440 | tf_op jit(solution)/shard_map/ppermute | solution.py:66
  58.2 10.8 %collective-permute-start.6 = (bf16[128,1536]{1,0:T(8,128)(2,1)}, bf16[128,1536]{1,0:T(8,128)(2,1)}, u32[]{:S(2)}, u32[]{:S(2)}) collective-permute-start(bf16[128,1536]{1,0:T(8,128)(2,1)} %collective-permute-done.5.refs_6_), channel_id=1, source_target_pairs={{0,2},{2,0},{4,6},{6,4},{8,10},{10,8},{12,14},{14,12},{16,18},{18,... | collective-permute-start | bytes 1179656 | tf_op jit(solution)/shard_map/ppermute | solution.py:66
  64.1 65.4 %copy-start = (bf16[1024,128]{1,0:T(8,128)(2,1)}, bf16[1024,128]{1,0:T(8,128)(2,1)S(1)}, u32[]{:S(2)}) copy-start(bf16[1024,128]{1,0:T(8,128)(2,1)S(1)} %collective-permute-done.27.refs_14_) | copy-start | bytes 786436
  64.1 5.2 %collective-permute-start.13 = (bf16[64,1536]{1,0:T(8,128)(2,1)S(1)}, bf16[64,1536]{1,0:T(8,128)(2,1)S(1)}, u32[]{:S(2)}, u32[]{:S(2)}) collective-permute-start(bf16[64,1536]{1,0:T(8,128)(2,1)S(1)} %slice.16), channel_id=1, source_target_pairs={{0,8},{2,10},{8,16},{10,18},{16,24},{18,26},{24,28},{26,30},{28,20... | collective-permute-start | bytes 589832 | tf_op jit(solution)/shard_map/ppermute | solution.py:66
  65.4 64.6 %copy-start.1 = (bf16[1024,128]{1,0:T(8,128)(2,1)}, bf16[1024,128]{1,0:T(8,128)(2,1)S(1)}, u32[]{:S(2)}) copy-start(bf16[1024,128]{1,0:T(8,128)(2,1)S(1)} %collective-permute-done.29.refs_16_) | copy-start | bytes 786436
  65.4 6.0 %collective-permute-start.14 = (bf16[64,1536]{1,0:T(8,128)(2,1)S(1)}, bf16[64,1536]{1,0:T(8,128)(2,1)S(1)}, u32[]{:S(2)}, u32[]{:S(2)}) collective-permute-start(bf16[64,1536]{1,0:T(8,128)(2,1)S(1)} %slice.17), channel_id=1, source_target_pairs={{8,0},{10,2},{16,8},{18,10},{24,16},{26,18},{28,24},{30,26},{20,28... | collective-permute-start | bytes 589832 | tf_op jit(solution)/shard_map/ppermute | solution.py:66
  65.6 9.1 %collective-permute-start.8 = (bf16[128,1536]{1,0:T(8,128)(2,1)}, bf16[128,1536]{1,0:T(8,128)(2,1)S(1)}, u32[]{:S(2)}, u32[]{:S(2)}) collective-permute-start(bf16[128,1536]{1,0:T(8,128)(2,1)} %collective-permute-done.7.refs_8_), channel_id=1, source_target_pairs={{0,2},{2,0},{4,6},{6,4},{8,10},{10,8},{12,14},{14,12},{16,18},{18,... | collective-permute-start | bytes 1179656 | tf_op jit(solution)/shard_map/ppermute | solution.py:66
  68.3 7.2 %collective-permute-start.10 = (bf16[128,1536]{1,0:T(8,128)(2,1)S(1)}, bf16[128,1536]{1,0:T(8,128)(2,1)S(1)}, u32[]{:S(2)}, u32[]{:S(2)}) collective-permute-start(bf16[128,1536]{1,0:T(8,128)(2,1)S(1)} %collective-permute-done.9.refs_10_), channel_id=1, source_target_pairs={{0,2},{2,0},{4,6},{6,4},{8,10},{10,8},{12,14},{14,12},{16,18},{18,... | collective-permute-start | bytes 1179656 | tf_op jit(solution)/shard_map/ppermute | solution.py:66
  68.9 7.0 %collective-permute-start.12 = (bf16[128,1536]{1,0:T(8,128)(2,1)}, bf16[128,1536]{1,0:T(8,128)(2,1)}, u32[]{:S(2)}, u32[]{:S(2)}) collective-permute-start(bf16[128,1536]{1,0:T(8,128)(2,1)} %collective-permute-done.11.refs_12_), channel_id=1, source_target_pairs={{0,2},{2,0},{4,6},{6,4},{8,10},{10,8},{12,14},{14,12},{16,18},{18,... | collective-permute-start | bytes 1179656 | tf_op jit(solution)/shard_map/ppermute | solution.py:66
  69.3 5.5 %collective-permute-start.15 = (bf16[64,1536]{1,0:T(8,128)(2,1)S(1)}, bf16[64,1536]{1,0:T(8,128)(2,1)}, u32[]{:S(2)}, u32[]{:S(2)}) collective-permute-start(bf16[64,1536]{1,0:T(8,128)(2,1)S(1)} %collective-permute-done.13.refs_14_), channel_id=1, source_target_pairs={{0,2},{2,0},{4,6},{6,4},{8,10},{10,8},{12,14},{14,12},{16,18},{18,... | collective-permute-start | bytes 589832 | tf_op jit(solution)/shard_map/ppermute | solution.py:66
  71.5 3.9 %collective-permute-start.16 = (bf16[64,1536]{1,0:T(8,128)(2,1)S(1)}, bf16[64,1536]{1,0:T(8,128)(2,1)}, u32[]{:S(2)}, u32[]{:S(2)}) collective-permute-start(bf16[64,1536]{1,0:T(8,128)(2,1)S(1)} %collective-permute-done.14.refs_15_), channel_id=1, source_target_pairs={{0,2},{2,0},{4,6},{6,4},{8,10},{10,8},{12,14},{14,12},{16,18},{18,... | collective-permute-start | bytes 589832 | tf_op jit(solution)/shard_map/ppermute | solution.py:66
  74.8 39.5 %collective-permute-start.18 = (bf16[1024,128]{1,0:T(8,128)(2,1)S(1)}, bf16[1024,128]{1,0:T(8,128)(2,1)S(1)}, u32[]{:S(2)}, u32[]{:S(2)}) collective-permute-start(bf16[1024,128]{1,0:T(8,128)(2,1)S(1)} %copy-done.3), channel_id=1, source_target_pairs={{0,2},{2,0},{4,6},{6,4},{8,10},{10,8},{12,14},{14,12},{16,18},{18,... | collective-permute-start | bytes 786440 | tf_op jit(solution)/shard_map/ppermute | solution.py:66
  74.9 54.5 %collective-permute-start.20 = (bf16[1024,128]{1,0:T(8,128)(2,1)S(1)}, bf16[1024,128]{1,0:T(8,128)(2,1)S(1)}, u32[]{:S(2)}, u32[]{:S(2)}) collective-permute-start(bf16[1024,128]{1,0:T(8,128)(2,1)S(1)} %collective-permute-done.19.refs_6_), channel_id=1, source_target_pairs={{0,2},{2,0},{4,6},{6,4},{8,10},{10,8},{12,14},{14,12},{16,18},{18,... | collective-permute-start | bytes 786440 | tf_op jit(solution)/shard_map/ppermute | solution.py:66
  75.4 54.1 %collective-permute-start.22 = (bf16[1024,128]{1,0:T(8,128)(2,1)S(1)}, bf16[1024,128]{1,0:T(8,128)(2,1)S(1)}, u32[]{:S(2)}, u32[]{:S(2)}) collective-permute-start(bf16[1024,128]{1,0:T(8,128)(2,1)S(1)} %collective-permute-done.21.refs_8_), channel_id=1, source_target_pairs={{0,2},{2,0},{4,6},{6,4},{8,10},{10,8},{12,14},{14,12},{16,18},{18,... | collective-permute-start | bytes 786440 | tf_op jit(solution)/shard_map/ppermute | solution.py:66
  75.5 54.6 %collective-permute-start.24 = (bf16[1024,128]{1,0:T(8,128)(2,1)S(1)}, bf16[1024,128]{1,0:T(8,128)(2,1)S(1)}, u32[]{:S(2)}, u32[]{:S(2)}) collective-permute-start(bf16[1024,128]{1,0:T(8,128)(2,1)S(1)} %collective-permute-done.23.refs_10_), channel_id=1, source_target_pairs={{0,2},{2,0},{4,6},{6,4},{8,10},{10,8},{12,14},{14,12},{16,18},{18,... | collective-permute-start | bytes 786440 | tf_op jit(solution)/shard_map/ppermute | solution.py:66
  76.0 54.2 %collective-permute-start.31 = (bf16[512,128]{1,0:T(8,128)(2,1)}, bf16[512,128]{1,0:T(8,128)(2,1)S(1)}, u32[]{:S(2)}, u32[]{:S(2)}) collective-permute-start(bf16[512,128]{1,0:T(8,128)(2,1)} %slice.18), channel_id=1, source_target_pairs={{0,8},{2,10},{8,16},{10,18},{16,24},{18,26},{24,28},{26,30},{28,20... | collective-permute-start | bytes 393224 | tf_op jit(solution)/shard_map/ppermute | solution.py:66
  114.3 16.4 %collective-permute-start.32 = (bf16[512,128]{1,0:T(8,128)(2,1)S(1)}, bf16[512,128]{1,0:T(8,128)(2,1)S(1)}, u32[]{:S(2)}, u32[]{:S(2)}) collective-permute-start(bf16[512,128]{1,0:T(8,128)(2,1)S(1)} %slice.19), channel_id=1, source_target_pairs={{8,0},{10,2},{16,8},{18,10},{24,16},{26,18},{28,24},{30,26},{20,28... | collective-permute-start | bytes 393224 | tf_op jit(solution)/shard_map/ppermute | solution.py:66
  129.4 16.3 %copy-start.9 = (bf16[1024,128]{1,0:T(8,128)(2,1)}, bf16[1024,128]{1,0:T(8,128)(2,1)S(1)}, u32[]{:S(2)}) copy-start(bf16[1024,128]{1,0:T(8,128)(2,1)S(1)} %collective-permute-done.20.refs_7_) | copy-start | bytes 786436
  129.4 16.3 %collective-permute-start.26 = (bf16[1024,128]{1,0:T(8,128)(2,1)S(1)}, bf16[1024,128]{1,0:T(8,128)(2,1)S(1)}, u32[]{:S(2)}, u32[]{:S(2)}) collective-permute-start(bf16[1024,128]{1,0:T(8,128)(2,1)S(1)} %collective-permute-done.25.refs_12_), channel_id=1, source_target_pairs={{0,2},{2,0},{4,6},{6,4},{8,10},{10,8},{12,14},{14,12},{16,18},{18,... | collective-permute-start | bytes 786440 | tf_op jit(solution)/shard_map/ppermute | solution.py:66
  129.5 16.3 %collective-permute-start.28 = (bf16[1024,128]{1,0:T(8,128)(2,1)S(1)}, bf16[1024,128]{1,0:T(8,128)(2,1)S(1)}, u32[]{:S(2)}, u32[]{:S(2)}) collective-permute-start(bf16[1024,128]{1,0:T(8,128)(2,1)S(1)} %collective-permute-done.27.refs_14_), channel_id=1, source_target_pairs={{0,2},{2,0},{4,6},{6,4},{8,10},{10,8},{12,14},{14,12},{16,18},{18,... | collective-permute-start | bytes 786440 | tf_op jit(solution)/shard_map/ppermute | solution.py:66
  130.1 15.7 %collective-permute-start.30 = (bf16[1024,128]{1,0:T(8,128)(2,1)S(1)}, bf16[1024,128]{1,0:T(8,128)(2,1)S(1)}, u32[]{:S(2)}, u32[]{:S(2)}) collective-permute-start(bf16[1024,128]{1,0:T(8,128)(2,1)S(1)} %collective-permute-done.29.refs_16_), channel_id=1, source_target_pairs={{0,2},{2,0},{4,6},{6,4},{8,10},{10,8},{12,14},{14,12},{16,18},{18,... | collective-permute-start | bytes 786440 | tf_op jit(solution)/shard_map/ppermute | solution.py:66
  130.2 15.6 %collective-permute-start.33 = (bf16[512,128]{1,0:T(8,128)(2,1)S(1)}, bf16[512,128]{1,0:T(8,128)(2,1)S(1)}, u32[]{:S(2)}, u32[]{:S(2)}) collective-permute-start(bf16[512,128]{1,0:T(8,128)(2,1)S(1)} %collective-permute-done.31.refs_18_), channel_id=1, source_target_pairs={{0,2},{2,0},{4,6},{6,4},{8,10},{10,8},{12,14},{14,12},{16,18},{18,... | collective-permute-start | bytes 393224 | tf_op jit(solution)/shard_map/ppermute | solution.py:66
  130.7 15.1 %collective-permute-start.34 = (bf16[512,128]{1,0:T(8,128)(2,1)S(1)}, bf16[512,128]{1,0:T(8,128)(2,1)S(1)}, u32[]{:S(2)}, u32[]{:S(2)}) collective-permute-start(bf16[512,128]{1,0:T(8,128)(2,1)S(1)} %collective-permute-done.32.refs_19_), channel_id=1, source_target_pairs={{0,2},{2,0},{4,6},{6,4},{8,10},{10,8},{12,14},{14,12},{16,18},{18,... | collective-permute-start | bytes 393224 | tf_op jit(solution)/shard_map/ppermute | solution.py:66
  150.6 8.2 %collective-permute-start.35 = (bf16[16,128,128]{2,1,0:T(8,128)(2,1)}, bf16[16,128,128]{2,1,0:T(8,128)(2,1)S(1)}, u32[]{:S(2)}, u32[]{:S(2)}) collective-permute-start(bf16[16,128,128]{2,1,0:T(8,128)(2,1)} %emit.3), channel_id=1, source_target_pairs={{0,1},{1,0},{2,3},{3,2},{4,5},{5,4},{6,7},{7,6},{8,9},{9,8},{10,11... | collective-permute-start | bytes 1572872 | tf_op jit(solution)/shard_map/ppermute | solution.py:443
  (20 other events, 133.9 us)

commit v2 on v1

v2 whole, which is shorter than its diff:
```python
import functools

import jax
import jax.numpy as jnp
from jax import lax
from jax.experimental import pallas as pl
from jax.experimental.pallas import tpu as pltpu
from jax.sharding import PartitionSpec as P

epsilon = 1e-05
score_scale = 0.015625
residual_scale = 0.22
rope_base = 10000000.0
masked_score = -1e30
key_block = 1024
score_chunk = 256
value_chunk = 256
token_tile = 128


def matmul(a, b):
    return jnp.dot(a, b, preferred_element_type=jnp.float32)


def vmem():
    return pl.BlockSpec(memory_space=pltpu.VMEM)


def smem():
    return pl.BlockSpec(memory_space=pltpu.SMEM)


def params(mebibytes):
    return pltpu.CompilerParams(vmem_limit_bytes=mebibytes * 1024 * 1024)


def cycle_tables(count):
    depth = count // 4
    walk = [(z, 0) for z in range(depth)] + [(z, 1) for z in reversed(range(depth))]
    device = lambda chip, core: (chip[0] * 2 + chip[1]) * 2 + core
    length = len(walk)
    ahead = [
        (device(walk[k], c), device(walk[(k + 1) % length], c))
        for k in range(length)
        for c in range(2)
    ]
    back = [(b, a) for a, b in ahead]
    swap = [(i, i ^ 1) for i in range(count)]
    order = [None] * count
    for k in range(length):
        for c in range(2):
            row = []
            for step in range(length // 2):
                sources = [walk[(k - step) % length], walk[(k + step) % length]]
                for chip in sources[: 1 if step == 0 else 2]:
                    row += [device(chip, c), device(chip, 1 - c)]
            far = walk[(k + length // 2) % length]
            row += [device(far, c), device(far, 1 - c)]
            order[device(walk[k], c)] = row
    return ahead, back, swap, order


def after(value, *others):
    return lax.optimization_barrier((value,) + others)[0]


class Ring:
    def __init__(self, shard, tables):
        self.ahead, self.back, self.swap, self.order = tables
        self.length = len(self.order) // 2
        self.half = shard.shape[0] // 2
        self.up = self.down = shard
        self.blocks = [shard, self.move(shard, self.swap)]

    def move(self, value, pairs):
        return lax.ppermute(value, "req", pairs)

    def step(self, *others):
        if others:
            self.up, self.down = lax.optimization_barrier((self.up, self.down) + others)[:2]
        self.up, self.down = self.move(self.up, self.ahead), self.move(self.down, self.back)
        self.blocks += [
            self.up,
            self.move(self.up, self.swap),
            self.down,
            self.move(self.down, self.swap),
        ]

    def last(self, *others):
        if others:
            self.up, self.down = lax.optimization_barrier((self.up, self.down) + others)[:2]
        first = self.move(self.up[: self.half], self.ahead)
        second = self.move(self.down[self.half :], self.back)
        ends = [first, second, self.move(first, self.swap), self.move(second, self.swap)]
        return self.blocks + ends


def prepare_kernel(heads, page, width, pages_step, first_page, aliased, table_ref, length_ref, *refs):
    pages = refs[:pages_step]
    key_ref, value_ref, wide = refs[pages_step + aliased :]
    step = pl.program_id(0)
    half = width // 2
    rows = value_ref.shape[1]
    pick_row = lax.broadcasted_iota(jnp.int32, (rows, width), 0)
    pick_lane = lax.broadcasted_iota(jnp.int32, (rows, width), 1)
    pick = jnp.where(pick_lane == pick_row + half, 1.0, 0.0).astype(jnp.bfloat16)
    ones = jnp.where(lax.broadcasted_iota(jnp.int32, (rows, page), 0) == half, 1.0, 0.0)
    for i in range(pages_step):
        wide[...] = pages[i][0].astype(jnp.float32)
        first = (first_page + step * pages_step + i) * page
        position = first + lax.broadcasted_iota(jnp.int32, (page, width), 0)
        lane = lax.broadcasted_iota(jnp.int32, (page, width), 1)
        bias = jnp.where((lane == half) & (position >= length_ref[0]), masked_score, 0.0)
        for h in range(heads):
            rows_h = wide[pl.ds(h, page, stride=heads), :]
            key_ref[h, pl.ds(i * page, page), :] = jnp.where(lane < half, rows_h, bias).astype(
                jnp.bfloat16
            )
            turned = lax.dot_general(
                pick,
                rows_h.astype(jnp.bfloat16),
                (((1,), (1,)), ((), ())),
                preferred_element_type=jnp.float32,
            )
            value_ref[h, :, pl.ds(i * page, page)] = (turned + ones).astype(jnp.bfloat16)


def with_ones(turned):
    row = lax.broadcasted_iota(jnp.int32, (16, turned.shape[1]), 0)
    return jnp.concatenate([turned, jnp.where(row == 0, 1.0, 0.0)], axis=0)


def prepare(cache, table, length, part, parts, before):
    pages, page, heads, width = cache.shape
    pages_step = 4
    rows = width // 2 + 16
    total = table.shape[0]
    steps = total // pages_step // parts
    flat = cache.reshape(pages, page * heads, width)
    at = part * steps
    page_spec = lambda i: pl.BlockSpec(
        (1, page * heads, width), lambda j, t, n: (t[(at + j) * pages_step + i], 0, 0)
    )
    kept = [pl.BlockSpec(memory_space=pl.ANY)] * len(before)
    return pl.pallas_call(
        functools.partial(
            prepare_kernel, heads, page, width, pages_step, at * pages_step, len(before)
        ),
        grid_spec=pltpu.PrefetchScalarGridSpec(
            num_scalar_prefetch=2,
            grid=(steps,),
            in_specs=[page_spec(i) for i in range(pages_step)] + kept,
            out_specs=[
                pl.BlockSpec((heads, pages_step * page, width), lambda j, t, n: (0, at + j, 0)),
                pl.BlockSpec((heads, rows, pages_step * page), lambda j, t, n: (0, 0, at + j)),
            ],
            scratch_shapes=[pltpu.VMEM((page * heads, width), jnp.float32)],
        ),
        out_shape=[
            jax.ShapeDtypeStruct((heads, total * page, width), jnp.bfloat16),
            jax.ShapeDtypeStruct((heads, rows, total * page), jnp.bfloat16),
        ],
        input_output_aliases={2 + pages_step + i: i for i in range(len(before))},
        cost_estimate=pl.CostEstimate(
            flops=0,
            bytes_accessed=3 * cache.size * cache.dtype.itemsize // parts,
            transcendentals=0,
        ),
        compiler_params=params(16),
        name="prepare",
    )(table, length, *([flat] * pages_step), *before)


def turn(pair, cosine, sines):
    half = pair.shape[0] // 2
    first, second = pair[:half], pair[half:]
    return jnp.concatenate(
        [first * cosine - second * sines, second * cosine + first * sines], axis=0
    )


def assembled(chunks, order_ref, weight):
    if len(chunks) == 1:
        return chunks[0]
    count = order_ref.shape[0]
    rows = weight.shape[0] // count
    for k in range(count):
        start = pl.multiple_of(order_ref[k] * rows, rows)
        if k < count - 2:
            weight[pl.ds(start, rows), :] = chunks[k][...]
        else:
            at = 2 * k - (count - 2)
            weight[pl.ds(start, rows), :] = jnp.concatenate(
                [chunks[at][...], chunks[at + 1][...]], axis=0
            )
    return weight


def query_kernel(heads, group, dim, blocks, order_ref, *refs):
    normed_ref, cos_ref, sin_ref, query_ref, weight = refs[blocks:]
    source = assembled(refs[:blocks], order_ref, weight)
    cosine, sines = cos_ref[...], sin_ref[...]
    tokens = cosine.shape[1]
    normed = normed_ref[...]
    width = group * dim
    row = lax.broadcasted_iota(jnp.int32, (dim, group * token_tile), 0)
    one_row = jnp.where(row == 0, 1.0, 0.0).astype(jnp.bfloat16)
    for h in range(heads):
        turned = jnp.transpose(matmul(normed, source[:, pl.ds(h * width, width)]))
        for g in range(group):
            rotated = turn(turned[g * dim : (g + 1) * dim], cosine, sines).astype(jnp.bfloat16)
            scaled = (rotated.astype(jnp.float32) * score_scale).astype(jnp.bfloat16)
            for q in range(tokens // token_tile):
                query_ref[h, q, pl.ds(0, dim), pl.ds(g * token_tile, token_tile)] = scaled[
                    :, q * token_tile : (q + 1) * token_tile
                ]
        for q in range(tokens // token_tile):
            query_ref[h, q, pl.ds(dim, dim), :] = one_row


def new_kernel(heads, dim, blocks, order_ref, *refs):
    normed_ref, cos_ref, sin_ref, key_ref, value_ref, weight = refs[blocks:]
    source = assembled(refs[:blocks], order_ref, weight)
    cosine, sines = cos_ref[...], sin_ref[...]
    normed = normed_ref[...]
    for h in range(heads):
        turned = jnp.transpose(matmul(normed, source[:, pl.ds(h * 2 * dim, 2 * dim)]))
        keys = turn(turned[:dim], cosine, sines)
        padded = jnp.concatenate([keys, jnp.zeros_like(keys)], axis=0)
        key_ref[h] = jnp.transpose(padded).astype(jnp.bfloat16)
        value_ref[h] = with_ones(turned[dim:]).astype(jnp.bfloat16)


def project(kernel, name, outs, normed, chunks, order, cosine, sines):
    tokens, width = normed.shape
    columns = chunks[0].shape[1]
    return pl.pallas_call(
        kernel,
        in_specs=[smem()] + [vmem()] * (len(chunks) + 3),
        out_specs=[vmem()] * len(outs),
        out_shape=[jax.ShapeDtypeStruct(shape, jnp.bfloat16) for shape in outs],
        scratch_shapes=[pltpu.VMEM((width, columns), jnp.bfloat16)],
        cost_estimate=pl.CostEstimate(
            flops=2 * tokens * width * columns,
            bytes_accessed=2 * width * columns,
            transcendentals=0,
        ),
        compiler_params=params(24),
        name=name,
    )(order, *chunks, normed, cosine, sines)


def project_query(normed, chunks, order, cosine, sines, heads, group, dim):
    tokens = normed.shape[0]
    outs = [(heads, tokens // token_tile, 2 * dim, group * token_tile)]
    kernel = functools.partial(query_kernel, heads, group, dim, len(chunks))
    return project(kernel, "query", outs, normed, chunks, order, cosine, sines)[0]


def project_new(normed, chunks, order, cosine, sines, heads, dim):
    tokens = normed.shape[0]
    outs = [(heads, tokens, 2 * dim), (heads, dim + 16, tokens)]
    kernel = functools.partial(new_kernel, heads, dim, len(chunks))
    return project(kernel, "new", outs, normed, chunks, order, cosine, sines)


def attend_kernel(
    group,
    dim,
    length_ref,
    span_ref,
    tile_ref,
    key_ref,
    value_ref,
    query_ref,
    new_key_ref,
    new_value_ref,
    out_ref,
    even,
    odd,
):
    lanes = query_ref.shape[3]
    span = new_key_ref.shape[1]
    length = length_ref[0]
    valid = span_ref[0]
    pair = 2 * key_block
    pairs = (length + pair - 1) // pair
    last_block = jnp.maximum(2 * pairs - 1, 0)

    def column_max(scores):
        return jnp.max(scores.reshape(scores.shape[0] // 8, 8, lanes), axis=0)

    q = tile_ref[0]

    def tile():
        def scores_of(block, c, target):
            start = pl.multiple_of(block * key_block + c * score_chunk, score_chunk)
            scores = matmul(key_ref[0, pl.ds(start, score_chunk), :], query_ref[0, q])
            target[pl.ds(c * score_chunk, score_chunk), :] = scores
            return column_max(scores)

        scores = matmul(new_key_ref[0], query_ref[0, q])
        source = lax.broadcasted_iota(jnp.int32, (span, lanes), 0)
        lane = lax.broadcasted_iota(jnp.int32, (span, lanes), 1)
        token = q * token_tile + lax.rem(lane, token_tile)
        scores = jnp.where((source <= token) & (source < valid), scores, masked_score)
        maximum = jnp.max(column_max(scores), axis=0, keepdims=True)
        weights = jnp.exp(scores - maximum).astype(jnp.bfloat16)
        total = matmul(new_value_ref[0], weights)

        top = scores_of(0, 0, even)
        for c in range(1, key_block // score_chunk):
            top = jnp.maximum(top, scores_of(0, c, even))

        def half(block, following, current, target, state):
            maximum, top, total = state
            new_maximum = jnp.maximum(maximum, jnp.max(top, axis=0, keepdims=True))
            total = total * jnp.exp(maximum - new_maximum)
            next_top = None
            ratio = value_chunk // score_chunk
            parts = []
            for c in range(key_block // score_chunk):
                seen = scores_of(following, c, target)
                next_top = seen if next_top is None else jnp.maximum(next_top, seen)
                part = jnp.exp(current[pl.ds(c * score_chunk, score_chunk), :] - new_maximum)
                parts.append(part.astype(jnp.bfloat16))
                if len(parts) == ratio:
                    weights = parts[0] if ratio == 1 else jnp.concatenate(parts, axis=0)
                    start = block * key_block + (c + 1 - ratio) * score_chunk
                    start = pl.multiple_of(start, value_chunk)
                    total = total + matmul(value_ref[0, :, pl.ds(start, value_chunk)], weights)
                    parts = []
            return new_maximum, next_top, total

        def advance(i, state):
            block = 2 * i
            state = half(block, block + 1, even, odd, state)
            following = jnp.minimum(block + 2, last_block)
            return half(block + 1, following, odd, even, state)

        _, _, total = lax.fori_loop(0, pairs, advance, (maximum, top, total))
        result = total[:dim] / total[dim : dim + 1]
        row = q * token_tile + lax.broadcasted_iota(jnp.int32, (token_tile, 2 * dim), 0)
        for g in range(0, group, 2):
            both = jnp.concatenate(
                [
                    result[:, g * token_tile : (g + 1) * token_tile],
                    result[:, (g + 1) * token_tile : (g + 2) * token_tile],
                ],
                axis=0,
            )
            kept = jnp.where(row < valid, jnp.transpose(both), 0.0)
            out_ref[:, pl.ds(g * dim, 2 * dim)] = kept.astype(jnp.bfloat16)

    pl.when(q * token_tile < valid)(tile)

    @pl.when(q * token_tile >= valid)
    def empty():
        out_ref[...] = jnp.zeros_like(out_ref)


def attend(head, tile, keys, values, queries, new_keys, new_values, length, valid):
    _, cached, width = keys.shape
    dim = width // 2
    lanes = queries.shape[3]
    group = lanes // token_tile
    block = lambda array: pl.BlockSpec(
        (1,) + array.shape[1:], lambda i: (head,) + (0,) * (array.ndim - 1)
    )
    arrays = (keys, values, queries, new_keys, new_values)
    return pl.pallas_call(
        functools.partial(attend_kernel, group, dim),
        grid=(1,),
        in_specs=[smem()] * 3 + [block(a) for a in arrays],
        out_specs=pl.BlockSpec((token_tile, group * dim), lambda i: (0, 0)),
        out_shape=jax.ShapeDtypeStruct((token_tile, group * dim), jnp.bfloat16),
        scratch_shapes=[pltpu.VMEM((key_block, lanes), jnp.float32)] * 2,
        cost_estimate=pl.CostEstimate(
            flops=2 * cached * lanes * 2 * width,
            bytes_accessed=2 * cached * 2 * width,
            transcendentals=cached * lanes,
        ),
        compiler_params=params(24),
        name="attend",
    )(length, valid, tile, *arrays)


def emit_kernel(heads, blocks, *refs):
    parts = refs[:heads]
    chunks = refs[heads : heads + blocks]
    out_ref = refs[heads + blocks]
    attended = jnp.concatenate([p[...] for p in parts], axis=1)
    count = out_ref.shape[0]
    for k in range(0, count, 2):
        if k < count - 2:
            weight = jnp.concatenate([chunks[k][...], chunks[k + 1][...]], axis=1)
        else:
            at = count - 2
            own = jnp.concatenate([chunks[at][...], chunks[at + 1][...]], axis=0)
            other = jnp.concatenate([chunks[at + 2][...], chunks[at + 3][...]], axis=0)
            weight = jnp.concatenate([own, other], axis=1)
        both = matmul(attended, weight).astype(jnp.bfloat16)
        width = both.shape[1] // 2
        out_ref[k] = both[:, :width]
        out_ref[k + 1] = both[:, width:]


def emit(parts, chunks, count):
    columns = chunks[0].shape[1]
    depth = chunks[0].shape[0]
    rows = parts[0].shape[0]
    return pl.pallas_call(
        functools.partial(emit_kernel, len(parts), len(chunks)),
        in_specs=[vmem()] * (len(parts) + len(chunks)),
        out_specs=vmem(),
        out_shape=jax.ShapeDtypeStruct((count, rows, columns), jnp.bfloat16),
        cost_estimate=pl.CostEstimate(
            flops=2 * rows * depth * columns * count,
            bytes_accessed=2 * depth * columns * count,
            transcendentals=0,
        ),
        compiler_params=params(24),
        name="emit",
    )(*parts, *chunks)


def combine_kernel(order_ref, own_ref, other_ref, out_ref):
    width = own_ref.shape[2]
    for k in range(own_ref.shape[0]):
        summed = own_ref[k].astype(jnp.float32) + other_ref[k].astype(jnp.float32)
        start = pl.multiple_of(order_ref[k] * width, width)
        out_ref[:, pl.ds(start, width)] = (residual_scale * summed).astype(jnp.bfloat16)


def combine(own, other, order):
    count, rows, columns = own.shape
    return pl.pallas_call(
        combine_kernel,
        in_specs=[smem(), vmem(), vmem()],
        out_specs=vmem(),
        out_shape=jax.ShapeDtypeStruct((rows, count * columns), jnp.bfloat16),
        compiler_params=params(16),
        name="combine",
    )(order, own, other)


def rope_tables(positions, dim):
    half_dim = dim // 2
    frequency = rope_base ** (-(jnp.arange(half_dim, dtype=jnp.float32) * 2.0 / dim))
    angles = positions.astype(jnp.float32)[None, :] * frequency[:, None]
    return jnp.cos(angles), jnp.sin(angles)


def body(req_count, tp_count, tokens, norm_gain, w_query, w_kv, w_out, kv_cache, page_table, cached_len, span_len):
    fast = tp_count == 2 and req_count == 16 and w_out.shape[1] % 128 == 0 and w_kv.shape[1] == 4
    device = lax.axis_index("req")
    rank = lax.axis_index("tp")
    heads = w_kv.shape[1]
    dim = w_kv.shape[2] // 2
    group = w_query.shape[1] // dim // heads
    own_rows = tokens.shape[0]
    length = lax.dynamic_slice_in_dim(cached_len, device, 1)
    table = page_table[0]
    if fast:
        tables = cycle_tables(req_count)
        order = jnp.array(tables[3], jnp.int32)[device]
        swap = [(0, 1), (1, 0)]
        ring_query = Ring(w_query, tables)
        ring_new = Ring(w_kv.reshape(w_kv.shape[0], -1), tables)
        ring_out = Ring(w_out, tables)
        other = lax.ppermute(tokens, "tp", swap)
        whole = jnp.concatenate(
            [jnp.where(rank == 0, tokens, other), jnp.where(rank == 0, other, tokens)], axis=0
        )
        parts = 4
        state = ()
        for part in range(parts):
            if part < parts - 1:
                ring_query.step(*state[:1])
                ring_new.step(*state[:1])
            else:
                query_chunks = ring_query.last(*state[:1])
                new_chunks = ring_new.last(*state[:1])
            state = prepare(kv_cache, table, length, part, parts, state)
        keys, values = state
    else:
        order = jnp.zeros((1,), jnp.int32)
        gather = lambda array: lax.all_gather(array, "req", axis=0, tiled=True)
        query_chunks = [gather(w_query)]
        new_chunks = [gather(w_kv.reshape(w_kv.shape[0], -1))]
        whole = lax.all_gather(tokens, "tp", axis=0, tiled=True)
        keys, values = prepare(kv_cache, table, length, 0, 1, ())
    hidden = whole.astype(jnp.float32)
    normed = (
        hidden * lax.rsqrt(jnp.mean(hidden * hidden, axis=-1, keepdims=True) + epsilon) * norm_gain
    ).astype(jnp.bfloat16)
    positions = length[0] + jnp.arange(normed.shape[0], dtype=jnp.int32)
    cosine, sines = rope_tables(positions, dim)
    new_keys, new_values = project_new(normed, new_chunks, order, cosine, sines, heads, dim)
    queries = project_query(normed, query_chunks, order, cosine, sines, heads, group, dim)

    def attend_at(head, tile, valid):
        return attend(head, tile, keys, values, queries, new_keys, new_values, length, valid)

    if not fast:
        tiles = [jnp.full((1,), q, jnp.int32) for q in range(normed.shape[0] // token_tile)]
        attended = jnp.concatenate(
            [
                jnp.concatenate([attend_at(h, tile, span_len) for h in range(heads)], axis=1)
                for tile in tiles
            ],
            axis=0,
        )
        gathered = lax.all_gather(w_out, "req", axis=1, tiled=True)
        partial = matmul(attended, gathered).astype(jnp.bfloat16)
        summed = lax.psum_scatter(partial, "tp", scatter_dimension=0, tiled=True)
        return (residual_scale * summed.astype(jnp.float32)).astype(jnp.bfloat16)
    theirs, ours = (1 - rank).reshape(1), rank.reshape(1)
    ring_out.step(ring_query.up)
    ring_out.step(queries)
    first = [attend_at(0, theirs, span_len)]
    first.append(attend_at(1, theirs, after(span_len, first[-1])))
    ring_out.step(first[-1])
    first.append(attend_at(2, theirs, after(span_len, first[-1])))
    first.append(attend_at(3, theirs, after(span_len, first[-1])))
    out_chunks = ring_out.last(first[-1])
    second = [attend_at(0, ours, after(span_len, first[-1]))]
    second.append(attend_at(1, ours, after(span_len, second[-1])))
    sent = emit(first, [after(out_chunks[0], second[-1])] + out_chunks[1:], req_count)
    received = lax.ppermute(sent, "tp", swap)
    second.append(attend_at(2, ours, after(span_len, sent)))
    second.append(attend_at(3, ours, after(span_len, second[-1])))
    kept = emit(second, out_chunks, req_count)
    return combine(kept, received, order)


def solution(mesh):
    in_specs = (
        P(("req", "tp"), None),
        P(),
        P("req", "tp"),
        P("req", "tp", None),
        P("tp", "req"),
        P("req", None, "tp", None),
        P("req", None),
        P(),
        P("req"),
    )
    out_specs = P(("req", "tp"), None)
    program = functools.partial(body, mesh.shape["req"], mesh.shape["tp"])
    return jax.shard_map(
        program, mesh=mesh, in_specs=in_specs, out_specs=out_specs, check_vma=False
    )
```

time: 164 us -> 205 us (1.25)
  the two profiles are of different devices: /device:TPU:17 before, /device:TPU:8 now
where the time goes in v2:
time: 205 us; the launch traced here: 203 us
  local copies, waits for them, and re-layouts  63 us (31%)
  starting transfers between devices  54.3 us (26%)
  Pallas kernels  51 us (25%)
  waiting for transfers between devices  29.7 us (14%)
  other arithmetic  3.27 us (2%)
    unnamed x121, local copies, waits for them, and re-layouts  59.1 us
    ppermute x51, starting transfers between devices, move(): return lax.ppermute(value, 'req', pairs)  45.2 us
    ppermute x51, waiting for transfers between devices, move(): return lax.ppermute(value, 'req', pairs)  29.7 us
    pallas_call x8, Pallas kernels, attend(): pl.pallas_call(functools.partial(attend_kernel, group, dim), grid=(1,), i...  28.9 us
    pallas_call x4, Pallas kernels, prepare(): pl.pallas_call(functools.partial(prepare_kernel, heads, page, width, page...  14.1 us
    ppermute x1, starting transfers between devices, body(): received = lax.ppermute(sent, 'tp', swap)  7.56 us
    pallas_call x2, Pallas kernels, project(): pl.pallas_call(kernel, in_specs=[smem()] + [vmem()] * (len(chunks) + 3),...  4.95 us
  transfers between devices with their start and end apart: 53, of which 12 were waited for; matrix products, arithmetic and copies ran while one was open for 4% of the time, Pallas kernels for 24%

profile of v2, /device:TPU:8, one launch (start us, length us, event | category | flops | bytes accessed | tf_op | source)
XLA Modules:
  0.0 202.6 jit_solution(5845506210129810217)
XLA Ops:
  0.0 1.6 collective-permute-start.1
  3.3 3.4 %copy-done = bf16[64,128,4,128]{3,2,1,0:T(4,128)(2,1)S(1)} copy-done((bf16[64,128,4,128]{3,2,1,0:T(4,128)(2,1)S(1)}, bf16[64,128,4,128]{3,2,1,0:T(4,128)(2,1)}, u32[]{:S(2)}) %copy-start) | copy-done | bytes 8388632
  7.3 3.5 %prepare.4 = (bf16[4,8192,128]{2,1,0:T(8,128)(2,1)S(1)}, bf16[4,80,8192]{2,1,0:T(8,128)(2,1)S(1)}) custom-call(s32[64]{0:T(128)S(1)} %bitcast.33, s32[1]{0:T(128)} %dynamic_slice.7.length_ref, bf16[64,512,128]{2,1,0:T(8,128)(2,1)S(1)} %bitcast.11, bf16[64,512,128]{2,1,0:T(8,128)(2,1)S(1)} %bitcast.12, bf16[64,512,128]{2,1,0:T(8,128)(2,1)S(1)} %bitcast.13, ...), custom_call_target="tpu_custom_call" | custom-call | bytes 6291456 | tf_op jit(solution)/shard_map/prepare/pallas_call | solution.py:145
  10.9 1.6 collective-permute-start.5
  13.0 1.6 collective-permute-start.19
  15.1 6.2 %collective-permute-done.19.refs_2_ = bf16[128,512]{1,0:T(8,128)(2,1)S(1)} collective-permute-done((bf16[128,512]{1,0:T(8,128)(2,1)S(1)}, bf16[128,512]{1,0:T(8,128)(2,1)S(1)}, u32[]{:S(2)}, u32[]{:S(2)}) %collective-permute-start.19) | collective-permute-done | bytes 131104 | tf_op jit(solution)/shard_map/ppermute | solution.py:76
  21.2 1.3 collective-permute-done.21.refs_4_
  22.5 1.6 collective-permute-start.23
  25.2 3.6 %prepare.5 = (bf16[4,8192,128]{2,1,0:T(8,128)(2,1)S(1)}, bf16[4,80,8192]{2,1,0:T(8,128)(2,1)S(1)}) custom-call(s32[64]{0:T(128)S(1)} %bitcast.34, s32[1]{0:T(128)} %dynamic_slice.7.length_ref, bf16[64,512,128]{2,1,0:T(8,128)(2,1)S(1)} %bitcast.15, bf16[64,512,128]{2,1,0:T(8,128)(2,1)S(1)} %bitcast.16, ...), custom_call_target="tpu_custom_call", output_to_operand_aliasing={{0}: (6, {}), {1}: (7, {})} | custom-call | bytes 6291456 | tf_op jit(solution)/shard_map/prepare/pallas_call | solution.py:145
  28.8 3.3 %copy-done.3 = bf16[4,8192,128]{2,1,0:T(8,128)(2,1)} copy-done((bf16[4,8192,128]{2,1,0:T(8,128)(2,1)}, bf16[4,8192,128]{2,1,0:T(8,128)(2,1)S(1)}, u32[]{:S(2)}) %copy-start.3) | copy-done | bytes 8388632
  32.1 2.4 %copy-done.9 = bf16[4,80,8192]{2,1,0:T(8,128)(2,1)} copy-done((bf16[4,80,8192]{2,1,0:T(8,128)(2,1)}, bf16[4,80,8192]{2,1,0:T(8,128)(2,1)S(1)}, u32[]{:S(2)}) %copy-start.9) | copy-done | bytes 5242904
  34.9 1.6 collective-permute-start.9
  37.2 1.5 collective-permute-start.17
  39.3 1.6 collective-permute-start.27
  42.6 3.6 %collective-permute-done.27.refs_10_ = bf16[128,512]{1,0:T(8,128)(2,1)} collective-permute-done((bf16[128,512]{1,0:T(8,128)(2,1)S(1)}, bf16[128,512]{1,0:T(8,128)(2,1)}, u32[]{:S(2)}, u32[]{:S(2)}) %collective-permute-start.27) | collective-permute-done | bytes 131104 | tf_op jit(solution)/shard_map/ppermute | solution.py:76
  48.9 3.4 %copy-done.1 = bf16[64,128,4,128]{3,2,1,0:T(4,128)(2,1)S(1)} copy-done((bf16[64,128,4,128]{3,2,1,0:T(4,128)(2,1)S(1)}, bf16[64,128,4,128]{3,2,1,0:T(4,128)(2,1)}, u32[]{:S(2)}) %copy-start.1) | copy-done | bytes 8388632
  52.3 3.4 %copy-done.4 = bf16[4,8192,128]{2,1,0:T(8,128)(2,1)S(1)} copy-done((bf16[4,8192,128]{2,1,0:T(8,128)(2,1)S(1)}, bf16[4,8192,128]{2,1,0:T(8,128)(2,1)}, u32[]{:S(2)}) %copy-start.4) | copy-done | bytes 8388632
  55.7 2.5 %copy-done.10 = bf16[4,80,8192]{2,1,0:T(8,128)(2,1)S(1)} copy-done((bf16[4,80,8192]{2,1,0:T(8,128)(2,1)S(1)}, bf16[4,80,8192]{2,1,0:T(8,128)(2,1)}, u32[]{:S(2)}) %copy-start.10) | copy-done | bytes 5242904
  58.2 3.5 %prepare.6 = (bf16[4,8192,128]{2,1,0:T(8,128)(2,1)S(1)}, bf16[4,80,8192]{2,1,0:T(8,128)(2,1)S(1)}) custom-call(s32[64]{0:T(128)S(1)} %bitcast.35, s32[1]{0:T(128)} %dynamic_slice.7.length_ref, bf16[64,512,128]{2,1,0:T(8,128)(2,1)S(1)} %bitcast.19, bf16[64,512,128]{2,1,0:T(8,128)(2,1)S(1)} %bitcast.20, ...), custom_call_target="tpu_custom_call", output_to_operand_aliasing={{0}: (6, {}), {1}: (7, {})} | custom-call | bytes 6291456 | tf_op jit(solution)/shard_map/prepare/pallas_call | solution.py:145
  61.7 3.3 %copy-done.5 = bf16[4,8192,128]{2,1,0:T(8,128)(2,1)} copy-done((bf16[4,8192,128]{2,1,0:T(8,128)(2,1)}, bf16[4,8192,128]{2,1,0:T(8,128)(2,1)S(1)}, u32[]{:S(2)}) %copy-start.5) | copy-done | bytes 8388632
  67.0 1.6 collective-permute-start.31
  70.5 1.5 collective-permute-start.13
  73.2 1.3 broadcast_select_fusion.1
  76.4 1.9 collective-permute-done.14.refs_15_
  79.8 1.5 collective-permute-start.36
  82.2 6.2 %collective-permute-done.36.refs_6_ = bf16[1024,128]{1,0:T(8,128)(2,1)S(1)} collective-permute-done((bf16[1024,128]{1,0:T(8,128)(2,1)S(1)}, bf16[1024,128]{1,0:T(8,128)(2,1)S(1)}, u32[]{:S(2)}, u32[]{:S(2)}) %collective-permute-start.36) | collective-permute-done | bytes 262176 | tf_op jit(solution)/shard_map/ppermute | solution.py:76
  90.6 2.2 %query.1.query_ref = bf16[4,2,128,512]{3,2,1,0:T(8,128)(2,1)S(1)} custom-call(s32[16]{0:T(128)S(1)} %dynamic-slice_bitcast_fusion.order_ref, bf16[128,1024]{1,0:T(8,128)(2,1)S(1)} %copy-done.21, bf16[128,1024]{1,0:T(8,128)(2,1)S(1)} %copy-done.31, bf16[128,1024]{1,0:T(8,128)(2,1)S(1)} %copy-done.23, bf16[128,1024]{1,0:T(8,128)(2,1)S(1)} %copy-done.33, ...), custom_call_target="tpu_custom_call" | custom-call | flops 1073741824 | bytes 4194304 | tf_op jit(solution)/shard_map/query/pallas_call | solution.py:237
  93.5 1.5 collective-permute-start.40
  106.6 2.7 %new.1 = (bf16[4,256,128]{2,1,0:T(8,128)(2,1)S(1)}, bf16[4,80,256]{2,1,0:T(8,128)(2,1)S(1)}) custom-call(s32[16]{0:T(128)S(1)} %dynamic-slice_bitcast_fusion.order_ref, bf16[128,512]{1,0:T(8,128)(2,1)S(1)} %bitcast.32, bf16[128,512]{1,0:T(8,128)(2,1)S(1)} %copy-done.43, bf16[128,512]{1,0:T(8,128)(2,1)S(1)} %copy-done.37, bf16[128,512]{1,0:T(8,128)(2,1)S(1)} %copy-done.45, ...), custom_call_target="tpu_custom_call" | custom-call | flops 536870912 | bytes 2097152 | tf_op jit(solution)/shard_map/new/pallas_call | solution.py:237
  109.3 3.4 %copy-done.2 = bf16[64,128,4,128]{3,2,1,0:T(4,128)(2,1)S(1)} copy-done((bf16[64,128,4,128]{3,2,1,0:T(4,128)(2,1)S(1)}, bf16[64,128,4,128]{3,2,1,0:T(4,128)(2,1)}, u32[]{:S(2)}) %copy-start.2) | copy-done | bytes 8388632
  112.7 3.4 %copy-done.6 = bf16[4,8192,128]{2,1,0:T(8,128)(2,1)S(1)} copy-done((bf16[4,8192,128]{2,1,0:T(8,128)(2,1)S(1)}, bf16[4,8192,128]{2,1,0:T(8,128)(2,1)}, u32[]{:S(2)}) %copy-start.6) | copy-done | bytes 8388632
  116.0 2.5 %copy-done.12 = bf16[4,80,8192]{2,1,0:T(8,128)(2,1)S(1)} copy-done((bf16[4,80,8192]{2,1,0:T(8,128)(2,1)S(1)}, bf16[4,80,8192]{2,1,0:T(8,128)(2,1)}, u32[]{:S(2)}) %copy-start.12) | copy-done | bytes 5242904
  118.5 3.5 %prepare.7 = (bf16[4,8192,128]{2,1,0:T(8,128)(2,1)S(1)}, bf16[4,80,8192]{2,1,0:T(8,128)(2,1)S(1)}) custom-call(s32[64]{0:T(128)S(1)} %bitcast.36, s32[1]{0:T(128)} %dynamic_slice.7.length_ref, bf16[64,512,128]{2,1,0:T(8,128)(2,1)S(1)} %bitcast.23, bf16[64,512,128]{2,1,0:T(8,128)(2,1)S(1)} %bitcast.24, ...), custom_call_target="tpu_custom_call", output_to_operand_aliasing={{0}: (6, {}), {1}: (7, {})} | custom-call | bytes 6291456 | tf_op jit(solution)/shard_map/prepare/pallas_call | solution.py:145
  122.1 3.3 %copy-done.7 = bf16[4,8192,128]{2,1,0:T(8,128)(2,1)} copy-done((bf16[4,8192,128]{2,1,0:T(8,128)(2,1)}, bf16[4,8192,128]{2,1,0:T(8,128)(2,1)S(1)}, u32[]{:S(2)}) %copy-start.7) | copy-done | bytes 8388632
  125.4 2.4 %copy-done.13 = bf16[4,80,8192]{2,1,0:T(8,128)(2,1)} copy-done((bf16[4,80,8192]{2,1,0:T(8,128)(2,1)}, bf16[4,80,8192]{2,1,0:T(8,128)(2,1)S(1)}, u32[]{:S(2)}) %copy-start.13) | copy-done | bytes 5242904
  127.8 3.4 %copy-done.8 = bf16[4,8192,128]{2,1,0:T(8,128)(2,1)S(1)} copy-done((bf16[4,8192,128]{2,1,0:T(8,128)(2,1)S(1)}, bf16[4,8192,128]{2,1,0:T(8,128)(2,1)}, u32[]{:S(2)}) %copy-start.8) | copy-done | bytes 8388632
  131.2 2.5 %copy-done.14 = bf16[4,80,8192]{2,1,0:T(8,128)(2,1)S(1)} copy-done((bf16[4,80,8192]{2,1,0:T(8,128)(2,1)S(1)}, bf16[4,80,8192]{2,1,0:T(8,128)(2,1)}, u32[]{:S(2)}) %copy-start.14) | copy-done | bytes 5242904
  134.2 7.7 %collective-permute-start.44 = (bf16[1024,128]{1,0:T(8,128)(2,1)S(1)}, bf16[1024,128]{1,0:T(8,128)(2,1)S(1)}, u32[]{:S(2)}, u32[]{:S(2)}) collective-permute-start(bf16[1024,128]{1,0:T(8,128)(2,1)S(1)} %collective-permute-done.40.refs_10_), channel_id=1, source_target_pairs={{0,8},{2,10},{8,16},{10,18},{16,24},{18,26},{24,28},{26,30},{28,20... | collective-permute-start | bytes 786440 | tf_op jit(solution)/shard_map/ppermute | solution.py:76
  142.6 5.1 %collective-permute-done.44.refs_14_ = bf16[1024,128]{1,0:T(8,128)(2,1)S(1)} collective-permute-done((bf16[1024,128]{1,0:T(8,128)(2,1)S(1)}, bf16[1024,128]{1,0:T(8,128)(2,1)S(1)}, u32[]{:S(2)}, u32[]{:S(2)}) %collective-permute-start.44) | collective-permute-done | bytes 262176 | tf_op jit(solution)/shard_map/ppermute | solution.py:76
  149.4 1.7 collective-permute-done.46.refs_16_
  151.2 10.2 %collective-permute-start.43 = (bf16[1024,128]{1,0:T(8,128)(2,1)S(1)}, bf16[1024,128]{1,0:T(8,128)(2,1)S(1)}, u32[]{:S(2)}, u32[]{:S(2)}) collective-permute-start(bf16[1024,128]{1,0:T(8,128)(2,1)S(1)} %collective-permute-done.42.refs_12_), channel_id=1, source_target_pairs={{0,2},{2,0},{4,6},{6,4},{8,10},{10,8},{12,14},{14,12},{16,18},{18,... | collective-permute-start | bytes 786440 | tf_op jit(solution)/shard_map/ppermute | solution.py:76
  162.1 1.4 collective-permute-start.49
  164.0 6.7 %attend.13.refs_1_ = bf16[128,256]{1,0:T(8,128)(2,1)S(1)} custom-call(s32[1]{0:T(128)} %dynamic_slice.7.length_ref, s32[1]{0:T(128)S(6)} %copy.26.span_ref, s32[1]{0:T(128)} %bitcast.5.tile_ref, bf16[4,8192,128]{2,1,0:T(8,128)(2,1)S(1)} %copy-done.8, bf16[4,80,8192]{2,1,0:T(8,128)(2,1)S(1)} %copy-done.14, bf16[4,2,128,512]{3,2,1,0:T(8,128)(2,1)S(1)} %query.1.query_ref, ...), custom_call_target="tpu_custom_call" | custom-call | flops 2147483648 | bytes 4194304 | tf_op jit(solution)/shard_map/attend/pallas_call | solution.py:371
  173.0 7.6 %collective-permute-start.52 = (bf16[16,128,128]{2,1,0:T(8,128)(2,1)S(1)}, bf16[16,128,128]{2,1,0:T(8,128)(2,1)S(1)}, u32[]{:S(2)}, u32[]{:S(2)}) collective-permute-start(bf16[16,128,128]{2,1,0:T(8,128)(2,1)S(1)} %emit.2), channel_id=1, source_target_pairs={{0,1},{1,0},{2,3},{3,2},{4,5},{5,4},{6,7},{7,6},{8,9},{9,8},{10,11... | collective-permute-start | bytes 1572872 | tf_op jit(solution)/shard_map/ppermute | solution.py:530
  180.6 6.5 %attend.12.refs_0_ = bf16[128,256]{1,0:T(8,128)(2,1)S(1)} custom-call(s32[1]{0:T(128)} %dynamic_slice.7.length_ref, s32[1]{0:T(128)S(6)} %copy.26.span_ref, s32[1]{0:T(128)} %bitcast.5.tile_ref, bf16[4,8192,128]{2,1,0:T(8,128)(2,1)S(1)} %bitcast.28, bf16[4,80,8192]{2,1,0:T(8,128)(2,1)S(1)} %copy-done.14, bf16[4,2,128,512]{3,2,1,0:T(8,128)(2,1)S(1)} %query.1.query_ref, ...), custom_call_target="tpu_custom_call" | custom-call | flops 2147483648 | bytes 4194304 | tf_op jit(solution)/shard_map/attend/pallas_call | solution.py:371
  187.1 6.7 %attend.14.refs_2_ = bf16[128,256]{1,0:T(8,128)(2,1)S(1)} custom-call(s32[1]{0:T(128)} %dynamic_slice.7.length_ref, s32[1]{0:T(128)S(6)} %copy.26.span_ref, s32[1]{0:T(128)} %bitcast.5.tile_ref, bf16[4,8192,128]{2,1,0:T(8,128)(2,1)S(1)} %bitcast.28, bf16[4,80,8192]{2,1,0:T(8,128)(2,1)S(1)} %copy-done.14, bf16[4,2,128,512]{3,2,1,0:T(8,128)(2,1)S(1)} %query.1.query_ref, ...), custom_call_target="tpu_custom_call" | custom-call | flops 2147483648 | bytes 4194304 | tf_op jit(solution)/shard_map/attend/pallas_call | solution.py:371
  193.8 6.5 %attend.15.refs_3_ = bf16[128,256]{1,0:T(8,128)(2,1)S(1)} custom-call(s32[1]{0:T(128)} %dynamic_slice.7.length_ref, s32[1]{0:T(128)S(6)} %copy.26.span_ref, s32[1]{0:T(128)} %bitcast.5.tile_ref, bf16[4,8192,128]{2,1,0:T(8,128)(2,1)S(1)} %bitcast.28, bf16[4,80,8192]{2,1,0:T(8,128)(2,1)S(1)} %copy-done.14, bf16[4,2,128,512]{3,2,1,0:T(8,128)(2,1)S(1)} %query.1.query_ref, ...), custom_call_target="tpu_custom_call" | custom-call | flops 2147483648 | bytes 4194304 | tf_op jit(solution)/shard_map/attend/pallas_call | solution.py:371
  201.1 1.5 combine.1
  (212 shorter events, 40.5 us)
Async XLA Ops:
  0.0 10.8 %collective-permute-start.1 = (bf16[128,1024]{1,0:T(8,128)(2,1)}, bf16[128,1024]{1,0:T(8,128)(2,1)S(1)}, u32[]{:S(2)}, u32[]{:S(2)}) collective-permute-start(bf16[128,1024]{1,0:T(8,128)(2,1)} %refs_0_.1), channel_id=1, source_target_pairs={{0,8},{2,10},{8,16},{10,18},{16,24},{18,26},{24,28},{26,30},{28,20... | collective-permute-start | bytes 786440 | tf_op jit(solution)/shard_map/ppermute | solution.py:76
  1.6 9.3 %collective-permute-start.3 = (bf16[128,1024]{1,0:T(8,128)(2,1)}, bf16[128,1024]{1,0:T(8,128)(2,1)S(1)}, u32[]{:S(2)}, u32[]{:S(2)}) collective-permute-start(bf16[128,1024]{1,0:T(8,128)(2,1)} %refs_0_.1), channel_id=1, source_target_pairs={{8,0},{10,2},{16,8},{18,10},{24,16},{26,18},{28,24},{30,26},{20,28... | collective-permute-start | bytes 786440 | tf_op jit(solution)/shard_map/ppermute | solution.py:76
  10.9 13.7 %collective-permute-start.5 = (bf16[128,1024]{1,0:T(8,128)(2,1)S(1)}, bf16[128,1024]{1,0:T(8,128)(2,1)S(1)}, u32[]{:S(2)}, u32[]{:S(2)}) collective-permute-start(bf16[128,1024]{1,0:T(8,128)(2,1)S(1)} %collective-permute-done.1.refs_2_), channel_id=1, source_target_pairs={{0,8},{2,10},{8,16},{10,18},{16,24},{18,26},{24,28},{26,30},{28,20... | collective-permute-start | bytes 786440 | tf_op jit(solution)/shard_map/ppermute | solution.py:76
  12.5 12.6 %collective-permute-start.7 = (bf16[128,1024]{1,0:T(8,128)(2,1)S(1)}, bf16[128,1024]{1,0:T(8,128)(2,1)S(1)}, u32[]{:S(2)}, u32[]{:S(2)}) collective-permute-start(bf16[128,1024]{1,0:T(8,128)(2,1)S(1)} %collective-permute-done.3.refs_4_), channel_id=1, source_target_pairs={{8,0},{10,2},{16,8},{18,10},{24,16},{26,18},{28,24},{30,26},{20,28... | collective-permute-start | bytes 786440 | tf_op jit(solution)/shard_map/ppermute | solution.py:76
  13.0 8.2 %collective-permute-start.19 = (bf16[128,512]{1,0:T(8,128)(2,1)S(1)}, bf16[128,512]{1,0:T(8,128)(2,1)S(1)}, u32[]{:S(2)}, u32[]{:S(2)}) collective-permute-start(bf16[128,512]{1,0:T(8,128)(2,1)S(1)} %bitcast.29), channel_id=1, source_target_pairs={{0,8},{2,10},{8,16},{10,18},{16,24},{18,26},{24,28},{26,30},{28,20... | collective-permute-start | bytes 393224 | tf_op jit(solution)/shard_map/ppermute | solution.py:76
  14.6 7.9 %collective-permute-start.21 = (bf16[128,512]{1,0:T(8,128)(2,1)S(1)}, bf16[128,512]{1,0:T(8,128)(2,1)S(1)}, u32[]{:S(2)}, u32[]{:S(2)}) collective-permute-start(bf16[128,512]{1,0:T(8,128)(2,1)S(1)} %bitcast.30), channel_id=1, source_target_pairs={{8,0},{10,2},{16,8},{18,10},{24,16},{26,18},{28,24},{30,26},{20,28... | collective-permute-start | bytes 393224 | tf_op jit(solution)/shard_map/ppermute | solution.py:76
  22.5 12.0 %collective-permute-start.23 = (bf16[128,512]{1,0:T(8,128)(2,1)S(1)}, bf16[128,512]{1,0:T(8,128)(2,1)S(1)}, u32[]{:S(2)}, u32[]{:S(2)}) collective-permute-start(bf16[128,512]{1,0:T(8,128)(2,1)S(1)} %collective-permute-done.19.refs_2_), channel_id=1, source_target_pairs={{0,8},{2,10},{8,16},{10,18},{16,24},{18,26},{24,28},{26,30},{28,20... | collective-permute-start | bytes 393224 | tf_op jit(solution)/shard_map/ppermute | solution.py:76
  24.1 10.8 %collective-permute-start.25 = (bf16[128,512]{1,0:T(8,128)(2,1)S(1)}, bf16[128,512]{1,0:T(8,128)(2,1)}, u32[]{:S(2)}, u32[]{:S(2)}) collective-permute-start(bf16[128,512]{1,0:T(8,128)(2,1)S(1)} %collective-permute-done.21.refs_4_), channel_id=1, source_target_pairs={{8,0},{10,2},{16,8},{18,10},{24,16},{26,18},{28,24},{30,26},{20,28... | collective-permute-start | bytes 393224 | tf_op jit(solution)/shard_map/ppermute | solution.py:76
  24.5 12.0 %collective-permute-start.18 = (bf16[128,512]{1,0:T(8,128)(2,1)S(1)}, bf16[128,512]{1,0:T(8,128)(2,1)S(1)}, u32[]{:S(2)}, u32[]{:S(2)}) collective-permute-start(bf16[128,512]{1,0:T(8,128)(2,1)S(1)} %bitcast.31), channel_id=1, source_target_pairs={{0,2},{2,0},{4,6},{6,4},{8,10},{10,8},{12,14},{14,12},{16,18},{18,... | collective-permute-start | bytes 393224 | tf_op jit(solution)/shard_map/ppermute | solution.py:76
  24.6 14.1 %collective-permute-start.20 = (bf16[128,512]{1,0:T(8,128)(2,1)S(1)}, bf16[128,512]{1,0:T(8,128)(2,1)S(1)}, u32[]{:S(2)}, u32[]{:S(2)}) collective-permute-start(bf16[128,512]{1,0:T(8,128)(2,1)S(1)} %collective-permute-done.19.refs_2_), channel_id=1, source_target_pairs={{0,2},{2,0},{4,6},{6,4},{8,10},{10,8},{12,14},{14,12},{16,18},{18,... | collective-permute-start | bytes 393224 | tf_op jit(solution)/shard_map/ppermute | solution.py:76
  25.1 15.8 %collective-permute-start.22 = (bf16[128,512]{1,0:T(8,128)(2,1)S(1)}, bf16[128,512]{1,0:T(8,128)(2,1)S(1)}, u32[]{:S(2)}, u32[]{:S(2)}) collective-permute-start(bf16[128,512]{1,0:T(8,128)(2,1)S(1)} %collective-permute-done.21.refs_4_), channel_id=1, source_target_pairs={{0,2},{2,0},{4,6},{6,4},{8,10},{10,8},{12,14},{14,12},{16,18},{18,... | collective-permute-start | bytes 393224 | tf_op jit(solution)/shard_map/ppermute | solution.py:76
  34.5 12.3 %collective-permute-start.11 = (bf16[128,1024]{1,0:T(8,128)(2,1)S(1)}, bf16[128,1024]{1,0:T(8,128)(2,1)S(1)}, u32[]{:S(2)}, u32[]{:S(2)}) collective-permute-start(bf16[128,1024]{1,0:T(8,128)(2,1)S(1)} %collective-permute-done.7.refs_8_), channel_id=1, source_target_pairs={{8,0},{10,2},{16,8},{18,10},{24,16},{26,18},{28,24},{30,26},{20,28... | collective-permute-start | bytes 786440 | tf_op jit(solution)/shard_map/ppermute | solution.py:76
  34.9 12.4 %collective-permute-start.9 = (bf16[128,1024]{1,0:T(8,128)(2,1)S(1)}, bf16[128,1024]{1,0:T(8,128)(2,1)S(1)}, u32[]{:S(2)}, u32[]{:S(2)}) collective-permute-start(bf16[128,1024]{1,0:T(8,128)(2,1)S(1)} %collective-permute-done.5.refs_6_), channel_id=1, source_target_pairs={{0,8},{2,10},{8,16},{10,18},{16,24},{18,26},{24,28},{26,30},{28,20... | collective-permute-start | bytes 786440 | tf_op jit(solution)/shard_map/ppermute | solution.py:76
  37.2 32.6 %collective-permute-start.17 = (bf16[128,2048]{1,0:T(8,128)(2,1)}, bf16[128,2048]{1,0:T(8,128)(2,1)}, u32[]{:S(2)}, u32[]{:S(2)}) collective-permute-start(bf16[128,2048]{1,0:T(8,128)(2,1)} %param.10), channel_id=1, source_target_pairs={{0,1},{1,0},{2,3},{3,2},{4,5},{5,4},{6,7},{7,6},{8,9},{9,8},{10,11... | collective-permute-start | bytes 1572872 | tf_op jit(solution)/shard_map/ppermute | solution.py:471
  39.3 6.9 %collective-permute-start.27 = (bf16[128,512]{1,0:T(8,128)(2,1)S(1)}, bf16[128,512]{1,0:T(8,128)(2,1)}, u32[]{:S(2)}, u32[]{:S(2)}) collective-permute-start(bf16[128,512]{1,0:T(8,128)(2,1)S(1)} %collective-permute-done.23.refs_6_), channel_id=1, source_target_pairs={{0,8},{2,10},{8,16},{10,18},{16,24},{18,26},{24,28},{26,30},{28,20... | collective-permute-start | bytes 393224 | tf_op jit(solution)/shard_map/ppermute | solution.py:76
  41.5 5.3 %collective-permute-start.29 = (bf16[128,512]{1,0:T(8,128)(2,1)}, bf16[128,512]{1,0:T(8,128)(2,1)}, u32[]{:S(2)}, u32[]{:S(2)}) collective-permute-start(bf16[128,512]{1,0:T(8,128)(2,1)} %collective-permute-done.25.refs_8_), channel_id=1, source_target_pairs={{8,0},{10,2},{16,8},{18,10},{24,16},{26,18},{28,24},{30,26},{20,28... | collective-permute-start | bytes 393224 | tf_op jit(solution)/shard_map/ppermute | solution.py:76
  46.2 20.8 %collective-permute-start = (bf16[128,1024]{1,0:T(8,128)(2,1)S(1)}, bf16[128,1024]{1,0:T(8,128)(2,1)S(1)}, u32[]{:S(2)}, u32[]{:S(2)}) collective-permute-start(bf16[128,1024]{1,0:T(8,128)(2,1)S(1)} %copy-done.20), channel_id=1, source_target_pairs={{0,2},{2,0},{4,6},{6,4},{8,10},{10,8},{12,14},{14,12},{16,18},{18,... | collective-permute-start | bytes 786440 | tf_op jit(solution)/shard_map/ppermute | solution.py:76
  46.8 21.8 %collective-permute-start.24 = (bf16[128,512]{1,0:T(8,128)(2,1)S(1)}, bf16[128,512]{1,0:T(8,128)(2,1)S(1)}, u32[]{:S(2)}, u32[]{:S(2)}) collective-permute-start(bf16[128,512]{1,0:T(8,128)(2,1)S(1)} %collective-permute-done.23.refs_6_), channel_id=1, source_target_pairs={{0,2},{2,0},{4,6},{6,4},{8,10},{10,8},{12,14},{14,12},{16,18},{18,... | collective-permute-start | bytes 393224 | tf_op jit(solution)/shard_map/ppermute | solution.py:76
  46.8 22.9 %collective-permute-start.2 = (bf16[128,1024]{1,0:T(8,128)(2,1)S(1)}, bf16[128,1024]{1,0:T(8,128)(2,1)S(1)}, u32[]{:S(2)}, u32[]{:S(2)}) collective-permute-start(bf16[128,1024]{1,0:T(8,128)(2,1)S(1)} %collective-permute-done.1.refs_2_), channel_id=1, source_target_pairs={{0,2},{2,0},{4,6},{6,4},{8,10},{10,8},{12,14},{14,12},{16,18},{18,... | collective-permute-start | bytes 786440 | tf_op jit(solution)/shard_map/ppermute | solution.py:76
  47.3 24.7 %collective-permute-start.4 = (bf16[128,1024]{1,0:T(8,128)(2,1)S(1)}, bf16[128,1024]{1,0:T(8,128)(2,1)S(1)}, u32[]{:S(2)}, u32[]{:S(2)}) collective-permute-start(bf16[128,1024]{1,0:T(8,128)(2,1)S(1)} %collective-permute-done.3.refs_4_), channel_id=1, source_target_pairs={{0,2},{2,0},{4,6},{6,4},{8,10},{10,8},{12,14},{14,12},{16,18},{18,... | collective-permute-start | bytes 786440 | tf_op jit(solution)/shard_map/ppermute | solution.py:76
  67.0 7.5 %collective-permute-start.31 = (bf16[64,512]{1,0:T(8,128)(2,1)S(1)}, bf16[64,512]{1,0:T(8,128)(2,1)}, u32[]{:S(2)}, u32[]{:S(2)}) collective-permute-start(bf16[64,512]{1,0:T(8,128)(2,1)S(1)} %slice.20), channel_id=1, source_target_pairs={{0,8},{2,10},{8,16},{10,18},{16,24},{18,26},{24,28},{26,30},{28,20... | collective-permute-start | bytes 196616 | tf_op jit(solution)/shard_map/ppermute | solution.py:76
  69.2 5.4 %collective-permute-start.32 = (bf16[64,512]{1,0:T(8,128)(2,1)S(1)}, bf16[64,512]{1,0:T(8,128)(2,1)}, u32[]{:S(2)}, u32[]{:S(2)}) collective-permute-start(bf16[64,512]{1,0:T(8,128)(2,1)S(1)} %slice.21), channel_id=1, source_target_pairs={{8,0},{10,2},{16,8},{18,10},{24,16},{26,18},{28,24},{30,26},{20,28... | collective-permute-start | bytes 196616 | tf_op jit(solution)/shard_map/ppermute | solution.py:76
  69.7 5.4 %collective-permute-start.6 = (bf16[128,1024]{1,0:T(8,128)(2,1)S(1)}, bf16[128,1024]{1,0:T(8,128)(2,1)S(1)}, u32[]{:S(2)}, u32[]{:S(2)}) collective-permute-start(bf16[128,1024]{1,0:T(8,128)(2,1)S(1)} %collective-permute-done.5.refs_6_), channel_id=1, source_target_pairs={{0,2},{2,0},{4,6},{6,4},{8,10},{10,8},{12,14},{14,12},{16,18},{18,... | collective-permute-start | bytes 786440 | tf_op jit(solution)/shard_map/ppermute | solution.py:76
  70.5 5.9 %collective-permute-start.13 = (bf16[64,1024]{1,0:T(8,128)(2,1)S(1)}, bf16[64,1024]{1,0:T(8,128)(2,1)S(1)}, u32[]{:S(2)}, u32[]{:S(2)}) collective-permute-start(bf16[64,1024]{1,0:T(8,128)(2,1)S(1)} %slice.18), channel_id=1, source_target_pairs={{0,8},{2,10},{8,16},{10,18},{16,24},{18,26},{24,28},{26,30},{28,20... | collective-permute-start | bytes 393224 | tf_op jit(solution)/shard_map/ppermute | solution.py:76
  72.7 5.6 %collective-permute-start.14 = (bf16[64,1024]{1,0:T(8,128)(2,1)S(1)}, bf16[64,1024]{1,0:T(8,128)(2,1)S(1)}, u32[]{:S(2)}, u32[]{:S(2)}) collective-permute-start(bf16[64,1024]{1,0:T(8,128)(2,1)S(1)} %slice.19), channel_id=1, source_target_pairs={{8,0},{10,2},{16,8},{18,10},{24,16},{26,18},{28,24},{30,26},{20,28... | collective-permute-start | bytes 393224 | tf_op jit(solution)/shard_map/ppermute | solution.py:76
  74.7 5.1 %collective-permute-start.10 = (bf16[128,1024]{1,0:T(8,128)(2,1)S(1)}, bf16[128,1024]{1,0:T(8,128)(2,1)S(1)}, u32[]{:S(2)}, u32[]{:S(2)}) collective-permute-start(bf16[128,1024]{1,0:T(8,128)(2,1)S(1)} %collective-permute-done.9.refs_10_), channel_id=1, source_target_pairs={{0,2},{2,0},{4,6},{6,4},{8,10},{10,8},{12,14},{14,12},{16,18},{18,... | collective-permute-start | bytes 786440 | tf_op jit(solution)/shard_map/ppermute | solution.py:76
  75.2 6.1 %collective-permute-start.12 = (bf16[128,1024]{1,0:T(8,128)(2,1)S(1)}, bf16[128,1024]{1,0:T(8,128)(2,1)S(1)}, u32[]{:S(2)}, u32[]{:S(2)}) collective-permute-start(bf16[128,1024]{1,0:T(8,128)(2,1)S(1)} %collective-permute-done.11.refs_12_), channel_id=1, source_target_pairs={{0,2},{2,0},{4,6},{6,4},{8,10},{10,8},{12,14},{14,12},{16,18},{18,... | collective-permute-start | bytes 786440 | tf_op jit(solution)/shard_map/ppermute | solution.py:76
  78.3 14.5 %collective-permute-start.26 = (bf16[128,512]{1,0:T(8,128)(2,1)}, bf16[128,512]{1,0:T(8,128)(2,1)S(1)}, u32[]{:S(2)}, u32[]{:S(2)}) collective-permute-start(bf16[128,512]{1,0:T(8,128)(2,1)} %collective-permute-done.25.refs_8_), channel_id=1, source_target_pairs={{0,2},{2,0},{4,6},{6,4},{8,10},{10,8},{12,14},{14,12},{16,18},{18,... | collective-permute-start | bytes 393224 | tf_op jit(solution)/shard_map/ppermute | solution.py:76
  78.8 16.2 %collective-permute-start.28 = (bf16[128,512]{1,0:T(8,128)(2,1)}, bf16[128,512]{1,0:T(8,128)(2,1)S(1)}, u32[]{:S(2)}, u32[]{:S(2)}) collective-permute-start(bf16[128,512]{1,0:T(8,128)(2,1)} %collective-permute-done.27.refs_10_), channel_id=1, source_target_pairs={{0,2},{2,0},{4,6},{6,4},{8,10},{10,8},{12,14},{14,12},{16,18},{18,... | collective-permute-start | bytes 393224 | tf_op jit(solution)/shard_map/ppermute | solution.py:76
  79.7 17.2 %collective-permute-start.30 = (bf16[128,512]{1,0:T(8,128)(2,1)}, bf16[128,512]{1,0:T(8,128)(2,1)}, u32[]{:S(2)}, u32[]{:S(2)}) collective-permute-start(bf16[128,512]{1,0:T(8,128)(2,1)} %collective-permute-done.29.refs_12_), channel_id=1, source_target_pairs={{0,2},{2,0},{4,6},{6,4},{8,10},{10,8},{12,14},{14,12},{16,18},{18,... | collective-permute-start | bytes 393224 | tf_op jit(solution)/shard_map/ppermute | solution.py:76
  79.8 8.6 %collective-permute-start.36 = (bf16[1024,128]{1,0:T(8,128)(2,1)S(1)}, bf16[1024,128]{1,0:T(8,128)(2,1)S(1)}, u32[]{:S(2)}, u32[]{:S(2)}) collective-permute-start(bf16[1024,128]{1,0:T(8,128)(2,1)S(1)} %copy-done.15), channel_id=1, source_target_pairs={{0,8},{2,10},{8,16},{10,18},{16,24},{18,26},{24,28},{26,30},{28,20... | collective-permute-start | bytes 786440 | tf_op jit(solution)/shard_map/ppermute | solution.py:76
  81.3 8.3 %collective-permute-start.38 = (bf16[1024,128]{1,0:T(8,128)(2,1)S(1)}, bf16[1024,128]{1,0:T(8,128)(2,1)S(1)}, u32[]{:S(2)}, u32[]{:S(2)}) collective-permute-start(bf16[1024,128]{1,0:T(8,128)(2,1)S(1)} %copy-done.15), channel_id=1, source_target_pairs={{8,0},{10,2},{16,8},{18,10},{24,16},{26,18},{28,24},{30,26},{20,28... | collective-permute-start | bytes 786440 | tf_op jit(solution)/shard_map/ppermute | solution.py:76
  88.4 8.5 %collective-permute-start.33 = (bf16[64,512]{1,0:T(8,128)(2,1)}, bf16[64,512]{1,0:T(8,128)(2,1)}, u32[]{:S(2)}, u32[]{:S(2)}) collective-permute-start(bf16[64,512]{1,0:T(8,128)(2,1)} %collective-permute-done.31.refs_14_), channel_id=1, source_target_pairs={{0,2},{2,0},{4,6},{6,4},{8,10},{10,8},{12,14},{14,12},{16,18},{18,... | collective-permute-start | bytes 196616 | tf_op jit(solution)/shard_map/ppermute | solution.py:76
  89.6 7.3 %collective-permute-start.34 = (bf16[64,512]{1,0:T(8,128)(2,1)}, bf16[64,512]{1,0:T(8,128)(2,1)}, u32[]{:S(2)}, u32[]{:S(2)}) collective-permute-start(bf16[64,512]{1,0:T(8,128)(2,1)} %collective-permute-done.32.refs_15_), channel_id=1, source_target_pairs={{0,2},{2,0},{4,6},{6,4},{8,10},{10,8},{12,14},{14,12},{16,18},{18,... | collective-permute-start | bytes 196616 | tf_op jit(solution)/shard_map/ppermute | solution.py:76
  93.5 40.7 %collective-permute-start.40 = (bf16[1024,128]{1,0:T(8,128)(2,1)S(1)}, bf16[1024,128]{1,0:T(8,128)(2,1)S(1)}, u32[]{:S(2)}, u32[]{:S(2)}) collective-permute-start(bf16[1024,128]{1,0:T(8,128)(2,1)S(1)} %collective-permute-done.36.refs_6_), channel_id=1, source_target_pairs={{0,8},{2,10},{8,16},{10,18},{16,24},{18,26},{24,28},{26,30},{28,20... | collective-permute-start | bytes 786440 | tf_op jit(solution)/shard_map/ppermute | solution.py:76
  95.7 38.5 %collective-permute-start.42 = (bf16[1024,128]{1,0:T(8,128)(2,1)S(1)}, bf16[1024,128]{1,0:T(8,128)(2,1)S(1)}, u32[]{:S(2)}, u32[]{:S(2)}) collective-permute-start(bf16[1024,128]{1,0:T(8,128)(2,1)S(1)} %collective-permute-done.38.refs_8_), channel_id=1, source_target_pairs={{8,0},{10,2},{16,8},{18,10},{24,16},{26,18},{28,24},{30,26},{20,28... | collective-permute-start | bytes 786440 | tf_op jit(solution)/shard_map/ppermute | solution.py:76
  134.2 13.5 %collective-permute-start.44 = (bf16[1024,128]{1,0:T(8,128)(2,1)S(1)}, bf16[1024,128]{1,0:T(8,128)(2,1)S(1)}, u32[]{:S(2)}, u32[]{:S(2)}) collective-permute-start(bf16[1024,128]{1,0:T(8,128)(2,1)S(1)} %collective-permute-done.40.refs_10_), channel_id=1, source_target_pairs={{0,8},{2,10},{8,16},{10,18},{16,24},{18,26},{24,28},{26,30},{28,20... | collective-permute-start | bytes 786440 | tf_op jit(solution)/shard_map/ppermute | solution.py:76
  141.9 19.5 %collective-permute-start.35 = (bf16[1024,128]{1,0:T(8,128)(2,1)S(1)}, bf16[1024,128]{1,0:T(8,128)(2,1)S(1)}, u32[]{:S(2)}, u32[]{:S(2)}) collective-permute-start(bf16[1024,128]{1,0:T(8,128)(2,1)S(1)} %copy-done.15), channel_id=1, source_target_pairs={{0,2},{2,0},{4,6},{6,4},{8,10},{10,8},{12,14},{14,12},{16,18},{18,... | collective-permute-start | bytes 786440 | tf_op jit(solution)/shard_map/ppermute | solution.py:76
  141.9 20.1 %collective-permute-start.37 = (bf16[1024,128]{1,0:T(8,128)(2,1)S(1)}, bf16[1024,128]{1,0:T(8,128)(2,1)S(1)}, u32[]{:S(2)}, u32[]{:S(2)}) collective-permute-start(bf16[1024,128]{1,0:T(8,128)(2,1)S(1)} %collective-permute-done.36.refs_6_), channel_id=1, source_target_pairs={{0,2},{2,0},{4,6},{6,4},{8,10},{10,8},{12,14},{14,12},{16,18},{18,... | collective-permute-start | bytes 786440 | tf_op jit(solution)/shard_map/ppermute | solution.py:76
  142.4 21.0 %collective-permute-start.39 = (bf16[1024,128]{1,0:T(8,128)(2,1)S(1)}, bf16[1024,128]{1,0:T(8,128)(2,1)S(1)}, u32[]{:S(2)}, u32[]{:S(2)}) collective-permute-start(bf16[1024,128]{1,0:T(8,128)(2,1)S(1)} %collective-permute-done.38.refs_8_), channel_id=1, source_target_pairs={{0,2},{2,0},{4,6},{6,4},{8,10},{10,8},{12,14},{14,12},{16,18},{18,... | collective-permute-start | bytes 786440 | tf_op jit(solution)/shard_map/ppermute | solution.py:76
  142.4 8.7 %collective-permute-start.46 = (bf16[1024,128]{1,0:T(8,128)(2,1)S(1)}, bf16[1024,128]{1,0:T(8,128)(2,1)S(1)}, u32[]{:S(2)}, u32[]{:S(2)}) collective-permute-start(bf16[1024,128]{1,0:T(8,128)(2,1)S(1)} %collective-permute-done.42.refs_12_), channel_id=1, source_target_pairs={{8,0},{10,2},{16,8},{18,10},{24,16},{26,18},{28,24},{30,26},{20,28... | collective-permute-start | bytes 786440 | tf_op jit(solution)/shard_map/ppermute | solution.py:76
  147.7 15.8 %collective-permute-start.41 = (bf16[1024,128]{1,0:T(8,128)(2,1)S(1)}, bf16[1024,128]{1,0:T(8,128)(2,1)S(1)}, u32[]{:S(2)}, u32[]{:S(2)}) collective-permute-start(bf16[1024,128]{1,0:T(8,128)(2,1)S(1)} %collective-permute-done.40.refs_10_), channel_id=1, source_target_pairs={{0,2},{2,0},{4,6},{6,4},{8,10},{10,8},{12,14},{14,12},{16,18},{18,... | collective-permute-start | bytes 786440 | tf_op jit(solution)/shard_map/ppermute | solution.py:76
  151.2 21.0 %collective-permute-start.43 = (bf16[1024,128]{1,0:T(8,128)(2,1)S(1)}, bf16[1024,128]{1,0:T(8,128)(2,1)S(1)}, u32[]{:S(2)}, u32[]{:S(2)}) collective-permute-start(bf16[1024,128]{1,0:T(8,128)(2,1)S(1)} %collective-permute-done.42.refs_12_), channel_id=1, source_target_pairs={{0,2},{2,0},{4,6},{6,4},{8,10},{10,8},{12,14},{14,12},{16,18},{18,... | collective-permute-start | bytes 786440 | tf_op jit(solution)/shard_map/ppermute | solution.py:76
  161.4 9.3 %collective-permute-start.48 = (bf16[512,128]{1,0:T(8,128)(2,1)S(1)}, bf16[512,128]{1,0:T(8,128)(2,1)S(1)}, u32[]{:S(2)}, u32[]{:S(2)}) collective-permute-start(bf16[512,128]{1,0:T(8,128)(2,1)S(1)} %slice.22), channel_id=1, source_target_pairs={{0,8},{2,10},{8,16},{10,18},{16,24},{18,26},{24,28},{26,30},{28,20... | collective-permute-start | bytes 393224 | tf_op jit(solution)/shard_map/ppermute | solution.py:76
  162.1 8.8 %collective-permute-start.49 = (bf16[512,128]{1,0:T(8,128)(2,1)S(1)}, bf16[512,128]{1,0:T(8,128)(2,1)S(1)}, u32[]{:S(2)}, u32[]{:S(2)}) collective-permute-start(bf16[512,128]{1,0:T(8,128)(2,1)S(1)} %slice.23), channel_id=1, source_target_pairs={{8,0},{10,2},{16,8},{18,10},{24,16},{26,18},{28,24},{30,26},{20,28... | collective-permute-start | bytes 393224 | tf_op jit(solution)/shard_map/ppermute | solution.py:76
  163.5 8.8 %collective-permute-start.45 = (bf16[1024,128]{1,0:T(8,128)(2,1)S(1)}, bf16[1024,128]{1,0:T(8,128)(2,1)S(1)}, u32[]{:S(2)}, u32[]{:S(2)}) collective-permute-start(bf16[1024,128]{1,0:T(8,128)(2,1)S(1)} %collective-permute-done.44.refs_14_), channel_id=1, source_target_pairs={{0,2},{2,0},{4,6},{6,4},{8,10},{10,8},{12,14},{14,12},{16,18},{18,... | collective-permute-start | bytes 786440 | tf_op jit(solution)/shard_map/ppermute | solution.py:76
  163.5 8.8 %collective-permute-start.47 = (bf16[1024,128]{1,0:T(8,128)(2,1)S(1)}, bf16[1024,128]{1,0:T(8,128)(2,1)S(1)}, u32[]{:S(2)}, u32[]{:S(2)}) collective-permute-start(bf16[1024,128]{1,0:T(8,128)(2,1)S(1)} %collective-permute-done.46.refs_16_), channel_id=1, source_target_pairs={{0,2},{2,0},{4,6},{6,4},{8,10},{10,8},{12,14},{14,12},{16,18},{18,... | collective-permute-start | bytes 786440 | tf_op jit(solution)/shard_map/ppermute | solution.py:76
  173.0 28.0 %collective-permute-start.52 = (bf16[16,128,128]{2,1,0:T(8,128)(2,1)S(1)}, bf16[16,128,128]{2,1,0:T(8,128)(2,1)S(1)}, u32[]{:S(2)}, u32[]{:S(2)}) collective-permute-start(bf16[16,128,128]{2,1,0:T(8,128)(2,1)S(1)} %emit.2), channel_id=1, source_target_pairs={{0,1},{1,0},{2,3},{3,2},{4,5},{5,4},{6,7},{7,6},{8,9},{9,8},{10,11... | collective-permute-start | bytes 1572872 | tf_op jit(solution)/shard_map/ppermute | solution.py:530
  (65 other events, 554.3 us)

commit v3 on v2

--- a/solution.py
+++ b/solution.py
@@ -166,7 +166,7 @@
             bytes_accessed=3 * cache.size * cache.dtype.itemsize // parts,
             transcendentals=0,
         ),
-        compiler_params=params(16),
+        compiler_params=params(60),
         name="prepare",
     )(table, length, *([flat] * pages_step), *before)
 
@@ -196,9 +196,10 @@
     return weight
 
 
-def query_kernel(heads, group, dim, blocks, order_ref, *refs):
-    normed_ref, cos_ref, sin_ref, query_ref, weight = refs[blocks:]
-    source = assembled(refs[:blocks], order_ref, weight)
+def project_kernel(heads, new_heads, group, dim, blocks, order_ref, *refs):
+    normed_ref, cos_ref, sin_ref = refs[blocks : blocks + 3]
+    query_ref = refs[blocks + 3]
+    source = assembled(refs[:blocks], order_ref, refs[-1])
     cosine, sines = cos_ref[...], sin_ref[...]
     tokens = cosine.shape[1]
     normed = normed_ref[...]
@@ -216,26 +217,24 @@
                 ]
         for q in range(tokens // token_tile):
             query_ref[h, q, pl.ds(dim, dim), :] = one_row
-
-
-def new_kernel(heads, dim, blocks, order_ref, *refs):
-    normed_ref, cos_ref, sin_ref, key_ref, value_ref, weight = refs[blocks:]
-    source = assembled(refs[:blocks], order_ref, weight)
-    cosine, sines = cos_ref[...], sin_ref[...]
-    normed = normed_ref[...]
-    for h in range(heads):
-        turned = jnp.transpose(matmul(normed, source[:, pl.ds(h * 2 * dim, 2 * dim)]))
+    for h in range(new_heads):
+        key_ref, value_ref = refs[blocks + 4 : blocks + 6]
+        at = heads * width + h * 2 * dim
+        turned = jnp.transpose(matmul(normed, source[:, pl.ds(at, 2 * dim)]))
         keys = turn(turned[:dim], cosine, sines)
         padded = jnp.concatenate([keys, jnp.zeros_like(keys)], axis=0)
         key_ref[h] = jnp.transpose(padded).astype(jnp.bfloat16)
         value_ref[h] = with_ones(turned[dim:]).astype(jnp.bfloat16)
 
 
-def project(kernel, name, outs, normed, chunks, order, cosine, sines):
+def project(normed, chunks, order, cosine, sines, heads, new_heads, group, dim):
     tokens, width = normed.shape
     columns = chunks[0].shape[1]
+    outs = [(heads, tokens // token_tile, 2 * dim, group * token_tile)]
+    if new_heads:
+        outs += [(new_heads, tokens, 2 * dim), (new_heads, dim + 16, tokens)]
     return pl.pallas_call(
-        kernel,
+        functools.partial(project_kernel, heads, new_heads, group, dim, len(chunks)),
         in_specs=[smem()] + [vmem()] * (len(chunks) + 3),
         out_specs=[vmem()] * len(outs),
         out_shape=[jax.ShapeDtypeStruct(shape, jnp.bfloat16) for shape in outs],
@@ -246,150 +245,197 @@
             transcendentals=0,
         ),
         compiler_params=params(24),
-        name=name,
+        name="project",
     )(order, *chunks, normed, cosine, sines)
 
 
-def project_query(normed, chunks, order, cosine, sines, heads, group, dim):
-    tokens = normed.shape[0]
-    outs = [(heads, tokens // token_tile, 2 * dim, group * token_tile)]
-    kernel = functools.partial(query_kernel, heads, group, dim, len(chunks))
-    return project(kernel, "query", outs, normed, chunks, order, cosine, sines)[0]
-
-
-def project_new(normed, chunks, order, cosine, sines, heads, dim):
-    tokens = normed.shape[0]
-    outs = [(heads, tokens, 2 * dim), (heads, dim + 16, tokens)]
-    kernel = functools.partial(new_kernel, heads, dim, len(chunks))
-    return project(kernel, "new", outs, normed, chunks, order, cosine, sines)
+def column_max(scores):
+    return jnp.max(scores.reshape(scores.shape[0] // 8, 8, scores.shape[1]), axis=0)
 
 
 def attend_kernel(
-    group,
-    dim,
+    head,
+    cache_head,
     length_ref,
     span_ref,
     tile_ref,
+    keys_hbm,
+    values_hbm,
+    query_ref,
+    out_ref,
+    token_ref,
+    even,
+    odd,
     key_ref,
     value_ref,
-    query_ref,
-    new_key_ref,
-    new_value_ref,
-    out_ref,
-    even,
-    odd,
+    key_sems,
+    value_sems,
 ):
     lanes = query_ref.shape[3]
-    span = new_key_ref.shape[1]
     length = length_ref[0]
-    valid = span_ref[0]
+    token_ref[0] = length
+    q = tile_ref[0]
     pair = 2 * key_block
-    pairs = (length + pair - 1) // pair
+    sum_row = values_hbm.shape[1] - 16
+    live = q * token_tile < span_ref[0]
+    pairs = jnp.where(live, (length + pair - 1) // pair, 0)
     last_block = jnp.maximum(2 * pairs - 1, 0)
 
-    def column_max(scores):
-        return jnp.max(scores.reshape(scores.shape[0] // 8, 8, lanes), axis=0)
-
-    q = tile_ref[0]
-
-    def tile():
-        def scores_of(block, c, target):
-            start = pl.multiple_of(block * key_block + c * score_chunk, score_chunk)
-            scores = matmul(key_ref[0, pl.ds(start, score_chunk), :], query_ref[0, q])
-            target[pl.ds(c * score_chunk, score_chunk), :] = scores
-            return column_max(scores)
-
-        scores = matmul(new_key_ref[0], query_ref[0, q])
-        source = lax.broadcasted_iota(jnp.int32, (span, lanes), 0)
-        lane = lax.broadcasted_iota(jnp.int32, (span, lanes), 1)
-        token = q * token_tile + lax.rem(lane, token_tile)
-        scores = jnp.where((source <= token) & (source < valid), scores, masked_score)
-        maximum = jnp.max(column_max(scores), axis=0, keepdims=True)
-        weights = jnp.exp(scores - maximum).astype(jnp.bfloat16)
-        total = matmul(new_value_ref[0], weights)
-
+    def key_copy(i):
+        piece = pl.ds(pl.multiple_of(i * pair, pair), pair)
+        return pltpu.make_async_copy(
+            keys_hbm.at[cache_head, piece], key_ref.at[piece], key_sems.at[i]
+        )
+
+    def value_copy(i):
+        piece = pl.ds(pl.multiple_of(i * pair, pair), pair)
+        return pltpu.make_async_copy(
+            values_hbm.at[cache_head, :, piece], value_ref.at[:, piece], value_sems.at[i]
+        )
+
+    for i in range(keys_hbm.shape[1] // pair):
+
+        @pl.when(i < pairs)
+        def fetch():
+            key_copy(i).start()
+            value_copy(i).start()
+
+    def scores_of(block, c, target):
+        start = pl.multiple_of(block * key_block + c * score_chunk, score_chunk)
+        scores = matmul(key_ref[pl.ds(start, score_chunk), :], query_ref[head, q])
+        target[pl.ds(c * score_chunk, score_chunk), :] = scores
+        return column_max(scores)
+
+    def half(block, following, current, target, state):
+        maximum, top, total = state
+        new_maximum = jnp.maximum(maximum, jnp.max(top, axis=0, keepdims=True))
+        total = total * jnp.exp(maximum - new_maximum)
+        next_top = None
+        ratio = value_chunk // score_chunk
+        parts = []
+        for c in range(key_block // score_chunk):
+            seen = scores_of(following, c, target)
+            next_top = seen if next_top is None else jnp.maximum(next_top, seen)
+            part = jnp.exp(current[pl.ds(c * score_chunk, score_chunk), :] - new_maximum)
+            parts.append(part.astype(jnp.bfloat16))
+            if len(parts) == ratio:
+                weights = parts[0] if ratio == 1 else jnp.concatenate(parts, axis=0)
+                start = block * key_block + (c + 1 - ratio) * score_chunk
+                start = pl.multiple_of(start, value_chunk)
+                total = total + matmul(value_ref[:, pl.ds(start, value_chunk)], weights)
+                parts = []
+        return new_maximum, next_top, total
+
+    def advance(i, state):
+        @pl.when(i + 1 < pairs)
+        def arrived():
+            key_copy(i + 1).wait()
+
+        value_copy(i).wait()
+        block = 2 * i
+        state = half(block, block + 1, even, odd, state)
+        following = jnp.minimum(block + 2, last_block)
+        return half(block + 1, following, odd, even, state)
+
+    @pl.when(pairs > 0)
+    def work():
+        key_copy(0).wait()
         top = scores_of(0, 0, even)
         for c in range(1, key_block // score_chunk):
             top = jnp.maximum(top, scores_of(0, c, even))
-
-        def half(block, following, current, target, state):
-            maximum, top, total = state
-            new_maximum = jnp.maximum(maximum, jnp.max(top, axis=0, keepdims=True))
-            total = total * jnp.exp(maximum - new_maximum)
-            next_top = None
-            ratio = value_chunk // score_chunk
-            parts = []
-            for c in range(key_block // score_chunk):
-                seen = scores_of(following, c, target)
-                next_top = seen if next_top is None else jnp.maximum(next_top, seen)
-                part = jnp.exp(current[pl.ds(c * score_chunk, score_chunk), :] - new_maximum)
-                parts.append(part.astype(jnp.bfloat16))
-                if len(parts) == ratio:
-                    weights = parts[0] if ratio == 1 else jnp.concatenate(parts, axis=0)
-                    start = block * key_block + (c + 1 - ratio) * score_chunk
-                    start = pl.multiple_of(start, value_chunk)
-                    total = total + matmul(value_ref[0, :, pl.ds(start, value_chunk)], weights)
-                    parts = []
-            return new_maximum, next_top, total
-
-        def advance(i, state):
-            block = 2 * i
-            state = half(block, block + 1, even, odd, state)
-            following = jnp.minimum(block + 2, last_block)
-            return half(block + 1, following, odd, even, state)
-
-        _, _, total = lax.fori_loop(0, pairs, advance, (maximum, top, total))
-        result = total[:dim] / total[dim : dim + 1]
-        row = q * token_tile + lax.broadcasted_iota(jnp.int32, (token_tile, 2 * dim), 0)
-        for g in range(0, group, 2):
-            both = jnp.concatenate(
-                [
-                    result[:, g * token_tile : (g + 1) * token_tile],
-                    result[:, (g + 1) * token_tile : (g + 2) * token_tile],
-                ],
-                axis=0,
-            )
-            kept = jnp.where(row < valid, jnp.transpose(both), 0.0)
-            out_ref[:, pl.ds(g * dim, 2 * dim)] = kept.astype(jnp.bfloat16)
-
-    pl.when(q * token_tile < valid)(tile)
-
-    @pl.when(q * token_tile >= valid)
-    def empty():
-        out_ref[...] = jnp.zeros_like(out_ref)
-
-
-def attend(head, tile, keys, values, queries, new_keys, new_values, length, valid):
+        start = (
+            jnp.full((1, lanes), masked_score, jnp.float32),
+            top,
+            jnp.zeros(out_ref.shape, jnp.float32),
+        )
+        maximum, _, total = lax.fori_loop(0, pairs, advance, start)
+        row = lax.broadcasted_iota(jnp.int32, out_ref.shape, 0)
+        out_ref[...] = jnp.where(row == sum_row + 1, maximum, total)
+
+    @pl.when(pairs == 0)
+    def nothing():
+        row = lax.broadcasted_iota(jnp.int32, out_ref.shape, 0)
+        out_ref[...] = jnp.where(row == sum_row + 1, masked_score, 0.0)
+
+
+def attend(head, cache_head, tile, keys, values, queries, token, valid):
     _, cached, width = keys.shape
-    dim = width // 2
+    rows = values.shape[1]
     lanes = queries.shape[3]
-    group = lanes // token_tile
-    block = lambda array: pl.BlockSpec(
-        (1,) + array.shape[1:], lambda i: (head,) + (0,) * (array.ndim - 1)
-    )
-    arrays = (keys, values, queries, new_keys, new_values)
+    pieces = cached // (2 * key_block)
+    anywhere = pl.BlockSpec(memory_space=pl.ANY)
     return pl.pallas_call(
-        functools.partial(attend_kernel, group, dim),
-        grid=(1,),
-        in_specs=[smem()] * 3 + [block(a) for a in arrays],
-        out_specs=pl.BlockSpec((token_tile, group * dim), lambda i: (0, 0)),
-        out_shape=jax.ShapeDtypeStruct((token_tile, group * dim), jnp.bfloat16),
-        scratch_shapes=[pltpu.VMEM((key_block, lanes), jnp.float32)] * 2,
+        functools.partial(attend_kernel, head, cache_head),
+        in_specs=[smem()] * 3 + [anywhere, anywhere, vmem()],
+        out_specs=[vmem(), smem()],
+        out_shape=[
+            jax.ShapeDtypeStruct((rows, lanes), jnp.float32),
+            jax.ShapeDtypeStruct((1,), jnp.int32),
+        ],
+        scratch_shapes=[pltpu.VMEM((key_block, lanes), jnp.float32)] * 2
+        + [
+            pltpu.VMEM((cached, width), jnp.bfloat16),
+            pltpu.VMEM((rows, cached), jnp.bfloat16),
+            pltpu.SemaphoreType.DMA((pieces,)),
+            pltpu.SemaphoreType.DMA((pieces,)),
+        ],
         cost_estimate=pl.CostEstimate(
             flops=2 * cached * lanes * 2 * width,
             bytes_accessed=2 * cached * 2 * width,
             transcendentals=cached * lanes,
         ),
-        compiler_params=params(24),
+        compiler_params=params(60),
         name="attend",
-    )(length, valid, tile, *arrays)
-
-
-def emit_kernel(heads, blocks, *refs):
-    parts = refs[:heads]
-    chunks = refs[heads : heads + blocks]
-    out_ref = refs[heads + blocks]
-    attended = jnp.concatenate([p[...] for p in parts], axis=1)
+    )(token, valid, tile, keys, values, queries)
+
+
+def finish_head(q, valid, group, dim, state, query, new_key, new_value):
+    lanes = query.shape[1]
+    span = new_key.shape[0]
+    scores = matmul(new_key, query)
+    source = lax.broadcasted_iota(jnp.int32, (span, lanes), 0)
+    lane = lax.broadcasted_iota(jnp.int32, (span, lanes), 1)
+    position = q * token_tile + lax.rem(lane, token_tile)
+    scores = jnp.where((source <= position) & (source < valid), scores, masked_score)
+    cached_maximum = state[dim + 1 : dim + 2]
+    maximum = jnp.maximum(jnp.max(column_max(scores), axis=0, keepdims=True), cached_maximum)
+    weights = jnp.exp(scores - maximum).astype(jnp.bfloat16)
+    total = state * jnp.exp(cached_maximum - maximum) + matmul(new_value, weights)
+    result = total[:dim] / total[dim : dim + 1]
+    row = q * token_tile + lax.broadcasted_iota(jnp.int32, (token_tile, 2 * dim), 0)
+    pieces = []
+    for g in range(0, group, 2):
+        both = jnp.concatenate(
+            [
+                result[:, g * token_tile : (g + 1) * token_tile],
+                result[:, (g + 1) * token_tile : (g + 2) * token_tile],
+            ],
+            axis=0,
+        )
+        pieces.append(jnp.where(row < valid, jnp.transpose(both), 0.0).astype(jnp.bfloat16))
+    return pieces
+
+
+def finish_kernel(heads, group, dim, sets, blocks, span_ref, tile_ref, *refs):
+    states = refs[:heads]
+    queries = refs[heads : heads + sets]
+    new_key_ref, new_value_ref = refs[heads + sets : heads + sets + 2]
+    chunks = refs[heads + sets + 2 : heads + sets + 2 + blocks]
+    out_ref = refs[heads + sets + 2 + blocks]
+    q = tile_ref[0]
+    pieces = []
+    for h in range(heads):
+        per_set = heads // sets
+        query = queries[h // per_set][h % per_set, q]
+        pieces += finish_head(
+            q, span_ref[0], group, dim, states[h][...], query, new_key_ref[h], new_value_ref[h]
+        )
+    attended = jnp.concatenate(pieces, axis=1)
+    if blocks == 0:
+        out_ref[...] = attended
+        return
+    token_ref = refs[heads + sets + 3 + blocks]
+    token_ref[0] = q
     count = out_ref.shape[0]
     for k in range(0, count, 2):
         if k < count - 2:
@@ -405,23 +451,34 @@
         out_ref[k + 1] = both[:, width:]
 
 
-def emit(parts, chunks, count):
-    columns = chunks[0].shape[1]
-    depth = chunks[0].shape[0]
-    rows = parts[0].shape[0]
+def finish(states, tile, valid, queries, new_keys, new_values, group, chunks, count):
+    heads = len(states)
+    dim = states[0].shape[0] - 16
+    if chunks:
+        columns = chunks[0].shape[1]
+        out_shape = [
+            jax.ShapeDtypeStruct((count, token_tile, columns), jnp.bfloat16),
+            jax.ShapeDtypeStruct((1,), jnp.int32),
+        ]
+        out_specs = [vmem(), smem()]
+    else:
+        columns = 0
+        out_shape = [jax.ShapeDtypeStruct((token_tile, heads * group * dim), jnp.bfloat16)]
+        out_specs = [vmem()]
+    depth = heads * group * dim
     return pl.pallas_call(
-        functools.partial(emit_kernel, len(parts), len(chunks)),
-        in_specs=[vmem()] * (len(parts) + len(chunks)),
-        out_specs=vmem(),
-        out_shape=jax.ShapeDtypeStruct((count, rows, columns), jnp.bfloat16),
+        functools.partial(finish_kernel, heads, group, dim, len(queries), len(chunks)),
+        in_specs=[smem()] * 2 + [vmem()] * (heads + len(queries) + 2 + len(chunks)),
+        out_specs=out_specs,
+        out_shape=out_shape,
         cost_estimate=pl.CostEstimate(
-            flops=2 * rows * depth * columns * count,
+            flops=2 * token_tile * depth * columns * count,
             bytes_accessed=2 * depth * columns * count,
             transcendentals=0,
         ),
         compiler_params=params(24),
-        name="emit",
-    )(*parts, *chunks)
+        name="finish",
+    )(valid, tile, *states, *queries, new_keys, new_values, *chunks)
 
 
 def combine_kernel(order_ref, own_ref, other_ref, out_ref):
@@ -461,12 +518,15 @@
     own_rows = tokens.shape[0]
     length = lax.dynamic_slice_in_dim(cached_len, device, 1)
     table = page_table[0]
+    w_new = w_kv.reshape(w_kv.shape[0], -1)
     if fast:
         tables = cycle_tables(req_count)
         order = jnp.array(tables[3], jnp.int32)[device]
         swap = [(0, 1), (1, 0)]
-        ring_query = Ring(w_query, tables)
-        ring_new = Ring(w_kv.reshape(w_kv.shape[0], -1), tables)
+        early = heads // 2
+        cut = early * group * dim
+        ring_first = Ring(w_query[:, :cut], tables)
+        ring_second = Ring(jnp.concatenate([w_query[:, cut:], w_new], axis=1), tables)
         ring_out = Ring(w_out, tables)
         other = lax.ppermute(tokens, "tp", swap)
         whole = jnp.concatenate(
@@ -475,19 +535,19 @@
         parts = 4
         state = ()
         for part in range(parts):
+            state = prepare(kv_cache, table, length, part, parts, state)
             if part < parts - 1:
-                ring_query.step(*state[:1])
-                ring_new.step(*state[:1])
+                ring_first.step()
+                ring_second.step()
             else:
-                query_chunks = ring_query.last(*state[:1])
-                new_chunks = ring_new.last(*state[:1])
-            state = prepare(kv_cache, table, length, part, parts, state)
+                first_chunks = ring_first.last()
+                second_chunks = ring_second.last()
         keys, values = state
     else:
         order = jnp.zeros((1,), jnp.int32)
+        early = 0
         gather = lambda array: lax.all_gather(array, "req", axis=0, tiled=True)
-        query_chunks = [gather(w_query)]
-        new_chunks = [gather(w_kv.reshape(w_kv.shape[0], -1))]
+        second_chunks = [gather(jnp.concatenate([w_query, w_new], axis=1))]
         whole = lax.all_gather(tokens, "tp", axis=0, tiled=True)
         keys, values = prepare(kv_cache, table, length, 0, 1, ())
     hidden = whole.astype(jnp.float32)
@@ -496,41 +556,49 @@
     ).astype(jnp.bfloat16)
     positions = length[0] + jnp.arange(normed.shape[0], dtype=jnp.int32)
     cosine, sines = rope_tables(positions, dim)
-    new_keys, new_values = project_new(normed, new_chunks, order, cosine, sines, heads, dim)
-    queries = project_query(normed, query_chunks, order, cosine, sines, heads, group, dim)
-
-    def attend_at(head, tile, valid):
-        return attend(head, tile, keys, values, queries, new_keys, new_values, length, valid)
+    queries = []
+    if early:
+        queries += project(normed, first_chunks, order, cosine, sines, early, 0, group, dim)
+    late, new_keys, new_values = project(
+        normed, second_chunks, order, cosine, sines, heads - early, heads, group, dim
+    )
+    queries.append(late)
+
+    def attend_tile(tile, which, token):
+        states = []
+        for h in which:
+            source, at = (queries[0], h) if h < early else (queries[-1], h - early)
+            state, token = attend(at, h, tile, keys, values, source, token, span_len)
+            states.append(state)
+        return states, token
+
+    def finish_tile(states, tile, chunks):
+        return finish(
+            states, tile, span_len, queries, new_keys, new_values, group, chunks, req_count
+        )
 
     if not fast:
-        tiles = [jnp.full((1,), q, jnp.int32) for q in range(normed.shape[0] // token_tile)]
-        attended = jnp.concatenate(
-            [
-                jnp.concatenate([attend_at(h, tile, span_len) for h in range(heads)], axis=1)
-                for tile in tiles
-            ],
-            axis=0,
-        )
+        rows = []
+        for q in range(normed.shape[0] // token_tile):
+            tile = jnp.full((1,), q, jnp.int32)
+            states, _ = attend_tile(tile, range(heads), length)
+            rows.append(finish_tile(states, tile, [])[0])
         gathered = lax.all_gather(w_out, "req", axis=1, tiled=True)
-        partial = matmul(attended, gathered).astype(jnp.bfloat16)
+        partial = matmul(jnp.concatenate(rows, axis=0), gathered).astype(jnp.bfloat16)
         summed = lax.psum_scatter(partial, "tp", scatter_dimension=0, tiled=True)
         return (residual_scale * summed.astype(jnp.float32)).astype(jnp.bfloat16)
     theirs, ours = (1 - rank).reshape(1), rank.reshape(1)
-    ring_out.step(ring_query.up)
-    ring_out.step(queries)
-    first = [attend_at(0, theirs, span_len)]
-    first.append(attend_at(1, theirs, after(span_len, first[-1])))
-    ring_out.step(first[-1])
-    first.append(attend_at(2, theirs, after(span_len, first[-1])))
-    first.append(attend_at(3, theirs, after(span_len, first[-1])))
-    out_chunks = ring_out.last(first[-1])
-    second = [attend_at(0, ours, after(span_len, first[-1]))]
-    second.append(attend_at(1, ours, after(span_len, second[-1])))
-    sent = emit(first, [after(out_chunks[0], second[-1])] + out_chunks[1:], req_count)
+    ring_out.step(ring_first.up)
+    ring_out.step()
+    ring_out.step()
+    out_chunks = ring_out.last()
+    sent_states, token = attend_tile(theirs, range(heads), length)
+    kept_states, token = attend_tile(ours, range(heads // 2), token)
+    sent, tile_token = finish_tile(sent_states, theirs, out_chunks)
     received = lax.ppermute(sent, "tp", swap)
-    second.append(attend_at(2, ours, after(span_len, sent)))
-    second.append(attend_at(3, ours, after(span_len, second[-1])))
-    kept = emit(second, out_chunks, req_count)
+    token = token + (tile_token - theirs)
+    more, token = attend_tile(ours, range(heads // 2, heads), token)
+    kept, _ = finish_tile(kept_states + more, ours, out_chunks)
     return combine(kept, received, order)
 
 

time: 205 us -> 207 us (level)
  the two profiles are of different devices: /device:TPU:8 before, /device:TPU:24 now
where the time goes in v3:
time: 207 us; the launch traced here: 204 us
  Pallas kernels  112 us (54%)
  local copies, waits for them, and re-layouts  34.5 us (17%)
  starting transfers between devices  28.6 us (14%)
  waiting for transfers between devices  23.2 us (11%)
  between operations  2.7 us (1%)
  other arithmetic  2.55 us (1%)
    pallas_call x8, Pallas kernels, attend(): pl.pallas_call(functools.partial(attend_kernel, head, cache_head), in_spe...  71.5 us
    unnamed x143, local copies, waits for them, and re-layouts  30.6 us
    pallas_call x4, Pallas kernels, prepare(): pl.pallas_call(functools.partial(prepare_kernel, heads, page, width, page...  25.8 us
    ppermute x51, starting transfers between devices, move(): return lax.ppermute(value, 'req', pairs)  25.6 us
    ppermute x51, waiting for transfers between devices, move(): return lax.ppermute(value, 'req', pairs)  23.2 us
    pallas_call x2, Pallas kernels, finish(): pl.pallas_call(functools.partial(finish_kernel, heads, group, dim, len(qu...  7.74 us
    pallas_call x2, Pallas kernels, project(): pl.pallas_call(functools.partial(project_kernel, heads, new_heads, group,...  4.95 us
  transfers between devices with their start and end apart: 53, of which 13 were waited for; matrix products, arithmetic and copies ran while one was open for 3% of the time, Pallas kernels for 52%

profile of v3, /device:TPU:24, one launch (start us, length us, event | category | flops | bytes accessed | tf_op | source)
XLA Modules:
  0.0 203.7 jit_solution(9825107194471164061)
XLA Ops:
  0.0 1.0 fusion.3
  1.0 1.6 collective-permute-start.1
  3.1 3.2 %collective-permute-done.1.refs_2_ = bf16[128,512]{1,0:T(8,128)(2,1)S(1)} collective-permute-done((bf16[128,512]{1,0:T(8,128)(2,1)S(1)}, bf16[128,512]{1,0:T(8,128)(2,1)S(1)}, u32[]{:S(2)}, u32[]{:S(2)}) %collective-permute-start.1) | collective-permute-done | bytes 131104 | tf_op jit(solution)/shard_map/ppermute | solution.py:76
  6.3 1.5 collective-permute-start.5
  9.9 1.4 collective-permute-done.5.refs_6_
  11.2 1.5 collective-permute-start.9
  13.7 1.2 collective-permute-start.21
  15.6 1.5 collective-permute-start.17
  18.1 1.2 dynamic_slice.7.length_ref
  20.0 1.1 collective-permute-done.19.refs_2_
  21.1 1.8 collective-permute-done.21.refs_4_
  23.3 1.0 collective-permute-done.11.refs_12_
  25.7 6.4 %prepare.4 = (bf16[4,8192,128]{2,1,0:T(8,128)(2,1)}, bf16[4,80,8192]{2,1,0:T(8,128)(2,1)}) custom-call(s32[64]{0:T(128)} %bitcast.29, s32[1]{0:T(128)} %dynamic_slice.7.length_ref, bf16[64,512,128]{2,1,0:T(8,128)(2,1)} %bitcast.11, bf16[64,512,128]{2,1,0:T(8,128)(2,1)} %bitcast.12, bf16[64,512,128]{2,1,0:T(8,128)(2,1)} %bitcast.13, ...), custom_call_target="tpu_custom_call" | custom-call | bytes 6291456 | tf_op jit(solution)/shard_map/prepare/pallas_call | solution.py:145
  32.1 6.4 %prepare.5 = (bf16[4,8192,128]{2,1,0:T(8,128)(2,1)}, bf16[4,80,8192]{2,1,0:T(8,128)(2,1)}) custom-call(s32[64]{0:T(128)} %bitcast.30, s32[1]{0:T(128)} %dynamic_slice.7.length_ref, bf16[64,512,128]{2,1,0:T(8,128)(2,1)} %bitcast.15, bf16[64,512,128]{2,1,0:T(8,128)(2,1)} %bitcast.16, ...), custom_call_target="tpu_custom_call", output_to_operand_aliasing={{0}: (6, {}), {1}: (7, {})} | custom-call | bytes 6291456 | tf_op jit(solution)/shard_map/prepare/pallas_call | solution.py:145
  38.5 6.5 %prepare.6 = (bf16[4,8192,128]{2,1,0:T(8,128)(2,1)}, bf16[4,80,8192]{2,1,0:T(8,128)(2,1)}) custom-call(s32[64]{0:T(128)} %bitcast.31, s32[1]{0:T(128)} %dynamic_slice.7.length_ref, bf16[64,512,128]{2,1,0:T(8,128)(2,1)} %bitcast.19, bf16[64,512,128]{2,1,0:T(8,128)(2,1)} %bitcast.20, ...), custom_call_target="tpu_custom_call", output_to_operand_aliasing={{0}: (6, {}), {1}: (7, {})} | custom-call | bytes 6291456 | tf_op jit(solution)/shard_map/prepare/pallas_call | solution.py:145
  45.0 6.5 %prepare.7 = (bf16[4,8192,128]{2,1,0:T(8,128)(2,1)}, bf16[4,80,8192]{2,1,0:T(8,128)(2,1)}) custom-call(s32[64]{0:T(128)} %bitcast.32, s32[1]{0:T(128)} %dynamic_slice.7.length_ref, bf16[64,512,128]{2,1,0:T(8,128)(2,1)} %bitcast.23, bf16[64,512,128]{2,1,0:T(8,128)(2,1)} %bitcast.24, ...), custom_call_target="tpu_custom_call", output_to_operand_aliasing={{0}: (6, {}), {1}: (7, {})} | custom-call | bytes 6291456 | tf_op jit(solution)/shard_map/prepare/pallas_call | solution.py:145
  51.6 1.6 collective-permute-start.14
  54.7 1.2 collective-permute-done.14.refs_15_
  56.9 1.1 broadcast_select_fusion.1
  59.3 3.4 %collective-permute-done.25.refs_8_ = bf16[128,1024]{1,0:T(8,128)(2,1)S(1)} collective-permute-done((bf16[128,1024]{1,0:T(8,128)(2,1)S(1)}, bf16[128,1024]{1,0:T(8,128)(2,1)S(1)}, u32[]{:S(2)}, u32[]{:S(2)}) %collective-permute-start.25) | collective-permute-done | bytes 262176 | tf_op jit(solution)/shard_map/ppermute | solution.py:76
  63.3 2.3 %collective-permute-done.27.refs_10_ = bf16[128,1024]{1,0:T(8,128)(2,1)S(1)} collective-permute-done((bf16[128,1024]{1,0:T(8,128)(2,1)S(1)}, bf16[128,1024]{1,0:T(8,128)(2,1)S(1)}, u32[]{:S(2)}, u32[]{:S(2)}) %collective-permute-start.27) | collective-permute-done | bytes 262176 | tf_op jit(solution)/shard_map/ppermute | solution.py:76
  65.7 1.6 collective-permute-start.29
  69.5 1.2 collective-permute-done.36.refs_10_
  72.8 4.8 %collective-permute-done.29.refs_12_ = bf16[128,1024]{1,0:T(8,128)(2,1)} collective-permute-done((bf16[128,1024]{1,0:T(8,128)(2,1)S(1)}, bf16[128,1024]{1,0:T(8,128)(2,1)}, u32[]{:S(2)}, u32[]{:S(2)}) %collective-permute-start.29) | collective-permute-done | bytes 262176 | tf_op jit(solution)/shard_map/ppermute | solution.py:76
  78.9 1.6 project.2.query_ref.refs_4_
  82.9 1.6 collective-permute-start.32
  86.3 9.0 %attend.8 = (f32[80,512]{1,0:T(8,128)}, s32[1]{0:T(128)}) custom-call(s32[1]{0:T(128)} %dynamic_slice.7.length_ref, s32[1]{0:T(128)S(6)} %copy.26.span_ref, s32[1]{0:T(128)} %bitcast.2.tile_ref, bf16[4,8192,128]{2,1,0:T(8,128)(2,1)} %get-tuple-element.42.keys_hbm, bf16[4,80,8192]{2,1,0:T(8,128)(2,1)} %get-tuple-element.43.values_hbm, ...), custom_call_target="tpu_custom_call" | custom-call | flops 2147483648 | bytes 4194304 | tf_op jit(solution)/shard_map/attend/pallas_call | solution.py:367
  95.8 9.0 %attend.9 = (f32[80,512]{1,0:T(8,128)}, s32[1]{0:T(128)}) custom-call(s32[1]{0:T(128)} %get-tuple-element.44.length_ref, s32[1]{0:T(128)S(6)} %copy.26.span_ref, s32[1]{0:T(128)} %bitcast.2.tile_ref, bf16[4,8192,128]{2,1,0:T(8,128)(2,1)} %get-tuple-element.42.keys_hbm, bf16[4,80,8192]{2,1,0:T(8,128)(2,1)} %get-tuple-element.43.values_hbm, ...), custom_call_target="tpu_custom_call" | custom-call | flops 2147483648 | bytes 4194304 | tf_op jit(solution)/shard_map/attend/pallas_call | solution.py:367
  109.0 0.9 copy-done.14
  109.9 0.9 copy-done.16
  110.9 0.9 copy-done.18
  111.8 0.9 copy-done.20
  113.7 0.9 copy-done.24
  114.7 0.9 copy-done.26
  116.6 0.9 copy-done.30
  117.5 0.9 copy-done.32
  121.8 3.4 %project.3 = (bf16[2,2,128,512]{3,2,1,0:T(8,128)(2,1)S(1)}, bf16[4,256,128]{2,1,0:T(8,128)(2,1)S(1)}, bf16[4,80,256]{2,1,0:T(8,128)(2,1)S(1)}) custom-call(s32[16]{0:T(128)S(1)} %copy-done.67, bf16[128,1024]{1,0:T(8,128)(2,1)S(1)} %pad_maximum_fusion.1.refs_0_, bf16[128,1024]{1,0:T(8,128)(2,1)S(1)} %copy-done.18, bf16[128,1024]{1,0:T(8,128)(2,1)S(1)} %copy-done.14, ...), custom_call_target="tpu_custom_call" | custom-call | flops 1073741824 | bytes 4194304 | tf_op jit(solution)/shard_map/project/pallas_call | solution.py:236
  126.8 8.9 %attend.10 = (f32[80,512]{1,0:T(8,128)}, s32[1]{0:T(128)}) custom-call(s32[1]{0:T(128)} %get-tuple-element.45.length_ref, s32[1]{0:T(128)S(6)} %copy.26.span_ref, s32[1]{0:T(128)} %bitcast.2.tile_ref, bf16[4,8192,128]{2,1,0:T(8,128)(2,1)} %get-tuple-element.42.keys_hbm, bf16[4,80,8192]{2,1,0:T(8,128)(2,1)} %get-tuple-element.43.values_hbm, ...), custom_call_target="tpu_custom_call" | custom-call | flops 2147483648 | bytes 4194304 | tf_op jit(solution)/shard_map/attend/pallas_call | solution.py:367
  135.8 2.0 collective-permute-start.48
  138.4 9.0 %attend.11 = (f32[80,512]{1,0:T(8,128)}, s32[1]{0:T(128)}) custom-call(s32[1]{0:T(128)} %get-tuple-element.47.length_ref, s32[1]{0:T(128)S(6)} %copy.26.span_ref, s32[1]{0:T(128)} %bitcast.2.tile_ref, bf16[4,8192,128]{2,1,0:T(8,128)(2,1)} %get-tuple-element.42.keys_hbm, bf16[4,80,8192]{2,1,0:T(8,128)(2,1)} %get-tuple-element.43.values_hbm, ...), custom_call_target="tpu_custom_call" | custom-call | flops 2147483648 | bytes 4194304 | tf_op jit(solution)/shard_map/attend/pallas_call | solution.py:367
  148.1 9.0 %attend.12 = (f32[80,512]{1,0:T(8,128)}, s32[1]{0:T(128)}) custom-call(s32[1]{0:T(128)} %get-tuple-element.48.length_ref, s32[1]{0:T(128)S(6)} %copy.26.span_ref, s32[1]{0:T(128)} %bitcast.1.tile_ref, bf16[4,8192,128]{2,1,0:T(8,128)(2,1)} %get-tuple-element.42.keys_hbm, bf16[4,80,8192]{2,1,0:T(8,128)(2,1)} %get-tuple-element.43.values_hbm, ...), custom_call_target="tpu_custom_call" | custom-call | flops 2147483648 | bytes 4194304 | tf_op jit(solution)/shard_map/attend/pallas_call | solution.py:367
  160.9 4.3 %finish.2 = (bf16[16,128,128]{2,1,0:T(8,128)(2,1)}, s32[1]{0:T(128)}) custom-call(s32[1]{0:T(128)S(6)} %copy.26.span_ref, s32[1]{0:T(128)} %bitcast.2.tile_ref, f32[80,512]{1,0:T(8,128)S(1)} %copy-done.33, f32[80,512]{1,0:T(8,128)S(1)} %copy-done.34, f32[80,512]{1,0:T(8,128)S(1)} %copy-done.35, f32[80,512]{1,0:T(8,128)S(1)} %copy-done.38, ...), custom_call_target="tpu_custom_call" | custom-call | flops 536870912 | bytes 4194304 | tf_op jit(solution)/shard_map/finish/pallas_call | solution.py:469
  165.1 1.6 collective-permute-start.52
  166.7 8.9 %attend.13 = (f32[80,512]{1,0:T(8,128)}, s32[1]{0:T(128)}) custom-call(s32[1]{0:T(128)} %get-tuple-element.50.length_ref, s32[1]{0:T(128)S(6)} %copy.26.span_ref, s32[1]{0:T(128)} %bitcast.1.tile_ref, bf16[4,8192,128]{2,1,0:T(8,128)(2,1)} %get-tuple-element.42.keys_hbm, bf16[4,80,8192]{2,1,0:T(8,128)(2,1)} %get-tuple-element.43.values_hbm, ...), custom_call_target="tpu_custom_call" | custom-call | flops 2147483648 | bytes 4194304 | tf_op jit(solution)/shard_map/attend/pallas_call | solution.py:367
  176.8 8.5 %attend.14 = (f32[80,512]{1,0:T(8,128)}, s32[1]{0:T(128)}) custom-call(s32[1]{0:T(128)S(6)} %add.33.length_ref, s32[1]{0:T(128)S(6)} %copy.26.span_ref, s32[1]{0:T(128)} %bitcast.1.tile_ref, bf16[4,8192,128]{2,1,0:T(8,128)(2,1)} %get-tuple-element.42.keys_hbm, bf16[4,80,8192]{2,1,0:T(8,128)(2,1)} %get-tuple-element.43.values_hbm, ...), custom_call_target="tpu_custom_call" | custom-call | flops 2147483648 | bytes 4194304 | tf_op jit(solution)/shard_map/attend/pallas_call | solution.py:367
  185.4 9.1 %attend.15 = (f32[80,512]{1,0:T(8,128)}, s32[1]{0:T(128)}) custom-call(s32[1]{0:T(128)} %get-tuple-element.63.length_ref, s32[1]{0:T(128)S(6)} %copy.26.span_ref, s32[1]{0:T(128)} %bitcast.1.tile_ref, bf16[4,8192,128]{2,1,0:T(8,128)(2,1)} %get-tuple-element.42.keys_hbm, bf16[4,80,8192]{2,1,0:T(8,128)(2,1)} %get-tuple-element.43.values_hbm, ...), custom_call_target="tpu_custom_call" | custom-call | flops 2147483648 | bytes 4194304 | tf_op jit(solution)/shard_map/attend/pallas_call | solution.py:367
  198.1 3.5 %finish.3 = (bf16[16,128,128]{2,1,0:T(8,128)(2,1)S(1)}, s32[1]{0:T(128)}) custom-call(s32[1]{0:T(128)S(6)} %copy.26.span_ref, s32[1]{0:T(128)} %bitcast.1.tile_ref, f32[80,512]{1,0:T(8,128)S(1)} %copy-done.36, f32[80,512]{1,0:T(8,128)S(1)} %copy-done.37, f32[80,512]{1,0:T(8,128)S(1)} %copy-done.39, f32[80,512]{1,0:T(8,128)S(1)} %copy-done.40, ...), custom_call_target="tpu_custom_call" | custom-call | flops 536870912 | bytes 4194304 | tf_op jit(solution)/shard_map/finish/pallas_call | solution.py:469
  201.6 2.0 combine.1
  (235 shorter events, 40.8 us)
Async XLA Ops:
  1.0 5.3 %collective-permute-start.1 = (bf16[128,512]{1,0:T(8,128)(2,1)S(1)}, bf16[128,512]{1,0:T(8,128)(2,1)S(1)}, u32[]{:S(2)}, u32[]{:S(2)}) collective-permute-start(bf16[128,512]{1,0:T(8,128)(2,1)S(1)} %get-tuple-element.70.refs_0_), channel_id=1, source_target_pairs={{0,8},{2,10},{8,16},{10,18},{16,24},{18,26},{24,28},{26,30},{28,20... | collective-permute-start | bytes 393224 | tf_op jit(solution)/shard_map/ppermute | solution.py:76
  2.6 5.2 %collective-permute-start.3 = (bf16[128,512]{1,0:T(8,128)(2,1)S(1)}, bf16[128,512]{1,0:T(8,128)(2,1)S(1)}, u32[]{:S(2)}, u32[]{:S(2)}) collective-permute-start(bf16[128,512]{1,0:T(8,128)(2,1)S(1)} %get-tuple-element.70.refs_0_), channel_id=1, source_target_pairs={{8,0},{10,2},{16,8},{18,10},{24,16},{26,18},{28,24},{30,26},{20,28... | collective-permute-start | bytes 393224 | tf_op jit(solution)/shard_map/ppermute | solution.py:76
  6.3 5.0 %collective-permute-start.5 = (bf16[128,512]{1,0:T(8,128)(2,1)S(1)}, bf16[128,512]{1,0:T(8,128)(2,1)S(1)}, u32[]{:S(2)}, u32[]{:S(2)}) collective-permute-start(bf16[128,512]{1,0:T(8,128)(2,1)S(1)} %collective-permute-done.1.refs_2_), channel_id=1, source_target_pairs={{0,8},{2,10},{8,16},{10,18},{16,24},{18,26},{24,28},{26,30},{28,20... | collective-permute-start | bytes 393224 | tf_op jit(solution)/shard_map/ppermute | solution.py:76
  7.8 5.0 %collective-permute-start = (bf16[128,512]{1,0:T(8,128)(2,1)S(1)}, bf16[128,512]{1,0:T(8,128)(2,1)S(1)}, u32[]{:S(2)}, u32[]{:S(2)}) collective-permute-start(bf16[128,512]{1,0:T(8,128)(2,1)S(1)} %get-tuple-element.70.refs_0_), channel_id=1, source_target_pairs={{0,2},{2,0},{4,6},{6,4},{8,10},{10,8},{12,14},{14,12},{16,18},{18,... | collective-permute-start | bytes 393224 | tf_op jit(solution)/shard_map/ppermute | solution.py:76
  7.8 5.9 %collective-permute-start.7 = (bf16[128,512]{1,0:T(8,128)(2,1)S(1)}, bf16[128,512]{1,0:T(8,128)(2,1)S(1)}, u32[]{:S(2)}, u32[]{:S(2)}) collective-permute-start(bf16[128,512]{1,0:T(8,128)(2,1)S(1)} %collective-permute-done.3.refs_4_), channel_id=1, source_target_pairs={{8,0},{10,2},{16,8},{18,10},{24,16},{26,18},{28,24},{30,26},{20,28... | collective-permute-start | bytes 393224 | tf_op jit(solution)/shard_map/ppermute | solution.py:76
  8.4 6.5 %collective-permute-start.2 = (bf16[128,512]{1,0:T(8,128)(2,1)S(1)}, bf16[128,512]{1,0:T(8,128)(2,1)S(1)}, u32[]{:S(2)}, u32[]{:S(2)}) collective-permute-start(bf16[128,512]{1,0:T(8,128)(2,1)S(1)} %collective-permute-done.1.refs_2_), channel_id=1, source_target_pairs={{0,2},{2,0},{4,6},{6,4},{8,10},{10,8},{12,14},{14,12},{16,18},{18,... | collective-permute-start | bytes 393224 | tf_op jit(solution)/shard_map/ppermute | solution.py:76
  9.5 5.4 %collective-permute-start.4 = (bf16[128,512]{1,0:T(8,128)(2,1)S(1)}, bf16[128,512]{1,0:T(8,128)(2,1)S(1)}, u32[]{:S(2)}, u32[]{:S(2)}) collective-permute-start(bf16[128,512]{1,0:T(8,128)(2,1)S(1)} %collective-permute-done.3.refs_4_), channel_id=1, source_target_pairs={{0,2},{2,0},{4,6},{6,4},{8,10},{10,8},{12,14},{14,12},{16,18},{18,... | collective-permute-start | bytes 393224 | tf_op jit(solution)/shard_map/ppermute | solution.py:76
  11.2 6.4 %collective-permute-start.9 = (bf16[128,512]{1,0:T(8,128)(2,1)S(1)}, bf16[128,512]{1,0:T(8,128)(2,1)S(1)}, u32[]{:S(2)}, u32[]{:S(2)}) collective-permute-start(bf16[128,512]{1,0:T(8,128)(2,1)S(1)} %collective-permute-done.5.refs_6_), channel_id=1, source_target_pairs={{0,8},{2,10},{8,16},{10,18},{16,24},{18,26},{24,28},{26,30},{28,20... | collective-permute-start | bytes 393224 | tf_op jit(solution)/shard_map/ppermute | solution.py:76
  12.8 8.3 %collective-permute-start.19 = (bf16[128,1024]{1,0:T(8,128)(2,1)S(1)}, bf16[128,1024]{1,0:T(8,128)(2,1)S(1)}, u32[]{:S(2)}, u32[]{:S(2)}) collective-permute-start(bf16[128,1024]{1,0:T(8,128)(2,1)S(1)} %pad_maximum_fusion.1.refs_0_), channel_id=1, source_target_pairs={{0,8},{2,10},{8,16},{10,18},{16,24},{18,26},{24,28},{26,30},{28,20... | collective-permute-start | bytes 786440 | tf_op jit(solution)/shard_map/ppermute | solution.py:76
  13.7 9.2 %collective-permute-start.21 = (bf16[128,1024]{1,0:T(8,128)(2,1)S(1)}, bf16[128,1024]{1,0:T(8,128)(2,1)S(1)}, u32[]{:S(2)}, u32[]{:S(2)}) collective-permute-start(bf16[128,1024]{1,0:T(8,128)(2,1)S(1)} %pad_maximum_fusion.1.refs_0_), channel_id=1, source_target_pairs={{8,0},{10,2},{16,8},{18,10},{24,16},{26,18},{28,24},{30,26},{20,28... | collective-permute-start | bytes 786440 | tf_op jit(solution)/shard_map/ppermute | solution.py:76
  14.9 8.0 %collective-permute-start.18 = (bf16[128,1024]{1,0:T(8,128)(2,1)S(1)}, bf16[128,1024]{1,0:T(8,128)(2,1)S(1)}, u32[]{:S(2)}, u32[]{:S(2)}) collective-permute-start(bf16[128,1024]{1,0:T(8,128)(2,1)S(1)} %pad_maximum_fusion.1.refs_0_), channel_id=1, source_target_pairs={{0,2},{2,0},{4,6},{6,4},{8,10},{10,8},{12,14},{14,12},{16,18},{18,... | collective-permute-start | bytes 786440 | tf_op jit(solution)/shard_map/ppermute | solution.py:76
  15.6 40.8 %collective-permute-start.17 = (bf16[128,2048]{1,0:T(8,128)(2,1)}, bf16[128,2048]{1,0:T(8,128)(2,1)}, u32[]{:S(2)}, u32[]{:S(2)}) collective-permute-start(bf16[128,2048]{1,0:T(8,128)(2,1)} %param.10), channel_id=1, source_target_pairs={{0,1},{1,0},{2,3},{3,2},{4,5},{5,4},{6,7},{7,6},{8,9},{9,8},{10,11... | collective-permute-start | bytes 1572872 | tf_op jit(solution)/shard_map/ppermute | solution.py:531
  17.6 6.7 %collective-permute-start.11 = (bf16[128,512]{1,0:T(8,128)(2,1)S(1)}, bf16[128,512]{1,0:T(8,128)(2,1)S(1)}, u32[]{:S(2)}, u32[]{:S(2)}) collective-permute-start(bf16[128,512]{1,0:T(8,128)(2,1)S(1)} %collective-permute-done.7.refs_8_), channel_id=1, source_target_pairs={{8,0},{10,2},{16,8},{18,10},{24,16},{26,18},{28,24},{30,26},{20,28... | collective-permute-start | bytes 393224 | tf_op jit(solution)/shard_map/ppermute | solution.py:76
  21.1 30.5 %collective-permute-start.6 = (bf16[128,512]{1,0:T(8,128)(2,1)S(1)}, bf16[128,512]{1,0:T(8,128)(2,1)S(1)}, u32[]{:S(2)}, u32[]{:S(2)}) collective-permute-start(bf16[128,512]{1,0:T(8,128)(2,1)S(1)} %collective-permute-done.5.refs_6_), channel_id=1, source_target_pairs={{0,2},{2,0},{4,6},{6,4},{8,10},{10,8},{12,14},{14,12},{16,18},{18,... | collective-permute-start | bytes 393224 | tf_op jit(solution)/shard_map/ppermute | solution.py:76
  22.9 31.0 %collective-permute-start.8 = (bf16[128,512]{1,0:T(8,128)(2,1)S(1)}, bf16[128,512]{1,0:T(8,128)(2,1)S(1)}, u32[]{:S(2)}, u32[]{:S(2)}) collective-permute-start(bf16[128,512]{1,0:T(8,128)(2,1)S(1)} %collective-permute-done.7.refs_8_), channel_id=1, source_target_pairs={{0,2},{2,0},{4,6},{6,4},{8,10},{10,8},{12,14},{14,12},{16,18},{18,... | collective-permute-start | bytes 393224 | tf_op jit(solution)/shard_map/ppermute | solution.py:76
  22.9 33.6 %collective-permute-start.23 = (bf16[128,1024]{1,0:T(8,128)(2,1)S(1)}, bf16[128,1024]{1,0:T(8,128)(2,1)S(1)}, u32[]{:S(2)}, u32[]{:S(2)}) collective-permute-start(bf16[128,1024]{1,0:T(8,128)(2,1)S(1)} %collective-permute-done.19.refs_2_), channel_id=1, source_target_pairs={{0,8},{2,10},{8,16},{10,18},{16,24},{18,26},{24,28},{26,30},{28,20... | collective-permute-start | bytes 786440 | tf_op jit(solution)/shard_map/ppermute | solution.py:76
  24.3 28.9 %collective-permute-start.13 = (bf16[64,512]{1,0:T(8,128)(2,1)S(1)}, bf16[64,512]{1,0:T(8,128)(2,1)S(1)}, u32[]{:S(2)}, u32[]{:S(2)}) collective-permute-start(bf16[64,512]{1,0:T(8,128)(2,1)S(1)} %slice.32), channel_id=1, source_target_pairs={{0,8},{2,10},{8,16},{10,18},{16,24},{18,26},{24,28},{26,30},{28,20... | collective-permute-start | bytes 196616 | tf_op jit(solution)/shard_map/ppermute | solution.py:76
  53.9 8.7 %collective-permute-start.25 = (bf16[128,1024]{1,0:T(8,128)(2,1)S(1)}, bf16[128,1024]{1,0:T(8,128)(2,1)S(1)}, u32[]{:S(2)}, u32[]{:S(2)}) collective-permute-start(bf16[128,1024]{1,0:T(8,128)(2,1)S(1)} %collective-permute-done.21.refs_4_), channel_id=1, source_target_pairs={{8,0},{10,2},{16,8},{18,10},{24,16},{26,18},{28,24},{30,26},{20,28... | collective-permute-start | bytes 786440 | tf_op jit(solution)/shard_map/ppermute | solution.py:76
  56.5 9.2 %collective-permute-start.27 = (bf16[128,1024]{1,0:T(8,128)(2,1)S(1)}, bf16[128,1024]{1,0:T(8,128)(2,1)S(1)}, u32[]{:S(2)}, u32[]{:S(2)}) collective-permute-start(bf16[128,1024]{1,0:T(8,128)(2,1)S(1)} %collective-permute-done.23.refs_6_), channel_id=1, source_target_pairs={{0,8},{2,10},{8,16},{10,18},{16,24},{18,26},{24,28},{26,30},{28,20... | collective-permute-start | bytes 786440 | tf_op jit(solution)/shard_map/ppermute | solution.py:76
  58.1 9.4 %collective-permute-start.20 = (bf16[128,1024]{1,0:T(8,128)(2,1)S(1)}, bf16[128,1024]{1,0:T(8,128)(2,1)S(1)}, u32[]{:S(2)}, u32[]{:S(2)}) collective-permute-start(bf16[128,1024]{1,0:T(8,128)(2,1)S(1)} %collective-permute-done.19.refs_2_), channel_id=1, source_target_pairs={{0,2},{2,0},{4,6},{6,4},{8,10},{10,8},{12,14},{14,12},{16,18},{18,... | collective-permute-start | bytes 786440 | tf_op jit(solution)/shard_map/ppermute | solution.py:76
  58.4 9.9 %collective-permute-start.22 = (bf16[128,1024]{1,0:T(8,128)(2,1)S(1)}, bf16[128,1024]{1,0:T(8,128)(2,1)S(1)}, u32[]{:S(2)}, u32[]{:S(2)}) collective-permute-start(bf16[128,1024]{1,0:T(8,128)(2,1)S(1)} %collective-permute-done.21.refs_4_), channel_id=1, source_target_pairs={{0,2},{2,0},{4,6},{6,4},{8,10},{10,8},{12,14},{14,12},{16,18},{18,... | collective-permute-start | bytes 786440 | tf_op jit(solution)/shard_map/ppermute | solution.py:76
  58.8 12.0 %collective-permute-start.36 = (bf16[1024,128]{1,0:T(8,128)(2,1)S(1)}, bf16[1024,128]{1,0:T(8,128)(2,1)S(1)}, u32[]{:S(2)}, u32[]{:S(2)}) collective-permute-start(bf16[1024,128]{1,0:T(8,128)(2,1)S(1)} %copy-done.6), channel_id=1, source_target_pairs={{0,8},{2,10},{8,16},{10,18},{16,24},{18,26},{24,28},{26,30},{28,20... | collective-permute-start | bytes 786440 | tf_op jit(solution)/shard_map/ppermute | solution.py:76
  62.7 9.2 %collective-permute-start.38 = (bf16[1024,128]{1,0:T(8,128)(2,1)S(1)}, bf16[1024,128]{1,0:T(8,128)(2,1)S(1)}, u32[]{:S(2)}, u32[]{:S(2)}) collective-permute-start(bf16[1024,128]{1,0:T(8,128)(2,1)S(1)} %copy-done.6), channel_id=1, source_target_pairs={{8,0},{10,2},{16,8},{18,10},{24,16},{26,18},{28,24},{30,26},{20,28... | collective-permute-start | bytes 786440 | tf_op jit(solution)/shard_map/ppermute | solution.py:76
  65.7 11.9 %collective-permute-start.29 = (bf16[128,1024]{1,0:T(8,128)(2,1)S(1)}, bf16[128,1024]{1,0:T(8,128)(2,1)}, u32[]{:S(2)}, u32[]{:S(2)}) collective-permute-start(bf16[128,1024]{1,0:T(8,128)(2,1)S(1)} %collective-permute-done.25.refs_8_), channel_id=1, source_target_pairs={{8,0},{10,2},{16,8},{18,10},{24,16},{26,18},{28,24},{30,26},{20,28... | collective-permute-start | bytes 786440 | tf_op jit(solution)/shard_map/ppermute | solution.py:76
  68.3 13.9 %collective-permute-start.24 = (bf16[128,1024]{1,0:T(8,128)(2,1)S(1)}, bf16[128,1024]{1,0:T(8,128)(2,1)S(1)}, u32[]{:S(2)}, u32[]{:S(2)}) collective-permute-start(bf16[128,1024]{1,0:T(8,128)(2,1)S(1)} %collective-permute-done.23.refs_6_), channel_id=1, source_target_pairs={{0,2},{2,0},{4,6},{6,4},{8,10},{10,8},{12,14},{14,12},{16,18},{18,... | collective-permute-start | bytes 786440 | tf_op jit(solution)/shard_map/ppermute | solution.py:76
  69.0 15.4 %collective-permute-start.26 = (bf16[128,1024]{1,0:T(8,128)(2,1)S(1)}, bf16[128,1024]{1,0:T(8,128)(2,1)S(1)}, u32[]{:S(2)}, u32[]{:S(2)}) collective-permute-start(bf16[128,1024]{1,0:T(8,128)(2,1)S(1)} %collective-permute-done.25.refs_8_), channel_id=1, source_target_pairs={{0,2},{2,0},{4,6},{6,4},{8,10},{10,8},{12,14},{14,12},{16,18},{18,... | collective-permute-start | bytes 786440 | tf_op jit(solution)/shard_map/ppermute | solution.py:76
  70.7 14.9 %collective-permute-start.40 = (bf16[1024,128]{1,0:T(8,128)(2,1)S(1)}, bf16[1024,128]{1,0:T(8,128)(2,1)S(1)}, u32[]{:S(2)}, u32[]{:S(2)}) collective-permute-start(bf16[1024,128]{1,0:T(8,128)(2,1)S(1)} %collective-permute-done.36.refs_10_), channel_id=1, source_target_pairs={{0,8},{2,10},{8,16},{10,18},{16,24},{18,26},{24,28},{26,30},{28,20... | collective-permute-start | bytes 786440 | tf_op jit(solution)/shard_map/ppermute | solution.py:76
  71.9 23.5 %collective-permute-start.42 = (bf16[1024,128]{1,0:T(8,128)(2,1)S(1)}, bf16[1024,128]{1,0:T(8,128)(2,1)S(1)}, u32[]{:S(2)}, u32[]{:S(2)}) collective-permute-start(bf16[1024,128]{1,0:T(8,128)(2,1)S(1)} %collective-permute-done.38.refs_12_), channel_id=1, source_target_pairs={{8,0},{10,2},{16,8},{18,10},{24,16},{26,18},{28,24},{30,26},{20,28... | collective-permute-start | bytes 786440 | tf_op jit(solution)/shard_map/ppermute | solution.py:76
  77.6 7.6 %collective-permute-start.31 = (bf16[64,1024]{1,0:T(8,128)(2,1)S(1)}, bf16[64,1024]{1,0:T(8,128)(2,1)S(1)}, u32[]{:S(2)}, u32[]{:S(2)}) collective-permute-start(bf16[64,1024]{1,0:T(8,128)(2,1)S(1)} %slice.34), channel_id=1, source_target_pairs={{0,8},{2,10},{8,16},{10,18},{16,24},{18,26},{24,28},{26,30},{28,20... | collective-permute-start | bytes 393224 | tf_op jit(solution)/shard_map/ppermute | solution.py:76
  82.9 12.4 %collective-permute-start.32 = (bf16[64,1024]{1,0:T(8,128)(2,1)S(1)}, bf16[64,1024]{1,0:T(8,128)(2,1)S(1)}, u32[]{:S(2)}, u32[]{:S(2)}) collective-permute-start(bf16[64,1024]{1,0:T(8,128)(2,1)S(1)} %slice.35), channel_id=1, source_target_pairs={{8,0},{10,2},{16,8},{18,10},{24,16},{26,18},{28,24},{30,26},{20,28... | collective-permute-start | bytes 393224 | tf_op jit(solution)/shard_map/ppermute | solution.py:76
  85.1 20.9 %collective-permute-start.28 = (bf16[128,1024]{1,0:T(8,128)(2,1)S(1)}, bf16[128,1024]{1,0:T(8,128)(2,1)S(1)}, u32[]{:S(2)}, u32[]{:S(2)}) collective-permute-start(bf16[128,1024]{1,0:T(8,128)(2,1)S(1)} %collective-permute-done.27.refs_10_), channel_id=1, source_target_pairs={{0,2},{2,0},{4,6},{6,4},{8,10},{10,8},{12,14},{14,12},{16,18},{18,... | collective-permute-start | bytes 786440 | tf_op jit(solution)/shard_map/ppermute | solution.py:76
  85.2 21.6 %collective-permute-start.30 = (bf16[128,1024]{1,0:T(8,128)(2,1)}, bf16[128,1024]{1,0:T(8,128)(2,1)}, u32[]{:S(2)}, u32[]{:S(2)}) collective-permute-start(bf16[128,1024]{1,0:T(8,128)(2,1)} %collective-permute-done.29.refs_12_), channel_id=1, source_target_pairs={{0,2},{2,0},{4,6},{6,4},{8,10},{10,8},{12,14},{14,12},{16,18},{18,... | collective-permute-start | bytes 786440 | tf_op jit(solution)/shard_map/ppermute | solution.py:76
  85.8 21.4 %collective-permute-start.44 = (bf16[1024,128]{1,0:T(8,128)(2,1)S(1)}, bf16[1024,128]{1,0:T(8,128)(2,1)S(1)}, u32[]{:S(2)}, u32[]{:S(2)}) collective-permute-start(bf16[1024,128]{1,0:T(8,128)(2,1)S(1)} %collective-permute-done.40.refs_14_), channel_id=1, source_target_pairs={{0,8},{2,10},{8,16},{10,18},{16,24},{18,26},{24,28},{26,30},{28,20... | collective-permute-start | bytes 786440 | tf_op jit(solution)/shard_map/ppermute | solution.py:76
  95.3 9.6 %collective-permute-start.33 = (bf16[64,1024]{1,0:T(8,128)(2,1)S(1)}, bf16[64,1024]{1,0:T(8,128)(2,1)S(1)}, u32[]{:S(2)}, u32[]{:S(2)}) collective-permute-start(bf16[64,1024]{1,0:T(8,128)(2,1)S(1)} %copy-done.58), channel_id=1, source_target_pairs={{0,2},{2,0},{4,6},{6,4},{8,10},{10,8},{12,14},{14,12},{16,18},{18,... | collective-permute-start | bytes 393224 | tf_op jit(solution)/shard_map/ppermute | solution.py:76
  95.4 10.2 %collective-permute-start.34 = (bf16[64,1024]{1,0:T(8,128)(2,1)S(1)}, bf16[64,1024]{1,0:T(8,128)(2,1)}, u32[]{:S(2)}, u32[]{:S(2)}) collective-permute-start(bf16[64,1024]{1,0:T(8,128)(2,1)S(1)} %collective-permute-done.32.refs_15_), channel_id=1, source_target_pairs={{0,2},{2,0},{4,6},{6,4},{8,10},{10,8},{12,14},{14,12},{16,18},{18,... | collective-permute-start | bytes 393224 | tf_op jit(solution)/shard_map/ppermute | solution.py:76
  105.5 30.3 %collective-permute-start.35 = (bf16[1024,128]{1,0:T(8,128)(2,1)S(1)}, bf16[1024,128]{1,0:T(8,128)(2,1)S(1)}, u32[]{:S(2)}, u32[]{:S(2)}) collective-permute-start(bf16[1024,128]{1,0:T(8,128)(2,1)S(1)} %copy-done.6), channel_id=1, source_target_pairs={{0,2},{2,0},{4,6},{6,4},{8,10},{10,8},{12,14},{14,12},{16,18},{18,... | collective-permute-start | bytes 786440 | tf_op jit(solution)/shard_map/ppermute | solution.py:76
  105.5 32.3 %collective-permute-start.37 = (bf16[1024,128]{1,0:T(8,128)(2,1)S(1)}, bf16[1024,128]{1,0:T(8,128)(2,1)S(1)}, u32[]{:S(2)}, u32[]{:S(2)}) collective-permute-start(bf16[1024,128]{1,0:T(8,128)(2,1)S(1)} %collective-permute-done.36.refs_10_), channel_id=1, source_target_pairs={{0,2},{2,0},{4,6},{6,4},{8,10},{10,8},{12,14},{14,12},{16,18},{18,... | collective-permute-start | bytes 786440 | tf_op jit(solution)/shard_map/ppermute | solution.py:76
  106.7 31.2 %collective-permute-start.39 = (bf16[1024,128]{1,0:T(8,128)(2,1)S(1)}, bf16[1024,128]{1,0:T(8,128)(2,1)S(1)}, u32[]{:S(2)}, u32[]{:S(2)}) collective-permute-start(bf16[1024,128]{1,0:T(8,128)(2,1)S(1)} %collective-permute-done.38.refs_12_), channel_id=1, source_target_pairs={{0,2},{2,0},{4,6},{6,4},{8,10},{10,8},{12,14},{14,12},{16,18},{18,... | collective-permute-start | bytes 786440 | tf_op jit(solution)/shard_map/ppermute | solution.py:76
  106.7 31.2 %collective-permute-start.41 = (bf16[1024,128]{1,0:T(8,128)(2,1)S(1)}, bf16[1024,128]{1,0:T(8,128)(2,1)}, u32[]{:S(2)}, u32[]{:S(2)}) collective-permute-start(bf16[1024,128]{1,0:T(8,128)(2,1)S(1)} %collective-permute-done.40.refs_14_), channel_id=1, source_target_pairs={{0,2},{2,0},{4,6},{6,4},{8,10},{10,8},{12,14},{14,12},{16,18},{18,... | collective-permute-start | bytes 786440 | tf_op jit(solution)/shard_map/ppermute | solution.py:76
  107.2 28.5 %collective-permute-start.46 = (bf16[1024,128]{1,0:T(8,128)(2,1)S(1)}, bf16[1024,128]{1,0:T(8,128)(2,1)S(1)}, u32[]{:S(2)}, u32[]{:S(2)}) collective-permute-start(bf16[1024,128]{1,0:T(8,128)(2,1)S(1)} %collective-permute-done.42.refs_16_), channel_id=1, source_target_pairs={{8,0},{10,2},{16,8},{18,10},{24,16},{26,18},{28,24},{30,26},{20,28... | collective-permute-start | bytes 786440 | tf_op jit(solution)/shard_map/ppermute | solution.py:76
  135.7 21.4 %collective-permute-start.43 = (bf16[1024,128]{1,0:T(8,128)(2,1)S(1)}, bf16[1024,128]{1,0:T(8,128)(2,1)}, u32[]{:S(2)}, u32[]{:S(2)}) collective-permute-start(bf16[1024,128]{1,0:T(8,128)(2,1)S(1)} %collective-permute-done.42.refs_16_), channel_id=1, source_target_pairs={{0,2},{2,0},{4,6},{6,4},{8,10},{10,8},{12,14},{14,12},{16,18},{18,... | collective-permute-start | bytes 786440 | tf_op jit(solution)/shard_map/ppermute | solution.py:76
  135.8 11.6 %collective-permute-start.48 = (bf16[512,128]{1,0:T(8,128)(2,1)S(1)}, bf16[512,128]{1,0:T(8,128)(2,1)}, u32[]{:S(2)}, u32[]{:S(2)}) collective-permute-start(bf16[512,128]{1,0:T(8,128)(2,1)S(1)} %slice.36), channel_id=1, source_target_pairs={{0,8},{2,10},{8,16},{10,18},{16,24},{18,26},{24,28},{26,30},{28,20... | collective-permute-start | bytes 393224 | tf_op jit(solution)/shard_map/ppermute | solution.py:76
  137.9 9.7 %collective-permute-start.49 = (bf16[512,128]{1,0:T(8,128)(2,1)S(1)}, bf16[512,128]{1,0:T(8,128)(2,1)}, u32[]{:S(2)}, u32[]{:S(2)}) collective-permute-start(bf16[512,128]{1,0:T(8,128)(2,1)S(1)} %slice.37), channel_id=1, source_target_pairs={{8,0},{10,2},{16,8},{18,10},{24,16},{26,18},{28,24},{30,26},{20,28... | collective-permute-start | bytes 393224 | tf_op jit(solution)/shard_map/ppermute | solution.py:76
  137.9 19.2 %collective-permute-start.45 = (bf16[1024,128]{1,0:T(8,128)(2,1)S(1)}, bf16[1024,128]{1,0:T(8,128)(2,1)}, u32[]{:S(2)}, u32[]{:S(2)}) collective-permute-start(bf16[1024,128]{1,0:T(8,128)(2,1)S(1)} %collective-permute-done.44.refs_18_), channel_id=1, source_target_pairs={{0,2},{2,0},{4,6},{6,4},{8,10},{10,8},{12,14},{14,12},{16,18},{18,... | collective-permute-start | bytes 786440 | tf_op jit(solution)/shard_map/ppermute | solution.py:76
  138.0 19.2 %collective-permute-start.47 = (bf16[1024,128]{1,0:T(8,128)(2,1)S(1)}, bf16[1024,128]{1,0:T(8,128)(2,1)}, u32[]{:S(2)}, u32[]{:S(2)}) collective-permute-start(bf16[1024,128]{1,0:T(8,128)(2,1)S(1)} %collective-permute-done.46.refs_20_), channel_id=1, source_target_pairs={{0,2},{2,0},{4,6},{6,4},{8,10},{10,8},{12,14},{14,12},{16,18},{18,... | collective-permute-start | bytes 786440 | tf_op jit(solution)/shard_map/ppermute | solution.py:76
  147.5 9.6 %collective-permute-start.50 = (bf16[512,128]{1,0:T(8,128)(2,1)}, bf16[512,128]{1,0:T(8,128)(2,1)}, u32[]{:S(2)}, u32[]{:S(2)}) collective-permute-start(bf16[512,128]{1,0:T(8,128)(2,1)} %collective-permute-done.48.refs_22_), channel_id=1, source_target_pairs={{0,2},{2,0},{4,6},{6,4},{8,10},{10,8},{12,14},{14,12},{16,18},{18,... | collective-permute-start | bytes 393224 | tf_op jit(solution)/shard_map/ppermute | solution.py:76
  147.6 9.6 %collective-permute-start.51 = (bf16[512,128]{1,0:T(8,128)(2,1)}, bf16[512,128]{1,0:T(8,128)(2,1)}, u32[]{:S(2)}, u32[]{:S(2)}) collective-permute-start(bf16[512,128]{1,0:T(8,128)(2,1)} %collective-permute-done.49.refs_23_), channel_id=1, source_target_pairs={{0,2},{2,0},{4,6},{6,4},{8,10},{10,8},{12,14},{14,12},{16,18},{18,... | collective-permute-start | bytes 393224 | tf_op jit(solution)/shard_map/ppermute | solution.py:76
  165.1 36.5 %collective-permute-start.52 = (bf16[16,128,128]{2,1,0:T(8,128)(2,1)}, bf16[16,128,128]{2,1,0:T(8,128)(2,1)}, u32[]{:S(2)}, u32[]{:S(2)}) collective-permute-start(bf16[16,128,128]{2,1,0:T(8,128)(2,1)} %get-tuple-element.66), channel_id=1, source_target_pairs={{0,1},{1,0},{2,3},{3,2},{4,5},{5,4},{6,7},{7,6},{8,9},{9,8},{10,11... | collective-permute-start | bytes 1572872 | tf_op jit(solution)/shard_map/ppermute | solution.py:598
  (76 other events, 673.5 us)

commit v4 on v3

--- a/solution.py
+++ b/solution.py
@@ -24,6 +24,10 @@
 
 def vmem():
     return pl.BlockSpec(memory_space=pltpu.VMEM)
+
+
+def anywhere():
+    return pl.BlockSpec(memory_space=pl.ANY)
 
 
 def smem():
@@ -68,7 +72,6 @@
     def __init__(self, shard, tables):
         self.ahead, self.back, self.swap, self.order = tables
         self.length = len(self.order) // 2
-        self.half = shard.shape[0] // 2
         self.up = self.down = shard
         self.blocks = [shard, self.move(shard, self.swap)]
 
@@ -86,13 +89,15 @@
             self.move(self.down, self.swap),
         ]
 
-    def last(self, *others):
+    def last(self, upward, *others):
         if others:
             self.up, self.down = lax.optimization_barrier((self.up, self.down) + others)[:2]
-        first = self.move(self.up[: self.half], self.ahead)
-        second = self.move(self.down[self.half :], self.back)
-        ends = [first, second, self.move(first, self.swap), self.move(second, self.swap)]
-        return self.blocks + ends
+        return self.move(self.up, self.ahead) if upward else self.move(self.down, self.back)
+
+    def all(self, end, *others):
+        if others:
+            end = lax.optimization_barrier((end,) + others)[0]
+        return self.blocks + [end, self.move(end, self.swap)]
 
 
 def prepare_kernel(heads, page, width, pages_step, first_page, aliased, table_ref, length_ref, *refs):
@@ -106,13 +111,13 @@
     pick = jnp.where(pick_lane == pick_row + half, 1.0, 0.0).astype(jnp.bfloat16)
     ones = jnp.where(lax.broadcasted_iota(jnp.int32, (rows, page), 0) == half, 1.0, 0.0)
     for i in range(pages_step):
-        wide[...] = pages[i][0].astype(jnp.float32)
+        wide[i] = pages[i][0].astype(jnp.float32)
         first = (first_page + step * pages_step + i) * page
         position = first + lax.broadcasted_iota(jnp.int32, (page, width), 0)
         lane = lax.broadcasted_iota(jnp.int32, (page, width), 1)
         bias = jnp.where((lane == half) & (position >= length_ref[0]), masked_score, 0.0)
         for h in range(heads):
-            rows_h = wide[pl.ds(h, page, stride=heads), :]
+            rows_h = wide[i, pl.ds(h, page, stride=heads), :]
             key_ref[h, pl.ds(i * page, page), :] = jnp.where(lane < half, rows_h, bias).astype(
                 jnp.bfloat16
             )
@@ -154,7 +159,7 @@
                 pl.BlockSpec((heads, pages_step * page, width), lambda j, t, n: (0, at + j, 0)),
                 pl.BlockSpec((heads, rows, pages_step * page), lambda j, t, n: (0, 0, at + j)),
             ],
-            scratch_shapes=[pltpu.VMEM((page * heads, width), jnp.float32)],
+            scratch_shapes=[pltpu.VMEM((pages_step, page * heads, width), jnp.float32)],
         ),
         out_shape=[
             jax.ShapeDtypeStruct((heads, total * page, width), jnp.bfloat16),
@@ -179,31 +184,23 @@
     )
 
 
-def assembled(chunks, order_ref, weight):
-    if len(chunks) == 1:
-        return chunks[0]
-    count = order_ref.shape[0]
-    rows = weight.shape[0] // count
-    for k in range(count):
+def project_kernel(heads, new_heads, group, dim, blocks, order_ref, *refs):
+    chunks = refs[:blocks]
+    normed_hbm, cos_ref, sin_ref, query_ref = refs[blocks : blocks + 4]
+    source, normed_ref, sems = refs[-3:]
+    rows = source.shape[0] // blocks
+    copies = [pltpu.make_async_copy(normed_hbm, normed_ref, sems.at[blocks])]
+    for k in range(blocks):
         start = pl.multiple_of(order_ref[k] * rows, rows)
-        if k < count - 2:
-            weight[pl.ds(start, rows), :] = chunks[k][...]
-        else:
-            at = 2 * k - (count - 2)
-            weight[pl.ds(start, rows), :] = jnp.concatenate(
-                [chunks[at][...], chunks[at + 1][...]], axis=0
-            )
-    return weight
-
-
-def project_kernel(heads, new_heads, group, dim, blocks, order_ref, *refs):
-    normed_ref, cos_ref, sin_ref = refs[blocks : blocks + 3]
-    query_ref = refs[blocks + 3]
-    source = assembled(refs[:blocks], order_ref, refs[-1])
+        copies.append(pltpu.make_async_copy(chunks[k], source.at[pl.ds(start, rows)], sems.at[k]))
+    for copy in copies:
+        copy.start()
     cosine, sines = cos_ref[...], sin_ref[...]
     tokens = cosine.shape[1]
+    width = group * dim
+    for copy in copies:
+        copy.wait()
     normed = normed_ref[...]
-    width = group * dim
     row = lax.broadcasted_iota(jnp.int32, (dim, group * token_tile), 0)
     one_row = jnp.where(row == 0, 1.0, 0.0).astype(jnp.bfloat16)
     for h in range(heads):
@@ -235,16 +232,20 @@
         outs += [(new_heads, tokens, 2 * dim), (new_heads, dim + 16, tokens)]
     return pl.pallas_call(
         functools.partial(project_kernel, heads, new_heads, group, dim, len(chunks)),
-        in_specs=[smem()] + [vmem()] * (len(chunks) + 3),
+        in_specs=[smem()] + [anywhere()] * (len(chunks) + 1) + [vmem()] * 2,
         out_specs=[vmem()] * len(outs),
         out_shape=[jax.ShapeDtypeStruct(shape, jnp.bfloat16) for shape in outs],
-        scratch_shapes=[pltpu.VMEM((width, columns), jnp.bfloat16)],
+        scratch_shapes=[
+            pltpu.VMEM((width, columns), jnp.bfloat16),
+            pltpu.VMEM((tokens, width), jnp.bfloat16),
+            pltpu.SemaphoreType.DMA((len(chunks) + 1,)),
+        ],
         cost_estimate=pl.CostEstimate(
             flops=2 * tokens * width * columns,
             bytes_accessed=2 * width * columns,
             transcendentals=0,
         ),
-        compiler_params=params(24),
+        compiler_params=params(60),
         name="project",
     )(order, *chunks, normed, cosine, sines)
 
@@ -254,24 +255,27 @@
 
 
 def attend_kernel(
-    head,
-    cache_head,
+    heads,
+    first_query,
+    first_head,
     length_ref,
     span_ref,
     tile_ref,
     keys_hbm,
     values_hbm,
-    query_ref,
+    queries_hbm,
     out_ref,
     token_ref,
     even,
     odd,
-    key_ref,
-    value_ref,
+    keys_ref,
+    values_ref,
+    queries_ref,
     key_sems,
     value_sems,
+    query_sems,
 ):
-    lanes = query_ref.shape[3]
+    lanes = out_ref.shape[2]
     length = length_ref[0]
     token_ref[0] = length
     q = tile_ref[0]
@@ -280,109 +284,132 @@
     live = q * token_tile < span_ref[0]
     pairs = jnp.where(live, (length + pair - 1) // pair, 0)
     last_block = jnp.maximum(2 * pairs - 1, 0)
-
-    def key_copy(i):
+    row = lax.broadcasted_iota(jnp.int32, out_ref.shape[1:], 0)
+
+    def key_copy(h, i):
         piece = pl.ds(pl.multiple_of(i * pair, pair), pair)
         return pltpu.make_async_copy(
-            keys_hbm.at[cache_head, piece], key_ref.at[piece], key_sems.at[i]
-        )
-
-    def value_copy(i):
+            keys_hbm.at[first_head + h, piece], keys_ref.at[h & 1, piece], key_sems.at[h & 1, i]
+        )
+
+    def value_copy(h, i):
         piece = pl.ds(pl.multiple_of(i * pair, pair), pair)
         return pltpu.make_async_copy(
-            values_hbm.at[cache_head, :, piece], value_ref.at[:, piece], value_sems.at[i]
-        )
-
-    for i in range(keys_hbm.shape[1] // pair):
-
-        @pl.when(i < pairs)
-        def fetch():
-            key_copy(i).start()
-            value_copy(i).start()
-
-    def scores_of(block, c, target):
-        start = pl.multiple_of(block * key_block + c * score_chunk, score_chunk)
-        scores = matmul(key_ref[pl.ds(start, score_chunk), :], query_ref[head, q])
-        target[pl.ds(c * score_chunk, score_chunk), :] = scores
-        return column_max(scores)
-
-    def half(block, following, current, target, state):
-        maximum, top, total = state
-        new_maximum = jnp.maximum(maximum, jnp.max(top, axis=0, keepdims=True))
-        total = total * jnp.exp(maximum - new_maximum)
-        next_top = None
-        ratio = value_chunk // score_chunk
-        parts = []
-        for c in range(key_block // score_chunk):
-            seen = scores_of(following, c, target)
-            next_top = seen if next_top is None else jnp.maximum(next_top, seen)
-            part = jnp.exp(current[pl.ds(c * score_chunk, score_chunk), :] - new_maximum)
-            parts.append(part.astype(jnp.bfloat16))
-            if len(parts) == ratio:
-                weights = parts[0] if ratio == 1 else jnp.concatenate(parts, axis=0)
-                start = block * key_block + (c + 1 - ratio) * score_chunk
-                start = pl.multiple_of(start, value_chunk)
-                total = total + matmul(value_ref[:, pl.ds(start, value_chunk)], weights)
-                parts = []
-        return new_maximum, next_top, total
-
-    def advance(i, state):
-        @pl.when(i + 1 < pairs)
-        def arrived():
-            key_copy(i + 1).wait()
-
-        value_copy(i).wait()
-        block = 2 * i
-        state = half(block, block + 1, even, odd, state)
-        following = jnp.minimum(block + 2, last_block)
-        return half(block + 1, following, odd, even, state)
-
-    @pl.when(pairs > 0)
-    def work():
-        key_copy(0).wait()
+            values_hbm.at[first_head + h, :, piece],
+            values_ref.at[h & 1, :, piece],
+            value_sems.at[h & 1, i],
+        )
+
+    def query_copy(h):
+        return pltpu.make_async_copy(
+            queries_hbm.at[first_query + h, q], queries_ref.at[h], query_sems.at[h]
+        )
+
+    def fetch(h):
+        def one(i, _):
+            key_copy(h, i).start()
+            value_copy(h, i).start()
+            return 0
+
+        lax.fori_loop(0, pairs, one, 0)
+
+    def attend_head(h, _):
+        query_copy(h).wait()
+        key_copy(h, 0).wait()
+
+        @pl.when(h + 1 < heads)
+        def ahead():
+            fetch(h + 1)
+
+        key_ref, value_ref, query_ref = keys_ref.at[h & 1], values_ref.at[h & 1], queries_ref.at[h]
+        def scores_of(block, c, target):
+            start = pl.multiple_of(block * key_block + c * score_chunk, score_chunk)
+            scores = matmul(key_ref[pl.ds(start, score_chunk), :], query_ref[...])
+            target[pl.ds(c * score_chunk, score_chunk), :] = scores
+            return column_max(scores)
+
+        def half(block, following, current, target, state):
+            maximum, top, total = state
+            new_maximum = jnp.maximum(maximum, jnp.max(top, axis=0, keepdims=True))
+            total = total * jnp.exp(maximum - new_maximum)
+            next_top = None
+            ratio = value_chunk // score_chunk
+            parts = []
+            for c in range(key_block // score_chunk):
+                seen = scores_of(following, c, target)
+                next_top = seen if next_top is None else jnp.maximum(next_top, seen)
+                part = jnp.exp(current[pl.ds(c * score_chunk, score_chunk), :] - new_maximum)
+                parts.append(part.astype(jnp.bfloat16))
+                if len(parts) == ratio:
+                    weights = parts[0] if ratio == 1 else jnp.concatenate(parts, axis=0)
+                    start = block * key_block + (c + 1 - ratio) * score_chunk
+                    start = pl.multiple_of(start, value_chunk)
+                    total = total + matmul(value_ref[:, pl.ds(start, value_chunk)], weights)
+                    parts = []
+            return new_maximum, next_top, total
+
+        def advance(i, state):
+            @pl.when(i + 1 < pairs)
+            def arrived():
+                key_copy(h, i + 1).wait()
+
+            value_copy(h, i).wait()
+            block = 2 * i
+            state = half(block, block + 1, even, odd, state)
+            following = jnp.minimum(block + 2, last_block)
+            return half(block + 1, following, odd, even, state)
+
         top = scores_of(0, 0, even)
         for c in range(1, key_block // score_chunk):
             top = jnp.maximum(top, scores_of(0, c, even))
         start = (
             jnp.full((1, lanes), masked_score, jnp.float32),
             top,
-            jnp.zeros(out_ref.shape, jnp.float32),
+            jnp.zeros(row.shape, jnp.float32),
         )
         maximum, _, total = lax.fori_loop(0, pairs, advance, start)
-        row = lax.broadcasted_iota(jnp.int32, out_ref.shape, 0)
-        out_ref[...] = jnp.where(row == sum_row + 1, maximum, total)
+        out_ref[h] = jnp.where(row == sum_row + 1, maximum, total)
+        return 0
+
+    @pl.when(pairs > 0)
+    def work():
+        for h in range(heads):
+            query_copy(h).start()
+        fetch(0)
+        lax.fori_loop(0, heads, attend_head, 0)
 
     @pl.when(pairs == 0)
     def nothing():
-        row = lax.broadcasted_iota(jnp.int32, out_ref.shape, 0)
-        out_ref[...] = jnp.where(row == sum_row + 1, masked_score, 0.0)
-
-
-def attend(head, cache_head, tile, keys, values, queries, token, valid):
+        for h in range(heads):
+            out_ref[h] = jnp.where(row == sum_row + 1, masked_score, 0.0)
+
+
+def attend(heads, first_query, first_head, tile, keys, values, queries, token, valid):
     _, cached, width = keys.shape
     rows = values.shape[1]
     lanes = queries.shape[3]
     pieces = cached // (2 * key_block)
-    anywhere = pl.BlockSpec(memory_space=pl.ANY)
     return pl.pallas_call(
-        functools.partial(attend_kernel, head, cache_head),
-        in_specs=[smem()] * 3 + [anywhere, anywhere, vmem()],
+        functools.partial(attend_kernel, heads, first_query, first_head),
+        in_specs=[smem()] * 3 + [anywhere()] * 3,
         out_specs=[vmem(), smem()],
         out_shape=[
-            jax.ShapeDtypeStruct((rows, lanes), jnp.float32),
+            jax.ShapeDtypeStruct((heads, rows, lanes), jnp.float32),
             jax.ShapeDtypeStruct((1,), jnp.int32),
         ],
         scratch_shapes=[pltpu.VMEM((key_block, lanes), jnp.float32)] * 2
         + [
-            pltpu.VMEM((cached, width), jnp.bfloat16),
-            pltpu.VMEM((rows, cached), jnp.bfloat16),
-            pltpu.SemaphoreType.DMA((pieces,)),
-            pltpu.SemaphoreType.DMA((pieces,)),
+            pltpu.VMEM((2, cached, width), jnp.bfloat16),
+            pltpu.VMEM((2, rows, cached), jnp.bfloat16),
+            pltpu.VMEM((heads, width, lanes), jnp.bfloat16),
+            pltpu.SemaphoreType.DMA((2, pieces)),
+            pltpu.SemaphoreType.DMA((2, pieces)),
+            pltpu.SemaphoreType.DMA((heads,)),
         ],
         cost_estimate=pl.CostEstimate(
-            flops=2 * cached * lanes * 2 * width,
-            bytes_accessed=2 * cached * 2 * width,
-            transcendentals=cached * lanes,
+            flops=8 * heads * cached * lanes * 2 * width,
+            bytes_accessed=2 * heads * cached * 2 * width,
+            transcendentals=heads * cached * lanes,
         ),
         compiler_params=params(60),
         name="attend",
@@ -416,67 +443,87 @@
     return pieces
 
 
-def finish_kernel(heads, group, dim, sets, blocks, span_ref, tile_ref, *refs):
-    states = refs[:heads]
-    queries = refs[heads : heads + sets]
-    new_key_ref, new_value_ref = refs[heads + sets : heads + sets + 2]
-    chunks = refs[heads + sets + 2 : heads + sets + 2 + blocks]
-    out_ref = refs[heads + sets + 2 + blocks]
+def finish_kernel(heads, sets, group, dim, blocks, span_ref, tile_ref, *refs):
+    states_hbm = refs[:sets]
+    queries_hbm = refs[sets : sets + len(heads)]
+    new_keys_hbm, new_values_hbm = refs[sets + len(heads) : sets + len(heads) + 2]
+    at = sets + len(heads) + 2
+    chunks = refs[at : at + blocks]
+    out_ref, token_ref = refs[at + blocks : at + blocks + 2]
+    states, queries, new_keys, new_values, weight, sems, weight_sems = refs[at + blocks + 2 :]
     q = tile_ref[0]
+    token_ref[0] = q
+    total = sum(heads)
+    per_set = total // sets
+    columns = weight.shape[1] // max(blocks, 1)
+    copies = []
+    for i in range(sets):
+        copies.append((states_hbm[i], states.at[pl.ds(i * per_set, per_set)]))
+    copies += [(new_keys_hbm, new_keys), (new_values_hbm, new_values)]
+    source = [(which, h) for which, count in enumerate(heads) for h in range(count)]
+    for h in range(total):
+        which, place = source[h]
+        copies.append((queries_hbm[which].at[place, q], queries.at[h]))
+    copies = [pltpu.make_async_copy(a, b, sems.at[i]) for i, (a, b) in enumerate(copies)]
+    loads = [
+        pltpu.make_async_copy(
+            chunks[k], weight.at[:, pl.ds(k * columns, columns)], weight_sems.at[k]
+        )
+        for k in range(blocks)
+    ]
+    for copy in copies + loads:
+        copy.start()
+    for copy in copies:
+        copy.wait()
     pieces = []
-    for h in range(heads):
-        per_set = heads // sets
-        query = queries[h // per_set][h % per_set, q]
+    for h in range(total):
         pieces += finish_head(
-            q, span_ref[0], group, dim, states[h][...], query, new_key_ref[h], new_value_ref[h]
+            q, span_ref[0], group, dim, states[h], queries[h], new_keys[h], new_values[h]
         )
     attended = jnp.concatenate(pieces, axis=1)
     if blocks == 0:
         out_ref[...] = attended
         return
-    token_ref = refs[heads + sets + 3 + blocks]
-    token_ref[0] = q
-    count = out_ref.shape[0]
-    for k in range(0, count, 2):
-        if k < count - 2:
-            weight = jnp.concatenate([chunks[k][...], chunks[k + 1][...]], axis=1)
-        else:
-            at = count - 2
-            own = jnp.concatenate([chunks[at][...], chunks[at + 1][...]], axis=0)
-            other = jnp.concatenate([chunks[at + 2][...], chunks[at + 3][...]], axis=0)
-            weight = jnp.concatenate([own, other], axis=1)
-        both = matmul(attended, weight).astype(jnp.bfloat16)
-        width = both.shape[1] // 2
-        out_ref[k] = both[:, :width]
-        out_ref[k + 1] = both[:, width:]
-
-
-def finish(states, tile, valid, queries, new_keys, new_values, group, chunks, count):
-    heads = len(states)
-    dim = states[0].shape[0] - 16
-    if chunks:
-        columns = chunks[0].shape[1]
-        out_shape = [
-            jax.ShapeDtypeStruct((count, token_tile, columns), jnp.bfloat16),
+    for copy in loads:
+        copy.wait()
+    for k in range(0, blocks, 2):
+        both = matmul(attended, weight[:, pl.ds(k * columns, 2 * columns)]).astype(jnp.bfloat16)
+        out_ref[k] = both[:, :columns]
+        out_ref[k + 1] = both[:, columns:]
+
+
+def finish(states, tile, valid, queries, new_keys, new_values, group, chunks):
+    heads = tuple(q.shape[0] for q in queries)
+    total = sum(heads)
+    rows, lanes = states[0].shape[1:]
+    dim = rows - 16
+    depth = total * group * dim
+    blocks = len(chunks)
+    columns = chunks[0].shape[1] if blocks else 128
+    out = (blocks, token_tile, columns) if blocks else (token_tile, depth)
+    return pl.pallas_call(
+        functools.partial(finish_kernel, heads, len(states), group, dim, blocks),
+        in_specs=[smem()] * 2 + [anywhere()] * (len(states) + len(queries) + 2 + blocks),
+        out_specs=[vmem(), smem()],
+        out_shape=[
+            jax.ShapeDtypeStruct(out, jnp.bfloat16),
             jax.ShapeDtypeStruct((1,), jnp.int32),
-        ]
-        out_specs = [vmem(), smem()]
-    else:
-        columns = 0
-        out_shape = [jax.ShapeDtypeStruct((token_tile, heads * group * dim), jnp.bfloat16)]
-        out_specs = [vmem()]
-    depth = heads * group * dim
-    return pl.pallas_call(
-        functools.partial(finish_kernel, heads, group, dim, len(queries), len(chunks)),
-        in_specs=[smem()] * 2 + [vmem()] * (heads + len(queries) + 2 + len(chunks)),
-        out_specs=out_specs,
-        out_shape=out_shape,
+        ],
+        scratch_shapes=[
+            pltpu.VMEM((total, rows, lanes), jnp.float32),
+            pltpu.VMEM((total,) + queries[0].shape[2:], jnp.bfloat16),
+            pltpu.VMEM(new_keys.shape, jnp.bfloat16),
+            pltpu.VMEM(new_values.shape, jnp.bfloat16),
+            pltpu.VMEM((depth if blocks else 16, max(blocks, 1) * columns), jnp.bfloat16),
+            pltpu.SemaphoreType.DMA((len(states) + 2 + total,)),
+            pltpu.SemaphoreType.DMA((max(blocks, 1),)),
+        ],
         cost_estimate=pl.CostEstimate(
-            flops=2 * token_tile * depth * columns * count,
-            bytes_accessed=2 * depth * columns * count,
+            flops=2 * token_tile * depth * columns * blocks,
+            bytes_accessed=2 * depth * columns * blocks,
             transcendentals=0,
         ),
-        compiler_params=params(24),
+        compiler_params=params(60),
         name="finish",
     )(valid, tile, *states, *queries, new_keys, new_values, *chunks)
 
@@ -496,7 +543,7 @@
         in_specs=[smem(), vmem(), vmem()],
         out_specs=vmem(),
         out_shape=jax.ShapeDtypeStruct((rows, count * columns), jnp.bfloat16),
-        compiler_params=params(16),
+        compiler_params=params(60),
         name="combine",
     )(order, own, other)
 
@@ -532,16 +579,15 @@
         whole = jnp.concatenate(
             [jnp.where(rank == 0, tokens, other), jnp.where(rank == 0, other, tokens)], axis=0
         )
-        parts = 4
+        parts = 2
         state = ()
+        ring_first.step()
+        ring_second.step()
         for part in range(parts):
             state = prepare(kv_cache, table, length, part, parts, state)
-            if part < parts - 1:
-                ring_first.step()
-                ring_second.step()
-            else:
-                first_chunks = ring_first.last()
-                second_chunks = ring_second.last()
+            ring_first.step()
+            ring_second.step(state[0])
+        first_chunks = ring_first.all(ring_first.last(True))
         keys, values = state
     else:
         order = jnp.zeros((1,), jnp.int32)
@@ -557,48 +603,48 @@
     positions = length[0] + jnp.arange(normed.shape[0], dtype=jnp.int32)
     cosine, sines = rope_tables(positions, dim)
     queries = []
-    if early:
-        queries += project(normed, first_chunks, order, cosine, sines, early, 0, group, dim)
-    late, new_keys, new_values = project(
-        normed, second_chunks, order, cosine, sines, heads - early, heads, group, dim
-    )
-    queries.append(late)
-
-    def attend_tile(tile, which, token):
-        states = []
-        for h in which:
-            source, at = (queries[0], h) if h < early else (queries[-1], h - early)
-            state, token = attend(at, h, tile, keys, values, source, token, span_len)
-            states.append(state)
-        return states, token
+
+    def attend_tile(tile, source, count, first, token):
+        return attend(count, 0, first, tile, keys, values, source, token, span_len)
 
     def finish_tile(states, tile, chunks):
-        return finish(
-            states, tile, span_len, queries, new_keys, new_values, group, chunks, req_count
-        )
+        return finish(states, tile, span_len, queries, new_keys, new_values, group, chunks)
 
     if not fast:
+        late, new_keys, new_values = project(
+            normed, second_chunks, order, cosine, sines, heads, heads, group, dim
+        )
+        queries.append(late)
         rows = []
         for q in range(normed.shape[0] // token_tile):
             tile = jnp.full((1,), q, jnp.int32)
-            states, _ = attend_tile(tile, range(heads), length)
-            rows.append(finish_tile(states, tile, [])[0])
+            state, _ = attend_tile(tile, late, heads, 0, length)
+            rows.append(finish_tile([state], tile, [])[0])
         gathered = lax.all_gather(w_out, "req", axis=1, tiled=True)
         partial = matmul(jnp.concatenate(rows, axis=0), gathered).astype(jnp.bfloat16)
         summed = lax.psum_scatter(partial, "tp", scatter_dimension=0, tiled=True)
         return (residual_scale * summed.astype(jnp.float32)).astype(jnp.bfloat16)
     theirs, ours = (1 - rank).reshape(1), rank.reshape(1)
     ring_out.step(ring_first.up)
-    ring_out.step()
-    ring_out.step()
-    out_chunks = ring_out.last()
-    sent_states, token = attend_tile(theirs, range(heads), length)
-    kept_states, token = attend_tile(ours, range(heads // 2), token)
-    sent, tile_token = finish_tile(sent_states, theirs, out_chunks)
+    soon = project(normed, first_chunks, order, cosine, sines, early, 0, group, dim)[0]
+    second_end = ring_second.last(False, soon)
+    ring_out.step(soon)
+    sent_first, token = attend_tile(theirs, soon, early, 0, length)
+    second_chunks = ring_second.all(second_end, sent_first)
+    ring_out.step(sent_first)
+    late, new_keys, new_values = project(
+        normed, second_chunks, order, cosine, sines, heads - early, heads, group, dim
+    )
+    queries += [soon, late]
+    sent_second, token = attend_tile(theirs, late, heads - early, early, token)
+    out_end = ring_out.last(True, sent_second)
+    kept_first, token = attend_tile(ours, soon, early, 0, token)
+    out_chunks = ring_out.all(out_end, kept_first)
+    sent, tile_token = finish_tile([sent_first, sent_second], theirs, out_chunks)
     received = lax.ppermute(sent, "tp", swap)
     token = token + (tile_token - theirs)
-    more, token = attend_tile(ours, range(heads // 2, heads), token)
-    kept, _ = finish_tile(kept_states + more, ours, out_chunks)
+    kept_second, token = attend_tile(ours, late, heads - early, early, token)
+    kept, _ = finish_tile([kept_first, kept_second], ours, out_chunks)
     return combine(kept, received, order)
 
 

time: 207 us -> 168 us (0.81)
  the two profiles are of different devices: /device:TPU:24 before, /device:TPU:0 now
where the time goes in v4:
time: 168 us
  Pallas kernels  99.6 us (59%)
  starting transfers between devices  31.6 us (19%)
  waiting for transfers between devices  24.1 us (14%)
  local copies, waits for them, and re-layouts  7.33 us (4%)
  other arithmetic  3.06 us (2%)
  between operations  2.6 us (2%)
    pallas_call x4, Pallas kernels, attend(): pl.pallas_call(functools.partial(attend_kernel, heads, first_query, first...  54.3 us
    ppermute x45, starting transfers between devices, move(): return lax.ppermute(value, 'req', pairs)  28.1 us
    ppermute x45, waiting for transfers between devices, move(): return lax.ppermute(value, 'req', pairs)  24.1 us
    pallas_call x2, Pallas kernels, prepare(): pl.pallas_call(functools.partial(prepare_kernel, heads, page, width, page...  20.6 us
    pallas_call x2, Pallas kernels, finish(): pl.pallas_call(functools.partial(finish_kernel, heads, len(states), group...  11.7 us
    pallas_call x2, Pallas kernels, project(): pl.pallas_call(functools.partial(project_kernel, heads, new_heads, group,...  10.8 us
    unnamed x99, local copies, waits for them, and re-layouts  3.84 us
  transfers between devices with their start and end apart: 47, of which 15 were waited for; matrix products, arithmetic and copies ran while one was open for 4% of the time, Pallas kernels for 54%

profile of v4, /device:TPU:0, one launch (start us, length us, event | category | flops | bytes accessed | tf_op | source)
XLA Modules:
  0.0 168.2 jit_solution(1824510089899586118)
XLA Ops:
  0.0 1.0 fusion.3
  1.0 3.1 %collective-permute-start.1 = (bf16[128,512]{1,0:T(8,128)(2,1)S(1)}, bf16[128,512]{1,0:T(8,128)(2,1)S(1)}, u32[]{:S(2)}, u32[]{:S(2)}) collective-permute-start(bf16[128,512]{1,0:T(8,128)(2,1)S(1)} %get-tuple-element.70.refs_0_), channel_id=1, source_target_pairs={{0,8},{2,10},{8,16},{10,18},{16,24},{18,26},{24,28},{26,30},{28,20... | collective-permute-start | bytes 393224 | tf_op jit(solution)/shard_map/ppermute | solution.py:79
  4.1 0.9 copy.15
  5.1 1.6 collective-permute-start.17
  7.2 1.9 %collective-permute-start.15 = (bf16[128,2048]{1,0:T(8,128)(2,1)}, bf16[128,2048]{1,0:T(8,128)(2,1)S(1)}, u32[]{:S(2)}, u32[]{:S(2)}) collective-permute-start(bf16[128,2048]{1,0:T(8,128)(2,1)} %param.10), channel_id=1, source_target_pairs={{0,1},{1,0},{2,3},{3,2},{4,5},{5,4},{6,7},{7,6},{8,9},{9,8},{10,11... | collective-permute-start | bytes 1572872 | tf_op jit(solution)/shard_map/ppermute | solution.py:578
  9.1 1.6 collective-permute-start.5
  10.7 1.2 dynamic_slice.7.length_ref
  11.9 0.6 add_convert_fusion
  12.5 3.5 %collective-permute-done.5.refs_6_ = bf16[128,512]{1,0:T(8,128)(2,1)S(1)} collective-permute-done((bf16[128,512]{1,0:T(8,128)(2,1)S(1)}, bf16[128,512]{1,0:T(8,128)(2,1)S(1)}, u32[]{:S(2)}, u32[]{:S(2)}) %collective-permute-start.5) | collective-permute-done | bytes 131104 | tf_op jit(solution)/shard_map/ppermute | solution.py:79
  16.0 1.8 %collective-permute-start.9 = (bf16[128,512]{1,0:T(8,128)(2,1)S(1)}, bf16[128,512]{1,0:T(8,128)(2,1)S(1)}, u32[]{:S(2)}, u32[]{:S(2)}) collective-permute-start(bf16[128,512]{1,0:T(8,128)(2,1)S(1)} %collective-permute-done.5.refs_6_), channel_id=1, source_target_pairs={{0,8},{2,10},{8,16},{10,18},{16,24},{18,26},{24,28},{26,30},{28,20... | collective-permute-start | bytes 393224 | tf_op jit(solution)/shard_map/ppermute | solution.py:79
  17.8 0.8 multiply_sine_fusion
  18.6 10.3 %prepare.2 = (bf16[4,8192,128]{2,1,0:T(8,128)(2,1)}, bf16[4,80,8192]{2,1,0:T(8,128)(2,1)}) custom-call(s32[64]{0:T(128)} %bitcast.21, s32[1]{0:T(128)} %dynamic_slice.7.length_ref, bf16[64,512,128]{2,1,0:T(8,128)(2,1)} %bitcast.11, bf16[64,512,128]{2,1,0:T(8,128)(2,1)} %bitcast.12, bf16[64,512,128]{2,1,0:T(8,128)(2,1)} %bitcast.13, ...), custom_call_target="tpu_custom_call" | custom-call | bytes 12582912 | tf_op jit(solution)/shard_map/prepare/pallas_call | solution.py:150
  28.9 1.3 dynamic-slice_bitcast_fusion.order_ref
  30.3 0.5 collective-permute-start.2
  31.0 10.3 %prepare.3 = (bf16[4,8192,128]{2,1,0:T(8,128)(2,1)}, bf16[4,80,8192]{2,1,0:T(8,128)(2,1)}) custom-call(s32[64]{0:T(128)} %bitcast.22, s32[1]{0:T(128)} %dynamic_slice.7.length_ref, bf16[64,512,128]{2,1,0:T(8,128)(2,1)} %bitcast.15, bf16[64,512,128]{2,1,0:T(8,128)(2,1)} %bitcast.16, ...), custom_call_target="tpu_custom_call", output_to_operand_aliasing={{0}: (6, {}), {1}: (7, {})} | custom-call | bytes 12582912 | tf_op jit(solution)/shard_map/prepare/pallas_call | solution.py:150
  41.4 1.8 %collective-permute-start.21 = (bf16[128,1024]{1,0:T(8,128)(2,1)S(1)}, bf16[128,1024]{1,0:T(8,128)(2,1)S(1)}, u32[]{:S(2)}, u32[]{:S(2)}) collective-permute-start(bf16[128,1024]{1,0:T(8,128)(2,1)S(1)} %collective-permute-done.17.refs_2_), channel_id=1, source_target_pairs={{0,8},{2,10},{8,16},{10,18},{16,24},{18,26},{24,28},{26,30},{28,20... | collective-permute-start | bytes 786440 | tf_op jit(solution)/shard_map/ppermute | solution.py:79
  43.7 5.9 %collective-permute-done.21.refs_6_ = bf16[128,1024]{1,0:T(8,128)(2,1)S(1)} collective-permute-done((bf16[128,1024]{1,0:T(8,128)(2,1)S(1)}, bf16[128,1024]{1,0:T(8,128)(2,1)S(1)}, u32[]{:S(2)}, u32[]{:S(2)}) %collective-permute-start.21) | collective-permute-done | bytes 262176 | tf_op jit(solution)/shard_map/ppermute | solution.py:79
  49.6 1.4 collective-permute-done.23.refs_8_
  51.3 0.8 collective-permute-start.11
  52.1 1.3 collective-permute-start.13
  53.5 3.8 %collective-permute-done.11.refs_12_ = bf16[128,512]{1,0:T(8,128)(2,1)S(1)} collective-permute-done((bf16[128,512]{1,0:T(8,128)(2,1)S(1)}, bf16[128,512]{1,0:T(8,128)(2,1)S(1)}, u32[]{:S(2)}, u32[]{:S(2)}) %collective-permute-start.11) | collective-permute-done | bytes 131104 | tf_op jit(solution)/shard_map/ppermute | solution.py:79
  57.3 1.6 collective-permute-start.25
  59.4 1.3 fusion.2.refs_16_
  60.7 1.6 collective-permute-start.32
  62.3 0.5 collective-permute-start.34
  63.0 0.5 copy-done.47
  63.5 4.4 %project.2.queries_hbm.refs_2_ = bf16[2,2,128,512]{3,2,1,0:T(8,128)(2,1)} custom-call(s32[16]{0:T(128)} %dynamic-slice_bitcast_fusion.order_ref, bf16[128,512]{1,0:T(8,128)(2,1)} %copy-done.19, bf16[128,512]{1,0:T(8,128)(2,1)} %copy-done.37, bf16[128,512]{1,0:T(8,128)(2,1)} %copy-done.33, bf16[128,512]{1,0:T(8,128)(2,1)} %copy-done.38, ...), custom_call_target="tpu_custom_call" | custom-call | flops 536870912 | bytes 2097152 | tf_op jit(solution)/shard_map/project/pallas_call | solution.py:233
  69.2 0.6 collective-permute-start.18
  69.8 1.8 %collective-permute-done.32.refs_8_ = bf16[1024,128]{1,0:T(8,128)(2,1)S(1)} collective-permute-done((bf16[1024,128]{1,0:T(8,128)(2,1)S(1)}, bf16[1024,128]{1,0:T(8,128)(2,1)S(1)}, u32[]{:S(2)}, u32[]{:S(2)}) %collective-permute-start.32) | collective-permute-done | bytes 262176 | tf_op jit(solution)/shard_map/ppermute | solution.py:79
  71.6 2.1 %collective-permute-done.34.refs_10_ = bf16[1024,128]{1,0:T(8,128)(2,1)S(1)} collective-permute-done((bf16[1024,128]{1,0:T(8,128)(2,1)S(1)}, bf16[1024,128]{1,0:T(8,128)(2,1)S(1)}, u32[]{:S(2)}, u32[]{:S(2)}) %collective-permute-start.34) | collective-permute-done | bytes 262176 | tf_op jit(solution)/shard_map/ppermute | solution.py:79
  73.7 1.6 collective-permute-start.36
  75.3 3.2 %collective-permute-done.29.refs_14_ = bf16[128,1024]{1,0:T(8,128)(2,1)S(1)} collective-permute-done((bf16[128,1024]{1,0:T(8,128)(2,1)S(1)}, bf16[128,1024]{1,0:T(8,128)(2,1)S(1)}, u32[]{:S(2)}, u32[]{:S(2)}) %collective-permute-start.29) | collective-permute-done | bytes 262176 | tf_op jit(solution)/shard_map/ppermute | solution.py:79
  79.0 13.7 %attend.4 = (f32[2,80,512]{2,1,0:T(8,128)}, s32[1]{0:T(128)}) custom-call(s32[1]{0:T(128)} %dynamic_slice.7.length_ref, s32[1]{0:T(128)S(6)} %copy.18.span_ref, s32[1]{0:T(128)} %bitcast.2.tile_ref, bf16[4,8192,128]{2,1,0:T(8,128)(2,1)} %get-tuple-element.38.keys_hbm, bf16[4,80,8192]{2,1,0:T(8,128)(2,1)} %get-tuple-element.39.values_hbm, ...), custom_call_target="tpu_custom_call" | custom-call | flops 17179869184 | bytes 8388608 | tf_op jit(solution)/shard_map/attend/pallas_call | solution.py:392
  92.8 0.5 collective-permute-start.24
  93.4 0.5 collective-permute-start.28
  95.4 1.6 collective-permute-start.40
  97.0 0.7 copy-done.32
  98.2 6.4 %project.3 = (bf16[2,2,128,512]{3,2,1,0:T(8,128)(2,1)}, bf16[4,256,128]{2,1,0:T(8,128)(2,1)}, bf16[4,80,256]{2,1,0:T(8,128)(2,1)}) custom-call(s32[16]{0:T(128)} %dynamic-slice_bitcast_fusion.order_ref, bf16[128,1024]{1,0:T(8,128)(2,1)} %copy-done, bf16[128,1024]{1,0:T(8,128)(2,1)} %copy-done.27, bf16[128,1024]{1,0:T(8,128)(2,1)} %copy-done.20, ...), custom_call_target="tpu_custom_call" | custom-call | flops 1073741824 | bytes 4194304 | tf_op jit(solution)/shard_map/project/pallas_call | solution.py:233
  104.5 13.8 %attend.5 = (f32[2,80,512]{2,1,0:T(8,128)}, s32[1]{0:T(128)}) custom-call(s32[1]{0:T(128)} %get-tuple-element.40.length_ref, s32[1]{0:T(128)S(6)} %copy.18.span_ref, s32[1]{0:T(128)} %bitcast.2.tile_ref, bf16[4,8192,128]{2,1,0:T(8,128)(2,1)} %get-tuple-element.38.keys_hbm, bf16[4,80,8192]{2,1,0:T(8,128)(2,1)} %get-tuple-element.39.values_hbm, ...), custom_call_target="tpu_custom_call" | custom-call | flops 17179869184 | bytes 8388608 | tf_op jit(solution)/shard_map/attend/pallas_call | solution.py:392
  118.4 1.8 %collective-permute-start.44 = (bf16[1024,128]{1,0:T(8,128)(2,1)S(1)}, bf16[1024,128]{1,0:T(8,128)(2,1)S(1)}, u32[]{:S(2)}, u32[]{:S(2)}) collective-permute-start(bf16[1024,128]{1,0:T(8,128)(2,1)S(1)} %collective-permute-done.40.refs_16_), channel_id=1, source_target_pairs={{0,8},{2,10},{8,16},{10,18},{16,24},{18,26},{24,28},{26,30},{28,20... | collective-permute-start | bytes 786440 | tf_op jit(solution)/shard_map/ppermute | solution.py:79
  120.2 13.8 %attend.6 = (f32[2,80,512]{2,1,0:T(8,128)}, s32[1]{0:T(128)}) custom-call(s32[1]{0:T(128)} %get-tuple-element.49.length_ref, s32[1]{0:T(128)S(6)} %copy.18.span_ref, s32[1]{0:T(128)} %bitcast.1.tile_ref, bf16[4,8192,128]{2,1,0:T(8,128)(2,1)} %get-tuple-element.38.keys_hbm, bf16[4,80,8192]{2,1,0:T(8,128)(2,1)} %get-tuple-element.39.values_hbm, ...), custom_call_target="tpu_custom_call" | custom-call | flops 17179869184 | bytes 8388608 | tf_op jit(solution)/shard_map/attend/pallas_call | solution.py:392
  134.2 0.5 collective-permute-start.41
  137.5 5.8 %finish.2 = (bf16[16,128,128]{2,1,0:T(8,128)(2,1)}, s32[1]{0:T(128)}) custom-call(s32[1]{0:T(128)S(6)} %copy.18.span_ref, s32[1]{0:T(128)} %bitcast.2.tile_ref, f32[2,80,512]{2,1,0:T(8,128)} %get-tuple-element.46.refs_0_, f32[2,80,512]{2,1,0:T(8,128)} %get-tuple-element.52.refs_1_, bf16[2,2,128,512]{3,2,1,0:T(8,128)(2,1)} %project.2.queries_hbm.refs_2_, ...), custom_call_target="tpu_custom_call" | custom-call | flops 536870912 | bytes 4194304 | tf_op jit(solution)/shard_map/finish/pallas_call | solution.py:504
  144.0 1.6 collective-permute-start.46
  146.3 13.1 %attend.7 = (f32[2,80,512]{2,1,0:T(8,128)}, s32[1]{0:T(128)}) custom-call(s32[1]{0:T(128)S(6)} %add.33.length_ref, s32[1]{0:T(128)S(6)} %copy.18.span_ref, s32[1]{0:T(128)} %bitcast.1.tile_ref, bf16[4,8192,128]{2,1,0:T(8,128)(2,1)} %get-tuple-element.38.keys_hbm, bf16[4,80,8192]{2,1,0:T(8,128)(2,1)} %get-tuple-element.39.values_hbm, ...), custom_call_target="tpu_custom_call" | custom-call | flops 17179869184 | bytes 8388608 | tf_op jit(solution)/shard_map/attend/pallas_call | solution.py:392
  159.4 5.8 %finish.3 = (bf16[16,128,128]{2,1,0:T(8,128)(2,1)}, s32[1]{0:T(128)}) custom-call(s32[1]{0:T(128)S(6)} %copy.18.span_ref, s32[1]{0:T(128)} %bitcast.1.tile_ref, f32[2,80,512]{2,1,0:T(8,128)} %get-tuple-element.50.refs_0_, f32[2,80,512]{2,1,0:T(8,128)} %get-tuple-element.64.refs_1_, bf16[2,2,128,512]{3,2,1,0:T(8,128)(2,1)} %project.2.queries_hbm.refs_2_, ...), custom_call_target="tpu_custom_call" | custom-call | flops 536870912 | bytes 4194304 | tf_op jit(solution)/shard_map/finish/pallas_call | solution.py:504
  165.3 0.8 copy-done.18
  166.0 2.2 %combine.1 = bf16[128,2048]{1,0:T(8,128)(2,1)} custom-call(s32[16]{0:T(128)} %dynamic-slice_bitcast_fusion.order_ref, bf16[16,128,128]{2,1,0:T(8,128)(2,1)} %get-tuple-element.65.own_ref, bf16[16,128,128]{2,1,0:T(8,128)(2,1)} %copy-done.18), custom_call_target="tpu_custom_call" | custom-call | tf_op jit(solution)/shard_map/combine/pallas_call | solution.py:541
  (167 shorter events, 8.3 us)
Async XLA Ops:
  1.0 8.1 %collective-permute-start.1 = (bf16[128,512]{1,0:T(8,128)(2,1)S(1)}, bf16[128,512]{1,0:T(8,128)(2,1)S(1)}, u32[]{:S(2)}, u32[]{:S(2)}) collective-permute-start(bf16[128,512]{1,0:T(8,128)(2,1)S(1)} %get-tuple-element.70.refs_0_), channel_id=1, source_target_pairs={{0,8},{2,10},{8,16},{10,18},{16,24},{18,26},{24,28},{26,30},{28,20... | collective-permute-start | bytes 393224 | tf_op jit(solution)/shard_map/ppermute | solution.py:79
  5.1 63.5 %copy-start = (bf16[128,1024]{1,0:T(8,128)(2,1)}, bf16[128,1024]{1,0:T(8,128)(2,1)S(1)}, u32[]{:S(2)}) copy-start(bf16[128,1024]{1,0:T(8,128)(2,1)S(1)} %pad_maximum_fusion.1.refs_0_) | copy-start | bytes 786436
  5.1 25.2 %collective-permute-start.17 = (bf16[128,1024]{1,0:T(8,128)(2,1)S(1)}, bf16[128,1024]{1,0:T(8,128)(2,1)S(1)}, u32[]{:S(2)}, u32[]{:S(2)}) collective-permute-start(bf16[128,1024]{1,0:T(8,128)(2,1)S(1)} %pad_maximum_fusion.1.refs_0_), channel_id=1, source_target_pairs={{0,8},{2,10},{8,16},{10,18},{16,24},{18,26},{24,28},{26,30},{28,20... | collective-permute-start | bytes 786440 | tf_op jit(solution)/shard_map/ppermute | solution.py:79
  6.7 24.1 %collective-permute-start.19 = (bf16[128,1024]{1,0:T(8,128)(2,1)S(1)}, bf16[128,1024]{1,0:T(8,128)(2,1)S(1)}, u32[]{:S(2)}, u32[]{:S(2)}) collective-permute-start(bf16[128,1024]{1,0:T(8,128)(2,1)S(1)} %pad_maximum_fusion.1.refs_0_), channel_id=1, source_target_pairs={{8,0},{10,2},{16,8},{18,10},{24,16},{26,18},{28,24},{30,26},{20,28... | collective-permute-start | bytes 786440 | tf_op jit(solution)/shard_map/ppermute | solution.py:79
  7.1 23.0 %collective-permute-start.3 = (bf16[128,512]{1,0:T(8,128)(2,1)S(1)}, bf16[128,512]{1,0:T(8,128)(2,1)S(1)}, u32[]{:S(2)}, u32[]{:S(2)}) collective-permute-start(bf16[128,512]{1,0:T(8,128)(2,1)S(1)} %get-tuple-element.70.refs_0_), channel_id=1, source_target_pairs={{8,0},{10,2},{16,8},{18,10},{24,16},{26,18},{28,24},{30,26},{20,28... | collective-permute-start | bytes 393224 | tf_op jit(solution)/shard_map/ppermute | solution.py:79
  7.2 36.1 %collective-permute-start.15 = (bf16[128,2048]{1,0:T(8,128)(2,1)}, bf16[128,2048]{1,0:T(8,128)(2,1)S(1)}, u32[]{:S(2)}, u32[]{:S(2)}) collective-permute-start(bf16[128,2048]{1,0:T(8,128)(2,1)} %param.10), channel_id=1, source_target_pairs={{0,1},{1,0},{2,3},{3,2},{4,5},{5,4},{6,7},{7,6},{8,9},{9,8},{10,11... | collective-permute-start | bytes 1572872 | tf_op jit(solution)/shard_map/ppermute | solution.py:578
  9.1 6.9 %collective-permute-start.5 = (bf16[128,512]{1,0:T(8,128)(2,1)S(1)}, bf16[128,512]{1,0:T(8,128)(2,1)S(1)}, u32[]{:S(2)}, u32[]{:S(2)}) collective-permute-start(bf16[128,512]{1,0:T(8,128)(2,1)S(1)} %collective-permute-done.1.refs_2_), channel_id=1, source_target_pairs={{0,8},{2,10},{8,16},{10,18},{16,24},{18,26},{24,28},{26,30},{28,20... | collective-permute-start | bytes 393224 | tf_op jit(solution)/shard_map/ppermute | solution.py:79
  16.0 25.4 %collective-permute-start.9 = (bf16[128,512]{1,0:T(8,128)(2,1)S(1)}, bf16[128,512]{1,0:T(8,128)(2,1)S(1)}, u32[]{:S(2)}, u32[]{:S(2)}) collective-permute-start(bf16[128,512]{1,0:T(8,128)(2,1)S(1)} %collective-permute-done.5.refs_6_), channel_id=1, source_target_pairs={{0,8},{2,10},{8,16},{10,18},{16,24},{18,26},{24,28},{26,30},{28,20... | collective-permute-start | bytes 393224 | tf_op jit(solution)/shard_map/ppermute | solution.py:79
  30.2 21.1 %collective-permute-start = (bf16[128,512]{1,0:T(8,128)(2,1)S(1)}, bf16[128,512]{1,0:T(8,128)(2,1)S(1)}, u32[]{:S(2)}, u32[]{:S(2)}) collective-permute-start(bf16[128,512]{1,0:T(8,128)(2,1)S(1)} %get-tuple-element.70.refs_0_), channel_id=1, source_target_pairs={{0,2},{2,0},{4,6},{6,4},{8,10},{10,8},{12,14},{14,12},{16,18},{18,... | collective-permute-start | bytes 393224 | tf_op jit(solution)/shard_map/ppermute | solution.py:79
  30.3 21.8 %collective-permute-start.2 = (bf16[128,512]{1,0:T(8,128)(2,1)S(1)}, bf16[128,512]{1,0:T(8,128)(2,1)S(1)}, u32[]{:S(2)}, u32[]{:S(2)}) collective-permute-start(bf16[128,512]{1,0:T(8,128)(2,1)S(1)} %collective-permute-done.1.refs_2_), channel_id=1, source_target_pairs={{0,2},{2,0},{4,6},{6,4},{8,10},{10,8},{12,14},{14,12},{16,18},{18,... | collective-permute-start | bytes 393224 | tf_op jit(solution)/shard_map/ppermute | solution.py:79
  30.8 12.8 %collective-permute-start.7 = (bf16[128,512]{1,0:T(8,128)(2,1)S(1)}, bf16[128,512]{1,0:T(8,128)(2,1)S(1)}, u32[]{:S(2)}, u32[]{:S(2)}) collective-permute-start(bf16[128,512]{1,0:T(8,128)(2,1)S(1)} %collective-permute-done.3.refs_4_), channel_id=1, source_target_pairs={{8,0},{10,2},{16,8},{18,10},{24,16},{26,18},{28,24},{30,26},{20,28... | collective-permute-start | bytes 393224 | tf_op jit(solution)/shard_map/ppermute | solution.py:79
  41.4 8.2 %collective-permute-start.21 = (bf16[128,1024]{1,0:T(8,128)(2,1)S(1)}, bf16[128,1024]{1,0:T(8,128)(2,1)S(1)}, u32[]{:S(2)}, u32[]{:S(2)}) collective-permute-start(bf16[128,1024]{1,0:T(8,128)(2,1)S(1)} %collective-permute-done.17.refs_2_), channel_id=1, source_target_pairs={{0,8},{2,10},{8,16},{10,18},{16,24},{18,26},{24,28},{26,30},{28,20... | collective-permute-start | bytes 786440 | tf_op jit(solution)/shard_map/ppermute | solution.py:79
  43.2 7.7 %collective-permute-start.23 = (bf16[128,1024]{1,0:T(8,128)(2,1)S(1)}, bf16[128,1024]{1,0:T(8,128)(2,1)S(1)}, u32[]{:S(2)}, u32[]{:S(2)}) collective-permute-start(bf16[128,1024]{1,0:T(8,128)(2,1)S(1)} %collective-permute-done.19.refs_4_), channel_id=1, source_target_pairs={{8,0},{10,2},{16,8},{18,10},{24,16},{26,18},{28,24},{30,26},{20,28... | collective-permute-start | bytes 786440 | tf_op jit(solution)/shard_map/ppermute | solution.py:79
  43.6 9.8 %collective-permute-start.4 = (bf16[128,512]{1,0:T(8,128)(2,1)S(1)}, bf16[128,512]{1,0:T(8,128)(2,1)S(1)}, u32[]{:S(2)}, u32[]{:S(2)}) collective-permute-start(bf16[128,512]{1,0:T(8,128)(2,1)S(1)} %collective-permute-done.3.refs_4_), channel_id=1, source_target_pairs={{0,2},{2,0},{4,6},{6,4},{8,10},{10,8},{12,14},{14,12},{16,18},{18,... | collective-permute-start | bytes 393224 | tf_op jit(solution)/shard_map/ppermute | solution.py:79
  49.6 7.7 %collective-permute-start.6 = (bf16[128,512]{1,0:T(8,128)(2,1)S(1)}, bf16[128,512]{1,0:T(8,128)(2,1)S(1)}, u32[]{:S(2)}, u32[]{:S(2)}) collective-permute-start(bf16[128,512]{1,0:T(8,128)(2,1)S(1)} %collective-permute-done.5.refs_6_), channel_id=1, source_target_pairs={{0,2},{2,0},{4,6},{6,4},{8,10},{10,8},{12,14},{14,12},{16,18},{18,... | collective-permute-start | bytes 393224 | tf_op jit(solution)/shard_map/ppermute | solution.py:79
  51.0 7.9 %collective-permute-start.8 = (bf16[128,512]{1,0:T(8,128)(2,1)S(1)}, bf16[128,512]{1,0:T(8,128)(2,1)S(1)}, u32[]{:S(2)}, u32[]{:S(2)}) collective-permute-start(bf16[128,512]{1,0:T(8,128)(2,1)S(1)} %collective-permute-done.7.refs_8_), channel_id=1, source_target_pairs={{0,2},{2,0},{4,6},{6,4},{8,10},{10,8},{12,14},{14,12},{16,18},{18,... | collective-permute-start | bytes 393224 | tf_op jit(solution)/shard_map/ppermute | solution.py:79
  51.3 6.0 %collective-permute-start.11 = (bf16[128,512]{1,0:T(8,128)(2,1)S(1)}, bf16[128,512]{1,0:T(8,128)(2,1)S(1)}, u32[]{:S(2)}, u32[]{:S(2)}) collective-permute-start(bf16[128,512]{1,0:T(8,128)(2,1)S(1)} %collective-permute-done.7.refs_8_), channel_id=1, source_target_pairs={{8,0},{10,2},{16,8},{18,10},{24,16},{26,18},{28,24},{30,26},{20,28... | collective-permute-start | bytes 393224 | tf_op jit(solution)/shard_map/ppermute | solution.py:79
  52.1 7.3 %collective-permute-start.13 = (bf16[128,512]{1,0:T(8,128)(2,1)S(1)}, bf16[128,512]{1,0:T(8,128)(2,1)S(1)}, u32[]{:S(2)}, u32[]{:S(2)}) collective-permute-start(bf16[128,512]{1,0:T(8,128)(2,1)S(1)} %collective-permute-done.9.refs_10_), channel_id=1, source_target_pairs={{0,8},{2,10},{8,16},{10,18},{16,24},{18,26},{24,28},{26,30},{28,20... | collective-permute-start | bytes 393224 | tf_op jit(solution)/shard_map/ppermute | solution.py:79
  53.4 7.3 %collective-permute-start.10 = (bf16[128,512]{1,0:T(8,128)(2,1)S(1)}, bf16[128,512]{1,0:T(8,128)(2,1)S(1)}, u32[]{:S(2)}, u32[]{:S(2)}) collective-permute-start(bf16[128,512]{1,0:T(8,128)(2,1)S(1)} %collective-permute-done.9.refs_10_), channel_id=1, source_target_pairs={{0,2},{2,0},{4,6},{6,4},{8,10},{10,8},{12,14},{14,12},{16,18},{18,... | collective-permute-start | bytes 393224 | tf_op jit(solution)/shard_map/ppermute | solution.py:79
  57.3 5.1 %collective-permute-start.12 = (bf16[128,512]{1,0:T(8,128)(2,1)S(1)}, bf16[128,512]{1,0:T(8,128)(2,1)S(1)}, u32[]{:S(2)}, u32[]{:S(2)}) collective-permute-start(bf16[128,512]{1,0:T(8,128)(2,1)S(1)} %collective-permute-done.11.refs_12_), channel_id=1, source_target_pairs={{0,2},{2,0},{4,6},{6,4},{8,10},{10,8},{12,14},{14,12},{16,18},{18,... | collective-permute-start | bytes 393224 | tf_op jit(solution)/shard_map/ppermute | solution.py:79
  57.3 10.6 %collective-permute-start.25 = (bf16[128,1024]{1,0:T(8,128)(2,1)S(1)}, bf16[128,1024]{1,0:T(8,128)(2,1)S(1)}, u32[]{:S(2)}, u32[]{:S(2)}) collective-permute-start(bf16[128,1024]{1,0:T(8,128)(2,1)S(1)} %collective-permute-done.21.refs_6_), channel_id=1, source_target_pairs={{0,8},{2,10},{8,16},{10,18},{16,24},{18,26},{24,28},{26,30},{28,20... | collective-permute-start | bytes 786440 | tf_op jit(solution)/shard_map/ppermute | solution.py:79
  58.9 9.2 %collective-permute-start.27 = (bf16[128,1024]{1,0:T(8,128)(2,1)S(1)}, bf16[128,1024]{1,0:T(8,128)(2,1)S(1)}, u32[]{:S(2)}, u32[]{:S(2)}) collective-permute-start(bf16[128,1024]{1,0:T(8,128)(2,1)S(1)} %collective-permute-done.23.refs_8_), channel_id=1, source_target_pairs={{8,0},{10,2},{16,8},{18,10},{24,16},{26,18},{28,24},{30,26},{20,28... | collective-permute-start | bytes 786440 | tf_op jit(solution)/shard_map/ppermute | solution.py:79
  59.4 3.5 %collective-permute-start.14 = (bf16[128,512]{1,0:T(8,128)(2,1)S(1)}, bf16[128,512]{1,0:T(8,128)(2,1)S(1)}, u32[]{:S(2)}, u32[]{:S(2)}) collective-permute-start(bf16[128,512]{1,0:T(8,128)(2,1)S(1)} %collective-permute-done.13.refs_14_), channel_id=1, source_target_pairs={{0,2},{2,0},{4,6},{6,4},{8,10},{10,8},{12,14},{14,12},{16,18},{18,... | collective-permute-start | bytes 393224 | tf_op jit(solution)/shard_map/ppermute | solution.py:79
  60.7 10.9 %collective-permute-start.32 = (bf16[1024,128]{1,0:T(8,128)(2,1)S(1)}, bf16[1024,128]{1,0:T(8,128)(2,1)S(1)}, u32[]{:S(2)}, u32[]{:S(2)}) collective-permute-start(bf16[1024,128]{1,0:T(8,128)(2,1)S(1)} %copy-done.1), channel_id=1, source_target_pairs={{0,8},{2,10},{8,16},{10,18},{16,24},{18,26},{24,28},{26,30},{28,20... | collective-permute-start | bytes 786440 | tf_op jit(solution)/shard_map/ppermute | solution.py:79
  62.3 11.4 %collective-permute-start.34 = (bf16[1024,128]{1,0:T(8,128)(2,1)S(1)}, bf16[1024,128]{1,0:T(8,128)(2,1)S(1)}, u32[]{:S(2)}, u32[]{:S(2)}) collective-permute-start(bf16[1024,128]{1,0:T(8,128)(2,1)S(1)} %copy-done.1), channel_id=1, source_target_pairs={{8,0},{10,2},{16,8},{18,10},{24,16},{26,18},{28,24},{30,26},{20,28... | collective-permute-start | bytes 786440 | tf_op jit(solution)/shard_map/ppermute | solution.py:79
  68.1 10.4 %collective-permute-start.29 = (bf16[128,1024]{1,0:T(8,128)(2,1)S(1)}, bf16[128,1024]{1,0:T(8,128)(2,1)S(1)}, u32[]{:S(2)}, u32[]{:S(2)}) collective-permute-start(bf16[128,1024]{1,0:T(8,128)(2,1)S(1)} %collective-permute-done.27.refs_12_), channel_id=1, source_target_pairs={{8,0},{10,2},{16,8},{18,10},{24,16},{26,18},{28,24},{30,26},{20,28... | collective-permute-start | bytes 786440 | tf_op jit(solution)/shard_map/ppermute | solution.py:79
  68.5 24.1 %collective-permute-start.16 = (bf16[128,1024]{1,0:T(8,128)(2,1)S(1)}, bf16[128,1024]{1,0:T(8,128)(2,1)S(1)}, u32[]{:S(2)}, u32[]{:S(2)}) collective-permute-start(bf16[128,1024]{1,0:T(8,128)(2,1)S(1)} %pad_maximum_fusion.1.refs_0_), channel_id=1, source_target_pairs={{0,2},{2,0},{4,6},{6,4},{8,10},{10,8},{12,14},{14,12},{16,18},{18,... | collective-permute-start | bytes 786440 | tf_op jit(solution)/shard_map/ppermute | solution.py:79
  69.2 23.5 %collective-permute-start.18 = (bf16[128,1024]{1,0:T(8,128)(2,1)S(1)}, bf16[128,1024]{1,0:T(8,128)(2,1)S(1)}, u32[]{:S(2)}, u32[]{:S(2)}) collective-permute-start(bf16[128,1024]{1,0:T(8,128)(2,1)S(1)} %collective-permute-done.17.refs_2_), channel_id=1, source_target_pairs={{0,2},{2,0},{4,6},{6,4},{8,10},{10,8},{12,14},{14,12},{16,18},{18,... | collective-permute-start | bytes 786440 | tf_op jit(solution)/shard_map/ppermute | solution.py:79
  71.6 21.7 %collective-permute-start.20 = (bf16[128,1024]{1,0:T(8,128)(2,1)S(1)}, bf16[128,1024]{1,0:T(8,128)(2,1)}, u32[]{:S(2)}, u32[]{:S(2)}) collective-permute-start(bf16[128,1024]{1,0:T(8,128)(2,1)S(1)} %collective-permute-done.19.refs_4_), channel_id=1, source_target_pairs={{0,2},{2,0},{4,6},{6,4},{8,10},{10,8},{12,14},{14,12},{16,18},{18,... | collective-permute-start | bytes 786440 | tf_op jit(solution)/shard_map/ppermute | solution.py:79
  73.7 19.7 %collective-permute-start.36 = (bf16[1024,128]{1,0:T(8,128)(2,1)S(1)}, bf16[1024,128]{1,0:T(8,128)(2,1)S(1)}, u32[]{:S(2)}, u32[]{:S(2)}) collective-permute-start(bf16[1024,128]{1,0:T(8,128)(2,1)S(1)} %collective-permute-done.32.refs_8_), channel_id=1, source_target_pairs={{0,8},{2,10},{8,16},{10,18},{16,24},{18,26},{24,28},{26,30},{28,20... | collective-permute-start | bytes 786440 | tf_op jit(solution)/shard_map/ppermute | solution.py:79
  78.5 15.4 %collective-permute-start.38 = (bf16[1024,128]{1,0:T(8,128)(2,1)S(1)}, bf16[1024,128]{1,0:T(8,128)(2,1)S(1)}, u32[]{:S(2)}, u32[]{:S(2)}) collective-permute-start(bf16[1024,128]{1,0:T(8,128)(2,1)S(1)} %collective-permute-done.34.refs_10_), channel_id=1, source_target_pairs={{8,0},{10,2},{16,8},{18,10},{24,16},{26,18},{28,24},{30,26},{20,28... | collective-permute-start | bytes 786440 | tf_op jit(solution)/shard_map/ppermute | solution.py:79
  92.7 1.7 %collective-permute-start.22 = (bf16[128,1024]{1,0:T(8,128)(2,1)S(1)}, bf16[128,1024]{1,0:T(8,128)(2,1)}, u32[]{:S(2)}, u32[]{:S(2)}) collective-permute-start(bf16[128,1024]{1,0:T(8,128)(2,1)S(1)} %collective-permute-done.21.refs_6_), channel_id=1, source_target_pairs={{0,2},{2,0},{4,6},{6,4},{8,10},{10,8},{12,14},{14,12},{16,18},{18,... | collective-permute-start | bytes 786440 | tf_op jit(solution)/shard_map/ppermute | solution.py:79
  92.8 1.9 %collective-permute-start.24 = (bf16[128,1024]{1,0:T(8,128)(2,1)S(1)}, bf16[128,1024]{1,0:T(8,128)(2,1)S(1)}, u32[]{:S(2)}, u32[]{:S(2)}) collective-permute-start(bf16[128,1024]{1,0:T(8,128)(2,1)S(1)} %collective-permute-done.23.refs_8_), channel_id=1, source_target_pairs={{0,2},{2,0},{4,6},{6,4},{8,10},{10,8},{12,14},{14,12},{16,18},{18,... | collective-permute-start | bytes 786440 | tf_op jit(solution)/shard_map/ppermute | solution.py:79
  93.3 1.7 %collective-permute-start.26 = (bf16[128,1024]{1,0:T(8,128)(2,1)S(1)}, bf16[128,1024]{1,0:T(8,128)(2,1)S(1)}, u32[]{:S(2)}, u32[]{:S(2)}) collective-permute-start(bf16[128,1024]{1,0:T(8,128)(2,1)S(1)} %collective-permute-done.25.refs_10_), channel_id=1, source_target_pairs={{0,2},{2,0},{4,6},{6,4},{8,10},{10,8},{12,14},{14,12},{16,18},{18,... | collective-permute-start | bytes 786440 | tf_op jit(solution)/shard_map/ppermute | solution.py:79
  93.4 2.0 %collective-permute-start.28 = (bf16[128,1024]{1,0:T(8,128)(2,1)S(1)}, bf16[128,1024]{1,0:T(8,128)(2,1)S(1)}, u32[]{:S(2)}, u32[]{:S(2)}) collective-permute-start(bf16[128,1024]{1,0:T(8,128)(2,1)S(1)} %collective-permute-done.27.refs_12_), channel_id=1, source_target_pairs={{0,2},{2,0},{4,6},{6,4},{8,10},{10,8},{12,14},{14,12},{16,18},{18,... | collective-permute-start | bytes 786440 | tf_op jit(solution)/shard_map/ppermute | solution.py:79
  93.9 3.1 %collective-permute-start.30 = (bf16[128,1024]{1,0:T(8,128)(2,1)S(1)}, bf16[128,1024]{1,0:T(8,128)(2,1)S(1)}, u32[]{:S(2)}, u32[]{:S(2)}) collective-permute-start(bf16[128,1024]{1,0:T(8,128)(2,1)S(1)} %collective-permute-done.29.refs_14_), channel_id=1, source_target_pairs={{0,2},{2,0},{4,6},{6,4},{8,10},{10,8},{12,14},{14,12},{16,18},{18,... | collective-permute-start | bytes 786440 | tf_op jit(solution)/shard_map/ppermute | solution.py:79
  94.4 39.7 %collective-permute-start.31 = (bf16[1024,128]{1,0:T(8,128)(2,1)S(1)}, bf16[1024,128]{1,0:T(8,128)(2,1)S(1)}, u32[]{:S(2)}, u32[]{:S(2)}) collective-permute-start(bf16[1024,128]{1,0:T(8,128)(2,1)S(1)} %copy-done.1), channel_id=1, source_target_pairs={{0,2},{2,0},{4,6},{6,4},{8,10},{10,8},{12,14},{14,12},{16,18},{18,... | collective-permute-start | bytes 786440 | tf_op jit(solution)/shard_map/ppermute | solution.py:79
  94.7 40.1 %collective-permute-start.33 = (bf16[1024,128]{1,0:T(8,128)(2,1)S(1)}, bf16[1024,128]{1,0:T(8,128)(2,1)S(1)}, u32[]{:S(2)}, u32[]{:S(2)}) collective-permute-start(bf16[1024,128]{1,0:T(8,128)(2,1)S(1)} %collective-permute-done.32.refs_8_), channel_id=1, source_target_pairs={{0,2},{2,0},{4,6},{6,4},{8,10},{10,8},{12,14},{14,12},{16,18},{18,... | collective-permute-start | bytes 786440 | tf_op jit(solution)/shard_map/ppermute | solution.py:79
  95.0 39.8 %collective-permute-start.35 = (bf16[1024,128]{1,0:T(8,128)(2,1)S(1)}, bf16[1024,128]{1,0:T(8,128)(2,1)S(1)}, u32[]{:S(2)}, u32[]{:S(2)}) collective-permute-start(bf16[1024,128]{1,0:T(8,128)(2,1)S(1)} %collective-permute-done.34.refs_10_), channel_id=1, source_target_pairs={{0,2},{2,0},{4,6},{6,4},{8,10},{10,8},{12,14},{14,12},{16,18},{18,... | collective-permute-start | bytes 786440 | tf_op jit(solution)/shard_map/ppermute | solution.py:79
  95.4 22.9 %collective-permute-start.40 = (bf16[1024,128]{1,0:T(8,128)(2,1)S(1)}, bf16[1024,128]{1,0:T(8,128)(2,1)S(1)}, u32[]{:S(2)}, u32[]{:S(2)}) collective-permute-start(bf16[1024,128]{1,0:T(8,128)(2,1)S(1)} %collective-permute-done.36.refs_12_), channel_id=1, source_target_pairs={{0,8},{2,10},{8,16},{10,18},{16,24},{18,26},{24,28},{26,30},{28,20... | collective-permute-start | bytes 786440 | tf_op jit(solution)/shard_map/ppermute | solution.py:79
  97.7 20.7 %collective-permute-start.42 = (bf16[1024,128]{1,0:T(8,128)(2,1)S(1)}, bf16[1024,128]{1,0:T(8,128)(2,1)S(1)}, u32[]{:S(2)}, u32[]{:S(2)}) collective-permute-start(bf16[1024,128]{1,0:T(8,128)(2,1)S(1)} %collective-permute-done.38.refs_14_), channel_id=1, source_target_pairs={{8,0},{10,2},{16,8},{18,10},{24,16},{26,18},{28,24},{30,26},{20,28... | collective-permute-start | bytes 786440 | tf_op jit(solution)/shard_map/ppermute | solution.py:79
  118.3 17.0 %collective-permute-start.37 = (bf16[1024,128]{1,0:T(8,128)(2,1)S(1)}, bf16[1024,128]{1,0:T(8,128)(2,1)S(1)}, u32[]{:S(2)}, u32[]{:S(2)}) collective-permute-start(bf16[1024,128]{1,0:T(8,128)(2,1)S(1)} %collective-permute-done.36.refs_12_), channel_id=1, source_target_pairs={{0,2},{2,0},{4,6},{6,4},{8,10},{10,8},{12,14},{14,12},{16,18},{18,... | collective-permute-start | bytes 786440 | tf_op jit(solution)/shard_map/ppermute | solution.py:79
  118.4 15.6 %collective-permute-start.44 = (bf16[1024,128]{1,0:T(8,128)(2,1)S(1)}, bf16[1024,128]{1,0:T(8,128)(2,1)S(1)}, u32[]{:S(2)}, u32[]{:S(2)}) collective-permute-start(bf16[1024,128]{1,0:T(8,128)(2,1)S(1)} %collective-permute-done.40.refs_16_), channel_id=1, source_target_pairs={{0,8},{2,10},{8,16},{10,18},{16,24},{18,26},{24,28},{26,30},{28,20... | collective-permute-start | bytes 786440 | tf_op jit(solution)/shard_map/ppermute | solution.py:79
  134.1 1.6 collective-permute-start.39
  134.2 1.9 %collective-permute-start.41 = (bf16[1024,128]{1,0:T(8,128)(2,1)S(1)}, bf16[1024,128]{1,0:T(8,128)(2,1)S(1)}, u32[]{:S(2)}, u32[]{:S(2)}) collective-permute-start(bf16[1024,128]{1,0:T(8,128)(2,1)S(1)} %collective-permute-done.40.refs_16_), channel_id=1, source_target_pairs={{0,2},{2,0},{4,6},{6,4},{8,10},{10,8},{12,14},{14,12},{16,18},{18,... | collective-permute-start | bytes 786440 | tf_op jit(solution)/shard_map/ppermute | solution.py:79
  134.7 1.7 %collective-permute-start.43 = (bf16[1024,128]{1,0:T(8,128)(2,1)S(1)}, bf16[1024,128]{1,0:T(8,128)(2,1)S(1)}, u32[]{:S(2)}, u32[]{:S(2)}) collective-permute-start(bf16[1024,128]{1,0:T(8,128)(2,1)S(1)} %collective-permute-done.42.refs_18_), channel_id=1, source_target_pairs={{0,2},{2,0},{4,6},{6,4},{8,10},{10,8},{12,14},{14,12},{16,18},{18,... | collective-permute-start | bytes 786440 | tf_op jit(solution)/shard_map/ppermute | solution.py:79
  134.8 2.0 %collective-permute-start.45 = (bf16[1024,128]{1,0:T(8,128)(2,1)S(1)}, bf16[1024,128]{1,0:T(8,128)(2,1)S(1)}, u32[]{:S(2)}, u32[]{:S(2)}) collective-permute-start(bf16[1024,128]{1,0:T(8,128)(2,1)S(1)} %collective-permute-done.44.refs_20_), channel_id=1, source_target_pairs={{0,2},{2,0},{4,6},{6,4},{8,10},{10,8},{12,14},{14,12},{16,18},{18,... | collective-permute-start | bytes 786440 | tf_op jit(solution)/shard_map/ppermute | solution.py:79
  144.0 21.2 %collective-permute-start.46 = (bf16[16,128,128]{2,1,0:T(8,128)(2,1)}, bf16[16,128,128]{2,1,0:T(8,128)(2,1)S(1)}, u32[]{:S(2)}, u32[]{:S(2)}) collective-permute-start(bf16[16,128,128]{2,1,0:T(8,128)(2,1)} %get-tuple-element.66), channel_id=1, source_target_pairs={{0,1},{1,0},{2,3},{3,2},{4,5},{5,4},{6,7},{7,6},{8,9},{9,8},{10,11... | collective-permute-start | bytes 1572872 | tf_op jit(solution)/shard_map/ppermute | solution.py:644
  (48 other events, 637.3 us)

commit v5 on v4

--- a/solution.py
+++ b/solution.py
@@ -68,12 +68,40 @@
     return lax.optimization_barrier((value,) + others)[0]
 
 
+def assemble_kernel(*refs):
+    *blocks, out_ref, sems = refs
+    rows = blocks[0].shape[0]
+    copies = [
+        pltpu.make_async_copy(block, out_ref.at[pl.ds(k * rows, rows)], sems.at[k])
+        for k, block in enumerate(blocks)
+    ]
+    for copy in copies:
+        copy.start()
+    for copy in copies:
+        copy.wait()
+
+
+def assemble(blocks):
+    rows, columns = blocks[0].shape
+    return pl.pallas_call(
+        assemble_kernel,
+        in_specs=[anywhere()] * len(blocks),
+        out_specs=vmem(),
+        out_shape=jax.ShapeDtypeStruct((len(blocks) * rows, columns), blocks[0].dtype),
+        scratch_shapes=[pltpu.SemaphoreType.DMA((len(blocks),))],
+        cost_estimate=pl.CostEstimate(
+            flops=0, bytes_accessed=4 * len(blocks) * rows * columns, transcendentals=0
+        ),
+        compiler_params=params(60),
+        name="assemble",
+    )(*blocks)
+
+
 class Ring:
     def __init__(self, shard, tables):
         self.ahead, self.back, self.swap, self.order = tables
-        self.length = len(self.order) // 2
         self.up = self.down = shard
-        self.blocks = [shard, self.move(shard, self.swap)]
+        self.blocks = [shard]
 
     def move(self, value, pairs):
         return lax.ppermute(value, "req", pairs)
@@ -82,22 +110,31 @@
         if others:
             self.up, self.down = lax.optimization_barrier((self.up, self.down) + others)[:2]
         self.up, self.down = self.move(self.up, self.ahead), self.move(self.down, self.back)
-        self.blocks += [
-            self.up,
-            self.move(self.up, self.swap),
-            self.down,
-            self.move(self.down, self.swap),
-        ]
+        self.blocks += [self.up, self.down]
 
     def last(self, upward, *others):
         if others:
             self.up, self.down = lax.optimization_barrier((self.up, self.down) + others)[:2]
         return self.move(self.up, self.ahead) if upward else self.move(self.down, self.back)
 
-    def all(self, end, *others):
+    def partner(self, *others):
+        blocks = self.blocks
         if others:
-            end = lax.optimization_barrier((end,) + others)[0]
-        return self.blocks + [end, self.move(end, self.swap)]
+            blocks = list(lax.optimization_barrier(tuple(blocks) + others)[: len(blocks)])
+        return self.move(assemble(blocks), self.swap)
+
+    def all(self, end, partner):
+        return self.blocks + [end, partner, self.move(end, self.swap)]
+
+
+def chunk_sources(refs):
+    *own, partner, end = refs
+    rows = own[0].shape[0]
+    sources = []
+    for k, block in enumerate(own):
+        at = partner.at[pl.ds(k * rows, rows)] if k < len(own) - 1 else end
+        sources += [block, at]
+    return sources
 
 
 def prepare_kernel(heads, page, width, pages_step, first_page, aliased, table_ref, length_ref, *refs):
@@ -188,11 +225,13 @@
     chunks = refs[:blocks]
     normed_hbm, cos_ref, sin_ref, query_ref = refs[blocks : blocks + 4]
     source, normed_ref, sems = refs[-3:]
-    rows = source.shape[0] // blocks
-    copies = [pltpu.make_async_copy(normed_hbm, normed_ref, sems.at[blocks])]
-    for k in range(blocks):
+    sources = chunks if blocks == 1 else chunk_sources(chunks)
+    count = len(sources)
+    rows = source.shape[0] // count
+    copies = [pltpu.make_async_copy(normed_hbm, normed_ref, sems.at[count])]
+    for k in range(count):
         start = pl.multiple_of(order_ref[k] * rows, rows)
-        copies.append(pltpu.make_async_copy(chunks[k], source.at[pl.ds(start, rows)], sems.at[k]))
+        copies.append(pltpu.make_async_copy(sources[k], source.at[pl.ds(start, rows)], sems.at[k]))
     for copy in copies:
         copy.start()
     cosine, sines = cos_ref[...], sin_ref[...]
@@ -238,7 +277,7 @@
         scratch_shapes=[
             pltpu.VMEM((width, columns), jnp.bfloat16),
             pltpu.VMEM((tokens, width), jnp.bfloat16),
-            pltpu.SemaphoreType.DMA((len(chunks) + 1,)),
+            pltpu.SemaphoreType.DMA((order.shape[0] + 1,)),
         ],
         cost_estimate=pl.CostEstimate(
             flops=2 * tokens * width * columns,
@@ -455,7 +494,9 @@
     token_ref[0] = q
     total = sum(heads)
     per_set = total // sets
-    columns = weight.shape[1] // max(blocks, 1)
+    chunks = chunk_sources(chunks) if blocks else []
+    count = len(chunks)
+    columns = weight.shape[1] // max(count, 1)
     copies = []
     for i in range(sets):
         copies.append((states_hbm[i], states.at[pl.ds(i * per_set, per_set)]))
@@ -469,7 +510,7 @@
         pltpu.make_async_copy(
             chunks[k], weight.at[:, pl.ds(k * columns, columns)], weight_sems.at[k]
         )
-        for k in range(blocks)
+        for k in range(count)
     ]
     for copy in copies + loads:
         copy.start()
@@ -486,7 +527,7 @@
         return
     for copy in loads:
         copy.wait()
-    for k in range(0, blocks, 2):
+    for k in range(0, count, 2):
         both = matmul(attended, weight[:, pl.ds(k * columns, 2 * columns)]).astype(jnp.bfloat16)
         out_ref[k] = both[:, :columns]
         out_ref[k + 1] = both[:, columns:]
@@ -499,8 +540,9 @@
     dim = rows - 16
     depth = total * group * dim
     blocks = len(chunks)
+    count = 2 * (blocks - 2) if blocks else 0
     columns = chunks[0].shape[1] if blocks else 128
-    out = (blocks, token_tile, columns) if blocks else (token_tile, depth)
+    out = (count, token_tile, columns) if blocks else (token_tile, depth)
     return pl.pallas_call(
         functools.partial(finish_kernel, heads, len(states), group, dim, blocks),
         in_specs=[smem()] * 2 + [anywhere()] * (len(states) + len(queries) + 2 + blocks),
@@ -514,13 +556,13 @@
             pltpu.VMEM((total,) + queries[0].shape[2:], jnp.bfloat16),
             pltpu.VMEM(new_keys.shape, jnp.bfloat16),
             pltpu.VMEM(new_values.shape, jnp.bfloat16),
-            pltpu.VMEM((depth if blocks else 16, max(blocks, 1) * columns), jnp.bfloat16),
+            pltpu.VMEM((depth if blocks else 16, max(count, 1) * columns), jnp.bfloat16),
             pltpu.SemaphoreType.DMA((len(states) + 2 + total,)),
-            pltpu.SemaphoreType.DMA((max(blocks, 1),)),
+            pltpu.SemaphoreType.DMA((max(count, 1),)),
         ],
         cost_estimate=pl.CostEstimate(
-            flops=2 * token_tile * depth * columns * blocks,
-            bytes_accessed=2 * depth * columns * blocks,
+            flops=2 * token_tile * depth * columns * count,
+            bytes_accessed=2 * depth * columns * count,
             transcendentals=0,
         ),
         compiler_params=params(60),
@@ -587,7 +629,9 @@
             state = prepare(kv_cache, table, length, part, parts, state)
             ring_first.step()
             ring_second.step(state[0])
-        first_chunks = ring_first.all(ring_first.last(True))
+        first_end = ring_first.last(True)
+        first_chunks = ring_first.all(first_end, ring_first.partner())
+        ring_out.step(first_end)
         keys, values = state
     else:
         order = jnp.zeros((1,), jnp.int32)
@@ -625,21 +669,21 @@
         summed = lax.psum_scatter(partial, "tp", scatter_dimension=0, tiled=True)
         return (residual_scale * summed.astype(jnp.float32)).astype(jnp.bfloat16)
     theirs, ours = (1 - rank).reshape(1), rank.reshape(1)
-    ring_out.step(ring_first.up)
     soon = project(normed, first_chunks, order, cosine, sines, early, 0, group, dim)[0]
     second_end = ring_second.last(False, soon)
     ring_out.step(soon)
     sent_first, token = attend_tile(theirs, soon, early, 0, length)
-    second_chunks = ring_second.all(second_end, sent_first)
+    second_chunks = ring_second.all(after(second_end, sent_first), ring_second.partner(sent_first))
     ring_out.step(sent_first)
+    kept_first, token = attend_tile(ours, soon, early, 0, token)
     late, new_keys, new_values = project(
         normed, second_chunks, order, cosine, sines, heads - early, heads, group, dim
     )
     queries += [soon, late]
+    out_end = ring_out.last(True, kept_first)
+    out_partner = ring_out.partner(kept_first)
     sent_second, token = attend_tile(theirs, late, heads - early, early, token)
-    out_end = ring_out.last(True, sent_second)
-    kept_first, token = attend_tile(ours, soon, early, 0, token)
-    out_chunks = ring_out.all(out_end, kept_first)
+    out_chunks = ring_out.all(after(out_end, sent_second), out_partner)
     sent, tile_token = finish_tile([sent_first, sent_second], theirs, out_chunks)
     received = lax.ppermute(sent, "tp", swap)
     token = token + (tile_token - theirs)

time: 168 us -> 157 us (0.935)
  the two profiles are of different devices: /device:TPU:0 before, /device:TPU:9 now
where the time goes in v5:
time: 157 us; the launch traced here: 156 us
  Pallas kernels  107 us (68%)
  starting transfers between devices  26.3 us (17%)
  local copies, waits for them, and re-layouts  10.1 us (6%)
  waiting for transfers between devices  6.03 us (4%)
  other arithmetic  4.08 us (3%)
  between operations  2.4 us (2%)
    pallas_call x4, Pallas kernels, attend(): pl.pallas_call(functools.partial(attend_kernel, heads, first_query, first...  54.3 us
    ppermute x27, starting transfers between devices, move(): return lax.ppermute(value, 'req', pairs)  22.5 us
    pallas_call x2, Pallas kernels, prepare(): pl.pallas_call(functools.partial(prepare_kernel, heads, page, width, page...  20.7 us
    pallas_call x2, Pallas kernels, finish(): pl.pallas_call(functools.partial(finish_kernel, heads, len(states), group...  11.7 us
    pallas_call x2, Pallas kernels, project(): pl.pallas_call(functools.partial(project_kernel, heads, new_heads, group,...  10.7 us
    pallas_call x3, Pallas kernels, assemble(): pl.pallas_call(assemble_kernel, in_specs=[anywhere()] * len(blocks), out_...  7.74 us
    unnamed x61, local copies, waits for them, and re-layouts  6.6 us
    ppermute x27, waiting for transfers between devices, move(): return lax.ppermute(value, 'req', pairs)  6.02 us
  transfers between devices with their start and end apart: 29, of which 4 were waited for; matrix products, arithmetic and copies ran while one was open for 5% of the time, Pallas kernels for 64%

profile of v5, /device:TPU:9, one launch (start us, length us, event | category | flops | bytes accessed | tf_op | source)
XLA Modules:
  0.0 156.2 jit_solution(2879652609085467812)
XLA Ops:
  0.0 1.0 fusion.3
  1.0 1.3 collective-permute-start
  2.5 0.9 copy.15
  3.4 2.0 %collective-permute-done.refs_1_ = bf16[128,512]{1,0:T(8,128)(2,1)S(1)} collective-permute-done((bf16[128,512]{1,0:T(8,128)(2,1)S(1)}, bf16[128,512]{1,0:T(8,128)(2,1)S(1)}, u32[]{:S(2)}, u32[]{:S(2)}) %collective-permute-start) | collective-permute-done | bytes 131104 | tf_op jit(solution)/shard_map/ppermute | solution.py:107
  5.4 1.3 collective-permute-start.2
  6.8 1.3 collective-permute-start.10
  8.3 1.2 collective-permute-start.9
  9.7 1.3 collective-permute-start.4
  11.0 1.2 dynamic_slice.7.length_ref
  12.2 10.4 %prepare.2 = (bf16[4,8192,128]{2,1,0:T(8,128)(2,1)}, bf16[4,80,8192]{2,1,0:T(8,128)(2,1)}) custom-call(s32[64]{0:T(128)} %bitcast.21, s32[1]{0:T(128)} %dynamic_slice.7.length_ref, bf16[64,512,128]{2,1,0:T(8,128)(2,1)} %bitcast.11, bf16[64,512,128]{2,1,0:T(8,128)(2,1)} %bitcast.12, bf16[64,512,128]{2,1,0:T(8,128)(2,1)} %bitcast.13, ...), custom_call_target="tpu_custom_call" | custom-call | bytes 12582912 | tf_op jit(solution)/shard_map/prepare/pallas_call | solution.py:187
  22.6 0.6 add_convert_fusion
  23.2 1.3 collective-permute-start.12
  24.9 1.3 collective-permute-start.6
  26.2 0.8 multiply_sine_fusion
  27.7 1.3 dynamic-slice_bitcast_fusion.order_ref
  29.0 10.4 %prepare.3 = (bf16[4,8192,128]{2,1,0:T(8,128)(2,1)}, bf16[4,80,8192]{2,1,0:T(8,128)(2,1)}) custom-call(s32[64]{0:T(128)} %bitcast.22, s32[1]{0:T(128)} %dynamic_slice.7.length_ref, bf16[64,512,128]{2,1,0:T(8,128)(2,1)} %bitcast.15, bf16[64,512,128]{2,1,0:T(8,128)(2,1)} %bitcast.16, ...), custom_call_target="tpu_custom_call", output_to_operand_aliasing={{0}: (6, {}), {1}: (7, {})} | custom-call | bytes 12582912 | tf_op jit(solution)/shard_map/prepare/pallas_call | solution.py:187
  39.4 0.6 copy-done.24
  40.0 2.3 %assemble.3 = bf16[896,512]{1,0:T(8,128)(2,1)} custom-call(bf16[128,512]{1,0:T(8,128)(2,1)} %copy-done.10, bf16[128,512]{1,0:T(8,128)(2,1)} %copy-done.19, bf16[128,512]{1,0:T(8,128)(2,1)} %copy-done.20, bf16[128,512]{1,0:T(8,128)(2,1)} %copy-done.21, bf16[128,512]{1,0:T(8,128)(2,1)} %copy-done.22, bf16[128,512]{1,0:T(8,128)(2,1)} %copy-done.23, ...), custom_call_target="tpu_custom_call" | custom-call | bytes 1835008 | tf_op jit(solution)/shard_map/assemble/pallas_call | solution.py:86
  42.3 5.1 %collective-permute-start.7 = (bf16[896,512]{1,0:T(8,128)(2,1)}, bf16[896,512]{1,0:T(8,128)(2,1)S(1)}, u32[]{:S(2)}, u32[]{:S(2)}) collective-permute-start(bf16[896,512]{1,0:T(8,128)(2,1)} %assemble.3), channel_id=1, source_target_pairs={{0,2},{2,0},{4,6},{6,4},{8,10},{10,8},{12,14},{14,12},{16,18},{18,... | collective-permute-start | bytes 2752520 | tf_op jit(solution)/shard_map/ppermute | solution.py:107
  47.5 1.3 collective-permute-start.14
  49.0 1.3 collective-permute-start.19
  50.3 0.9 collective-permute-start.8
  51.2 1.1 broadcast_select_fusion.1
  52.9 1.3 fusion.2.refs_10_
  54.2 0.9 copy-done.18
  55.1 4.4 %project.2.queries_hbm.refs_2_ = bf16[2,2,128,512]{3,2,1,0:T(8,128)(2,1)} custom-call(s32[16]{0:T(128)} %dynamic-slice_bitcast_fusion.order_ref, bf16[128,512]{1,0:T(8,128)(2,1)} %copy-done.10, bf16[128,512]{1,0:T(8,128)(2,1)} %copy-done.19, bf16[128,512]{1,0:T(8,128)(2,1)} %copy-done.20, bf16[128,512]{1,0:T(8,128)(2,1)} %copy-done.21, ...), custom_call_target="tpu_custom_call" | custom-call | flops 536870912 | bytes 2097152 | tf_op jit(solution)/shard_map/project/pallas_call | solution.py:272
  59.7 1.2 collective-permute-done.19.refs_1_.refs_7_
  61.0 1.0 collective-permute-done.20.refs_2_.refs_8_
  62.0 1.2 collective-permute-start.21
  63.4 13.7 %attend.4 = (f32[2,80,512]{2,1,0:T(8,128)}, s32[1]{0:T(128)}) custom-call(s32[1]{0:T(128)} %dynamic_slice.7.length_ref, s32[1]{0:T(128)S(6)} %copy.18.span_ref, s32[1]{0:T(128)} %bitcast.2.tile_ref, bf16[4,8192,128]{2,1,0:T(8,128)(2,1)} %get-tuple-element.52.keys_hbm, bf16[4,80,8192]{2,1,0:T(8,128)(2,1)} %get-tuple-element.53.values_hbm, ...), custom_call_target="tpu_custom_call" | custom-call | flops 17179869184 | bytes 8388608 | tf_op jit(solution)/shard_map/attend/pallas_call | solution.py:431
  77.2 2.7 %assemble.4 = bf16[896,1024]{1,0:T(8,128)(2,1)} custom-call(bf16[128,1024]{1,0:T(8,128)(2,1)} %copy-done.1, bf16[128,1024]{1,0:T(8,128)(2,1)} %copy-done.11, bf16[128,1024]{1,0:T(8,128)(2,1)} %copy-done.12, bf16[128,1024]{1,0:T(8,128)(2,1)} %copy-done.13, bf16[128,1024]{1,0:T(8,128)(2,1)} %copy-done.14, bf16[128,1024]{1,0:T(8,128)(2,1)} %copy-done.15, ...), custom_call_target="tpu_custom_call" | custom-call | bytes 3670016 | tf_op jit(solution)/shard_map/assemble/pallas_call | solution.py:86
  80.6 1.5 collective-permute-start.24
  82.0 13.7 %attend.5 = (f32[2,80,512]{2,1,0:T(8,128)}, s32[1]{0:T(128)}) custom-call(s32[1]{0:T(128)} %get-tuple-element.54.length_ref, s32[1]{0:T(128)S(6)} %copy.18.span_ref, s32[1]{0:T(128)} %bitcast.1.tile_ref, bf16[4,8192,128]{2,1,0:T(8,128)(2,1)} %get-tuple-element.52.keys_hbm, bf16[4,80,8192]{2,1,0:T(8,128)(2,1)} %get-tuple-element.53.values_hbm, ...), custom_call_target="tpu_custom_call" | custom-call | flops 17179869184 | bytes 8388608 | tf_op jit(solution)/shard_map/attend/pallas_call | solution.py:431
  95.9 0.6 copy-done.7
  96.5 2.7 %assemble.5 = bf16[7168,128]{1,0:T(8,128)(2,1)} custom-call(bf16[1024,128]{1,0:T(8,128)(2,1)} %refs_6_.3, bf16[1024,128]{1,0:T(8,128)(2,1)} %copy-done.3, bf16[1024,128]{1,0:T(8,128)(2,1)} %copy-done.4, bf16[1024,128]{1,0:T(8,128)(2,1)} %copy-done.5, bf16[1024,128]{1,0:T(8,128)(2,1)} %copy-done.6, bf16[1024,128]{1,0:T(8,128)(2,1)} %copy-done.7, ...), custom_call_target="tpu_custom_call" | custom-call | bytes 3670016 | tf_op jit(solution)/shard_map/assemble/pallas_call | solution.py:86
  99.3 0.7 collective-permute-start.26
  100.0 1.2 copy-done.9
  101.2 6.4 %project.3 = (bf16[2,2,128,512]{3,2,1,0:T(8,128)(2,1)}, bf16[4,256,128]{2,1,0:T(8,128)(2,1)}, bf16[4,80,256]{2,1,0:T(8,128)(2,1)}) custom-call(s32[16]{0:T(128)} %dynamic-slice_bitcast_fusion.order_ref, bf16[128,1024]{1,0:T(8,128)(2,1)} %copy-done.1, bf16[128,1024]{1,0:T(8,128)(2,1)} %copy-done.11, bf16[128,1024]{1,0:T(8,128)(2,1)} %copy-done.12, ...), custom_call_target="tpu_custom_call" | custom-call | flops 1073741824 | bytes 4194304 | tf_op jit(solution)/shard_map/project/pallas_call | solution.py:272
  107.6 13.9 %attend.6 = (f32[2,80,512]{2,1,0:T(8,128)}, s32[1]{0:T(128)}) custom-call(s32[1]{0:T(128)} %get-tuple-element.56.length_ref, s32[1]{0:T(128)S(6)} %copy.18.span_ref, s32[1]{0:T(128)} %bitcast.2.tile_ref, bf16[4,8192,128]{2,1,0:T(8,128)(2,1)} %get-tuple-element.52.keys_hbm, bf16[4,80,8192]{2,1,0:T(8,128)(2,1)} %get-tuple-element.53.values_hbm, ...), custom_call_target="tpu_custom_call" | custom-call | flops 17179869184 | bytes 8388608 | tf_op jit(solution)/shard_map/attend/pallas_call | solution.py:431
  121.6 1.7 %collective-permute-done.27.refs_15_ = bf16[1024,128]{1,0:T(8,128)(2,1)S(1)} collective-permute-done((bf16[1024,128]{1,0:T(8,128)(2,1)}, bf16[1024,128]{1,0:T(8,128)(2,1)S(1)}, u32[]{:S(2)}, u32[]{:S(2)}) %collective-permute-start.27) | collective-permute-done | bytes 262176 | tf_op jit(solution)/shard_map/ppermute | solution.py:107
  123.3 0.7 copy-done.17
  124.0 0.6 copy-done
  124.6 5.8 %finish.2 = (bf16[16,128,128]{2,1,0:T(8,128)(2,1)}, s32[1]{0:T(128)}) custom-call(s32[1]{0:T(128)S(6)} %copy.18.span_ref, s32[1]{0:T(128)} %bitcast.2.tile_ref, f32[2,80,512]{2,1,0:T(8,128)} %get-tuple-element.62.refs_0_, f32[2,80,512]{2,1,0:T(8,128)} %get-tuple-element.73.refs_1_, bf16[2,2,128,512]{3,2,1,0:T(8,128)(2,1)} %project.2.queries_hbm.refs_2_, ...), custom_call_target="tpu_custom_call" | custom-call | flops 536870912 | bytes 4194304 | tf_op jit(solution)/shard_map/finish/pallas_call | solution.py:546
  131.1 2.6 %collective-permute-start.28 = (bf16[16,128,128]{2,1,0:T(8,128)(2,1)}, bf16[16,128,128]{2,1,0:T(8,128)(2,1)S(1)}, u32[]{:S(2)}, u32[]{:S(2)}) collective-permute-start(bf16[16,128,128]{2,1,0:T(8,128)(2,1)} %get-tuple-element.94), channel_id=1, source_target_pairs={{0,1},{1,0},{2,3},{3,2},{4,5},{5,4},{6,7},{7,6},{8,9},{9,8},{10,11... | collective-permute-start | bytes 1572872 | tf_op jit(solution)/shard_map/ppermute | solution.py:688
  134.3 13.1 %attend.7 = (f32[2,80,512]{2,1,0:T(8,128)}, s32[1]{0:T(128)}) custom-call(s32[1]{0:T(128)S(6)} %add.33.length_ref, s32[1]{0:T(128)S(6)} %copy.18.span_ref, s32[1]{0:T(128)} %bitcast.1.tile_ref, bf16[4,8192,128]{2,1,0:T(8,128)(2,1)} %get-tuple-element.52.keys_hbm, bf16[4,80,8192]{2,1,0:T(8,128)(2,1)} %get-tuple-element.53.values_hbm, ...), custom_call_target="tpu_custom_call" | custom-call | flops 17179869184 | bytes 8388608 | tf_op jit(solution)/shard_map/attend/pallas_call | solution.py:431
  147.4 5.8 %finish.3 = (bf16[16,128,128]{2,1,0:T(8,128)(2,1)}, s32[1]{0:T(128)}) custom-call(s32[1]{0:T(128)S(6)} %copy.18.span_ref, s32[1]{0:T(128)} %bitcast.1.tile_ref, f32[2,80,512]{2,1,0:T(8,128)} %get-tuple-element.55.refs_0_, f32[2,80,512]{2,1,0:T(8,128)} %get-tuple-element.92.refs_1_, bf16[2,2,128,512]{3,2,1,0:T(8,128)(2,1)} %project.2.queries_hbm.refs_2_, ...), custom_call_target="tpu_custom_call" | custom-call | flops 536870912 | bytes 4194304 | tf_op jit(solution)/shard_map/finish/pallas_call | solution.py:546
  153.3 0.8 copy-done.26
  154.1 2.2 %combine.1 = bf16[128,2048]{1,0:T(8,128)(2,1)} custom-call(s32[16]{0:T(128)} %dynamic-slice_bitcast_fusion.order_ref, bf16[16,128,128]{2,1,0:T(8,128)(2,1)} %get-tuple-element.93.own_ref, bf16[16,128,128]{2,1,0:T(8,128)(2,1)} %copy-done.26), custom_call_target="tpu_custom_call" | custom-call | tf_op jit(solution)/shard_map/combine/pallas_call | solution.py:583
  (96 shorter events, 3.1 us)
Async XLA Ops:
  1.0 21.6 %copy-start.10 = (bf16[128,512]{1,0:T(8,128)(2,1)}, bf16[128,512]{1,0:T(8,128)(2,1)S(1)}, u32[]{:S(2)}) copy-start(bf16[128,512]{1,0:T(8,128)(2,1)S(1)} %get-tuple-element.98.refs_0_) | copy-start | bytes 393220
  1.0 4.4 %collective-permute-start = (bf16[128,512]{1,0:T(8,128)(2,1)S(1)}, bf16[128,512]{1,0:T(8,128)(2,1)S(1)}, u32[]{:S(2)}, u32[]{:S(2)}) collective-permute-start(bf16[128,512]{1,0:T(8,128)(2,1)S(1)} %get-tuple-element.98.refs_0_), channel_id=1, source_target_pairs={{0,8},{2,10},{8,16},{10,18},{16,24},{18,26},{24,28},{26,30},{28,20... | collective-permute-start | bytes 393224 | tf_op jit(solution)/shard_map/ppermute | solution.py:107
  2.3 7.2 %collective-permute-start.1 = (bf16[128,512]{1,0:T(8,128)(2,1)S(1)}, bf16[128,512]{1,0:T(8,128)(2,1)S(1)}, u32[]{:S(2)}, u32[]{:S(2)}) collective-permute-start(bf16[128,512]{1,0:T(8,128)(2,1)S(1)} %get-tuple-element.98.refs_0_), channel_id=1, source_target_pairs={{8,0},{10,2},{16,8},{18,10},{24,16},{26,18},{28,24},{30,26},{20,28... | collective-permute-start | bytes 393224 | tf_op jit(solution)/shard_map/ppermute | solution.py:107
  5.4 17.1 %copy-start.19 = (bf16[128,512]{1,0:T(8,128)(2,1)}, bf16[128,512]{1,0:T(8,128)(2,1)S(1)}, u32[]{:S(2)}) copy-start(bf16[128,512]{1,0:T(8,128)(2,1)S(1)} %collective-permute-done.refs_1_) | copy-start | bytes 393220
  5.4 4.2 %collective-permute-start.2 = (bf16[128,512]{1,0:T(8,128)(2,1)S(1)}, bf16[128,512]{1,0:T(8,128)(2,1)S(1)}, u32[]{:S(2)}, u32[]{:S(2)}) collective-permute-start(bf16[128,512]{1,0:T(8,128)(2,1)S(1)} %collective-permute-done.refs_1_), channel_id=1, source_target_pairs={{0,8},{2,10},{8,16},{10,18},{16,24},{18,26},{24,28},{26,30},{28,20... | collective-permute-start | bytes 393224 | tf_op jit(solution)/shard_map/ppermute | solution.py:107
  6.8 15.8 %copy-start.1 = (bf16[128,1024]{1,0:T(8,128)(2,1)}, bf16[128,1024]{1,0:T(8,128)(2,1)S(1)}, u32[]{:S(2)}) copy-start(bf16[128,1024]{1,0:T(8,128)(2,1)S(1)} %pad_maximum_fusion.1.refs_0_) | copy-start | bytes 786436
  6.8 16.4 %collective-permute-start.10 = (bf16[128,1024]{1,0:T(8,128)(2,1)S(1)}, bf16[128,1024]{1,0:T(8,128)(2,1)S(1)}, u32[]{:S(2)}, u32[]{:S(2)}) collective-permute-start(bf16[128,1024]{1,0:T(8,128)(2,1)S(1)} %pad_maximum_fusion.1.refs_0_), channel_id=1, source_target_pairs={{0,8},{2,10},{8,16},{10,18},{16,24},{18,26},{24,28},{26,30},{28,20... | collective-permute-start | bytes 786440 | tf_op jit(solution)/shard_map/ppermute | solution.py:107
  8.1 15.1 %collective-permute-start.11 = (bf16[128,1024]{1,0:T(8,128)(2,1)S(1)}, bf16[128,1024]{1,0:T(8,128)(2,1)S(1)}, u32[]{:S(2)}, u32[]{:S(2)}) collective-permute-start(bf16[128,1024]{1,0:T(8,128)(2,1)S(1)} %pad_maximum_fusion.1.refs_0_), channel_id=1, source_target_pairs={{8,0},{10,2},{16,8},{18,10},{24,16},{26,18},{28,24},{30,26},{20,28... | collective-permute-start | bytes 786440 | tf_op jit(solution)/shard_map/ppermute | solution.py:107
  8.3 42.0 %collective-permute-start.9 = (bf16[128,2048]{1,0:T(8,128)(2,1)}, bf16[128,2048]{1,0:T(8,128)(2,1)}, u32[]{:S(2)}, u32[]{:S(2)}) collective-permute-start(bf16[128,2048]{1,0:T(8,128)(2,1)} %param.10), channel_id=1, source_target_pairs={{0,1},{1,0},{2,3},{3,2},{4,5},{5,4},{6,7},{7,6},{8,9},{9,8},{10,11... | collective-permute-start | bytes 1572872 | tf_op jit(solution)/shard_map/ppermute | solution.py:620
  9.5 13.1 %copy-start.20 = (bf16[128,512]{1,0:T(8,128)(2,1)}, bf16[128,512]{1,0:T(8,128)(2,1)S(1)}, u32[]{:S(2)}) copy-start(bf16[128,512]{1,0:T(8,128)(2,1)S(1)} %collective-permute-done.1.refs_2_) | copy-start | bytes 393220
  9.5 15.2 %collective-permute-start.3 = (bf16[128,512]{1,0:T(8,128)(2,1)S(1)}, bf16[128,512]{1,0:T(8,128)(2,1)S(1)}, u32[]{:S(2)}, u32[]{:S(2)}) collective-permute-start(bf16[128,512]{1,0:T(8,128)(2,1)S(1)} %collective-permute-done.1.refs_2_), channel_id=1, source_target_pairs={{8,0},{10,2},{16,8},{18,10},{24,16},{26,18},{28,24},{30,26},{20,28... | collective-permute-start | bytes 393224 | tf_op jit(solution)/shard_map/ppermute | solution.py:107
  9.7 12.9 %copy-start.21 = (bf16[128,512]{1,0:T(8,128)(2,1)}, bf16[128,512]{1,0:T(8,128)(2,1)S(1)}, u32[]{:S(2)}) copy-start(bf16[128,512]{1,0:T(8,128)(2,1)S(1)} %collective-permute-done.2.refs_3_) | copy-start | bytes 393220
  9.7 15.2 %collective-permute-start.4 = (bf16[128,512]{1,0:T(8,128)(2,1)S(1)}, bf16[128,512]{1,0:T(8,128)(2,1)S(1)}, u32[]{:S(2)}, u32[]{:S(2)}) collective-permute-start(bf16[128,512]{1,0:T(8,128)(2,1)S(1)} %collective-permute-done.2.refs_3_), channel_id=1, source_target_pairs={{0,8},{2,10},{8,16},{10,18},{16,24},{18,26},{24,28},{26,30},{28,20... | collective-permute-start | bytes 393224 | tf_op jit(solution)/shard_map/ppermute | solution.py:107
  23.2 16.2 %copy-start.11 = (bf16[128,1024]{1,0:T(8,128)(2,1)}, bf16[128,1024]{1,0:T(8,128)(2,1)S(1)}, u32[]{:S(2)}) copy-start(bf16[128,1024]{1,0:T(8,128)(2,1)S(1)} %collective-permute-done.10.refs_1_) | copy-start | bytes 786436
  23.2 16.1 %copy-start.12 = (bf16[128,1024]{1,0:T(8,128)(2,1)}, bf16[128,1024]{1,0:T(8,128)(2,1)S(1)}, u32[]{:S(2)}) copy-start(bf16[128,1024]{1,0:T(8,128)(2,1)S(1)} %collective-permute-done.11.refs_2_) | copy-start | bytes 786436
  23.2 24.2 %collective-permute-start.12 = (bf16[128,1024]{1,0:T(8,128)(2,1)S(1)}, bf16[128,1024]{1,0:T(8,128)(2,1)S(1)}, u32[]{:S(2)}, u32[]{:S(2)}) collective-permute-start(bf16[128,1024]{1,0:T(8,128)(2,1)S(1)} %collective-permute-done.10.refs_1_), channel_id=1, source_target_pairs={{0,8},{2,10},{8,16},{10,18},{16,24},{18,26},{24,28},{26,30},{28,20... | collective-permute-start | bytes 786440 | tf_op jit(solution)/shard_map/ppermute | solution.py:107
  24.6 22.9 %collective-permute-start.13 = (bf16[128,1024]{1,0:T(8,128)(2,1)S(1)}, bf16[128,1024]{1,0:T(8,128)(2,1)S(1)}, u32[]{:S(2)}, u32[]{:S(2)}) collective-permute-start(bf16[128,1024]{1,0:T(8,128)(2,1)S(1)} %collective-permute-done.11.refs_2_), channel_id=1, source_target_pairs={{8,0},{10,2},{16,8},{18,10},{24,16},{26,18},{28,24},{30,26},{20,28... | collective-permute-start | bytes 786440 | tf_op jit(solution)/shard_map/ppermute | solution.py:107
  24.7 14.6 %copy-start.22 = (bf16[128,512]{1,0:T(8,128)(2,1)}, bf16[128,512]{1,0:T(8,128)(2,1)S(1)}, u32[]{:S(2)}) copy-start(bf16[128,512]{1,0:T(8,128)(2,1)S(1)} %collective-permute-done.3.refs_4_) | copy-start | bytes 393220
  24.7 14.6 %collective-permute-start.5 = (bf16[128,512]{1,0:T(8,128)(2,1)S(1)}, bf16[128,512]{1,0:T(8,128)(2,1)S(1)}, u32[]{:S(2)}, u32[]{:S(2)}) collective-permute-start(bf16[128,512]{1,0:T(8,128)(2,1)S(1)} %collective-permute-done.3.refs_4_), channel_id=1, source_target_pairs={{8,0},{10,2},{16,8},{18,10},{24,16},{26,18},{28,24},{30,26},{20,28... | collective-permute-start | bytes 393224 | tf_op jit(solution)/shard_map/ppermute | solution.py:107
  24.9 14.4 %copy-start.23 = (bf16[128,512]{1,0:T(8,128)(2,1)}, bf16[128,512]{1,0:T(8,128)(2,1)S(1)}, u32[]{:S(2)}) copy-start(bf16[128,512]{1,0:T(8,128)(2,1)S(1)} %collective-permute-done.4.refs_5_) | copy-start | bytes 393220
  24.9 24.1 %collective-permute-start.6 = (bf16[128,512]{1,0:T(8,128)(2,1)S(1)}, bf16[128,512]{1,0:T(8,128)(2,1)S(1)}, u32[]{:S(2)}, u32[]{:S(2)}) collective-permute-start(bf16[128,512]{1,0:T(8,128)(2,1)S(1)} %collective-permute-done.4.refs_5_), channel_id=1, source_target_pairs={{0,8},{2,10},{8,16},{10,18},{16,24},{18,26},{24,28},{26,30},{28,20... | collective-permute-start | bytes 393224 | tf_op jit(solution)/shard_map/ppermute | solution.py:107
  29.0 20.0 %copy-start.2 = (bf16[1024,128]{1,0:T(8,128)(2,1)S(1)}, bf16[1024,128]{1,0:T(8,128)(2,1)}, u32[]{:S(2)}) copy-start(bf16[1024,128]{1,0:T(8,128)(2,1)} %refs_6_.3) | copy-start | bytes 786436
  39.3 13.5 %copy-start.29 = (f32[2048]{0:T(1024)S(1)}, f32[2048]{0:T(1024)}, u32[]{:S(2)}) copy-start(f32[2048]{0:T(1024)} %param.11) | copy-start | bytes 24580
  40.0 11.2 %copy-start.25 = (bf16[128,2048]{1,0:T(8,128)(2,1)S(1)}, bf16[128,2048]{1,0:T(8,128)(2,1)}, u32[]{:S(2)}) copy-start(bf16[128,2048]{1,0:T(8,128)(2,1)} %param.10) | copy-start | bytes 1572868
  42.3 11.8 %collective-permute-start.7 = (bf16[896,512]{1,0:T(8,128)(2,1)}, bf16[896,512]{1,0:T(8,128)(2,1)S(1)}, u32[]{:S(2)}, u32[]{:S(2)}) collective-permute-start(bf16[896,512]{1,0:T(8,128)(2,1)} %assemble.3), channel_id=1, source_target_pairs={{0,2},{2,0},{4,6},{6,4},{8,10},{10,8},{12,14},{14,12},{16,18},{18,... | collective-permute-start | bytes 2752520 | tf_op jit(solution)/shard_map/ppermute | solution.py:107
  47.4 6.7 %copy-start.13 = (bf16[128,1024]{1,0:T(8,128)(2,1)}, bf16[128,1024]{1,0:T(8,128)(2,1)S(1)}, u32[]{:S(2)}) copy-start(bf16[128,1024]{1,0:T(8,128)(2,1)S(1)} %collective-permute-done.12.refs_3_) | copy-start | bytes 786436
  47.5 12.0 %collective-permute-start.14 = (bf16[128,1024]{1,0:T(8,128)(2,1)S(1)}, bf16[128,1024]{1,0:T(8,128)(2,1)S(1)}, u32[]{:S(2)}, u32[]{:S(2)}) collective-permute-start(bf16[128,1024]{1,0:T(8,128)(2,1)S(1)} %collective-permute-done.12.refs_3_), channel_id=1, source_target_pairs={{0,8},{2,10},{8,16},{10,18},{16,24},{18,26},{24,28},{26,30},{28,20... | collective-permute-start | bytes 786440 | tf_op jit(solution)/shard_map/ppermute | solution.py:107
  48.8 10.7 %collective-permute-start.15 = (bf16[128,1024]{1,0:T(8,128)(2,1)S(1)}, bf16[128,1024]{1,0:T(8,128)(2,1)S(1)}, u32[]{:S(2)}, u32[]{:S(2)}) collective-permute-start(bf16[128,1024]{1,0:T(8,128)(2,1)S(1)} %collective-permute-done.13.refs_4_), channel_id=1, source_target_pairs={{8,0},{10,2},{16,8},{18,10},{24,16},{26,18},{28,24},{30,26},{20,28... | collective-permute-start | bytes 786440 | tf_op jit(solution)/shard_map/ppermute | solution.py:107
  49.0 12.0 %collective-permute-start.19 = (bf16[1024,128]{1,0:T(8,128)(2,1)S(1)}, bf16[1024,128]{1,0:T(8,128)(2,1)S(1)}, u32[]{:S(2)}, u32[]{:S(2)}) collective-permute-start(bf16[1024,128]{1,0:T(8,128)(2,1)S(1)} %copy-done.2), channel_id=1, source_target_pairs={{0,8},{2,10},{8,16},{10,18},{16,24},{18,26},{24,28},{26,30},{28,20... | collective-permute-start | bytes 786440 | tf_op jit(solution)/shard_map/ppermute | solution.py:107
  50.3 2.3 %collective-permute-start.8 = (bf16[128,512]{1,0:T(8,128)(2,1)S(1)}, bf16[128,512]{1,0:T(8,128)(2,1)S(1)}, u32[]{:S(2)}, u32[]{:S(2)}) collective-permute-start(bf16[128,512]{1,0:T(8,128)(2,1)S(1)} %collective-permute-done.6.refs_7_), channel_id=1, source_target_pairs={{0,2},{2,0},{4,6},{6,4},{8,10},{10,8},{12,14},{14,12},{16,18},{18,... | collective-permute-start | bytes 393224 | tf_op jit(solution)/shard_map/ppermute | solution.py:107
  52.6 9.3 %collective-permute-start.20 = (bf16[1024,128]{1,0:T(8,128)(2,1)S(1)}, bf16[1024,128]{1,0:T(8,128)(2,1)S(1)}, u32[]{:S(2)}, u32[]{:S(2)}) collective-permute-start(bf16[1024,128]{1,0:T(8,128)(2,1)S(1)} %copy-done.2), channel_id=1, source_target_pairs={{8,0},{10,2},{16,8},{18,10},{24,16},{26,18},{28,24},{30,26},{20,28... | collective-permute-start | bytes 786440 | tf_op jit(solution)/shard_map/ppermute | solution.py:107
  59.5 17.6 %copy-start.15 = (bf16[128,1024]{1,0:T(8,128)(2,1)}, bf16[128,1024]{1,0:T(8,128)(2,1)S(1)}, u32[]{:S(2)}) copy-start(bf16[128,1024]{1,0:T(8,128)(2,1)S(1)} %collective-permute-done.14.refs_5_) | copy-start | bytes 786436
  59.5 17.6 %copy-start.16 = (bf16[128,1024]{1,0:T(8,128)(2,1)}, bf16[128,1024]{1,0:T(8,128)(2,1)S(1)}, u32[]{:S(2)}) copy-start(bf16[128,1024]{1,0:T(8,128)(2,1)S(1)} %collective-permute-done.15.refs_6_) | copy-start | bytes 786436
  59.5 20.5 %collective-permute-start.16 = (bf16[128,1024]{1,0:T(8,128)(2,1)S(1)}, bf16[128,1024]{1,0:T(8,128)(2,1)}, u32[]{:S(2)}, u32[]{:S(2)}) collective-permute-start(bf16[128,1024]{1,0:T(8,128)(2,1)S(1)} %collective-permute-done.15.refs_6_), channel_id=1, source_target_pairs={{8,0},{10,2},{16,8},{18,10},{24,16},{26,18},{28,24},{30,26},{20,28... | collective-permute-start | bytes 786440 | tf_op jit(solution)/shard_map/ppermute | solution.py:107
  61.0 16.2 %copy-start.3 = (bf16[1024,128]{1,0:T(8,128)(2,1)}, bf16[1024,128]{1,0:T(8,128)(2,1)S(1)}, u32[]{:S(2)}) copy-start(bf16[1024,128]{1,0:T(8,128)(2,1)S(1)} %collective-permute-done.19.refs_1_.refs_7_) | copy-start | bytes 786436
  62.0 15.2 %copy-start.4 = (bf16[1024,128]{1,0:T(8,128)(2,1)}, bf16[1024,128]{1,0:T(8,128)(2,1)S(1)}, u32[]{:S(2)}) copy-start(bf16[1024,128]{1,0:T(8,128)(2,1)S(1)} %collective-permute-done.20.refs_2_.refs_8_) | copy-start | bytes 786436
  62.0 18.5 %collective-permute-start.21 = (bf16[1024,128]{1,0:T(8,128)(2,1)S(1)}, bf16[1024,128]{1,0:T(8,128)(2,1)S(1)}, u32[]{:S(2)}, u32[]{:S(2)}) collective-permute-start(bf16[1024,128]{1,0:T(8,128)(2,1)S(1)} %collective-permute-done.19.refs_1_.refs_7_), channel_id=1, source_target_pairs={{0,8},{2,10},{8,16},{10,18},{16,24},{18,26},{24,28},{26,30},{28,20... | collective-permute-start | bytes 786440 | tf_op jit(solution)/shard_map/ppermute | solution.py:107
  63.2 17.3 %collective-permute-start.22 = (bf16[1024,128]{1,0:T(8,128)(2,1)S(1)}, bf16[1024,128]{1,0:T(8,128)(2,1)S(1)}, u32[]{:S(2)}, u32[]{:S(2)}) collective-permute-start(bf16[1024,128]{1,0:T(8,128)(2,1)S(1)} %collective-permute-done.20.refs_2_.refs_8_), channel_id=1, source_target_pairs={{8,0},{10,2},{16,8},{18,10},{24,16},{26,18},{28,24},{30,26},{20,28... | collective-permute-start | bytes 786440 | tf_op jit(solution)/shard_map/ppermute | solution.py:107
  79.9 20.1 %collective-permute-start.17 = (bf16[896,1024]{1,0:T(8,128)(2,1)}, bf16[896,1024]{1,0:T(8,128)(2,1)S(1)}, u32[]{:S(2)}, u32[]{:S(2)}) collective-permute-start(bf16[896,1024]{1,0:T(8,128)(2,1)} %assemble.4), channel_id=1, source_target_pairs={{0,2},{2,0},{4,6},{6,4},{8,10},{10,8},{12,14},{14,12},{16,18},{18,... | collective-permute-start | bytes 5505032 | tf_op jit(solution)/shard_map/ppermute | solution.py:107
  80.0 20.0 %collective-permute-start.18 = (bf16[128,1024]{1,0:T(8,128)(2,1)}, bf16[128,1024]{1,0:T(8,128)(2,1)}, u32[]{:S(2)}, u32[]{:S(2)}) collective-permute-start(bf16[128,1024]{1,0:T(8,128)(2,1)} %collective-permute-done.16.refs_7_), channel_id=1, source_target_pairs={{0,2},{2,0},{4,6},{6,4},{8,10},{10,8},{12,14},{14,12},{16,18},{18,... | collective-permute-start | bytes 786440 | tf_op jit(solution)/shard_map/ppermute | solution.py:107
  80.5 15.2 %copy-start.5 = (bf16[1024,128]{1,0:T(8,128)(2,1)}, bf16[1024,128]{1,0:T(8,128)(2,1)S(1)}, u32[]{:S(2)}) copy-start(bf16[1024,128]{1,0:T(8,128)(2,1)S(1)} %collective-permute-done.21.refs_3_.refs_9_) | copy-start | bytes 786436
  80.5 15.2 %copy-start.6 = (bf16[1024,128]{1,0:T(8,128)(2,1)}, bf16[1024,128]{1,0:T(8,128)(2,1)S(1)}, u32[]{:S(2)}) copy-start(bf16[1024,128]{1,0:T(8,128)(2,1)S(1)} %collective-permute-done.22.refs_4_.refs_10_) | copy-start | bytes 786436
  80.5 15.2 %collective-permute-start.23 = (bf16[1024,128]{1,0:T(8,128)(2,1)S(1)}, bf16[1024,128]{1,0:T(8,128)(2,1)S(1)}, u32[]{:S(2)}, u32[]{:S(2)}) collective-permute-start(bf16[1024,128]{1,0:T(8,128)(2,1)S(1)} %collective-permute-done.21.refs_3_.refs_9_), channel_id=1, source_target_pairs={{0,8},{2,10},{8,16},{10,18},{16,24},{18,26},{24,28},{26,30},{28,20... | collective-permute-start | bytes 786440 | tf_op jit(solution)/shard_map/ppermute | solution.py:107
  80.6 15.2 %collective-permute-start.24 = (bf16[1024,128]{1,0:T(8,128)(2,1)S(1)}, bf16[1024,128]{1,0:T(8,128)(2,1)S(1)}, u32[]{:S(2)}, u32[]{:S(2)}) collective-permute-start(bf16[1024,128]{1,0:T(8,128)(2,1)S(1)} %collective-permute-done.22.refs_4_.refs_10_), channel_id=1, source_target_pairs={{8,0},{10,2},{16,8},{18,10},{24,16},{26,18},{28,24},{30,26},{20,28... | collective-permute-start | bytes 786440 | tf_op jit(solution)/shard_map/ppermute | solution.py:107
  95.8 25.7 %collective-permute-start.25 = (bf16[1024,128]{1,0:T(8,128)(2,1)S(1)}, bf16[1024,128]{1,0:T(8,128)(2,1)}, u32[]{:S(2)}, u32[]{:S(2)}) collective-permute-start(bf16[1024,128]{1,0:T(8,128)(2,1)S(1)} %collective-permute-done.23.refs_5_.refs_11_), channel_id=1, source_target_pairs={{0,8},{2,10},{8,16},{10,18},{16,24},{18,26},{24,28},{26,30},{28,20... | collective-permute-start | bytes 786440 | tf_op jit(solution)/shard_map/ppermute | solution.py:107
  99.3 24.0 %collective-permute-start.26 = (bf16[7168,128]{1,0:T(8,128)(2,1)}, bf16[7168,128]{1,0:T(8,128)(2,1)S(1)}, u32[]{:S(2)}, u32[]{:S(2)}) collective-permute-start(bf16[7168,128]{1,0:T(8,128)(2,1)} %assemble.5), channel_id=1, source_target_pairs={{0,2},{2,0},{4,6},{6,4},{8,10},{10,8},{12,14},{14,12},{16,18},{18,... | collective-permute-start | bytes 5505032 | tf_op jit(solution)/shard_map/ppermute | solution.py:107
  121.5 1.8 %collective-permute-start.27 = (bf16[1024,128]{1,0:T(8,128)(2,1)}, bf16[1024,128]{1,0:T(8,128)(2,1)S(1)}, u32[]{:S(2)}, u32[]{:S(2)}) collective-permute-start(bf16[1024,128]{1,0:T(8,128)(2,1)} %collective-permute-done.25.refs_13_), channel_id=1, source_target_pairs={{0,2},{2,0},{4,6},{6,4},{8,10},{10,8},{12,14},{14,12},{16,18},{18,... | collective-permute-start | bytes 786440 | tf_op jit(solution)/shard_map/ppermute | solution.py:107
  131.1 22.1 %collective-permute-start.28 = (bf16[16,128,128]{2,1,0:T(8,128)(2,1)}, bf16[16,128,128]{2,1,0:T(8,128)(2,1)S(1)}, u32[]{:S(2)}, u32[]{:S(2)}) collective-permute-start(bf16[16,128,128]{2,1,0:T(8,128)(2,1)} %get-tuple-element.94), channel_id=1, source_target_pairs={{0,1},{1,0},{2,3},{3,2},{4,5},{5,4},{6,7},{7,6},{8,9},{9,8},{10,11... | collective-permute-start | bytes 1572872 | tf_op jit(solution)/shard_map/ppermute | solution.py:688
  (11 other events, 20.5 us)

commit v6 on v5

--- a/solution.py
+++ b/solution.py
@@ -16,6 +16,7 @@
 score_chunk = 256
 value_chunk = 256
 token_tile = 128
+prepare_pages = 8
 
 
 def matmul(a, b):
@@ -174,7 +175,7 @@
 
 def prepare(cache, table, length, part, parts, before):
     pages, page, heads, width = cache.shape
-    pages_step = 4
+    pages_step = prepare_pages
     rows = width // 2 + 16
     total = table.shape[0]
     steps = total // pages_step // parts
@@ -221,7 +222,8 @@
     )
 
 
-def project_kernel(heads, new_heads, group, dim, blocks, order_ref, *refs):
+def project_kernel(heads, new_heads, group, dim, blocks, device_ref, order_ref, *refs):
+    device = device_ref[0]
     chunks = refs[:blocks]
     normed_hbm, cos_ref, sin_ref, query_ref = refs[blocks : blocks + 4]
     source, normed_ref, sems = refs[-3:]
@@ -230,7 +232,7 @@
     rows = source.shape[0] // count
     copies = [pltpu.make_async_copy(normed_hbm, normed_ref, sems.at[count])]
     for k in range(count):
-        start = pl.multiple_of(order_ref[k] * rows, rows)
+        start = pl.multiple_of(order_ref[device, k] * rows, rows)
         copies.append(pltpu.make_async_copy(sources[k], source.at[pl.ds(start, rows)], sems.at[k]))
     for copy in copies:
         copy.start()
@@ -263,7 +265,7 @@
         value_ref[h] = with_ones(turned[dim:]).astype(jnp.bfloat16)
 
 
-def project(normed, chunks, order, cosine, sines, heads, new_heads, group, dim):
+def project(normed, chunks, device, order, cosine, sines, heads, new_heads, group, dim):
     tokens, width = normed.shape
     columns = chunks[0].shape[1]
     outs = [(heads, tokens // token_tile, 2 * dim, group * token_tile)]
@@ -271,13 +273,13 @@
         outs += [(new_heads, tokens, 2 * dim), (new_heads, dim + 16, tokens)]
     return pl.pallas_call(
         functools.partial(project_kernel, heads, new_heads, group, dim, len(chunks)),
-        in_specs=[smem()] + [anywhere()] * (len(chunks) + 1) + [vmem()] * 2,
+        in_specs=[smem()] * 2 + [anywhere()] * (len(chunks) + 1) + [vmem()] * 2,
         out_specs=[vmem()] * len(outs),
         out_shape=[jax.ShapeDtypeStruct(shape, jnp.bfloat16) for shape in outs],
         scratch_shapes=[
             pltpu.VMEM((width, columns), jnp.bfloat16),
             pltpu.VMEM((tokens, width), jnp.bfloat16),
-            pltpu.SemaphoreType.DMA((order.shape[0] + 1,)),
+            pltpu.SemaphoreType.DMA((order.shape[1] + 1,)),
         ],
         cost_estimate=pl.CostEstimate(
             flops=2 * tokens * width * columns,
@@ -286,7 +288,7 @@
         ),
         compiler_params=params(60),
         name="project",
-    )(order, *chunks, normed, cosine, sines)
+    )(device, order, *chunks, normed, cosine, sines)
 
 
 def column_max(scores):
@@ -482,7 +484,10 @@
     return pieces
 
 
-def finish_kernel(heads, sets, group, dim, blocks, span_ref, tile_ref, *refs):
+def finish_kernel(heads, sets, group, dim, blocks, final, span_ref, tile_ref, *refs):
+    if final:
+        device_ref, order_ref, other_hbm, *refs = refs
+        *refs, other, other_sem = refs
     states_hbm = refs[:sets]
     queries_hbm = refs[sets : sets + len(heads)]
     new_keys_hbm, new_values_hbm = refs[sets + len(heads) : sets + len(heads) + 2]
@@ -496,7 +501,7 @@
     per_set = total // sets
     chunks = chunk_sources(chunks) if blocks else []
     count = len(chunks)
-    columns = weight.shape[1] // max(count, 1)
+    columns = weight.shape[2]
     copies = []
     for i in range(sets):
         copies.append((states_hbm[i], states.at[pl.ds(i * per_set, per_set)]))
@@ -508,10 +513,12 @@
     copies = [pltpu.make_async_copy(a, b, sems.at[i]) for i, (a, b) in enumerate(copies)]
     loads = [
         pltpu.make_async_copy(
-            chunks[k], weight.at[:, pl.ds(k * columns, columns)], weight_sems.at[k]
+            chunks[k], weight.at[k], weight_sems.at[k]
         )
         for k in range(count)
     ]
+    if final:
+        loads.append(pltpu.make_async_copy(other_hbm, other, other_sem))
     for copy in copies + loads:
         copy.start()
     for copy in copies:
@@ -528,12 +535,19 @@
     for copy in loads:
         copy.wait()
     for k in range(0, count, 2):
-        both = matmul(attended, weight[:, pl.ds(k * columns, 2 * columns)]).astype(jnp.bfloat16)
-        out_ref[k] = both[:, :columns]
-        out_ref[k + 1] = both[:, columns:]
-
-
-def finish(states, tile, valid, queries, new_keys, new_values, group, chunks):
+        wide = jnp.concatenate([weight[k], weight[k + 1]], axis=1)
+        both = matmul(attended, wide).astype(jnp.bfloat16)
+        for i in range(2):
+            term = both[:, i * columns : (i + 1) * columns]
+            if final:
+                summed = term.astype(jnp.float32) + other[k + i].astype(jnp.float32)
+                start = pl.multiple_of(order_ref[device_ref[0], k + i] * columns, columns)
+                out_ref[:, pl.ds(start, columns)] = (residual_scale * summed).astype(jnp.bfloat16)
+            else:
+                out_ref[k + i] = term
+
+
+def finish(states, tile, valid, queries, new_keys, new_values, group, chunks, final=()):
     heads = tuple(q.shape[0] for q in queries)
     total = sum(heads)
     rows, lanes = states[0].shape[1:]
@@ -543,9 +557,15 @@
     count = 2 * (blocks - 2) if blocks else 0
     columns = chunks[0].shape[1] if blocks else 128
     out = (count, token_tile, columns) if blocks else (token_tile, depth)
+    landing = []
+    if final:
+        out = (token_tile, count * columns)
+        landing = [pltpu.VMEM(final[2].shape, jnp.bfloat16), pltpu.SemaphoreType.DMA(())]
     return pl.pallas_call(
-        functools.partial(finish_kernel, heads, len(states), group, dim, blocks),
-        in_specs=[smem()] * 2 + [anywhere()] * (len(states) + len(queries) + 2 + blocks),
+        functools.partial(finish_kernel, heads, len(states), group, dim, blocks, bool(final)),
+        in_specs=[smem()] * 2
+        + ([smem(), smem(), anywhere()] if final else [])
+        + [anywhere()] * (len(states) + len(queries) + 2 + blocks),
         out_specs=[vmem(), smem()],
         out_shape=[
             jax.ShapeDtypeStruct(out, jnp.bfloat16),
@@ -556,10 +576,11 @@
             pltpu.VMEM((total,) + queries[0].shape[2:], jnp.bfloat16),
             pltpu.VMEM(new_keys.shape, jnp.bfloat16),
             pltpu.VMEM(new_values.shape, jnp.bfloat16),
-            pltpu.VMEM((depth if blocks else 16, max(count, 1) * columns), jnp.bfloat16),
+            pltpu.VMEM((max(count, 1), depth if blocks else 16, columns), jnp.bfloat16),
             pltpu.SemaphoreType.DMA((len(states) + 2 + total,)),
             pltpu.SemaphoreType.DMA((max(count, 1),)),
-        ],
+        ]
+        + landing,
         cost_estimate=pl.CostEstimate(
             flops=2 * token_tile * depth * columns * count,
             bytes_accessed=2 * depth * columns * count,
@@ -567,27 +588,7 @@
         ),
         compiler_params=params(60),
         name="finish",
-    )(valid, tile, *states, *queries, new_keys, new_values, *chunks)
-
-
-def combine_kernel(order_ref, own_ref, other_ref, out_ref):
-    width = own_ref.shape[2]
-    for k in range(own_ref.shape[0]):
-        summed = own_ref[k].astype(jnp.float32) + other_ref[k].astype(jnp.float32)
-        start = pl.multiple_of(order_ref[k] * width, width)
-        out_ref[:, pl.ds(start, width)] = (residual_scale * summed).astype(jnp.bfloat16)
-
-
-def combine(own, other, order):
-    count, rows, columns = own.shape
-    return pl.pallas_call(
-        combine_kernel,
-        in_specs=[smem(), vmem(), vmem()],
-        out_specs=vmem(),
-        out_shape=jax.ShapeDtypeStruct((rows, count * columns), jnp.bfloat16),
-        compiler_params=params(60),
-        name="combine",
-    )(order, own, other)
+    )(valid, tile, *final, *states, *queries, new_keys, new_values, *chunks)
 
 
 def rope_tables(positions, dim):
@@ -605,12 +606,15 @@
     dim = w_kv.shape[2] // 2
     group = w_query.shape[1] // dim // heads
     own_rows = tokens.shape[0]
-    length = lax.dynamic_slice_in_dim(cached_len, device, 1)
+    length = jnp.sum(
+        jnp.where(jnp.arange(cached_len.shape[0]) == device, cached_len, 0), keepdims=True
+    )
     table = page_table[0]
     w_new = w_kv.reshape(w_kv.shape[0], -1)
     if fast:
         tables = cycle_tables(req_count)
-        order = jnp.array(tables[3], jnp.int32)[device]
+        order = jnp.array(tables[3], jnp.int32)
+        place = device.reshape(1)
         swap = [(0, 1), (1, 0)]
         early = heads // 2
         cut = early * group * dim
@@ -634,7 +638,8 @@
         ring_out.step(first_end)
         keys, values = state
     else:
-        order = jnp.zeros((1,), jnp.int32)
+        order = jnp.zeros((1, 1), jnp.int32)
+        place = jnp.zeros((1,), jnp.int32)
         early = 0
         gather = lambda array: lax.all_gather(array, "req", axis=0, tiled=True)
         second_chunks = [gather(jnp.concatenate([w_query, w_new], axis=1))]
@@ -651,12 +656,12 @@
     def attend_tile(tile, source, count, first, token):
         return attend(count, 0, first, tile, keys, values, source, token, span_len)
 
-    def finish_tile(states, tile, chunks):
-        return finish(states, tile, span_len, queries, new_keys, new_values, group, chunks)
+    def finish_tile(states, tile, chunks, final=()):
+        return finish(states, tile, span_len, queries, new_keys, new_values, group, chunks, final)
 
     if not fast:
         late, new_keys, new_values = project(
-            normed, second_chunks, order, cosine, sines, heads, heads, group, dim
+            normed, second_chunks, place, order, cosine, sines, heads, heads, group, dim
         )
         queries.append(late)
         rows = []
@@ -669,7 +674,7 @@
         summed = lax.psum_scatter(partial, "tp", scatter_dimension=0, tiled=True)
         return (residual_scale * summed.astype(jnp.float32)).astype(jnp.bfloat16)
     theirs, ours = (1 - rank).reshape(1), rank.reshape(1)
-    soon = project(normed, first_chunks, order, cosine, sines, early, 0, group, dim)[0]
+    soon = project(normed, first_chunks, place, order, cosine, sines, early, 0, group, dim)[0]
     second_end = ring_second.last(False, soon)
     ring_out.step(soon)
     sent_first, token = attend_tile(theirs, soon, early, 0, length)
@@ -677,7 +682,7 @@
     ring_out.step(sent_first)
     kept_first, token = attend_tile(ours, soon, early, 0, token)
     late, new_keys, new_values = project(
-        normed, second_chunks, order, cosine, sines, heads - early, heads, group, dim
+        normed, second_chunks, place, order, cosine, sines, heads - early, heads, group, dim
     )
     queries += [soon, late]
     out_end = ring_out.last(True, kept_first)
@@ -688,8 +693,8 @@
     received = lax.ppermute(sent, "tp", swap)
     token = token + (tile_token - theirs)
     kept_second, token = attend_tile(ours, late, heads - early, early, token)
-    kept, _ = finish_tile([kept_first, kept_second], ours, out_chunks)
-    return combine(kept, received, order)
+    final = (place, order, received)
+    return finish_tile([kept_first, kept_second], ours, out_chunks, final)[0]
 
 
 def solution(mesh):

time: 157 us -> 154 us (0.981)
  the two profiles are of different devices: /device:TPU:9 before, /device:TPU:24 now
where the time goes in v6:
time: 154 us; the launch traced here: 151 us
  Pallas kernels  78.9 us (51%)
  starting transfers between devices  46.1 us (30%)
  waiting for transfers between devices  10.8 us (7%)
  local copies, waits for them, and re-layouts  6.94 us (5%)
  other arithmetic  5.45 us (4%)
  between operations  2.62 us (2%)
    ppermute x27, starting transfers between devices, move(): return lax.ppermute(value, 'req', pairs)  30.9 us
    pallas_call x4, Pallas kernels, attend(): pl.pallas_call(functools.partial(attend_kernel, heads, first_query, first...  30.1 us
    pallas_call x2, Pallas kernels, prepare(): pl.pallas_call(functools.partial(prepare_kernel, heads, page, width, page...  17.6 us
    ppermute x1, starting transfers between devices, body(): received = lax.ppermute(sent, 'tp', swap)  13.7 us
    pallas_call x2, Pallas kernels, finish(): pl.pallas_call(functools.partial(finish_kernel, heads, len(states), group...  12.6 us
    pallas_call x2, Pallas kernels, project(): pl.pallas_call(functools.partial(project_kernel, heads, new_heads, group,...  10.9 us
    ppermute x27, waiting for transfers between devices, move(): return lax.ppermute(value, 'req', pairs)  10.8 us
    pallas_call x3, Pallas kernels, assemble(): pl.pallas_call(assemble_kernel, in_specs=[anywhere()] * len(blocks), out_...  7.75 us
  transfers between devices with their start and end apart: 29, of which 8 were waited for; matrix products, arithmetic and copies ran while one was open for 4% of the time, Pallas kernels for 44%

profile of v6, /device:TPU:24, one launch (start us, length us, event | category | flops | bytes accessed | tf_op | source)
XLA Modules:
  0.0 150.8 jit_solution(12037943710400225814)
XLA Ops:
  0.0 1.0 fusion.4
  1.0 1.6 %collective-permute-start = (bf16[128,512]{1,0:T(8,128)(2,1)S(1)}, bf16[128,512]{1,0:T(8,128)(2,1)S(1)}, u32[]{:S(2)}, u32[]{:S(2)}) collective-permute-start(bf16[128,512]{1,0:T(8,128)(2,1)S(1)} %get-tuple-element.98.refs_0_), channel_id=1, source_target_pairs={{0,8},{2,10},{8,16},{10,18},{16,24},{18,26},{24,28},{26,30},{28,20... | collective-permute-start | bytes 393224 | tf_op jit(solution)/shard_map/ppermute | solution.py:108
  2.6 0.9 copy.15
  4.0 1.6 %collective-permute-start.11 = (bf16[128,1024]{1,0:T(8,128)(2,1)S(1)}, bf16[128,1024]{1,0:T(8,128)(2,1)S(1)}, u32[]{:S(2)}, u32[]{:S(2)}) collective-permute-start(bf16[128,1024]{1,0:T(8,128)(2,1)S(1)} %pad_maximum_fusion.1.refs_0_), channel_id=1, source_target_pairs={{8,0},{10,2},{16,8},{18,10},{24,16},{26,18},{28,24},{30,26},{20,28... | collective-permute-start | bytes 786440 | tf_op jit(solution)/shard_map/ppermute | solution.py:108
  6.1 0.7 collective-permute-done.refs_1_
  6.8 2.1 %collective-permute-start.2 = (bf16[128,512]{1,0:T(8,128)(2,1)S(1)}, bf16[128,512]{1,0:T(8,128)(2,1)S(1)}, u32[]{:S(2)}, u32[]{:S(2)}) collective-permute-start(bf16[128,512]{1,0:T(8,128)(2,1)S(1)} %collective-permute-done.refs_1_), channel_id=1, source_target_pairs={{0,8},{2,10},{8,16},{10,18},{16,24},{18,26},{24,28},{26,30},{28,20... | collective-permute-start | bytes 393224 | tf_op jit(solution)/shard_map/ppermute | solution.py:108
  8.9 1.5 collective-permute-start.9
  10.4 1.3 fusion.3
  11.7 2.6 %collective-permute-done.1.refs_2_ = bf16[128,512]{1,0:T(8,128)(2,1)S(1)} collective-permute-done((bf16[128,512]{1,0:T(8,128)(2,1)S(1)}, bf16[128,512]{1,0:T(8,128)(2,1)S(1)}, u32[]{:S(2)}, u32[]{:S(2)}) %collective-permute-start.1) | collective-permute-done | bytes 131104 | tf_op jit(solution)/shard_map/ppermute | solution.py:108
  14.3 1.6 %collective-permute-start.3 = (bf16[128,512]{1,0:T(8,128)(2,1)S(1)}, bf16[128,512]{1,0:T(8,128)(2,1)S(1)}, u32[]{:S(2)}, u32[]{:S(2)}) collective-permute-start(bf16[128,512]{1,0:T(8,128)(2,1)S(1)} %collective-permute-done.1.refs_2_), channel_id=1, source_target_pairs={{8,0},{10,2},{16,8},{18,10},{24,16},{26,18},{28,24},{30,26},{20,28... | collective-permute-start | bytes 393224 | tf_op jit(solution)/shard_map/ppermute | solution.py:108
  16.4 0.6 add_convert_fusion
  17.0 8.7 %prepare.2 = (bf16[4,8192,128]{2,1,0:T(8,128)(2,1)}, bf16[4,80,8192]{2,1,0:T(8,128)(2,1)}) custom-call(s32[64]{0:T(128)} %bitcast.28, s32[1]{0:T(128)} %bitcast.3.length_ref, bf16[64,512,128]{2,1,0:T(8,128)(2,1)} %bitcast.10, bf16[64,512,128]{2,1,0:T(8,128)(2,1)} %bitcast.11, bf16[64,512,128]{2,1,0:T(8,128)(2,1)} %bitcast.12, ...), custom_call_target="tpu_custom_call" | custom-call | bytes 12582912 | tf_op jit(solution)/shard_map/prepare/pallas_call | solution.py:188
  26.3 1.6 %collective-permute-start.13 = (bf16[128,1024]{1,0:T(8,128)(2,1)S(1)}, bf16[128,1024]{1,0:T(8,128)(2,1)S(1)}, u32[]{:S(2)}, u32[]{:S(2)}) collective-permute-start(bf16[128,1024]{1,0:T(8,128)(2,1)S(1)} %collective-permute-done.11.refs_2_), channel_id=1, source_target_pairs={{8,0},{10,2},{16,8},{18,10},{24,16},{26,18},{28,24},{30,26},{20,28... | collective-permute-start | bytes 786440 | tf_op jit(solution)/shard_map/ppermute | solution.py:108
  28.6 1.6 %collective-permute-start.5 = (bf16[128,512]{1,0:T(8,128)(2,1)S(1)}, bf16[128,512]{1,0:T(8,128)(2,1)S(1)}, u32[]{:S(2)}, u32[]{:S(2)}) collective-permute-start(bf16[128,512]{1,0:T(8,128)(2,1)S(1)} %collective-permute-done.3.refs_4_), channel_id=1, source_target_pairs={{8,0},{10,2},{16,8},{18,10},{24,16},{26,18},{28,24},{30,26},{20,28... | collective-permute-start | bytes 393224 | tf_op jit(solution)/shard_map/ppermute | solution.py:108
  30.7 0.8 multiply_sine_fusion
  31.5 8.8 %prepare.3 = (bf16[4,8192,128]{2,1,0:T(8,128)(2,1)}, bf16[4,80,8192]{2,1,0:T(8,128)(2,1)}) custom-call(s32[64]{0:T(128)} %bitcast.29, s32[1]{0:T(128)} %bitcast.3.length_ref, bf16[64,512,128]{2,1,0:T(8,128)(2,1)} %bitcast.18, bf16[64,512,128]{2,1,0:T(8,128)(2,1)} %bitcast.19, ...), custom_call_target="tpu_custom_call", output_to_operand_aliasing={{0}: (10, {}), {1}: (11, {})} | custom-call | bytes 12582912 | tf_op jit(solution)/shard_map/prepare/pallas_call | solution.py:188
  40.4 0.6 copy-done.24
  41.0 2.3 %assemble.3 = bf16[896,512]{1,0:T(8,128)(2,1)} custom-call(bf16[128,512]{1,0:T(8,128)(2,1)} %copy-done.10, bf16[128,512]{1,0:T(8,128)(2,1)} %copy-done.19, bf16[128,512]{1,0:T(8,128)(2,1)} %copy-done.20, bf16[128,512]{1,0:T(8,128)(2,1)} %copy-done.21, bf16[128,512]{1,0:T(8,128)(2,1)} %copy-done.22, bf16[128,512]{1,0:T(8,128)(2,1)} %copy-done.23, ...), custom_call_target="tpu_custom_call" | custom-call | bytes 1835008 | tf_op jit(solution)/shard_map/assemble/pallas_call | solution.py:87
  44.0 1.6 %collective-permute-start.15 = (bf16[128,1024]{1,0:T(8,128)(2,1)S(1)}, bf16[128,1024]{1,0:T(8,128)(2,1)S(1)}, u32[]{:S(2)}, u32[]{:S(2)}) collective-permute-start(bf16[128,1024]{1,0:T(8,128)(2,1)S(1)} %collective-permute-done.13.refs_4_), channel_id=1, source_target_pairs={{8,0},{10,2},{16,8},{18,10},{24,16},{26,18},{28,24},{30,26},{20,28... | collective-permute-start | bytes 786440 | tf_op jit(solution)/shard_map/ppermute | solution.py:108
  46.1 1.1 broadcast_select_fusion.1
  47.5 1.6 %collective-permute-start.20 = (bf16[1024,128]{1,0:T(8,128)(2,1)S(1)}, bf16[1024,128]{1,0:T(8,128)(2,1)S(1)}, u32[]{:S(2)}, u32[]{:S(2)}) collective-permute-start(bf16[1024,128]{1,0:T(8,128)(2,1)S(1)} %copy-done.2), channel_id=1, source_target_pairs={{8,0},{10,2},{16,8},{18,10},{24,16},{26,18},{28,24},{30,26},{20,28... | collective-permute-start | bytes 786440 | tf_op jit(solution)/shard_map/ppermute | solution.py:108
  49.1 1.3 fusion.2.refs_10_
  50.4 0.9 copy-done.18
  51.3 4.4 %project.2.queries_hbm.refs_2_.refs_5_ = bf16[2,2,128,512]{3,2,1,0:T(8,128)(2,1)} custom-call(s32[1]{0:T(128)} %bitcast.1.device_ref.refs_0_, s32[16,16]{1,0:T(8,128)} %constant.28.clone.order_ref.refs_1_, bf16[128,512]{1,0:T(8,128)(2,1)} %copy-done.10, bf16[128,512]{1,0:T(8,128)(2,1)} %copy-done.19, bf16[128,512]{1,0:T(8,128)(2,1)} %copy-done.20, ...), custom_call_target="tpu_custom_call" | custom-call | flops 536870912 | bytes 2097152 | tf_op jit(solution)/shard_map/project/pallas_call | solution.py:274
  55.8 1.6 %collective-permute-start.16 = (bf16[128,1024]{1,0:T(8,128)(2,1)S(1)}, bf16[128,1024]{1,0:T(8,128)(2,1)}, u32[]{:S(2)}, u32[]{:S(2)}) collective-permute-start(bf16[128,1024]{1,0:T(8,128)(2,1)S(1)} %collective-permute-done.15.refs_6_), channel_id=1, source_target_pairs={{8,0},{10,2},{16,8},{18,10},{24,16},{26,18},{28,24},{30,26},{20,28... | collective-permute-start | bytes 786440 | tf_op jit(solution)/shard_map/ppermute | solution.py:108
  58.4 1.6 %collective-permute-start.22 = (bf16[1024,128]{1,0:T(8,128)(2,1)S(1)}, bf16[1024,128]{1,0:T(8,128)(2,1)S(1)}, u32[]{:S(2)}, u32[]{:S(2)}) collective-permute-start(bf16[1024,128]{1,0:T(8,128)(2,1)S(1)} %collective-permute-done.20.refs_2_.refs_8_.refs_11_), channel_id=1, source_target_pairs={{8,0},{10,2},{16,8},{18,10},{24,16},{26,18},{28,24},{30,26},{20,28... | collective-permute-start | bytes 786440 | tf_op jit(solution)/shard_map/ppermute | solution.py:108
  60.0 1.5 %attend.4 = (f32[2,80,512]{2,1,0:T(8,128)}, s32[1]{0:T(128)}) custom-call(s32[1]{0:T(128)} %bitcast.3.length_ref, s32[1]{0:T(128)S(6)} %copy.18.span_ref, s32[1]{0:T(128)} %bitcast.2.tile_ref, bf16[4,8192,128]{2,1,0:T(8,128)(2,1)} %get-tuple-element.52.keys_hbm, bf16[4,80,8192]{2,1,0:T(8,128)(2,1)} %get-tuple-element.53.values_hbm, ...), custom_call_target="tpu_custom_call" | custom-call | flops 17179869184 | bytes 8388608 | tf_op jit(solution)/shard_map/attend/pallas_call | solution.py:433
  61.6 2.7 %assemble.4 = bf16[896,1024]{1,0:T(8,128)(2,1)} custom-call(bf16[128,1024]{1,0:T(8,128)(2,1)} %copy-done.1, bf16[128,1024]{1,0:T(8,128)(2,1)} %copy-done.11, bf16[128,1024]{1,0:T(8,128)(2,1)} %copy-done.12, bf16[128,1024]{1,0:T(8,128)(2,1)} %copy-done.13, bf16[128,1024]{1,0:T(8,128)(2,1)} %copy-done.14, bf16[128,1024]{1,0:T(8,128)(2,1)} %copy-done.15, ...), custom_call_target="tpu_custom_call" | custom-call | bytes 3670016 | tf_op jit(solution)/shard_map/assemble/pallas_call | solution.py:87
  64.4 0.7 collective-permute-done.16.refs_7_
  65.1 0.6 collective-permute-done.21.refs_3_.refs_9_.refs_12_
  65.7 4.2 %collective-permute-done.22.refs_4_.refs_10_.refs_13_ = bf16[1024,128]{1,0:T(8,128)(2,1)S(1)} collective-permute-done((bf16[1024,128]{1,0:T(8,128)(2,1)S(1)}, bf16[1024,128]{1,0:T(8,128)(2,1)S(1)}, u32[]{:S(2)}, u32[]{:S(2)}) %collective-permute-start.22) | collective-permute-done | bytes 262176 | tf_op jit(solution)/shard_map/ppermute | solution.py:108
  69.9 7.7 %collective-permute-start.23 = (bf16[1024,128]{1,0:T(8,128)(2,1)S(1)}, bf16[1024,128]{1,0:T(8,128)(2,1)S(1)}, u32[]{:S(2)}, u32[]{:S(2)}) collective-permute-start(bf16[1024,128]{1,0:T(8,128)(2,1)S(1)} %collective-permute-done.21.refs_3_.refs_9_.refs_12_), channel_id=1, source_target_pairs={{0,8},{2,10},{8,16},{10,18},{16,24},{18,26},{24,28},{26,30},{28,20... | collective-permute-start | bytes 786440 | tf_op jit(solution)/shard_map/ppermute | solution.py:108
  77.6 1.2 collective-permute-start.24
  78.8 13.7 %attend.5 = (f32[2,80,512]{2,1,0:T(8,128)}, s32[1]{0:T(128)}) custom-call(s32[1]{0:T(128)} %get-tuple-element.55.length_ref, s32[1]{0:T(128)S(6)} %copy.18.span_ref, s32[1]{0:T(128)} %bitcast.tile_ref, bf16[4,8192,128]{2,1,0:T(8,128)(2,1)} %get-tuple-element.52.keys_hbm, bf16[4,80,8192]{2,1,0:T(8,128)(2,1)} %get-tuple-element.53.values_hbm, ...), custom_call_target="tpu_custom_call" | custom-call | flops 17179869184 | bytes 8388608 | tf_op jit(solution)/shard_map/attend/pallas_call | solution.py:433
  92.6 0.9 collective-permute-start.25
  93.5 2.7 %assemble.5 = bf16[7168,128]{1,0:T(8,128)(2,1)} custom-call(bf16[1024,128]{1,0:T(8,128)(2,1)} %refs_9_.1, bf16[1024,128]{1,0:T(8,128)(2,1)} %copy-done.3, bf16[1024,128]{1,0:T(8,128)(2,1)} %copy-done.4, bf16[1024,128]{1,0:T(8,128)(2,1)} %copy-done.5, bf16[1024,128]{1,0:T(8,128)(2,1)} %copy-done.6, bf16[1024,128]{1,0:T(8,128)(2,1)} %copy-done.7, ...), custom_call_target="tpu_custom_call" | custom-call | bytes 3670016 | tf_op jit(solution)/shard_map/assemble/pallas_call | solution.py:87
  96.3 1.2 copy-done.9
  97.6 6.5 %project.3 = (bf16[2,2,128,512]{3,2,1,0:T(8,128)(2,1)}, bf16[4,256,128]{2,1,0:T(8,128)(2,1)}, bf16[4,80,256]{2,1,0:T(8,128)(2,1)}) custom-call(s32[1]{0:T(128)} %bitcast.1.device_ref.refs_0_, s32[16,16]{1,0:T(8,128)} %constant.28.clone.order_ref.refs_1_, bf16[128,1024]{1,0:T(8,128)(2,1)} %copy-done.1, bf16[128,1024]{1,0:T(8,128)(2,1)} %copy-done.11, ...), custom_call_target="tpu_custom_call" | custom-call | flops 1073741824 | bytes 4194304 | tf_op jit(solution)/shard_map/project/pallas_call | solution.py:274
  104.0 1.8 %attend.6 = (f32[2,80,512]{2,1,0:T(8,128)}, s32[1]{0:T(128)}) custom-call(s32[1]{0:T(128)} %get-tuple-element.56.length_ref, s32[1]{0:T(128)S(6)} %copy.18.span_ref, s32[1]{0:T(128)} %bitcast.2.tile_ref, bf16[4,8192,128]{2,1,0:T(8,128)(2,1)} %get-tuple-element.52.keys_hbm, bf16[4,80,8192]{2,1,0:T(8,128)(2,1)} %get-tuple-element.53.values_hbm, ...), custom_call_target="tpu_custom_call" | custom-call | flops 17179869184 | bytes 8388608 | tf_op jit(solution)/shard_map/attend/pallas_call | solution.py:433
  105.8 0.5 collective-permute-start.27
  106.4 1.4 collective-permute-done.27.refs_15_.refs_18_
  107.7 0.7 copy-done.17
  108.4 0.6 copy-done
  109.1 5.8 %finish.2 = (bf16[16,128,128]{2,1,0:T(8,128)(2,1)}, s32[1]{0:T(128)}) custom-call(s32[1]{0:T(128)S(6)} %copy.18.span_ref, s32[1]{0:T(128)} %bitcast.2.tile_ref, f32[2,80,512]{2,1,0:T(8,128)} %get-tuple-element.54.refs_0_, f32[2,80,512]{2,1,0:T(8,128)} %get-tuple-element.71.refs_1_, bf16[2,2,128,512]{3,2,1,0:T(8,128)(2,1)} %project.2.queries_hbm.refs_2_.refs_5_, ...), custom_call_target="tpu_custom_call" | custom-call | flops 536870912 | bytes 4194304 | tf_op jit(solution)/shard_map/finish/pallas_call | solution.py:564
  114.9 13.7 %collective-permute-start.28 = (bf16[16,128,128]{2,1,0:T(8,128)(2,1)}, bf16[16,128,128]{2,1,0:T(8,128)(2,1)S(1)}, u32[]{:S(2)}, u32[]{:S(2)}) collective-permute-start(bf16[16,128,128]{2,1,0:T(8,128)(2,1)} %get-tuple-element.90), channel_id=1, source_target_pairs={{0,1},{1,0},{2,3},{3,2},{4,5},{5,4},{6,7},{7,6},{8,9},{9,8},{10,11... | collective-permute-start | bytes 1572872 | tf_op jit(solution)/shard_map/ppermute | solution.py:693
  129.9 13.1 %attend.7 = (f32[2,80,512]{2,1,0:T(8,128)}, s32[1]{0:T(128)}) custom-call(s32[1]{0:T(128)S(6)} %add.28.length_ref, s32[1]{0:T(128)S(6)} %copy.18.span_ref, s32[1]{0:T(128)} %bitcast.tile_ref, bf16[4,8192,128]{2,1,0:T(8,128)(2,1)} %get-tuple-element.52.keys_hbm, bf16[4,80,8192]{2,1,0:T(8,128)(2,1)} %get-tuple-element.53.values_hbm, ...), custom_call_target="tpu_custom_call" | custom-call | flops 17179869184 | bytes 8388608 | tf_op jit(solution)/shard_map/attend/pallas_call | solution.py:433
  143.0 0.8 copy-done.26
  143.8 6.8 %finish.3 = (bf16[128,2048]{1,0:T(8,128)(2,1)}, s32[1]{0:T(128)}) custom-call(s32[1]{0:T(128)S(6)} %copy.18.span_ref, s32[1]{0:T(128)} %bitcast.tile_ref, s32[1]{0:T(128)} %bitcast.1.device_ref.refs_0_, s32[16,16]{1,0:T(8,128)} %constant.28.clone.order_ref.refs_1_, bf16[16,128,128]{2,1,0:T(8,128)(2,1)} %copy-done.26, ...), custom_call_target="tpu_custom_call" | custom-call | flops 536870912 | bytes 4194304 | tf_op jit(solution)/shard_map/finish/pallas_call | solution.py:564
  (94 shorter events, 5.1 us)
Async XLA Ops:
  1.0 24.8 %copy-start.10 = (bf16[128,512]{1,0:T(8,128)(2,1)}, bf16[128,512]{1,0:T(8,128)(2,1)S(1)}, u32[]{:S(2)}) copy-start(bf16[128,512]{1,0:T(8,128)(2,1)S(1)} %get-tuple-element.98.refs_0_) | copy-start | bytes 393220
  1.0 5.8 %collective-permute-start = (bf16[128,512]{1,0:T(8,128)(2,1)S(1)}, bf16[128,512]{1,0:T(8,128)(2,1)S(1)}, u32[]{:S(2)}, u32[]{:S(2)}) collective-permute-start(bf16[128,512]{1,0:T(8,128)(2,1)S(1)} %get-tuple-element.98.refs_0_), channel_id=1, source_target_pairs={{0,8},{2,10},{8,16},{10,18},{16,24},{18,26},{24,28},{26,30},{28,20... | collective-permute-start | bytes 393224 | tf_op jit(solution)/shard_map/ppermute | solution.py:108
  3.5 22.2 %copy-start.1 = (bf16[128,1024]{1,0:T(8,128)(2,1)}, bf16[128,1024]{1,0:T(8,128)(2,1)S(1)}, u32[]{:S(2)}) copy-start(bf16[128,1024]{1,0:T(8,128)(2,1)S(1)} %pad_maximum_fusion.1.refs_0_) | copy-start | bytes 786436
  3.5 22.3 %collective-permute-start.10 = (bf16[128,1024]{1,0:T(8,128)(2,1)S(1)}, bf16[128,1024]{1,0:T(8,128)(2,1)S(1)}, u32[]{:S(2)}, u32[]{:S(2)}) collective-permute-start(bf16[128,1024]{1,0:T(8,128)(2,1)S(1)} %pad_maximum_fusion.1.refs_0_), channel_id=1, source_target_pairs={{0,8},{2,10},{8,16},{10,18},{16,24},{18,26},{24,28},{26,30},{28,20... | collective-permute-start | bytes 786440 | tf_op jit(solution)/shard_map/ppermute | solution.py:108
  4.0 21.8 %collective-permute-start.11 = (bf16[128,1024]{1,0:T(8,128)(2,1)S(1)}, bf16[128,1024]{1,0:T(8,128)(2,1)S(1)}, u32[]{:S(2)}, u32[]{:S(2)}) collective-permute-start(bf16[128,1024]{1,0:T(8,128)(2,1)S(1)} %pad_maximum_fusion.1.refs_0_), channel_id=1, source_target_pairs={{8,0},{10,2},{16,8},{18,10},{24,16},{26,18},{28,24},{30,26},{20,28... | collective-permute-start | bytes 786440 | tf_op jit(solution)/shard_map/ppermute | solution.py:108
  5.6 8.7 %collective-permute-start.1 = (bf16[128,512]{1,0:T(8,128)(2,1)S(1)}, bf16[128,512]{1,0:T(8,128)(2,1)S(1)}, u32[]{:S(2)}, u32[]{:S(2)}) collective-permute-start(bf16[128,512]{1,0:T(8,128)(2,1)S(1)} %get-tuple-element.98.refs_0_), channel_id=1, source_target_pairs={{8,0},{10,2},{16,8},{18,10},{24,16},{26,18},{28,24},{30,26},{20,28... | collective-permute-start | bytes 393224 | tf_op jit(solution)/shard_map/ppermute | solution.py:108
  6.8 18.9 %copy-start.19 = (bf16[128,512]{1,0:T(8,128)(2,1)}, bf16[128,512]{1,0:T(8,128)(2,1)S(1)}, u32[]{:S(2)}) copy-start(bf16[128,512]{1,0:T(8,128)(2,1)S(1)} %collective-permute-done.refs_1_) | copy-start | bytes 393220
  6.8 9.1 %collective-permute-start.2 = (bf16[128,512]{1,0:T(8,128)(2,1)S(1)}, bf16[128,512]{1,0:T(8,128)(2,1)S(1)}, u32[]{:S(2)}, u32[]{:S(2)}) collective-permute-start(bf16[128,512]{1,0:T(8,128)(2,1)S(1)} %collective-permute-done.refs_1_), channel_id=1, source_target_pairs={{0,8},{2,10},{8,16},{10,18},{16,24},{18,26},{24,28},{26,30},{28,20... | collective-permute-start | bytes 393224 | tf_op jit(solution)/shard_map/ppermute | solution.py:108
  8.9 37.1 %collective-permute-start.9 = (bf16[128,2048]{1,0:T(8,128)(2,1)}, bf16[128,2048]{1,0:T(8,128)(2,1)}, u32[]{:S(2)}, u32[]{:S(2)}) collective-permute-start(bf16[128,2048]{1,0:T(8,128)(2,1)} %param.10), channel_id=1, source_target_pairs={{0,1},{1,0},{2,3},{3,2},{4,5},{5,4},{6,7},{7,6},{8,9},{9,8},{10,11... | collective-permute-start | bytes 1572872 | tf_op jit(solution)/shard_map/ppermute | solution.py:624
  14.3 11.4 %copy-start.20 = (bf16[128,512]{1,0:T(8,128)(2,1)}, bf16[128,512]{1,0:T(8,128)(2,1)S(1)}, u32[]{:S(2)}) copy-start(bf16[128,512]{1,0:T(8,128)(2,1)S(1)} %collective-permute-done.1.refs_2_) | copy-start | bytes 393220
  14.3 14.2 %collective-permute-start.3 = (bf16[128,512]{1,0:T(8,128)(2,1)S(1)}, bf16[128,512]{1,0:T(8,128)(2,1)S(1)}, u32[]{:S(2)}, u32[]{:S(2)}) collective-permute-start(bf16[128,512]{1,0:T(8,128)(2,1)S(1)} %collective-permute-done.1.refs_2_), channel_id=1, source_target_pairs={{8,0},{10,2},{16,8},{18,10},{24,16},{26,18},{28,24},{30,26},{20,28... | collective-permute-start | bytes 393224 | tf_op jit(solution)/shard_map/ppermute | solution.py:108
  15.9 9.9 %copy-start.21 = (bf16[128,512]{1,0:T(8,128)(2,1)}, bf16[128,512]{1,0:T(8,128)(2,1)S(1)}, u32[]{:S(2)}) copy-start(bf16[128,512]{1,0:T(8,128)(2,1)S(1)} %collective-permute-done.2.refs_3_) | copy-start | bytes 393220
  15.9 14.3 %collective-permute-start.4 = (bf16[128,512]{1,0:T(8,128)(2,1)S(1)}, bf16[128,512]{1,0:T(8,128)(2,1)S(1)}, u32[]{:S(2)}, u32[]{:S(2)}) collective-permute-start(bf16[128,512]{1,0:T(8,128)(2,1)S(1)} %collective-permute-done.2.refs_3_), channel_id=1, source_target_pairs={{0,8},{2,10},{8,16},{10,18},{16,24},{18,26},{24,28},{26,30},{28,20... | collective-permute-start | bytes 393224 | tf_op jit(solution)/shard_map/ppermute | solution.py:108
  25.8 14.6 %copy-start.11 = (bf16[128,1024]{1,0:T(8,128)(2,1)}, bf16[128,1024]{1,0:T(8,128)(2,1)S(1)}, u32[]{:S(2)}) copy-start(bf16[128,1024]{1,0:T(8,128)(2,1)S(1)} %collective-permute-done.10.refs_1_) | copy-start | bytes 786436
  25.8 14.5 %copy-start.12 = (bf16[128,1024]{1,0:T(8,128)(2,1)}, bf16[128,1024]{1,0:T(8,128)(2,1)S(1)}, u32[]{:S(2)}) copy-start(bf16[128,1024]{1,0:T(8,128)(2,1)S(1)} %collective-permute-done.11.refs_2_) | copy-start | bytes 786436
  25.8 17.6 %collective-permute-start.12 = (bf16[128,1024]{1,0:T(8,128)(2,1)S(1)}, bf16[128,1024]{1,0:T(8,128)(2,1)S(1)}, u32[]{:S(2)}, u32[]{:S(2)}) collective-permute-start(bf16[128,1024]{1,0:T(8,128)(2,1)S(1)} %collective-permute-done.10.refs_1_), channel_id=1, source_target_pairs={{0,8},{2,10},{8,16},{10,18},{16,24},{18,26},{24,28},{26,30},{28,20... | collective-permute-start | bytes 786440 | tf_op jit(solution)/shard_map/ppermute | solution.py:108
  26.3 17.1 %collective-permute-start.13 = (bf16[128,1024]{1,0:T(8,128)(2,1)S(1)}, bf16[128,1024]{1,0:T(8,128)(2,1)S(1)}, u32[]{:S(2)}, u32[]{:S(2)}) collective-permute-start(bf16[128,1024]{1,0:T(8,128)(2,1)S(1)} %collective-permute-done.11.refs_2_), channel_id=1, source_target_pairs={{8,0},{10,2},{16,8},{18,10},{24,16},{26,18},{28,24},{30,26},{20,28... | collective-permute-start | bytes 786440 | tf_op jit(solution)/shard_map/ppermute | solution.py:108
  28.6 11.8 %copy-start.22 = (bf16[128,512]{1,0:T(8,128)(2,1)}, bf16[128,512]{1,0:T(8,128)(2,1)S(1)}, u32[]{:S(2)}) copy-start(bf16[128,512]{1,0:T(8,128)(2,1)S(1)} %collective-permute-done.3.refs_4_) | copy-start | bytes 393220
  28.6 11.8 %collective-permute-start.5 = (bf16[128,512]{1,0:T(8,128)(2,1)S(1)}, bf16[128,512]{1,0:T(8,128)(2,1)S(1)}, u32[]{:S(2)}, u32[]{:S(2)}) collective-permute-start(bf16[128,512]{1,0:T(8,128)(2,1)S(1)} %collective-permute-done.3.refs_4_), channel_id=1, source_target_pairs={{8,0},{10,2},{16,8},{18,10},{24,16},{26,18},{28,24},{30,26},{20,28... | collective-permute-start | bytes 393224 | tf_op jit(solution)/shard_map/ppermute | solution.py:108
  30.2 10.1 %copy-start.23 = (bf16[128,512]{1,0:T(8,128)(2,1)}, bf16[128,512]{1,0:T(8,128)(2,1)S(1)}, u32[]{:S(2)}) copy-start(bf16[128,512]{1,0:T(8,128)(2,1)S(1)} %collective-permute-done.4.refs_5_) | copy-start | bytes 393220
  30.2 15.3 %collective-permute-start.6 = (bf16[128,512]{1,0:T(8,128)(2,1)S(1)}, bf16[128,512]{1,0:T(8,128)(2,1)S(1)}, u32[]{:S(2)}, u32[]{:S(2)}) collective-permute-start(bf16[128,512]{1,0:T(8,128)(2,1)S(1)} %collective-permute-done.4.refs_5_), channel_id=1, source_target_pairs={{0,8},{2,10},{8,16},{10,18},{16,24},{18,26},{24,28},{26,30},{28,20... | collective-permute-start | bytes 393224 | tf_op jit(solution)/shard_map/ppermute | solution.py:108
  31.5 14.0 %copy-start.2 = (bf16[1024,128]{1,0:T(8,128)(2,1)S(1)}, bf16[1024,128]{1,0:T(8,128)(2,1)}, u32[]{:S(2)}) copy-start(bf16[1024,128]{1,0:T(8,128)(2,1)} %refs_9_.1) | copy-start | bytes 786436
  40.4 8.7 %copy-start.29 = (f32[2048]{0:T(1024)S(1)}, f32[2048]{0:T(1024)}, u32[]{:S(2)}) copy-start(f32[2048]{0:T(1024)} %param.11) | copy-start | bytes 24580
  41.0 5.0 %copy-start.25 = (bf16[128,2048]{1,0:T(8,128)(2,1)S(1)}, bf16[128,2048]{1,0:T(8,128)(2,1)}, u32[]{:S(2)}) copy-start(bf16[128,2048]{1,0:T(8,128)(2,1)} %param.10) | copy-start | bytes 1572868
  43.3 7.1 %collective-permute-start.7 = (bf16[896,512]{1,0:T(8,128)(2,1)}, bf16[896,512]{1,0:T(8,128)(2,1)S(1)}, u32[]{:S(2)}, u32[]{:S(2)}) collective-permute-start(bf16[896,512]{1,0:T(8,128)(2,1)} %assemble.3), channel_id=1, source_target_pairs={{0,2},{2,0},{4,6},{6,4},{8,10},{10,8},{12,14},{14,12},{16,18},{18,... | collective-permute-start | bytes 2752520 | tf_op jit(solution)/shard_map/ppermute | solution.py:108
  43.4 7.0 %copy-start.13 = (bf16[128,1024]{1,0:T(8,128)(2,1)}, bf16[128,1024]{1,0:T(8,128)(2,1)S(1)}, u32[]{:S(2)}) copy-start(bf16[128,1024]{1,0:T(8,128)(2,1)S(1)} %collective-permute-done.12.refs_3_) | copy-start | bytes 786436
  43.4 7.0 %copy-start.14 = (bf16[128,1024]{1,0:T(8,128)(2,1)}, bf16[128,1024]{1,0:T(8,128)(2,1)S(1)}, u32[]{:S(2)}) copy-start(bf16[128,1024]{1,0:T(8,128)(2,1)S(1)} %collective-permute-done.13.refs_4_) | copy-start | bytes 786436
  43.5 12.3 %collective-permute-start.14 = (bf16[128,1024]{1,0:T(8,128)(2,1)S(1)}, bf16[128,1024]{1,0:T(8,128)(2,1)S(1)}, u32[]{:S(2)}, u32[]{:S(2)}) collective-permute-start(bf16[128,1024]{1,0:T(8,128)(2,1)S(1)} %collective-permute-done.12.refs_3_), channel_id=1, source_target_pairs={{0,8},{2,10},{8,16},{10,18},{16,24},{18,26},{24,28},{26,30},{28,20... | collective-permute-start | bytes 786440 | tf_op jit(solution)/shard_map/ppermute | solution.py:108
  44.0 11.8 %collective-permute-start.15 = (bf16[128,1024]{1,0:T(8,128)(2,1)S(1)}, bf16[128,1024]{1,0:T(8,128)(2,1)S(1)}, u32[]{:S(2)}, u32[]{:S(2)}) collective-permute-start(bf16[128,1024]{1,0:T(8,128)(2,1)S(1)} %collective-permute-done.13.refs_4_), channel_id=1, source_target_pairs={{8,0},{10,2},{16,8},{18,10},{24,16},{26,18},{28,24},{30,26},{20,28... | collective-permute-start | bytes 786440 | tf_op jit(solution)/shard_map/ppermute | solution.py:108
  45.5 4.9 %copy-start.27 = (bf16[128,512]{1,0:T(8,128)(2,1)}, bf16[128,512]{1,0:T(8,128)(2,1)S(1)}, u32[]{:S(2)}) copy-start(bf16[128,512]{1,0:T(8,128)(2,1)S(1)} %collective-permute-done.6.refs_7_) | copy-start | bytes 393220
  45.5 12.3 %collective-permute-start.19 = (bf16[1024,128]{1,0:T(8,128)(2,1)S(1)}, bf16[1024,128]{1,0:T(8,128)(2,1)S(1)}, u32[]{:S(2)}, u32[]{:S(2)}) collective-permute-start(bf16[1024,128]{1,0:T(8,128)(2,1)S(1)} %copy-done.2), channel_id=1, source_target_pairs={{0,8},{2,10},{8,16},{10,18},{16,24},{18,26},{24,28},{26,30},{28,20... | collective-permute-start | bytes 786440 | tf_op jit(solution)/shard_map/ppermute | solution.py:108
  46.0 1.4 collective-permute-start.8
  47.5 10.5 %collective-permute-start.20 = (bf16[1024,128]{1,0:T(8,128)(2,1)S(1)}, bf16[1024,128]{1,0:T(8,128)(2,1)S(1)}, u32[]{:S(2)}, u32[]{:S(2)}) collective-permute-start(bf16[1024,128]{1,0:T(8,128)(2,1)S(1)} %copy-done.2), channel_id=1, source_target_pairs={{8,0},{10,2},{16,8},{18,10},{24,16},{26,18},{28,24},{30,26},{20,28... | collective-permute-start | bytes 786440 | tf_op jit(solution)/shard_map/ppermute | solution.py:108
  55.8 5.8 %copy-start.15 = (bf16[128,1024]{1,0:T(8,128)(2,1)}, bf16[128,1024]{1,0:T(8,128)(2,1)S(1)}, u32[]{:S(2)}) copy-start(bf16[128,1024]{1,0:T(8,128)(2,1)S(1)} %collective-permute-done.14.refs_5_) | copy-start | bytes 786436
  55.8 5.8 %copy-start.16 = (bf16[128,1024]{1,0:T(8,128)(2,1)}, bf16[128,1024]{1,0:T(8,128)(2,1)S(1)}, u32[]{:S(2)}) copy-start(bf16[128,1024]{1,0:T(8,128)(2,1)S(1)} %collective-permute-done.15.refs_6_) | copy-start | bytes 786436
  55.8 9.3 %collective-permute-start.16 = (bf16[128,1024]{1,0:T(8,128)(2,1)S(1)}, bf16[128,1024]{1,0:T(8,128)(2,1)}, u32[]{:S(2)}, u32[]{:S(2)}) collective-permute-start(bf16[128,1024]{1,0:T(8,128)(2,1)S(1)} %collective-permute-done.15.refs_6_), channel_id=1, source_target_pairs={{8,0},{10,2},{16,8},{18,10},{24,16},{26,18},{28,24},{30,26},{20,28... | collective-permute-start | bytes 786440 | tf_op jit(solution)/shard_map/ppermute | solution.py:108
  58.0 7.7 %collective-permute-start.21 = (bf16[1024,128]{1,0:T(8,128)(2,1)S(1)}, bf16[1024,128]{1,0:T(8,128)(2,1)S(1)}, u32[]{:S(2)}, u32[]{:S(2)}) collective-permute-start(bf16[1024,128]{1,0:T(8,128)(2,1)S(1)} %collective-permute-done.19.refs_1_.refs_7_.refs_10_), channel_id=1, source_target_pairs={{0,8},{2,10},{8,16},{10,18},{16,24},{18,26},{24,28},{26,30},{28,20... | collective-permute-start | bytes 786440 | tf_op jit(solution)/shard_map/ppermute | solution.py:108
  58.4 11.5 %collective-permute-start.22 = (bf16[1024,128]{1,0:T(8,128)(2,1)S(1)}, bf16[1024,128]{1,0:T(8,128)(2,1)S(1)}, u32[]{:S(2)}, u32[]{:S(2)}) collective-permute-start(bf16[1024,128]{1,0:T(8,128)(2,1)S(1)} %collective-permute-done.20.refs_2_.refs_8_.refs_11_), channel_id=1, source_target_pairs={{8,0},{10,2},{16,8},{18,10},{24,16},{26,18},{28,24},{30,26},{20,28... | collective-permute-start | bytes 786440 | tf_op jit(solution)/shard_map/ppermute | solution.py:108
  64.3 32.0 %collective-permute-start.17 = (bf16[896,1024]{1,0:T(8,128)(2,1)}, bf16[896,1024]{1,0:T(8,128)(2,1)S(1)}, u32[]{:S(2)}, u32[]{:S(2)}) collective-permute-start(bf16[896,1024]{1,0:T(8,128)(2,1)} %assemble.4), channel_id=1, source_target_pairs={{0,2},{2,0},{4,6},{6,4},{8,10},{10,8},{12,14},{14,12},{16,18},{18,... | collective-permute-start | bytes 5505032 | tf_op jit(solution)/shard_map/ppermute | solution.py:108
  65.1 31.2 %collective-permute-start.18 = (bf16[128,1024]{1,0:T(8,128)(2,1)}, bf16[128,1024]{1,0:T(8,128)(2,1)}, u32[]{:S(2)}, u32[]{:S(2)}) collective-permute-start(bf16[128,1024]{1,0:T(8,128)(2,1)} %collective-permute-done.16.refs_7_), channel_id=1, source_target_pairs={{0,2},{2,0},{4,6},{6,4},{8,10},{10,8},{12,14},{14,12},{16,18},{18,... | collective-permute-start | bytes 786440 | tf_op jit(solution)/shard_map/ppermute | solution.py:108
  65.7 26.8 %copy-start.5 = (bf16[1024,128]{1,0:T(8,128)(2,1)}, bf16[1024,128]{1,0:T(8,128)(2,1)S(1)}, u32[]{:S(2)}) copy-start(bf16[1024,128]{1,0:T(8,128)(2,1)S(1)} %collective-permute-done.21.refs_3_.refs_9_.refs_12_) | copy-start | bytes 786436
  69.9 22.6 %copy-start.6 = (bf16[1024,128]{1,0:T(8,128)(2,1)}, bf16[1024,128]{1,0:T(8,128)(2,1)S(1)}, u32[]{:S(2)}) copy-start(bf16[1024,128]{1,0:T(8,128)(2,1)S(1)} %collective-permute-done.22.refs_4_.refs_10_.refs_13_) | copy-start | bytes 786436
  69.9 22.6 %collective-permute-start.23 = (bf16[1024,128]{1,0:T(8,128)(2,1)S(1)}, bf16[1024,128]{1,0:T(8,128)(2,1)S(1)}, u32[]{:S(2)}, u32[]{:S(2)}) collective-permute-start(bf16[1024,128]{1,0:T(8,128)(2,1)S(1)} %collective-permute-done.21.refs_3_.refs_9_.refs_12_), channel_id=1, source_target_pairs={{0,8},{2,10},{8,16},{10,18},{16,24},{18,26},{24,28},{26,30},{28,20... | collective-permute-start | bytes 786440 | tf_op jit(solution)/shard_map/ppermute | solution.py:108
  77.6 14.9 %collective-permute-start.24 = (bf16[1024,128]{1,0:T(8,128)(2,1)S(1)}, bf16[1024,128]{1,0:T(8,128)(2,1)S(1)}, u32[]{:S(2)}, u32[]{:S(2)}) collective-permute-start(bf16[1024,128]{1,0:T(8,128)(2,1)S(1)} %collective-permute-done.22.refs_4_.refs_10_.refs_13_), channel_id=1, source_target_pairs={{8,0},{10,2},{16,8},{18,10},{24,16},{26,18},{28,24},{30,26},{20,28... | collective-permute-start | bytes 786440 | tf_op jit(solution)/shard_map/ppermute | solution.py:108
  92.6 13.2 %collective-permute-start.25 = (bf16[1024,128]{1,0:T(8,128)(2,1)S(1)}, bf16[1024,128]{1,0:T(8,128)(2,1)}, u32[]{:S(2)}, u32[]{:S(2)}) collective-permute-start(bf16[1024,128]{1,0:T(8,128)(2,1)S(1)} %collective-permute-done.23.refs_5_.refs_11_.refs_14_), channel_id=1, source_target_pairs={{0,8},{2,10},{8,16},{10,18},{16,24},{18,26},{24,28},{26,30},{28,20... | collective-permute-start | bytes 786440 | tf_op jit(solution)/shard_map/ppermute | solution.py:108
  96.2 11.5 %collective-permute-start.26 = (bf16[7168,128]{1,0:T(8,128)(2,1)}, bf16[7168,128]{1,0:T(8,128)(2,1)S(1)}, u32[]{:S(2)}, u32[]{:S(2)}) collective-permute-start(bf16[7168,128]{1,0:T(8,128)(2,1)} %assemble.5), channel_id=1, source_target_pairs={{0,2},{2,0},{4,6},{6,4},{8,10},{10,8},{12,14},{14,12},{16,18},{18,... | collective-permute-start | bytes 5505032 | tf_op jit(solution)/shard_map/ppermute | solution.py:108
  105.8 1.9 %collective-permute-start.27 = (bf16[1024,128]{1,0:T(8,128)(2,1)}, bf16[1024,128]{1,0:T(8,128)(2,1)S(1)}, u32[]{:S(2)}, u32[]{:S(2)}) collective-permute-start(bf16[1024,128]{1,0:T(8,128)(2,1)} %collective-permute-done.25.refs_13_.refs_16_), channel_id=1, source_target_pairs={{0,2},{2,0},{4,6},{6,4},{8,10},{10,8},{12,14},{14,12},{16,18},{18,... | collective-permute-start | bytes 786440 | tf_op jit(solution)/shard_map/ppermute | solution.py:108
  114.9 28.1 %collective-permute-start.28 = (bf16[16,128,128]{2,1,0:T(8,128)(2,1)}, bf16[16,128,128]{2,1,0:T(8,128)(2,1)S(1)}, u32[]{:S(2)}, u32[]{:S(2)}) collective-permute-start(bf16[16,128,128]{2,1,0:T(8,128)(2,1)} %get-tuple-element.90), channel_id=1, source_target_pairs={{0,1},{1,0},{2,3},{3,2},{4,5},{5,4},{6,7},{7,6},{8,9},{9,8},{10,11... | collective-permute-start | bytes 1572872 | tf_op jit(solution)/shard_map/ppermute | solution.py:693
  (11 other events, 17.8 us)

commit v7 on v6

--- a/solution.py
+++ b/solution.py
@@ -143,11 +143,6 @@
     key_ref, value_ref, wide = refs[pages_step + aliased :]
     step = pl.program_id(0)
     half = width // 2
-    rows = value_ref.shape[1]
-    pick_row = lax.broadcasted_iota(jnp.int32, (rows, width), 0)
-    pick_lane = lax.broadcasted_iota(jnp.int32, (rows, width), 1)
-    pick = jnp.where(pick_lane == pick_row + half, 1.0, 0.0).astype(jnp.bfloat16)
-    ones = jnp.where(lax.broadcasted_iota(jnp.int32, (rows, page), 0) == half, 1.0, 0.0)
     for i in range(pages_step):
         wide[i] = pages[i][0].astype(jnp.float32)
         first = (first_page + step * pages_step + i) * page
@@ -159,13 +154,8 @@
             key_ref[h, pl.ds(i * page, page), :] = jnp.where(lane < half, rows_h, bias).astype(
                 jnp.bfloat16
             )
-            turned = lax.dot_general(
-                pick,
-                rows_h.astype(jnp.bfloat16),
-                (((1,), (1,)), ((), ())),
-                preferred_element_type=jnp.float32,
-            )
-            value_ref[h, :, pl.ds(i * page, page)] = (turned + ones).astype(jnp.bfloat16)
+            turned = with_ones(jnp.transpose(rows_h)[half:])
+            value_ref[h, :, pl.ds(i * page, page)] = turned.astype(jnp.bfloat16)
 
 
 def with_ones(turned):
@@ -222,15 +212,30 @@
     )
 
 
-def project_kernel(heads, new_heads, group, dim, blocks, device_ref, order_ref, *refs):
+def project_kernel(heads, new_heads, group, dim, blocks, fresh, device_ref, order_ref, *refs):
     device = device_ref[0]
+    if fresh:
+        rank_ref, gain_ref, own_hbm, other_hbm, *refs = refs
+        *refs, fresh_sems = refs
     chunks = refs[:blocks]
-    normed_hbm, cos_ref, sin_ref, query_ref = refs[blocks : blocks + 4]
+    if fresh:
+        cos_ref, sin_ref, query_ref, normed_out = refs[blocks : blocks + 4]
+    else:
+        normed_hbm, cos_ref, sin_ref, query_ref = refs[blocks : blocks + 4]
     source, normed_ref, sems = refs[-3:]
     sources = chunks if blocks == 1 else chunk_sources(chunks)
     count = len(sources)
     rows = source.shape[0] // count
-    copies = [pltpu.make_async_copy(normed_hbm, normed_ref, sems.at[count])]
+    if fresh:
+        size = own_hbm.shape[0]
+        first = pl.ds(pl.multiple_of(rank_ref[0] * size, size), size)
+        second = pl.ds(pl.multiple_of((1 - rank_ref[0]) * size, size), size)
+        copies = [
+            pltpu.make_async_copy(own_hbm, normed_ref.at[first], fresh_sems.at[0]),
+            pltpu.make_async_copy(other_hbm, normed_ref.at[second], fresh_sems.at[1]),
+        ]
+    else:
+        copies = [pltpu.make_async_copy(normed_hbm, normed_ref, sems.at[count])]
     for k in range(count):
         start = pl.multiple_of(order_ref[device, k] * rows, rows)
         copies.append(pltpu.make_async_copy(sources[k], source.at[pl.ds(start, rows)], sems.at[k]))
@@ -239,6 +244,15 @@
     cosine, sines = cos_ref[...], sin_ref[...]
     tokens = cosine.shape[1]
     width = group * dim
+    if fresh:
+        for copy in copies[:2]:
+            copy.wait()
+        hidden = normed_ref[...].astype(jnp.float32)
+        scale = lax.rsqrt(jnp.mean(hidden * hidden, axis=-1, keepdims=True) + epsilon)
+        normed = (hidden * scale * gain_ref[...]).astype(jnp.bfloat16)
+        normed_out[...] = normed
+        normed_ref[...] = normed
+        copies = copies[2:]
     for copy in copies:
         copy.wait()
     normed = normed_ref[...]
@@ -266,21 +280,30 @@
 
 
 def project(normed, chunks, device, order, cosine, sines, heads, new_heads, group, dim):
-    tokens, width = normed.shape
+    fresh = isinstance(normed, tuple)
+    inputs = [*normed[2:], *chunks] if fresh else [*chunks, normed]
+    scalars = list(normed[:2]) if fresh else []
+    tokens, width = (2 * normed[2].shape[0], normed[2].shape[1]) if fresh else normed.shape
     columns = chunks[0].shape[1]
     outs = [(heads, tokens // token_tile, 2 * dim, group * token_tile)]
     if new_heads:
         outs += [(new_heads, tokens, 2 * dim), (new_heads, dim + 16, tokens)]
+    if fresh:
+        outs.append((tokens, width))
     return pl.pallas_call(
-        functools.partial(project_kernel, heads, new_heads, group, dim, len(chunks)),
-        in_specs=[smem()] * 2 + [anywhere()] * (len(chunks) + 1) + [vmem()] * 2,
+        functools.partial(project_kernel, heads, new_heads, group, dim, len(chunks), fresh),
+        in_specs=[smem()] * 2
+        + ([smem(), vmem()] if fresh else [])
+        + [anywhere()] * len(inputs)
+        + [vmem()] * 2,
         out_specs=[vmem()] * len(outs),
         out_shape=[jax.ShapeDtypeStruct(shape, jnp.bfloat16) for shape in outs],
         scratch_shapes=[
             pltpu.VMEM((width, columns), jnp.bfloat16),
             pltpu.VMEM((tokens, width), jnp.bfloat16),
             pltpu.SemaphoreType.DMA((order.shape[1] + 1,)),
-        ],
+        ]
+        + ([pltpu.SemaphoreType.DMA((2,))] if fresh else []),
         cost_estimate=pl.CostEstimate(
             flops=2 * tokens * width * columns,
             bytes_accessed=2 * width * columns,
@@ -288,7 +311,7 @@
         ),
         compiler_params=params(60),
         name="project",
-    )(device, order, *chunks, normed, cosine, sines)
+    )(device, order, *scalars, *inputs, cosine, sines)
 
 
 def column_max(scores):
@@ -622,9 +645,6 @@
         ring_second = Ring(jnp.concatenate([w_query[:, cut:], w_new], axis=1), tables)
         ring_out = Ring(w_out, tables)
         other = lax.ppermute(tokens, "tp", swap)
-        whole = jnp.concatenate(
-            [jnp.where(rank == 0, tokens, other), jnp.where(rank == 0, other, tokens)], axis=0
-        )
         parts = 2
         state = ()
         ring_first.step()
@@ -645,11 +665,12 @@
         second_chunks = [gather(jnp.concatenate([w_query, w_new], axis=1))]
         whole = lax.all_gather(tokens, "tp", axis=0, tiled=True)
         keys, values = prepare(kv_cache, table, length, 0, 1, ())
-    hidden = whole.astype(jnp.float32)
-    normed = (
-        hidden * lax.rsqrt(jnp.mean(hidden * hidden, axis=-1, keepdims=True) + epsilon) * norm_gain
-    ).astype(jnp.bfloat16)
-    positions = length[0] + jnp.arange(normed.shape[0], dtype=jnp.int32)
+    if not fast:
+        hidden = whole.astype(jnp.float32)
+        normed = (
+            hidden * lax.rsqrt(jnp.mean(hidden * hidden, axis=-1, keepdims=True) + epsilon) * norm_gain
+        ).astype(jnp.bfloat16)
+    positions = length[0] + jnp.arange(tp_count * own_rows, dtype=jnp.int32)
     cosine, sines = rope_tables(positions, dim)
     queries = []
 
@@ -674,7 +695,10 @@
         summed = lax.psum_scatter(partial, "tp", scatter_dimension=0, tiled=True)
         return (residual_scale * summed.astype(jnp.float32)).astype(jnp.bfloat16)
     theirs, ours = (1 - rank).reshape(1), rank.reshape(1)
-    soon = project(normed, first_chunks, place, order, cosine, sines, early, 0, group, dim)[0]
+    fresh = (rank.reshape(1), norm_gain.reshape(1, -1), tokens, other)
+    soon, normed = project(
+        fresh, first_chunks, place, order, cosine, sines, early, 0, group, dim
+    )
     second_end = ring_second.last(False, soon)
     ring_out.step(soon)
     sent_first, token = attend_tile(theirs, soon, early, 0, length)

time: 154 us -> 156 us (1.013)
  Pallas kernels: 78.9 us -> 102 us
  starting transfers between devices: 46.1 us -> 23.5 us
  waiting for transfers between devices: 10.8 us -> 15.1 us
  other arithmetic: 5.45 us -> 2.7 us
    pallas_call x4, Pallas kernels: 30.1 us -> 54.5 us  [attend(): pl.pallas_call(functools.partial(attend_kernel, heads, first_query, first...]
    ppermute x1, starting transfers between devices: 13.7 us -> 0.6 us  [body(): received = lax.ppermute(sent, 'tp', swap)]
    ppermute x27, starting transfers between devices: 30.9 us -> 21.5 us  [move(): return lax.ppermute(value, 'req', pairs)]
    ppermute x27, waiting for transfers between devices: 10.8 us -> 15.1 us  [move(): return lax.ppermute(value, 'req', pairs)]
    pallas_call x2, Pallas kernels: 17.6 us -> 16 us  [prepare(): pl.pallas_call(functools.partial(prepare_kernel, heads, page, width, page...]
    unnamed x61 -> x59, local copies, waits for them, and re-layouts: 5.95 us -> 6.65 us
  transfers between devices with their start and end apart: 29 -> 29, of which waited for: 8 -> 7; matrix products, arithmetic and copies ran while one was open for 4% -> 2% of each run, Pallas kernels for 44% -> 57%
where the time goes in v7:
time: 156 us; the launch traced here: 154 us
  Pallas kernels  102 us (65%)
  starting transfers between devices  23.5 us (15%)
  waiting for transfers between devices  15.1 us (10%)
  local copies, waits for them, and re-layouts  7.63 us (5%)
  other arithmetic  2.7 us (2%)
  between operations  2.65 us (2%)
    pallas_call x4, Pallas kernels, attend(): pl.pallas_call(functools.partial(attend_kernel, heads, first_query, first...  54.5 us
    ppermute x27, starting transfers between devices, move(): return lax.ppermute(value, 'req', pairs)  21.5 us
    pallas_call x2, Pallas kernels, prepare(): pl.pallas_call(functools.partial(prepare_kernel, heads, page, width, page...  16 us
    ppermute x27, waiting for transfers between devices, move(): return lax.ppermute(value, 'req', pairs)  15.1 us
    pallas_call x2, Pallas kernels, finish(): pl.pallas_call(functools.partial(finish_kernel, heads, len(states), group...  12.6 us
    pallas_call x2, Pallas kernels, project(): pl.pallas_call(functools.partial(project_kernel, heads, new_heads, group,...  11.6 us
    pallas_call x3, Pallas kernels, assemble(): pl.pallas_call(assemble_kernel, in_specs=[anywhere()] * len(blocks), out_...  7.68 us
    unnamed x59, local copies, waits for them, and re-layouts  6.65 us
  transfers between devices with their start and end apart: 29, of which 7 were waited for; matrix products, arithmetic and copies ran while one was open for 2% of the time, Pallas kernels for 57%

profile of v7, /device:TPU:24, one launch (start us, length us, event | category | flops | bytes accessed | tf_op | source)
XLA Modules:
  0.0 153.9 jit_solution(9133426366562147590)
XLA Ops:
  0.0 1.0 fusion.1
  1.0 1.6 %collective-permute-start.1 = (bf16[128,512]{1,0:T(8,128)(2,1)S(1)}, bf16[128,512]{1,0:T(8,128)(2,1)S(1)}, u32[]{:S(2)}, u32[]{:S(2)}) collective-permute-start(bf16[128,512]{1,0:T(8,128)(2,1)S(1)} %get-tuple-element.100.refs_0_.refs_4_), channel_id=1, source_target_pairs={{0,8},{2,10},{8,16},{10,18},{16,24},{18,26},{24,28},{26,30},{28,20... | collective-permute-start | bytes 393224 | tf_op jit(solution)/shard_map/ppermute | solution.py:108
  2.6 0.5 collective-permute-start.2
  3.1 3.2 %collective-permute-done.1.refs_1_.refs_5_ = bf16[128,512]{1,0:T(8,128)(2,1)S(1)} collective-permute-done((bf16[128,512]{1,0:T(8,128)(2,1)S(1)}, bf16[128,512]{1,0:T(8,128)(2,1)S(1)}, u32[]{:S(2)}, u32[]{:S(2)}) %collective-permute-start.1) | collective-permute-done | bytes 131104 | tf_op jit(solution)/shard_map/ppermute | solution.py:108
  6.3 1.5 collective-permute-start.3
  7.8 0.5 collective-permute-start.4
  8.3 2.9 %collective-permute-done.3.refs_3_.refs_7_ = bf16[128,512]{1,0:T(8,128)(2,1)S(1)} collective-permute-done((bf16[128,512]{1,0:T(8,128)(2,1)S(1)}, bf16[128,512]{1,0:T(8,128)(2,1)S(1)}, u32[]{:S(2)}, u32[]{:S(2)}) %collective-permute-start.3) | collective-permute-done | bytes 131104 | tf_op jit(solution)/shard_map/ppermute | solution.py:108
  11.3 1.5 collective-permute-start.5
  13.3 2.9 %collective-permute-done.5.refs_5_.refs_9_ = bf16[128,512]{1,0:T(8,128)(2,1)S(1)} collective-permute-done((bf16[128,512]{1,0:T(8,128)(2,1)S(1)}, bf16[128,512]{1,0:T(8,128)(2,1)S(1)}, u32[]{:S(2)}, u32[]{:S(2)}) %collective-permute-start.5) | collective-permute-done | bytes 131104 | tf_op jit(solution)/shard_map/ppermute | solution.py:108
  16.2 1.5 collective-permute-done.6.refs_6_.refs_10_
  17.8 0.6 copy-done.24
  18.5 2.2 %assemble.3 = bf16[896,512]{1,0:T(8,128)(2,1)} custom-call(bf16[128,512]{1,0:T(8,128)(2,1)} %copy-done.10, bf16[128,512]{1,0:T(8,128)(2,1)} %copy-done.19, bf16[128,512]{1,0:T(8,128)(2,1)} %copy-done.20, bf16[128,512]{1,0:T(8,128)(2,1)} %copy-done.21, bf16[128,512]{1,0:T(8,128)(2,1)} %copy-done.22, bf16[128,512]{1,0:T(8,128)(2,1)} %copy-done.23, ...), custom_call_target="tpu_custom_call" | custom-call | bytes 1835008 | tf_op jit(solution)/shard_map/assemble/pallas_call | solution.py:87
  20.8 0.9 copy.15
  21.7 0.6 collective-permute-start.10
  22.4 1.4 collective-permute-start.11
  23.8 1.5 collective-permute-start
  25.3 0.6 collective-permute-start.7
  25.9 1.3 fusion
  27.2 7.9 %prepare.2 = (bf16[4,8192,128]{2,1,0:T(8,128)(2,1)}, bf16[4,80,8192]{2,1,0:T(8,128)(2,1)}) custom-call(s32[64]{0:T(128)} %bitcast.30, s32[1]{0:T(128)} %bitcast.3.length_ref, bf16[64,512,128]{2,1,0:T(8,128)(2,1)} %bitcast.11, bf16[64,512,128]{2,1,0:T(8,128)(2,1)} %bitcast.12, bf16[64,512,128]{2,1,0:T(8,128)(2,1)} %bitcast.13, ...), custom_call_target="tpu_custom_call" | custom-call | bytes 12582912 | tf_op jit(solution)/shard_map/prepare/pallas_call | solution.py:178
  35.6 1.6 %collective-permute-start.13 = (bf16[128,1024]{1,0:T(8,128)(2,1)S(1)}, bf16[128,1024]{1,0:T(8,128)(2,1)S(1)}, u32[]{:S(2)}, u32[]{:S(2)}) collective-permute-start(bf16[128,1024]{1,0:T(8,128)(2,1)S(1)} %collective-permute-done.11.refs_2_), channel_id=1, source_target_pairs={{8,0},{10,2},{16,8},{18,10},{24,16},{26,18},{28,24},{30,26},{20,28... | collective-permute-start | bytes 786440 | tf_op jit(solution)/shard_map/ppermute | solution.py:108
  38.0 0.6 add_convert_fusion
  38.5 8.0 %prepare.3 = (bf16[4,8192,128]{2,1,0:T(8,128)(2,1)}, bf16[4,80,8192]{2,1,0:T(8,128)(2,1)}) custom-call(s32[64]{0:T(128)} %bitcast.31, s32[1]{0:T(128)} %bitcast.3.length_ref, bf16[64,512,128]{2,1,0:T(8,128)(2,1)} %bitcast.19, bf16[64,512,128]{2,1,0:T(8,128)(2,1)} %bitcast.20, ...), custom_call_target="tpu_custom_call", output_to_operand_aliasing={{0}: (10, {}), {1}: (11, {})} | custom-call | bytes 12582912 | tf_op jit(solution)/shard_map/prepare/pallas_call | solution.py:178
  47.1 1.6 %collective-permute-start.15 = (bf16[128,1024]{1,0:T(8,128)(2,1)S(1)}, bf16[128,1024]{1,0:T(8,128)(2,1)S(1)}, u32[]{:S(2)}, u32[]{:S(2)}) collective-permute-start(bf16[128,1024]{1,0:T(8,128)(2,1)S(1)} %collective-permute-done.13.refs_4_), channel_id=1, source_target_pairs={{8,0},{10,2},{16,8},{18,10},{24,16},{26,18},{28,24},{30,26},{20,28... | collective-permute-start | bytes 786440 | tf_op jit(solution)/shard_map/ppermute | solution.py:108
  49.2 1.6 %collective-permute-start.20 = (bf16[1024,128]{1,0:T(8,128)(2,1)S(1)}, bf16[1024,128]{1,0:T(8,128)(2,1)S(1)}, u32[]{:S(2)}, u32[]{:S(2)}) collective-permute-start(bf16[1024,128]{1,0:T(8,128)(2,1)S(1)} %copy-done.2), channel_id=1, source_target_pairs={{8,0},{10,2},{16,8},{18,10},{24,16},{26,18},{28,24},{30,26},{20,28... | collective-permute-start | bytes 786440 | tf_op jit(solution)/shard_map/ppermute | solution.py:108
  50.8 0.8 multiply_sine_fusion
  51.7 0.9 copy-done.18
  52.6 5.1 %project.2 = (bf16[2,2,128,512]{3,2,1,0:T(8,128)(2,1)}, bf16[256,2048]{1,0:T(8,128)(2,1)}) custom-call(s32[1]{0:T(128)} %bitcast.1.device_ref.refs_0_, s32[16,16]{1,0:T(8,128)} %constant.21.clone.order_ref.refs_1_, s32[1]{0:T(128)} %bitcast.refs_0_.tile_ref, f32[1,2048]{1,0:T(1,128)} %bitcast.29, bf16[128,2048]{1,0:T(8,128)(2,1)} %refs_2_.1, ...), custom_call_target="tpu_custom_call" | custom-call | flops 536870912 | bytes 2097152 | tf_op jit(solution)/shard_map/project/pallas_call | solution.py:293
  57.7 1.5 collective-permute-start.16
  59.2 1.8 %collective-permute-done.19.refs_1_.refs_7_.refs_10_ = bf16[1024,128]{1,0:T(8,128)(2,1)S(1)} collective-permute-done((bf16[1024,128]{1,0:T(8,128)(2,1)S(1)}, bf16[1024,128]{1,0:T(8,128)(2,1)S(1)}, u32[]{:S(2)}, u32[]{:S(2)}) %collective-permute-start.19) | collective-permute-done | bytes 262176 | tf_op jit(solution)/shard_map/ppermute | solution.py:108
  61.0 1.0 collective-permute-done.20.refs_2_.refs_8_.refs_11_
  62.4 1.6 %collective-permute-start.22 = (bf16[1024,128]{1,0:T(8,128)(2,1)S(1)}, bf16[1024,128]{1,0:T(8,128)(2,1)S(1)}, u32[]{:S(2)}, u32[]{:S(2)}) collective-permute-start(bf16[1024,128]{1,0:T(8,128)(2,1)S(1)} %collective-permute-done.20.refs_2_.refs_8_.refs_11_), channel_id=1, source_target_pairs={{8,0},{10,2},{16,8},{18,10},{24,16},{26,18},{28,24},{30,26},{20,28... | collective-permute-start | bytes 786440 | tf_op jit(solution)/shard_map/ppermute | solution.py:108
  64.0 13.7 %attend.4 = (f32[2,80,512]{2,1,0:T(8,128)}, s32[1]{0:T(128)}) custom-call(s32[1]{0:T(128)} %bitcast.3.length_ref, s32[1]{0:T(128)S(6)} %copy.18.span_ref, s32[1]{0:T(128)} %bitcast.2.tile_ref, bf16[4,8192,128]{2,1,0:T(8,128)(2,1)} %get-tuple-element.54.keys_hbm, bf16[4,80,8192]{2,1,0:T(8,128)(2,1)} %get-tuple-element.55.values_hbm, ...), custom_call_target="tpu_custom_call" | custom-call | flops 17179869184 | bytes 8388608 | tf_op jit(solution)/shard_map/attend/pallas_call | solution.py:456
  77.7 2.7 %assemble.4 = bf16[896,1024]{1,0:T(8,128)(2,1)} custom-call(bf16[128,1024]{1,0:T(8,128)(2,1)} %copy-done.1, bf16[128,1024]{1,0:T(8,128)(2,1)} %copy-done.11, bf16[128,1024]{1,0:T(8,128)(2,1)} %copy-done.12, bf16[128,1024]{1,0:T(8,128)(2,1)} %copy-done.13, bf16[128,1024]{1,0:T(8,128)(2,1)} %copy-done.14, bf16[128,1024]{1,0:T(8,128)(2,1)} %copy-done.15, ...), custom_call_target="tpu_custom_call" | custom-call | bytes 3670016 | tf_op jit(solution)/shard_map/assemble/pallas_call | solution.py:87
  81.1 2.0 %collective-permute-start.24 = (bf16[1024,128]{1,0:T(8,128)(2,1)S(1)}, bf16[1024,128]{1,0:T(8,128)(2,1)S(1)}, u32[]{:S(2)}, u32[]{:S(2)}) collective-permute-start(bf16[1024,128]{1,0:T(8,128)(2,1)S(1)} %collective-permute-done.22.refs_4_.refs_10_.refs_13_), channel_id=1, source_target_pairs={{8,0},{10,2},{16,8},{18,10},{24,16},{26,18},{28,24},{30,26},{20,28... | collective-permute-start | bytes 786440 | tf_op jit(solution)/shard_map/ppermute | solution.py:108
  83.1 13.8 %attend.5 = (f32[2,80,512]{2,1,0:T(8,128)}, s32[1]{0:T(128)}) custom-call(s32[1]{0:T(128)} %get-tuple-element.58.length_ref, s32[1]{0:T(128)S(6)} %copy.18.span_ref, s32[1]{0:T(128)} %bitcast.refs_0_.tile_ref, bf16[4,8192,128]{2,1,0:T(8,128)(2,1)} %get-tuple-element.54.keys_hbm, bf16[4,80,8192]{2,1,0:T(8,128)(2,1)} %get-tuple-element.55.values_hbm, ...), custom_call_target="tpu_custom_call" | custom-call | flops 17179869184 | bytes 8388608 | tf_op jit(solution)/shard_map/attend/pallas_call | solution.py:456
  97.0 0.6 copy-done.7
  97.7 2.7 %assemble.5 = bf16[7168,128]{1,0:T(8,128)(2,1)} custom-call(bf16[1024,128]{1,0:T(8,128)(2,1)} %refs_9_.1, bf16[1024,128]{1,0:T(8,128)(2,1)} %copy-done.3, bf16[1024,128]{1,0:T(8,128)(2,1)} %copy-done.4, bf16[1024,128]{1,0:T(8,128)(2,1)} %copy-done.5, bf16[1024,128]{1,0:T(8,128)(2,1)} %copy-done.6, bf16[1024,128]{1,0:T(8,128)(2,1)} %copy-done.7, ...), custom_call_target="tpu_custom_call" | custom-call | bytes 3670016 | tf_op jit(solution)/shard_map/assemble/pallas_call | solution.py:87
  100.6 1.2 copy-done.9
  101.8 6.4 %project.3 = (bf16[2,2,128,512]{3,2,1,0:T(8,128)(2,1)}, bf16[4,256,128]{2,1,0:T(8,128)(2,1)}, bf16[4,80,256]{2,1,0:T(8,128)(2,1)}) custom-call(s32[1]{0:T(128)} %bitcast.1.device_ref.refs_0_, s32[16,16]{1,0:T(8,128)} %constant.21.clone.order_ref.refs_1_, bf16[128,1024]{1,0:T(8,128)(2,1)} %copy-done.1, bf16[128,1024]{1,0:T(8,128)(2,1)} %copy-done.11, ...), custom_call_target="tpu_custom_call" | custom-call | flops 1073741824 | bytes 4194304 | tf_op jit(solution)/shard_map/project/pallas_call | solution.py:293
  108.3 13.9 %attend.6 = (f32[2,80,512]{2,1,0:T(8,128)}, s32[1]{0:T(128)}) custom-call(s32[1]{0:T(128)} %get-tuple-element.59.length_ref, s32[1]{0:T(128)S(6)} %copy.18.span_ref, s32[1]{0:T(128)} %bitcast.2.tile_ref, bf16[4,8192,128]{2,1,0:T(8,128)(2,1)} %get-tuple-element.54.keys_hbm, bf16[4,80,8192]{2,1,0:T(8,128)(2,1)} %get-tuple-element.55.values_hbm, ...), custom_call_target="tpu_custom_call" | custom-call | flops 17179869184 | bytes 8388608 | tf_op jit(solution)/shard_map/attend/pallas_call | solution.py:456
  122.3 1.7 %collective-permute-done.27.refs_15_.refs_18_ = bf16[1024,128]{1,0:T(8,128)(2,1)S(1)} collective-permute-done((bf16[1024,128]{1,0:T(8,128)(2,1)}, bf16[1024,128]{1,0:T(8,128)(2,1)S(1)}, u32[]{:S(2)}, u32[]{:S(2)}) %collective-permute-start.27) | collective-permute-done | bytes 262176 | tf_op jit(solution)/shard_map/ppermute | solution.py:108
  124.0 0.7 copy-done.17
  124.7 0.6 copy-done
  125.4 5.8 %finish.2 = (bf16[16,128,128]{2,1,0:T(8,128)(2,1)}, s32[1]{0:T(128)}) custom-call(s32[1]{0:T(128)S(6)} %copy.18.span_ref, s32[1]{0:T(128)} %bitcast.2.tile_ref, f32[2,80,512]{2,1,0:T(8,128)} %get-tuple-element.57.refs_0_, f32[2,80,512]{2,1,0:T(8,128)} %get-tuple-element.75.refs_1_, bf16[2,2,128,512]{3,2,1,0:T(8,128)(2,1)} %get-tuple-element.56.queries_hbm.refs_2_.refs_5_, ...), custom_call_target="tpu_custom_call" | custom-call | flops 536870912 | bytes 4194304 | tf_op jit(solution)/shard_map/finish/pallas_call | solution.py:587
  131.2 0.6 collective-permute-start.28
  133.0 13.1 %attend.7 = (f32[2,80,512]{2,1,0:T(8,128)}, s32[1]{0:T(128)}) custom-call(s32[1]{0:T(128)S(6)} %add.15.length_ref, s32[1]{0:T(128)S(6)} %copy.18.span_ref, s32[1]{0:T(128)} %bitcast.refs_0_.tile_ref, bf16[4,8192,128]{2,1,0:T(8,128)(2,1)} %get-tuple-element.54.keys_hbm, bf16[4,80,8192]{2,1,0:T(8,128)(2,1)} %get-tuple-element.55.values_hbm, ...), custom_call_target="tpu_custom_call" | custom-call | flops 17179869184 | bytes 8388608 | tf_op jit(solution)/shard_map/attend/pallas_call | solution.py:456
  146.2 0.8 copy-done.25
  147.0 6.8 %finish.3 = (bf16[128,2048]{1,0:T(8,128)(2,1)}, s32[1]{0:T(128)}) custom-call(s32[1]{0:T(128)S(6)} %copy.18.span_ref, s32[1]{0:T(128)} %bitcast.refs_0_.tile_ref, s32[1]{0:T(128)} %bitcast.1.device_ref.refs_0_, s32[16,16]{1,0:T(8,128)} %constant.21.clone.order_ref.refs_1_, bf16[16,128,128]{2,1,0:T(8,128)(2,1)} %copy-done.25, ...), custom_call_target="tpu_custom_call" | custom-call | flops 536870912 | bytes 4194304 | tf_op jit(solution)/shard_map/finish/pallas_call | solution.py:587
  (88 shorter events, 3.6 us)
Async XLA Ops:
  1.0 16.8 %copy-start.10 = (bf16[128,512]{1,0:T(8,128)(2,1)}, bf16[128,512]{1,0:T(8,128)(2,1)S(1)}, u32[]{:S(2)}) copy-start(bf16[128,512]{1,0:T(8,128)(2,1)S(1)} %get-tuple-element.100.refs_0_.refs_4_) | copy-start | bytes 393220
  1.0 5.3 %collective-permute-start.1 = (bf16[128,512]{1,0:T(8,128)(2,1)S(1)}, bf16[128,512]{1,0:T(8,128)(2,1)S(1)}, u32[]{:S(2)}, u32[]{:S(2)}) collective-permute-start(bf16[128,512]{1,0:T(8,128)(2,1)S(1)} %get-tuple-element.100.refs_0_.refs_4_), channel_id=1, source_target_pairs={{0,8},{2,10},{8,16},{10,18},{16,24},{18,26},{24,28},{26,30},{28,20... | collective-permute-start | bytes 393224 | tf_op jit(solution)/shard_map/ppermute | solution.py:108
  2.6 5.2 %collective-permute-start.2 = (bf16[128,512]{1,0:T(8,128)(2,1)S(1)}, bf16[128,512]{1,0:T(8,128)(2,1)S(1)}, u32[]{:S(2)}, u32[]{:S(2)}) collective-permute-start(bf16[128,512]{1,0:T(8,128)(2,1)S(1)} %get-tuple-element.100.refs_0_.refs_4_), channel_id=1, source_target_pairs={{8,0},{10,2},{16,8},{18,10},{24,16},{26,18},{28,24},{30,26},{20,28... | collective-permute-start | bytes 393224 | tf_op jit(solution)/shard_map/ppermute | solution.py:108
  6.3 11.5 %copy-start.19 = (bf16[128,512]{1,0:T(8,128)(2,1)}, bf16[128,512]{1,0:T(8,128)(2,1)S(1)}, u32[]{:S(2)}) copy-start(bf16[128,512]{1,0:T(8,128)(2,1)S(1)} %collective-permute-done.1.refs_1_.refs_5_) | copy-start | bytes 393220
  6.3 5.0 %collective-permute-start.3 = (bf16[128,512]{1,0:T(8,128)(2,1)S(1)}, bf16[128,512]{1,0:T(8,128)(2,1)S(1)}, u32[]{:S(2)}, u32[]{:S(2)}) collective-permute-start(bf16[128,512]{1,0:T(8,128)(2,1)S(1)} %collective-permute-done.1.refs_1_.refs_5_), channel_id=1, source_target_pairs={{0,8},{2,10},{8,16},{10,18},{16,24},{18,26},{24,28},{26,30},{28,20... | collective-permute-start | bytes 393224 | tf_op jit(solution)/shard_map/ppermute | solution.py:108
  7.8 9.9 %copy-start.20 = (bf16[128,512]{1,0:T(8,128)(2,1)}, bf16[128,512]{1,0:T(8,128)(2,1)S(1)}, u32[]{:S(2)}) copy-start(bf16[128,512]{1,0:T(8,128)(2,1)S(1)} %collective-permute-done.2.refs_2_.refs_6_) | copy-start | bytes 393220
  7.8 5.0 %collective-permute-start.4 = (bf16[128,512]{1,0:T(8,128)(2,1)S(1)}, bf16[128,512]{1,0:T(8,128)(2,1)S(1)}, u32[]{:S(2)}, u32[]{:S(2)}) collective-permute-start(bf16[128,512]{1,0:T(8,128)(2,1)S(1)} %collective-permute-done.2.refs_2_.refs_6_), channel_id=1, source_target_pairs={{8,0},{10,2},{16,8},{18,10},{24,16},{26,18},{28,24},{30,26},{20,28... | collective-permute-start | bytes 393224 | tf_op jit(solution)/shard_map/ppermute | solution.py:108
  11.3 6.5 %copy-start.21 = (bf16[128,512]{1,0:T(8,128)(2,1)}, bf16[128,512]{1,0:T(8,128)(2,1)S(1)}, u32[]{:S(2)}) copy-start(bf16[128,512]{1,0:T(8,128)(2,1)S(1)} %collective-permute-done.3.refs_3_.refs_7_) | copy-start | bytes 393220
  11.3 5.0 %collective-permute-start.5 = (bf16[128,512]{1,0:T(8,128)(2,1)S(1)}, bf16[128,512]{1,0:T(8,128)(2,1)S(1)}, u32[]{:S(2)}, u32[]{:S(2)}) collective-permute-start(bf16[128,512]{1,0:T(8,128)(2,1)S(1)} %collective-permute-done.3.refs_3_.refs_7_), channel_id=1, source_target_pairs={{0,8},{2,10},{8,16},{10,18},{16,24},{18,26},{24,28},{26,30},{28,20... | collective-permute-start | bytes 393224 | tf_op jit(solution)/shard_map/ppermute | solution.py:108
  12.8 5.0 %copy-start.22 = (bf16[128,512]{1,0:T(8,128)(2,1)}, bf16[128,512]{1,0:T(8,128)(2,1)S(1)}, u32[]{:S(2)}) copy-start(bf16[128,512]{1,0:T(8,128)(2,1)S(1)} %collective-permute-done.4.refs_4_.refs_8_) | copy-start | bytes 393220
  12.8 5.0 %collective-permute-start.6 = (bf16[128,512]{1,0:T(8,128)(2,1)S(1)}, bf16[128,512]{1,0:T(8,128)(2,1)S(1)}, u32[]{:S(2)}, u32[]{:S(2)}) collective-permute-start(bf16[128,512]{1,0:T(8,128)(2,1)S(1)} %collective-permute-done.4.refs_4_.refs_8_), channel_id=1, source_target_pairs={{8,0},{10,2},{16,8},{18,10},{24,16},{26,18},{28,24},{30,26},{20,28... | collective-permute-start | bytes 393224 | tf_op jit(solution)/shard_map/ppermute | solution.py:108
  20.7 30.9 %collective-permute-start.8 = (bf16[896,512]{1,0:T(8,128)(2,1)}, bf16[896,512]{1,0:T(8,128)(2,1)S(1)}, u32[]{:S(2)}, u32[]{:S(2)}) collective-permute-start(bf16[896,512]{1,0:T(8,128)(2,1)} %assemble.3), channel_id=1, source_target_pairs={{0,2},{2,0},{4,6},{6,4},{8,10},{10,8},{12,14},{14,12},{16,18},{18,... | collective-permute-start | bytes 2752520 | tf_op jit(solution)/shard_map/ppermute | solution.py:108
  21.7 13.4 %copy-start.1 = (bf16[128,1024]{1,0:T(8,128)(2,1)}, bf16[128,1024]{1,0:T(8,128)(2,1)S(1)}, u32[]{:S(2)}) copy-start(bf16[128,1024]{1,0:T(8,128)(2,1)S(1)} %pad_maximum_fusion.refs_0_) | copy-start | bytes 786436
  21.7 13.4 %collective-permute-start.10 = (bf16[128,1024]{1,0:T(8,128)(2,1)S(1)}, bf16[128,1024]{1,0:T(8,128)(2,1)S(1)}, u32[]{:S(2)}, u32[]{:S(2)}) collective-permute-start(bf16[128,1024]{1,0:T(8,128)(2,1)S(1)} %pad_maximum_fusion.refs_0_), channel_id=1, source_target_pairs={{0,8},{2,10},{8,16},{10,18},{16,24},{18,26},{24,28},{26,30},{28,20... | collective-permute-start | bytes 786440 | tf_op jit(solution)/shard_map/ppermute | solution.py:108
  22.4 12.8 %collective-permute-start.11 = (bf16[128,1024]{1,0:T(8,128)(2,1)S(1)}, bf16[128,1024]{1,0:T(8,128)(2,1)S(1)}, u32[]{:S(2)}, u32[]{:S(2)}) collective-permute-start(bf16[128,1024]{1,0:T(8,128)(2,1)S(1)} %pad_maximum_fusion.refs_0_), channel_id=1, source_target_pairs={{8,0},{10,2},{16,8},{18,10},{24,16},{26,18},{28,24},{30,26},{20,28... | collective-permute-start | bytes 786440 | tf_op jit(solution)/shard_map/ppermute | solution.py:108
  23.8 24.9 %collective-permute-start = (bf16[128,2048]{1,0:T(8,128)(2,1)}, bf16[128,2048]{1,0:T(8,128)(2,1)S(1)}, u32[]{:S(2)}, u32[]{:S(2)}) collective-permute-start(bf16[128,2048]{1,0:T(8,128)(2,1)} %refs_2_.1), channel_id=1, source_target_pairs={{0,1},{1,0},{2,3},{3,2},{4,5},{5,4},{6,7},{7,6},{8,9},{9,8},{10,11... | collective-permute-start | bytes 1572872 | tf_op jit(solution)/shard_map/ppermute | solution.py:647
  25.3 11.9 %collective-permute-start.7 = (bf16[128,512]{1,0:T(8,128)(2,1)}, bf16[128,512]{1,0:T(8,128)(2,1)S(1)}, u32[]{:S(2)}, u32[]{:S(2)}) collective-permute-start(bf16[128,512]{1,0:T(8,128)(2,1)} %copy-done.23), channel_id=1, source_target_pairs={{0,8},{2,10},{8,16},{10,18},{16,24},{18,26},{24,28},{26,30},{28,20... | collective-permute-start | bytes 393224 | tf_op jit(solution)/shard_map/ppermute | solution.py:108
  35.1 11.5 %copy-start.11 = (bf16[128,1024]{1,0:T(8,128)(2,1)}, bf16[128,1024]{1,0:T(8,128)(2,1)S(1)}, u32[]{:S(2)}) copy-start(bf16[128,1024]{1,0:T(8,128)(2,1)S(1)} %collective-permute-done.10.refs_1_) | copy-start | bytes 786436
  35.1 11.4 %copy-start.12 = (bf16[128,1024]{1,0:T(8,128)(2,1)}, bf16[128,1024]{1,0:T(8,128)(2,1)S(1)}, u32[]{:S(2)}) copy-start(bf16[128,1024]{1,0:T(8,128)(2,1)S(1)} %collective-permute-done.11.refs_2_) | copy-start | bytes 786436
  35.1 11.5 %collective-permute-start.12 = (bf16[128,1024]{1,0:T(8,128)(2,1)S(1)}, bf16[128,1024]{1,0:T(8,128)(2,1)S(1)}, u32[]{:S(2)}, u32[]{:S(2)}) collective-permute-start(bf16[128,1024]{1,0:T(8,128)(2,1)S(1)} %collective-permute-done.10.refs_1_), channel_id=1, source_target_pairs={{0,8},{2,10},{8,16},{10,18},{16,24},{18,26},{24,28},{26,30},{28,20... | collective-permute-start | bytes 786440 | tf_op jit(solution)/shard_map/ppermute | solution.py:108
  35.6 11.0 %collective-permute-start.13 = (bf16[128,1024]{1,0:T(8,128)(2,1)S(1)}, bf16[128,1024]{1,0:T(8,128)(2,1)S(1)}, u32[]{:S(2)}, u32[]{:S(2)}) collective-permute-start(bf16[128,1024]{1,0:T(8,128)(2,1)S(1)} %collective-permute-done.11.refs_2_), channel_id=1, source_target_pairs={{8,0},{10,2},{16,8},{18,10},{24,16},{26,18},{28,24},{30,26},{20,28... | collective-permute-start | bytes 786440 | tf_op jit(solution)/shard_map/ppermute | solution.py:108
  37.2 9.4 %copy-start.27 = (bf16[128,512]{1,0:T(8,128)(2,1)}, bf16[128,512]{1,0:T(8,128)(2,1)S(1)}, u32[]{:S(2)}) copy-start(bf16[128,512]{1,0:T(8,128)(2,1)S(1)} %collective-permute-done.7.refs_11_) | copy-start | bytes 393220
  37.2 12.0 %collective-permute-start.9 = (bf16[128,512]{1,0:T(8,128)(2,1)S(1)}, bf16[128,512]{1,0:T(8,128)(2,1)S(1)}, u32[]{:S(2)}, u32[]{:S(2)}) collective-permute-start(bf16[128,512]{1,0:T(8,128)(2,1)S(1)} %collective-permute-done.7.refs_11_), channel_id=1, source_target_pairs={{0,2},{2,0},{4,6},{6,4},{8,10},{10,8},{12,14},{14,12},{16,18},{18,... | collective-permute-start | bytes 393224 | tf_op jit(solution)/shard_map/ppermute | solution.py:108
  38.5 10.2 %copy-start.2 = (bf16[1024,128]{1,0:T(8,128)(2,1)S(1)}, bf16[1024,128]{1,0:T(8,128)(2,1)}, u32[]{:S(2)}) copy-start(bf16[1024,128]{1,0:T(8,128)(2,1)} %refs_9_.1) | copy-start | bytes 786436
  46.6 31.0 %copy-start.13 = (bf16[128,1024]{1,0:T(8,128)(2,1)}, bf16[128,1024]{1,0:T(8,128)(2,1)S(1)}, u32[]{:S(2)}) copy-start(bf16[128,1024]{1,0:T(8,128)(2,1)S(1)} %collective-permute-done.12.refs_3_) | copy-start | bytes 786436
  46.6 31.0 %copy-start.14 = (bf16[128,1024]{1,0:T(8,128)(2,1)}, bf16[128,1024]{1,0:T(8,128)(2,1)S(1)}, u32[]{:S(2)}) copy-start(bf16[128,1024]{1,0:T(8,128)(2,1)S(1)} %collective-permute-done.13.refs_4_) | copy-start | bytes 786436
  46.6 11.1 %collective-permute-start.14 = (bf16[128,1024]{1,0:T(8,128)(2,1)S(1)}, bf16[128,1024]{1,0:T(8,128)(2,1)S(1)}, u32[]{:S(2)}, u32[]{:S(2)}) collective-permute-start(bf16[128,1024]{1,0:T(8,128)(2,1)S(1)} %collective-permute-done.12.refs_3_), channel_id=1, source_target_pairs={{0,8},{2,10},{8,16},{10,18},{16,24},{18,26},{24,28},{26,30},{28,20... | collective-permute-start | bytes 786440 | tf_op jit(solution)/shard_map/ppermute | solution.py:108
  47.1 10.6 %collective-permute-start.15 = (bf16[128,1024]{1,0:T(8,128)(2,1)S(1)}, bf16[128,1024]{1,0:T(8,128)(2,1)S(1)}, u32[]{:S(2)}, u32[]{:S(2)}) collective-permute-start(bf16[128,1024]{1,0:T(8,128)(2,1)S(1)} %collective-permute-done.13.refs_4_), channel_id=1, source_target_pairs={{8,0},{10,2},{16,8},{18,10},{24,16},{26,18},{28,24},{30,26},{20,28... | collective-permute-start | bytes 786440 | tf_op jit(solution)/shard_map/ppermute | solution.py:108
  48.7 2.9 %copy-start.26 = (bf16[128,2048]{1,0:T(8,128)(2,1)}, bf16[128,2048]{1,0:T(8,128)(2,1)S(1)}, u32[]{:S(2)}) copy-start(bf16[128,2048]{1,0:T(8,128)(2,1)S(1)} %collective-permute-done.refs_3_) | copy-start | bytes 1572868
  48.7 12.3 %collective-permute-start.19 = (bf16[1024,128]{1,0:T(8,128)(2,1)S(1)}, bf16[1024,128]{1,0:T(8,128)(2,1)S(1)}, u32[]{:S(2)}, u32[]{:S(2)}) collective-permute-start(bf16[1024,128]{1,0:T(8,128)(2,1)S(1)} %copy-done.2), channel_id=1, source_target_pairs={{0,8},{2,10},{8,16},{10,18},{16,24},{18,26},{24,28},{26,30},{28,20... | collective-permute-start | bytes 786440 | tf_op jit(solution)/shard_map/ppermute | solution.py:108
  49.2 12.7 %collective-permute-start.20 = (bf16[1024,128]{1,0:T(8,128)(2,1)S(1)}, bf16[1024,128]{1,0:T(8,128)(2,1)S(1)}, u32[]{:S(2)}, u32[]{:S(2)}) collective-permute-start(bf16[1024,128]{1,0:T(8,128)(2,1)S(1)} %copy-done.2), channel_id=1, source_target_pairs={{8,0},{10,2},{16,8},{18,10},{24,16},{26,18},{28,24},{30,26},{20,28... | collective-permute-start | bytes 786440 | tf_op jit(solution)/shard_map/ppermute | solution.py:108
  57.7 20.0 %copy-start.15 = (bf16[128,1024]{1,0:T(8,128)(2,1)}, bf16[128,1024]{1,0:T(8,128)(2,1)S(1)}, u32[]{:S(2)}) copy-start(bf16[128,1024]{1,0:T(8,128)(2,1)S(1)} %collective-permute-done.14.refs_5_) | copy-start | bytes 786436
  57.7 19.9 %copy-start.16 = (bf16[128,1024]{1,0:T(8,128)(2,1)}, bf16[128,1024]{1,0:T(8,128)(2,1)S(1)}, u32[]{:S(2)}) copy-start(bf16[128,1024]{1,0:T(8,128)(2,1)S(1)} %collective-permute-done.15.refs_6_) | copy-start | bytes 786436
  57.7 22.8 %collective-permute-start.16 = (bf16[128,1024]{1,0:T(8,128)(2,1)S(1)}, bf16[128,1024]{1,0:T(8,128)(2,1)}, u32[]{:S(2)}, u32[]{:S(2)}) collective-permute-start(bf16[128,1024]{1,0:T(8,128)(2,1)S(1)} %collective-permute-done.15.refs_6_), channel_id=1, source_target_pairs={{8,0},{10,2},{16,8},{18,10},{24,16},{26,18},{28,24},{30,26},{20,28... | collective-permute-start | bytes 786440 | tf_op jit(solution)/shard_map/ppermute | solution.py:108
  61.0 16.7 %copy-start.3 = (bf16[1024,128]{1,0:T(8,128)(2,1)}, bf16[1024,128]{1,0:T(8,128)(2,1)S(1)}, u32[]{:S(2)}) copy-start(bf16[1024,128]{1,0:T(8,128)(2,1)S(1)} %collective-permute-done.19.refs_1_.refs_7_.refs_10_) | copy-start | bytes 786436
  61.9 15.7 %copy-start.4 = (bf16[1024,128]{1,0:T(8,128)(2,1)}, bf16[1024,128]{1,0:T(8,128)(2,1)S(1)}, u32[]{:S(2)}) copy-start(bf16[1024,128]{1,0:T(8,128)(2,1)S(1)} %collective-permute-done.20.refs_2_.refs_8_.refs_11_) | copy-start | bytes 786436
  61.9 19.1 %collective-permute-start.21 = (bf16[1024,128]{1,0:T(8,128)(2,1)S(1)}, bf16[1024,128]{1,0:T(8,128)(2,1)S(1)}, u32[]{:S(2)}, u32[]{:S(2)}) collective-permute-start(bf16[1024,128]{1,0:T(8,128)(2,1)S(1)} %collective-permute-done.19.refs_1_.refs_7_.refs_10_), channel_id=1, source_target_pairs={{0,8},{2,10},{8,16},{10,18},{16,24},{18,26},{24,28},{26,30},{28,20... | collective-permute-start | bytes 786440 | tf_op jit(solution)/shard_map/ppermute | solution.py:108
  62.4 18.6 %collective-permute-start.22 = (bf16[1024,128]{1,0:T(8,128)(2,1)S(1)}, bf16[1024,128]{1,0:T(8,128)(2,1)S(1)}, u32[]{:S(2)}, u32[]{:S(2)}) collective-permute-start(bf16[1024,128]{1,0:T(8,128)(2,1)S(1)} %collective-permute-done.20.refs_2_.refs_8_.refs_11_), channel_id=1, source_target_pairs={{8,0},{10,2},{16,8},{18,10},{24,16},{26,18},{28,24},{30,26},{20,28... | collective-permute-start | bytes 786440 | tf_op jit(solution)/shard_map/ppermute | solution.py:108
  80.4 20.1 %collective-permute-start.17 = (bf16[896,1024]{1,0:T(8,128)(2,1)}, bf16[896,1024]{1,0:T(8,128)(2,1)S(1)}, u32[]{:S(2)}, u32[]{:S(2)}) collective-permute-start(bf16[896,1024]{1,0:T(8,128)(2,1)} %assemble.4), channel_id=1, source_target_pairs={{0,2},{2,0},{4,6},{6,4},{8,10},{10,8},{12,14},{14,12},{16,18},{18,... | collective-permute-start | bytes 5505032 | tf_op jit(solution)/shard_map/ppermute | solution.py:108
  80.5 20.0 %collective-permute-start.18 = (bf16[128,1024]{1,0:T(8,128)(2,1)}, bf16[128,1024]{1,0:T(8,128)(2,1)}, u32[]{:S(2)}, u32[]{:S(2)}) collective-permute-start(bf16[128,1024]{1,0:T(8,128)(2,1)} %collective-permute-done.16.refs_7_), channel_id=1, source_target_pairs={{0,2},{2,0},{4,6},{6,4},{8,10},{10,8},{12,14},{14,12},{16,18},{18,... | collective-permute-start | bytes 786440 | tf_op jit(solution)/shard_map/ppermute | solution.py:108
  81.0 15.9 %copy-start.5 = (bf16[1024,128]{1,0:T(8,128)(2,1)}, bf16[1024,128]{1,0:T(8,128)(2,1)S(1)}, u32[]{:S(2)}) copy-start(bf16[1024,128]{1,0:T(8,128)(2,1)S(1)} %collective-permute-done.21.refs_3_.refs_9_.refs_12_) | copy-start | bytes 786436
  81.0 15.9 %copy-start.6 = (bf16[1024,128]{1,0:T(8,128)(2,1)}, bf16[1024,128]{1,0:T(8,128)(2,1)S(1)}, u32[]{:S(2)}) copy-start(bf16[1024,128]{1,0:T(8,128)(2,1)S(1)} %collective-permute-done.22.refs_4_.refs_10_.refs_13_) | copy-start | bytes 786436
  81.0 15.9 %collective-permute-start.23 = (bf16[1024,128]{1,0:T(8,128)(2,1)S(1)}, bf16[1024,128]{1,0:T(8,128)(2,1)S(1)}, u32[]{:S(2)}, u32[]{:S(2)}) collective-permute-start(bf16[1024,128]{1,0:T(8,128)(2,1)S(1)} %collective-permute-done.21.refs_3_.refs_9_.refs_12_), channel_id=1, source_target_pairs={{0,8},{2,10},{8,16},{10,18},{16,24},{18,26},{24,28},{26,30},{28,20... | collective-permute-start | bytes 786440 | tf_op jit(solution)/shard_map/ppermute | solution.py:108
  81.1 15.8 %collective-permute-start.24 = (bf16[1024,128]{1,0:T(8,128)(2,1)S(1)}, bf16[1024,128]{1,0:T(8,128)(2,1)S(1)}, u32[]{:S(2)}, u32[]{:S(2)}) collective-permute-start(bf16[1024,128]{1,0:T(8,128)(2,1)S(1)} %collective-permute-done.22.refs_4_.refs_10_.refs_13_), channel_id=1, source_target_pairs={{8,0},{10,2},{16,8},{18,10},{24,16},{26,18},{28,24},{30,26},{20,28... | collective-permute-start | bytes 786440 | tf_op jit(solution)/shard_map/ppermute | solution.py:108
  97.0 25.2 %collective-permute-start.25 = (bf16[1024,128]{1,0:T(8,128)(2,1)S(1)}, bf16[1024,128]{1,0:T(8,128)(2,1)}, u32[]{:S(2)}, u32[]{:S(2)}) collective-permute-start(bf16[1024,128]{1,0:T(8,128)(2,1)S(1)} %collective-permute-done.23.refs_5_.refs_11_.refs_14_), channel_id=1, source_target_pairs={{0,8},{2,10},{8,16},{10,18},{16,24},{18,26},{24,28},{26,30},{28,20... | collective-permute-start | bytes 786440 | tf_op jit(solution)/shard_map/ppermute | solution.py:108
  100.5 23.6 %collective-permute-start.26 = (bf16[7168,128]{1,0:T(8,128)(2,1)}, bf16[7168,128]{1,0:T(8,128)(2,1)S(1)}, u32[]{:S(2)}, u32[]{:S(2)}) collective-permute-start(bf16[7168,128]{1,0:T(8,128)(2,1)} %assemble.5), channel_id=1, source_target_pairs={{0,2},{2,0},{4,6},{6,4},{8,10},{10,8},{12,14},{14,12},{16,18},{18,... | collective-permute-start | bytes 5505032 | tf_op jit(solution)/shard_map/ppermute | solution.py:108
  122.2 1.8 %collective-permute-start.27 = (bf16[1024,128]{1,0:T(8,128)(2,1)}, bf16[1024,128]{1,0:T(8,128)(2,1)S(1)}, u32[]{:S(2)}, u32[]{:S(2)}) collective-permute-start(bf16[1024,128]{1,0:T(8,128)(2,1)} %collective-permute-done.25.refs_13_.refs_16_), channel_id=1, source_target_pairs={{0,2},{2,0},{4,6},{6,4},{8,10},{10,8},{12,14},{14,12},{16,18},{18,... | collective-permute-start | bytes 786440 | tf_op jit(solution)/shard_map/ppermute | solution.py:108
  131.2 15.0 %collective-permute-start.28 = (bf16[16,128,128]{2,1,0:T(8,128)(2,1)}, bf16[16,128,128]{2,1,0:T(8,128)(2,1)S(1)}, u32[]{:S(2)}, u32[]{:S(2)}) collective-permute-start(bf16[16,128,128]{2,1,0:T(8,128)(2,1)} %get-tuple-element.94), channel_id=1, source_target_pairs={{0,1},{1,0},{2,3},{3,2},{4,5},{5,4},{6,7},{7,6},{8,9},{9,8},{10,11... | collective-permute-start | bytes 1572872 | tf_op jit(solution)/shard_map/ppermute | solution.py:717
  (10 other events, 11.1 us)
